TPU v7x, 32 devices: a whole 2x2x4 slice. The times are simulated.
32 devices in a mesh: section: 4 (over y, x), expert: 8 (over z, core).
Axes of the slice: x: 2, y: 2, z: 4, core: 2. Of those that a mesh axis runs over, the one named last changes fastest.
Arguments:
- inputs: bfloat16 [4, 2, 512, 2560], P('section', None, 'expert'), may hold values from -6 to 6
- teacher: bfloat16 [4, 2, 512, 2560], P('section', None, 'expert'), may hold values from -6 to 6
- gate: float32 [4, 2, 512], P('section', None, 'expert'), may hold values from 0.2 to 1
- route: int32 [4, 2, 512], P('section', None, 'expert'), may hold values from 0 to 7, as said below
- slot: int32 [4, 2, 512], P('section', None, 'expert'), may hold values from 0 to 15
- factor: bfloat16 [4, 2560, 768], P('section'), may hold values from -0.125 to 0.125
- cores: bfloat16 [4, 8, 768, 768], P('section', 'expert'), may hold values from -0.21875 to 0.21875
Outputs:
- factor_grad: float32 [4, 2560, 768], P('section', 'expert')
- core_grad: bfloat16 [4, 8, 768, 768], P('section', 'expert')
Inputs may be any that keep to these rules, and one draw needn't show every extreme that they name: Within each layer, micro-batch and aligned block of 64 tokens (those of one device), no two tokens share both route and slot, so an expert takes at most 16 tokens of a block; in every block some expert takes exactly 16.
All inputs are finite; a program needn't handle non-finite values.
Results may differ from a plain program's by a relative error of at most 0.012.
Values may be sent and summed in bfloat16 or wider, within the bound.
No kernel may reach another device: no remote copies, remote signals or barrier semaphores. Data moves between devices by JAX's collectives and lax.ppermute only.
A program may use at most 128 MiB of HBM per device.

v0:
```python
import jax
import jax.numpy as jnp
from jax import lax
from jax.experimental import pallas as pl
from jax.experimental.pallas import tpu as pltpu
from jax.sharding import PartitionSpec as P


def from_behind(value, axis, steps):
    count = lax.axis_size(axis)
    leading, last = (max(0, -steps), min(count, count - steps))
    return lax.ppermute(value, axis, [(source, source + steps) for source in range(leading, last)])


def silu_slope(values):
    sigmoid = jax.nn.sigmoid(values)
    return sigmoid * (1.0 + values * (1.0 - sigmoid))


def times_transposed(left, shared):
    return lax.dot_general(
        left, shared, (((1,), (1,)), ((), ())), preferred_element_type=jnp.float32
    )


def factor_terms(tokens_flat, proj_flat, mixed_flat, hidden_flat):

    def factor_rows(start, count):
        first_term = lax.dot_general(
            tokens_flat, proj_flat, (((0,), (0,)), ((), ())), preferred_element_type=jnp.float32
        )
        second_term = lax.dot_general(
            mixed_flat, hidden_flat, (((0,), (0,)), ((), ())), preferred_element_type=jnp.float32
        )
        return first_term + second_term

    return factor_rows


def store_slice(store, fresh, picked, usable):
    former = lax.dynamic_index_in_dim(store, picked, 0, keepdims=False)
    kept = jnp.where(usable, fresh, former)
    return lax.dynamic_update_index_in_dim(store, kept, picked, 0)


def general_plan(inputs, teacher, gate, route, slot, factor, cores):
    tokens_all = inputs[0]
    targets_all = teacher[0]
    weights_all = gate[0]
    shared = factor[0]
    blocks = cores[0]
    micro_count, token_count, channels = tokens_all.shape
    ranks = shared.shape[1]
    local_experts = blocks.shape[0]
    expert_devices = lax.axis_size("expert")
    capacity = max(2, 2 * token_count // (local_experts * expert_devices))
    slot_count = local_experts * expert_devices * capacity
    places_all = route[0] * capacity + slot[0]
    micro_range = jnp.arange(micro_count, dtype=jnp.int32)[:, None]
    token_proj = jnp.dot(
        tokens_all.reshape(-1, channels), shared, preferred_element_type=jnp.float32
    ).astype(jnp.bfloat16)
    token_proj = token_proj.reshape(micro_count, token_count, ranks)
    proj_slots = (
        jnp.zeros((micro_count, slot_count, ranks), jnp.bfloat16)
        .at[micro_range, places_all]
        .set(token_proj)
    )
    projected = lax.all_to_all(proj_slots, "expert", split_axis=1, concat_axis=1, tiled=True)
    projected = projected.reshape(micro_count, expert_devices, local_experts, capacity, ranks)
    pre = jnp.einsum("mnecr,erk->mneck", projected, blocks, preferred_element_type=jnp.float32)
    active = jax.nn.silu(pre).astype(jnp.bfloat16)
    returned = lax.all_to_all(
        active.reshape(micro_count, slot_count, ranks),
        "expert",
        split_axis=1,
        concat_axis=1,
        tiled=True,
    )
    hidden = jnp.take_along_axis(returned, places_all[:, :, None], axis=1)
    mixed = times_transposed(hidden.reshape(-1, ranks), shared).reshape(
        micro_count, token_count, channels
    )
    output = tokens_all.astype(jnp.float32) + weights_all[:, :, None] * mixed
    errors = output - targets_all.astype(jnp.float32)
    section_count = lax.axis_size("section")
    section_here = lax.axis_index("section")
    incoming = jnp.zeros((token_count, channels), jnp.bfloat16)
    mixed_store = jnp.zeros((micro_count, token_count, channels), jnp.bfloat16)
    proj_store = jnp.zeros((micro_count, token_count, ranks), jnp.bfloat16)
    pre_store = jnp.zeros(
        (micro_count, expert_devices, local_experts, capacity, ranks), jnp.bfloat16
    )
    turn_total = micro_count + section_count - 1
    for turn_index in range(turn_total):
        micro_now = turn_index - (section_count - 1 - section_here)
        usable = jnp.logical_and(micro_now >= 0, micro_now < micro_count)
        picked = jnp.clip(micro_now, 0, micro_count - 1)
        grad_out = lax.dynamic_index_in_dim(errors, picked, 0, keepdims=False) + incoming.astype(
            jnp.float32
        )
        weight_now = lax.dynamic_index_in_dim(weights_all, picked, 0, keepdims=False)
        places = lax.dynamic_index_in_dim(places_all, picked, 0, keepdims=False)
        grad_mixed = (weight_now[:, None] * grad_out).astype(jnp.bfloat16)
        grad_hidden = jnp.dot(grad_mixed, shared, preferred_element_type=jnp.float32).astype(
            jnp.bfloat16
        )
        grad_slots = jnp.zeros((slot_count, ranks), jnp.bfloat16).at[places].set(grad_hidden)
        grad_recv = lax.all_to_all(grad_slots, "expert", split_axis=0, concat_axis=0, tiled=True)
        grad_recv = grad_recv.reshape(expert_devices, local_experts, capacity, ranks)
        pre_now = lax.dynamic_index_in_dim(pre, picked, 0, keepdims=False)
        grad_pre = (grad_recv.astype(jnp.float32) * silu_slope(pre_now)).astype(jnp.bfloat16)
        grad_routed = jnp.einsum(
            "neck,erk->necr", grad_pre, blocks, preferred_element_type=jnp.float32
        ).astype(jnp.bfloat16)
        grad_home = lax.all_to_all(
            grad_routed.reshape(slot_count, ranks),
            "expert",
            split_axis=0,
            concat_axis=0,
            tiled=True,
        )
        grad_proj = grad_home[places]
        grad_in = (grad_out + times_transposed(grad_proj, shared)).astype(jnp.bfloat16)
        if turn_index + 1 < turn_total:
            incoming = from_behind(grad_in, "section", -1)
        mixed_store = store_slice(mixed_store, grad_mixed, picked, usable)
        proj_store = store_slice(proj_store, grad_proj, picked, usable)
        pre_store = store_slice(pre_store, grad_pre, picked, usable)
    core_total = jnp.einsum(
        "mnecr,mneck->erk", projected, pre_store, preferred_element_type=jnp.float32
    )
    all_rows = factor_terms(
        tokens_all.reshape(-1, channels),
        proj_store.reshape(-1, ranks),
        mixed_store.reshape(-1, channels),
        hidden.reshape(-1, ranks),
    )
    factor_share = lax.psum_scatter(
        all_rows(jnp.int32(0), channels // expert_devices * lax.axis_size("expert")),
        "expert",
        scatter_dimension=0,
        tiled=True,
    )
    return (factor_share[None], core_total.astype(jnp.bfloat16)[None])


CORES = 2
CHIPS = 4
LAYERS = 4
ROOM = 24 * 2**20


def dot(left, right):
    return jnp.dot(left, right, preferred_element_type=jnp.float32)


def dot_first(left, right):
    return lax.dot_general(
        left, right, (((0,), (0,)), ((), ())), preferred_element_type=jnp.float32
    )


def on_chips(value, pairs):
    perm = [
        (CORES * source + core, CORES * target + core)
        for source, target in pairs
        for core in range(CORES)
    ]
    return lax.ppermute(value, "expert", perm)


def swap_cores(value):
    count = lax.axis_size("expert")
    return lax.ppermute(value, "expert", [(index, index ^ 1) for index in range(count)])


def between_layers(value, pairs):
    return lax.ppermute(value, "section", pairs)


def gather_cores(core, middle):
    beside = on_chips(core, [(0, 1), (1, 0), (2, 3), (3, 2)])
    across = on_chips(core, [(1, 2), (2, 1)])
    far_across = on_chips(beside, [(1, 2), (2, 1)])
    outward = on_chips(across, [(1, 0), (2, 3)])
    far_outward = on_chips(far_across, [(1, 0), (2, 3)])
    second = jnp.where(middle, across, outward)
    third = jnp.where(middle, far_across, far_outward)
    held = [core, beside, second, third]
    return held + [swap_cores(piece) for piece in held]


def held_chips(chip, middle):
    near, far = chip ^ 3, chip ^ 2
    return [chip, chip ^ 1, jnp.where(middle, near, far), jnp.where(middle, far, near)]


def across_chips(value, step):
    return on_chips(value, [(chip, chip ^ step) for chip in range(CHIPS)])


def gather_rows(rows):
    held = [rows] + [across_chips(rows, step) for step in range(1, CHIPS)]
    return held + [swap_cores(piece) for piece in held]


def chip_blocks(wide, chip, core):
    count = wide.shape[0] // (CHIPS * CORES)
    blocks = [
        lax.dynamic_slice_in_dim(wide, (CORES * (chip ^ step) + core) * count, count, 0)
        for step in range(CHIPS)
    ]
    return jnp.concatenate(blocks, axis=0)


def chip_columns(wide, chip, core):
    theirs = swap_cores(chip_blocks(wide, chip, 1 - core))
    return jnp.concatenate([chip_blocks(wide, chip, core), theirs], axis=1)


def both_cores(partial):
    rows = partial.shape[0] // CORES
    return partial[:rows] + swap_cores(partial[rows:])


def gram_pair(left, right):
    partial = dot_first(left, right).astype(jnp.bfloat16)
    return partial, swap_cores(partial)


def gram_sum(pair):
    return (pair[0].astype(jnp.float32) + pair[1].astype(jnp.float32)).astype(jnp.bfloat16)


def expert_ids(chips, core):
    return jnp.stack(
        [CORES * chip + core for chip in chips] + [CORES * chip + 1 - core for chip in chips]
    ).astype(jnp.int32)


def routed_product(rows, route, ids_ref, core_refs, transposed):
    dims = (((1,), (1 if transposed else 0,)), ((), ()))
    total = None
    for place, core_ref in enumerate(core_refs):
        chosen = jnp.where(route == ids_ref[place], rows, jnp.zeros_like(rows))
        term = lax.dot_general(
            chosen, core_ref[...], dims, preferred_element_type=jnp.float32
        )
        total = term if total is None else total + term
    return total


def backward_rows(score, weight, slope, route, ids_ref, core_refs):
    grad_hidden = (weight * score).astype(jnp.bfloat16)
    grad_pre = (grad_hidden.astype(jnp.float32) * slope).astype(jnp.bfloat16)
    grad_proj = routed_product(grad_pre, route, ids_ref, core_refs, True)
    return grad_pre, grad_proj.astype(jnp.bfloat16)


def first_kernel(ids_ref, proj_ref, route_ref, weight_ref, own_ref, gram_ref, *refs):
    count = len(refs) - 6
    core_refs = refs[:count]
    hidden_ref, scaled_ref, slope_ref, score_ref, grad_ref, chain_ref = refs[count:]
    route = route_ref[...]
    weight = weight_ref[...]
    pre = routed_product(proj_ref[...], route, ids_ref, core_refs, False)
    sigmoid = 1.0 / (1.0 + jnp.exp(-pre))
    hidden = (pre * sigmoid).astype(jnp.bfloat16)
    slope = sigmoid * (1.0 + pre * (1.0 - sigmoid))
    scaled = (weight * hidden.astype(jnp.float32)).astype(jnp.bfloat16)
    score = own_ref[...] + dot(scaled, gram_ref[...])
    hidden_ref[...] = hidden
    scaled_ref[...] = scaled
    slope_ref[...] = slope
    score_ref[...] = score
    grad_pre, grad_proj = backward_rows(score, weight, slope, route, ids_ref, core_refs)
    grad_ref[...] = grad_pre
    chain_ref[...] = (scaled.astype(jnp.float32) + grad_proj.astype(jnp.float32)).astype(
        jnp.bfloat16
    )


def turn_kernel(terms, ids_ref, route_ref, weight_ref, scaled_ref, slope_ref, score_ref, *refs):
    core_refs = refs[2 * terms : len(refs) - 4]
    next_ref, grad_ref, proj_ref, chain_ref = refs[len(refs) - 4 :]
    score = score_ref[...]
    for term in range(terms):
        score = score + dot(refs[2 * term][...], refs[2 * term + 1][...])
    next_ref[...] = score
    grad_pre, grad_proj = backward_rows(
        score, weight_ref[...], slope_ref[...], route_ref[...], ids_ref, core_refs
    )
    grad_ref[...] = grad_pre
    proj_ref[...] = grad_proj
    chain_ref[...] = (scaled_ref[...].astype(jnp.float32) + grad_proj.astype(jnp.float32)).astype(
        jnp.bfloat16
    )


def call_rows(body, outs, scalars, arrays, flops):
    in_bytes = sum(array.size * array.dtype.itemsize for array in arrays)
    return pl.pallas_call(
        body,
        out_shape=[jax.ShapeDtypeStruct(shape, kind) for shape, kind in outs],
        in_specs=[pl.BlockSpec(memory_space=pltpu.SMEM)]
        + [pl.BlockSpec(memory_space=pltpu.VMEM)] * len(arrays),
        out_specs=[pl.BlockSpec(memory_space=pltpu.VMEM)] * len(outs),
        compiler_params=pltpu.CompilerParams(vmem_limit_bytes=ROOM),
        cost_estimate=pl.CostEstimate(flops=flops, bytes_accessed=in_bytes, transcendentals=0),
    )(scalars, *arrays)


def spread_kernel(terms, last, base_ref, *refs):
    total = base_ref[...].astype(jnp.float32)
    for term in range(terms):
        half_ref, near_ref, far_ref = refs[3 * term : 3 * term + 3]
        values = jnp.concatenate([near_ref[...], far_ref[...]], axis=0)
        total = total + times_transposed(half_ref[...], values)
    outs = refs[3 * terms :]
    if not last:
        outs[0][...] = total
        return
    count = total.shape[0] // CHIPS
    for step in range(CHIPS):
        outs[step][...] = total[step * count : (step + 1) * count].astype(jnp.bfloat16)


def spread(base, terms, last):
    arrays = [base] + [array for term in terms for array in term]
    height, width = base.shape
    if last:
        outs = [jax.ShapeDtypeStruct((height // CHIPS, width), jnp.bfloat16)] * CHIPS
    else:
        outs = [jax.ShapeDtypeStruct((height, width), jnp.float32)]

    def body(*refs):
        spread_kernel(len(terms), last, *refs)

    return pl.pallas_call(
        body,
        out_shape=outs,
        in_specs=[pl.BlockSpec(memory_space=pltpu.VMEM)] * len(arrays),
        out_specs=[pl.BlockSpec(memory_space=pltpu.VMEM)] * len(outs),
        compiler_params=pltpu.CompilerParams(vmem_limit_bytes=ROOM),
        cost_estimate=pl.CostEstimate(
            flops=2 * height * width * terms[0][0].shape[1] * len(terms),
            bytes_accessed=sum(array.size * array.dtype.itemsize for array in arrays),
            transcendentals=0,
        ),
    )(*arrays)


def pair_products(block_ref, near_ref, far_ref):
    return dot(block_ref[...], jnp.concatenate([near_ref[...], far_ref[...]], axis=0))


def factor_kernel(start, *refs):
    total_ref = refs[-1]
    total = refs[0][...] if start else None
    refs = refs[1:-1] if start else refs[:-1]
    for step in range(CHIPS):
        term = pair_products(refs[step], refs[CHIPS + step], refs[2 * CHIPS + step])
        total = term if total is None else total + term
    total_ref[...] = total


def factor_rows(total, blocks, pieces):
    arrays = ([] if total is None else [total]) + blocks + pieces
    count, ranks = blocks[0].shape[0], pieces[0].shape[1]

    def body(*refs):
        factor_kernel(total is not None, *refs)

    return pl.pallas_call(
        body,
        out_shape=jax.ShapeDtypeStruct((count, ranks), jnp.float32),
        in_specs=[pl.BlockSpec(memory_space=pltpu.VMEM)] * len(arrays),
        out_specs=pl.BlockSpec(memory_space=pltpu.VMEM),
        compiler_params=pltpu.CompilerParams(vmem_limit_bytes=ROOM),
        cost_estimate=pl.CostEstimate(
            flops=2 * count * ranks * len(pieces) * pieces[0].shape[0],
            bytes_accessed=sum(array.size * array.dtype.itemsize for array in arrays),
            transcendentals=0,
        ),
    )(*arrays)


def after(value, earlier):
    return lax.optimization_barrier((value, earlier))[0]


def gathered_plan(inputs, teacher, gate, route, slot, factor, cores):
    bf16, f32 = jnp.bfloat16, jnp.float32
    shared = factor[0]
    channels, ranks = shared.shape
    devices = lax.axis_size("expert")
    micro_count, token_count = route.shape[1:]
    rows = micro_count * token_count
    here = lax.axis_index("expert")
    chip, core = here // CORES, here % CORES
    middle = jnp.logical_or(chip == 1, chip == 2)
    tokens = inputs[0].reshape(rows, channels)
    weight = gate[0].reshape(rows, 1)
    chosen = route[0].reshape(rows, 1)

    pieces = gather_cores(cores[0, 0], middle)
    ids = expert_ids(held_chips(chip, middle), core)

    down = [(3, 2), (1, 0)]
    two_down = [(3, 1), (2, 0)]
    crossed = [(0, 1), (1, 0)]
    own_half = chip_blocks(shared, chip, core)
    half_down = between_layers(own_half, down)
    half_two = between_layers(own_half, two_down)
    half_cross = between_layers(half_two, crossed)
    difference = tokens.astype(f32) - teacher[0].reshape(rows, channels).astype(f32)
    difference = chip_columns(difference.astype(bf16).T, chip, core)
    step_down = between_layers(difference, down)
    step_two = between_layers(difference, two_down)
    step_cross = between_layers(step_two, crossed)

    capacity = max(2, 2 * token_count // devices)
    slots = micro_count * capacity
    micro = jnp.arange(rows, dtype=jnp.int32) // token_count
    place = route[0].reshape(rows) * slots + micro * capacity + slot[0].reshape(rows)
    picks = (jnp.arange(devices * slots, dtype=jnp.int32)[:, None] == place[None, :]).astype(bf16)

    def to_slots(values):
        return dot(picks, values).astype(bf16).reshape(devices, slots, ranks)

    projected = dot(tokens, shared).astype(bf16)
    own_gram = gram_pair(own_half, own_half)
    proj_slots = to_slots(projected)
    gram = gram_sum(own_gram)
    own_score = both_cores(dot_first(difference, own_half))
    turned = chip_columns(tokens.T, chip, core)
    token_blocks = [
        turned[step * channels // devices : (step + 1) * channels // devices]
        for step in range(CHIPS)
    ]
    down_gram = gram_sum(gram_pair(half_down, own_half))
    two_gram = gram_sum(gram_pair(half_two, own_half))
    down_score = both_cores(dot_first(step_down, own_half))

    wide = (rows, ranks)
    product_flops = 2 * rows * ranks * ranks
    _, scaled, slope, score, _, chain = call_rows(
        first_kernel,
        [(wide, bf16), (wide, bf16), (wide, f32), (wide, f32), (wide, bf16), (wide, bf16)],
        ids,
        [projected, chosen, weight, own_score, gram, *pieces],
        product_flops * (2 * devices + 1),
    )

    def turn(score, terms):
        arrays = [array for pair in terms for array in pair]

        def body(*refs):
            turn_kernel(len(terms), *refs)

        return call_rows(
            body,
            [(wide, f32), (wide, bf16), (wide, bf16), (wide, bf16)],
            ids,
            [chosen, weight, scaled, slope, score, *arrays, *pieces],
            product_flops * (devices + len(terms)),
        )

    def with_swap(values):
        return values, swap_cores(values)

    chain_first = chain
    first_down = between_layers(chain, [(3, 2)])
    first_two = between_layers(chain, [(3, 1)])
    own_steps = after(difference, chain)
    scaled_pair = with_swap(scaled)
    spread_rows = spread(own_steps, [(own_half, *scaled_pair)], False)[0]
    proj_slots = lax.all_to_all(after(proj_slots, chain), "expert", 0, 0, tiled=True)
    token_blocks = token_blocks[:1] + [
        across_chips(after(token_blocks[step], chain), step) for step in range(1, CHIPS)
    ]
    score, _, _, chain = turn(score + down_score, [(first_down, down_gram)])

    second_cross = between_layers(chain, [(2, 1)])
    second_two = between_layers(chain, [(2, 0)])
    first_three = between_layers(after(chain_first, chain), [(3, 0)])
    half_cross = after(half_cross, chain)
    step_cross = after(step_cross, chain)
    cross_pair = gram_pair(half_cross, own_half)
    late_steps = (step_two.astype(f32) + step_cross.astype(f32)).astype(bf16)
    late_score = both_cores(dot_first(late_steps, own_half))
    cross_product = gram_sum(cross_pair)
    score, _, _, chain = turn(
        score + late_score, [(first_two, two_gram), (second_cross, cross_product)]
    )

    third_down = between_layers(chain, [(1, 0)])
    two_values = with_swap(first_two + after(second_two, chain))
    cross_values = with_swap(second_cross + after(first_three, chain))
    down_values = with_swap(after(first_down, chain))
    other_steps = step_down.astype(f32) + late_steps.astype(f32)
    spread_rows = spread(
        spread_rows + after(other_steps, chain),
        [(half_two, *two_values), (half_cross, *cross_values), (half_down, *down_values)],
        False,
    )[0]
    scaled_rows = [scaled] + [across_chips(after(scaled, chain), step) for step in range(1, CHIPS)]
    score, grad_pre, grad_proj, _ = turn(
        score, [(second_two, two_gram), (first_three, cross_product), (third_down, down_gram)]
    )

    third_pair = with_swap(third_down)
    mixed_blocks = list(spread(spread_rows, [(half_down, *third_pair)], True))
    scaled_rows = [after(rows, mixed_blocks[0]) for rows in scaled_rows]
    grad_slots = after(to_slots(grad_pre), mixed_blocks[0])
    mixed_blocks = mixed_blocks[:1] + [
        across_chips(mixed_blocks[step], step) for step in range(1, CHIPS)
    ]
    scaled_rows = scaled_rows + [scaled_pair[1]] + [swap_cores(rows) for rows in scaled_rows[1:]]
    share = factor_rows(None, mixed_blocks, scaled_rows)
    share = factor_rows(share, token_blocks, gather_rows(grad_proj))
    grad_slots = lax.all_to_all(grad_slots, "expert", 0, 0, tiled=True)
    core_total = dot_first(proj_slots.reshape(-1, ranks), grad_slots.reshape(-1, ranks))
    return (share[None], core_total.astype(bf16)[None, None])


def solution(mesh):
    placed = (
        P("section", None, "expert", None),
        P("section", None, "expert", None),
        P("section", None, "expert"),
        P("section", None, "expert"),
        P("section", None, "expert"),
        P("section", None, None),
        P("section", "expert", None, None),
    )
    drawn_for = (LAYERS, CHIPS * CORES)

    def per_device(*arrays):
        local_experts = arrays[-1].shape[1]
        if (mesh.shape["section"], mesh.shape["expert"]) == drawn_for and local_experts == 1:
            return gathered_plan(*arrays)
        return general_plan(*arrays)

    return jax.shard_map(
        per_device,
        mesh=mesh,
        in_specs=placed,
        out_specs=(P("section", "expert", None), P("section", "expert", None, None)),
        check_vma=False,
    )
```

profile of v0, /device:TPU:0, one launch (start us, length us, event | category | flops | bytes accessed | tf_op | source)
XLA Modules:
  0.0 279.6 jit_solution(8852956810938628896)
XLA Ops:
  0.6 3.1 %collective-permute-start.3 = (bf16[768,768]{1,0:T(8,128)(2,1)}, bf16[768,768]{1,0:T(8,128)(2,1)S(1)}, u32[]{:S(2)}, u32[]{:S(2)}) collective-permute-start(bf16[768,768]{1,0:T(8,128)(2,1)} %bitcast.84), channel_id=1, source_target_pairs={{0,2},{1,3},{2,0},{3,1},{4,6},{5,7},{6,4},{7,5},{8,10},{9,11},{10,... | collective-permute-start | bytes 3538952 | tf_op jit(solution)/shard_map/ppermute | solution.py:170
  3.7 1.7 collective-permute-start.4
  5.5 1.6 dynamic-slice_bitcast_fusion.3
  7.2 1.4 collective-permute-start.18
  8.7 1.3 collective-permute-start.22
  10.0 1.3 bitcast_convert_fusion.1
  11.3 2.8 %copy.20 = f32[128,2560]{0,1:T(8,128)} copy(f32[128,2560]{1,0:T(8,128)} %bitcast_convert_fusion.1) | data formatting | bytes 2621440 | tf_op jit(solution)/shard_map/convert_element_type | solution.py:417
  14.1 2.2 copy.19
  16.2 2.4 subtract_convert_fusion
  18.7 1.9 dynamic-slice_bitcast_fusion.19
  21.5 3.0 %fusion.3.proj_ref = bf16[128,768]{1,0:T(8,128)(2,1)S(1)} fusion(bf16[128,2560]{1,0:T(8,128)(2,1)} %bitcast.92, bf16[1,2560,768]{2,1,0:T(8,128)(2,1)} %param.12), kind=kOutput, calls=%fused_computation.20 | convolution fusion | flops 503414784 | bytes 4784128 | tf_op jit(solution)/shard_map/dot_general | solution.py:155
  24.5 5.4 %collective-permute-done.3.refs_1_.refs_9_.refs_11_.refs_13_ = bf16[768,768]{1,0:T(8,128)(2,1)S(1)} collective-permute-done((bf16[768,768]{1,0:T(8,128)(2,1)}, bf16[768,768]{1,0:T(8,128)(2,1)S(1)}, u32[]{:S(2)}, u32[]{:S(2)}) %collective-permute-start.3) | collective-permute-done | bytes 1179680 | tf_op jit(solution)/shard_map/ppermute | solution.py:170
  29.9 1.7 collective-permute-start.6
  31.6 1.7 fusion.14
  37.0 1.3 dynamic-slice_bitcast_fusion.11
  38.2 1.3 collective-permute-start.5
  40.6 1.6 collective-permute-start.13
  42.2 1.7 convolution_convert_fusion.3
  44.0 1.3 collective-permute-start.7
  45.3 22.3 %collective-permute-done.13 = bf16[1280,256]{1,0:T(8,128)(2,1)S(1)} collective-permute-done((bf16[1280,256]{1,0:T(8,128)(2,1)S(1)}, bf16[1280,256]{1,0:T(8,128)(2,1)S(1)}, u32[]{:S(2)}, u32[]{:S(2)}) %collective-permute-start.13) | collective-permute-done | bytes 655392 | tf_op jit(solution)/shard_map/ppermute | solution.py:179
  70.1 1.3 collective-permute-start.14
  71.4 3.3 %convolution_convert_fusion.2 = bf16[768,768]{1,0:T(8,128)(2,1)S(1)} fusion(bf16[1280,768]{1,0:T(8,128)(2,1)} %collective-permute-done.18.refs_7_.refs_1_, bf16[1280,768]{1,0:T(8,128)(2,1)S(1)} %pad_maximum_fusion.refs_1_), kind=kOutput, calls=%fused_computation.10 | convolution fusion | flops 1510539264 | bytes 5111808 | tf_op jit(solution)/shard_map/dot_general | solution.py:159
  74.8 20.4 %collective-permute-done.7 = bf16[768,768]{1,0:T(8,128)(2,1)S(1)} collective-permute-done((bf16[768,768]{1,0:T(8,128)(2,1)}, bf16[768,768]{1,0:T(8,128)(2,1)S(1)}, u32[]{:S(2)}, u32[]{:S(2)}) %collective-permute-start.7) | collective-permute-done | bytes 1179680 | tf_op jit(solution)/shard_map/ppermute | solution.py:170
  95.9 3.6 %collective-permute-start.25 = (bf16[1280,768]{1,0:T(8,128)(2,1)}, bf16[1280,768]{1,0:T(8,128)(2,1)S(1)}, u32[]{:S(2)}, u32[]{:S(2)}) collective-permute-start(bf16[1280,768]{1,0:T(8,128)(2,1)} %collective-permute-done.22.refs_1_), channel_id=1, source_target_pairs={{0,8},{8,0},{1,9},{9,1},{2,10},{10,2},{3,11},{11,3},{4,12},{12,4},... | collective-permute-start | bytes 5898248 | tf_op jit(solution)/shard_map/ppermute | solution.py:179
  101.2 3.3 %convolution_convert_fusion.1 = bf16[768,768]{1,0:T(8,128)(2,1)S(1)} fusion(bf16[1280,768]{1,0:T(8,128)(2,1)} %collective-permute-done.22.refs_1_, bf16[1280,768]{1,0:T(8,128)(2,1)S(1)} %pad_maximum_fusion.refs_1_), kind=kOutput, calls=%fused_computation.9 | convolution fusion | flops 1510539264 | bytes 5111808 | tf_op jit(solution)/shard_map/dot_general | solution.py:159
  105.5 2.4 collective-permute-start.15
  108.1 6.8 %shard_map.86 = (bf16[128,768]{1,0:T(8,128)(2,1)}, bf16[128,768]{1,0:T(8,128)(2,1)S(1)}, f32[128,768]{1,0:T(8,128)S(1)}, f32[128,768]{1,0:T(8,128)S(1)}, bf16[12...) custom-call(s32[8]{0:T(128)S(1)} %stack.35.ids_ref.refs_0_, bf16[128,768]{1,0:T(8,128)(2,1)S(1)} %fusion.3.proj_ref, ...), custom_call_target="tpu_custom_call" | custom-call | flops 2566914048 | bytes 11207680 | tf_op jit(solution)/shard_map/pallas_call | solution.py:303
  115.9 4.3 %shard_map.88 = (f32[128,768]{1,0:T(8,128)S(1)}, bf16[128,768]{1,0:T(8,128)(2,1)}, bf16[128,768]{1,0:T(8,128)(2,1)}, bf16[128,768]{1,0:T(8,128)(2,1)S(1)}) custom-call(s32[8]{0:T(128)S(1)} %stack.35.ids_ref.refs_0_, s32[128,1]{1,0:T(8,128)S(1)} %copy-done.28, f32[128,1]{1,0:T(8,128)S(1)} %copy-done.30, ...), custom_call_target="tpu_custom_call" | custom-call | flops 1358954496 | bytes 11797504 | tf_op jit(solution)/shard_map/pallas_call | solution.py:303
  120.2 23.5 %collective-permute-done.25.refs_4_ = bf16[1280,768]{1,0:T(8,128)(2,1)S(1)} collective-permute-done((bf16[1280,768]{1,0:T(8,128)(2,1)}, bf16[1280,768]{1,0:T(8,128)(2,1)S(1)}, u32[]{:S(2)}, u32[]{:S(2)}) %collective-permute-start.25) | collective-permute-done | bytes 1966112 | tf_op jit(solution)/shard_map/ppermute | solution.py:179
  143.7 2.8 convolution_convert_fusion
  146.7 10.2 %collective-permute-done.15 = bf16[1280,256]{1,0:T(8,128)(2,1)S(1)} collective-permute-done((bf16[1280,256]{1,0:T(8,128)(2,1)S(1)}, bf16[1280,256]{1,0:T(8,128)(2,1)S(1)}, u32[]{:S(2)}, u32[]{:S(2)}) %collective-permute-start.15) | collective-permute-done | bytes 655392 | tf_op jit(solution)/shard_map/ppermute | solution.py:179
  159.4 1.3 add_convert_fusion.1.refs_7_
  161.3 1.3 collective-permute-start.21
  163.5 4.1 %all-to-all-start = ((bf16[8,32,768]{2,1,0:T(8,128)(2,1)}), bf16[8,32,768]{2,1,0:T(8,128)(2,1)}, u32[]{:S(2)}, u32[]{:S(2)}) async-start(bf16[8,32,768]{2,1,0:T(8,128)(2,1)} %bitcast.93), calls=%async_computation | async-start | bytes 786432 | tf_op jit(solution)/shard_map/all_to_all | solution.py:479
  168.3 1.4 fusion.6.refs_5_
  169.8 1.6 collective-permute-start.27
  171.3 1.9 add_convert_fusion.refs_9_
  173.3 1.3 collective-permute-start.29
  175.9 1.3 copy-done.13
  177.2 1.3 copy-done.16
  178.5 1.3 copy-done.20
  179.7 5.1 %shard_map.89 = (f32[128,768]{1,0:T(8,128)S(1)}, bf16[128,768]{1,0:T(8,128)(2,1)}, bf16[128,768]{1,0:T(8,128)(2,1)}, bf16[128,768]{1,0:T(8,128)(2,1)S(1)}) custom-call(s32[8]{0:T(128)S(1)} %stack.35.ids_ref.refs_0_, s32[128,1]{1,0:T(8,128)S(1)} %copy-done.29, f32[128,1]{1,0:T(8,128)S(1)} %copy-done.31, ...), custom_call_target="tpu_custom_call" | custom-call | flops 1509949440 | bytes 13173760 | tf_op jit(solution)/shard_map/pallas_call | solution.py:303
  184.8 1.7 collective-permute-start.32
  186.8 1.7 shard_map.87
  190.9 4.7 %collective-permute-done.32.refs_2_.refs_10_ = bf16[128,768]{1,0:T(8,128)(2,1)S(1)} collective-permute-done((bf16[128,768]{1,0:T(8,128)(2,1)S(1)}, bf16[128,768]{1,0:T(8,128)(2,1)S(1)}, u32[]{:S(2)}, u32[]{:S(2)}) %collective-permute-start.32) | collective-permute-done | bytes 196640 | tf_op jit(solution)/shard_map/ppermute | solution.py:179
  195.6 4.9 %shard_map.93 = (f32[128,768]{1,0:T(8,128)}, bf16[128,768]{1,0:T(8,128)(2,1)S(1)}, bf16[128,768]{1,0:T(8,128)(2,1)S(1)}, bf16[128,768]{1,0:T(8,128)(2,1)}) custom-call(s32[8]{0:T(128)S(1)} %stack.35.ids_ref.refs_0_, s32[128,1]{1,0:T(8,128)S(1)} %copy-done.29, f32[128,1]{1,0:T(8,128)S(1)} %copy-done.31, ...), custom_call_target="tpu_custom_call" | custom-call | flops 1660944384 | bytes 14550016 | tf_op jit(solution)/shard_map/pallas_call | solution.py:303
  201.6 2.2 collective-permute-start.45
  203.8 1.6 collective-permute-start.37
  205.8 3.9 %shard_map.90.refs_0_ = f32[1280,256]{1,0:T(8,128)S(1)} custom-call(f32[1280,256]{1,0:T(8,128)S(1)} %add.192.refs_0_, bf16[1280,768]{1,0:T(8,128)(2,1)} %collective-permute-done.22.refs_1_, bf16[128,768]{1,0:T(8,128)(2,1)S(1)} %add.193.refs_2_, bf16[128,768]{1,0:T(8,128)(2,1)S(1)} %collective-permute-done.28.refs_3_, bf16[1280,768]{1,0:T(8,128)(2,1)S(1)} %copy-done.27, ...), custom_call_target="tpu_custom_call" | custom-call | flops 1509949440 | bytes 8388608 | tf_op jit(solution)/shard_map/pallas_call | solution.py:340
  209.7 2.3 shard_map.91
  212.0 3.8 %all-to-all-start.1 = ((bf16[8,32,768]{2,1,0:T(8,128)(2,1)}), bf16[8,32,768]{2,1,0:T(8,128)(2,1)S(1)}, u32[]{:S(2)}, u32[]{:S(2)}) async-start(bf16[8,32,768]{2,1,0:T(8,128)(2,1)} %bitcast.34), calls=%async_computation.1 | async-start | bytes 786432 | tf_op jit(solution)/shard_map/all_to_all | solution.py:523
  215.8 3.8 %collective-permute-start.39 = (bf16[128,768]{1,0:T(8,128)(2,1)S(1)}, bf16[128,768]{1,0:T(8,128)(2,1)S(1)}, u32[]{:S(2)}, u32[]{:S(2)}) collective-permute-start(bf16[128,768]{1,0:T(8,128)(2,1)S(1)} %get-tuple-element.54.refs_2_.refs_3_.refs_4_), channel_id=1, source_target_pairs={{0,6},{1,7},{2,4},{3,5},{4,2},{5,3},{6,0},{7,1},{8,14},{9,15},{10,... | collective-permute-start | bytes 589832 | tf_op jit(solution)/shard_map/ppermute | solution.py:170
  220.3 3.8 %collective-permute-start.49 = (bf16[128,768]{1,0:T(8,128)(2,1)S(1)}, bf16[128,768]{1,0:T(8,128)(2,1)S(1)}, u32[]{:S(2)}, u32[]{:S(2)}) collective-permute-start(bf16[128,768]{1,0:T(8,128)(2,1)S(1)} %get-tuple-element.62.refs_5_), channel_id=1, source_target_pairs={{0,6},{1,7},{2,4},{3,5},{4,2},{5,3},{6,0},{7,1},{8,14},{9,15},{10,... | collective-permute-start | bytes 589832 | tf_op jit(solution)/shard_map/ppermute | solution.py:170
  224.0 5.9 %collective-permute-start.34 = (bf16[320,256]{1,0:T(8,128)(2,1)S(1)}, bf16[320,256]{1,0:T(8,128)(2,1)S(1)}, u32[]{:S(2)}, u32[]{:S(2)}) collective-permute-start(bf16[320,256]{1,0:T(8,128)(2,1)S(1)} %get-tuple-element.50), channel_id=1, source_target_pairs={{0,2},{1,3},{2,0},{3,1},{4,6},{5,7},{6,4},{7,5},{8,10},{9,11},{10,... | collective-permute-start | bytes 491528 | tf_op jit(solution)/shard_map/ppermute | solution.py:170
  229.9 2.1 collective-permute-done.39.refs_7_
  232.0 3.8 %collective-permute-done.47.refs_6_ = bf16[128,768]{1,0:T(8,128)(2,1)S(1)} collective-permute-done((bf16[128,768]{1,0:T(8,128)(2,1)S(1)}, bf16[128,768]{1,0:T(8,128)(2,1)S(1)}, u32[]{:S(2)}, u32[]{:S(2)}) %collective-permute-start.47) | collective-permute-done | bytes 196640 | tf_op jit(solution)/shard_map/ppermute | solution.py:170
  235.9 15.2 %collective-permute-done.48.refs_7_ = bf16[128,768]{1,0:T(8,128)(2,1)S(1)} collective-permute-done((bf16[128,768]{1,0:T(8,128)(2,1)S(1)}, bf16[128,768]{1,0:T(8,128)(2,1)S(1)}, u32[]{:S(2)}, u32[]{:S(2)}) %collective-permute-start.48) | collective-permute-done | bytes 196640 | tf_op jit(solution)/shard_map/ppermute | solution.py:170
  251.1 2.8 %collective-permute-start.36 = (bf16[320,256]{1,0:T(8,128)(2,1)S(1)}, bf16[320,256]{1,0:T(8,128)(2,1)S(1)}, u32[]{:S(2)}, u32[]{:S(2)}) collective-permute-start(bf16[320,256]{1,0:T(8,128)(2,1)S(1)} %get-tuple-element.52), channel_id=1, source_target_pairs={{0,6},{1,7},{2,4},{3,5},{4,2},{5,3},{6,0},{7,1},{8,14},{9,15},{10,... | collective-permute-start | bytes 491528 | tf_op jit(solution)/shard_map/ppermute | solution.py:170
  253.9 11.4 %collective-permute-done.35.refs_2_ = bf16[320,256]{1,0:T(8,128)(2,1)S(1)} collective-permute-done((bf16[320,256]{1,0:T(8,128)(2,1)S(1)}, bf16[320,256]{1,0:T(8,128)(2,1)S(1)}, u32[]{:S(2)}, u32[]{:S(2)}) %collective-permute-start.35) | collective-permute-done | bytes 163872 | tf_op jit(solution)/shard_map/ppermute | solution.py:170
  266.4 3.3 %collective-permute-start.46 = (bf16[320,256]{1,0:T(8,128)(2,1)S(1)}, bf16[320,256]{1,0:T(8,128)(2,1)S(1)}, u32[]{:S(2)}, u32[]{:S(2)}) collective-permute-start(bf16[320,256]{1,0:T(8,128)(2,1)S(1)} %copy-done.51), channel_id=1, source_target_pairs={{0,6},{1,7},{2,4},{3,5},{4,2},{5,3},{6,0},{7,1},{8,14},{9,15},{10,... | collective-permute-start | bytes 491528 | tf_op jit(solution)/shard_map/ppermute | solution.py:170
  269.6 1.6 shard_map.92.refs_0_
  271.3 3.2 %collective-permute-done.46.refs_4_ = bf16[320,256]{1,0:T(8,128)(2,1)S(1)} collective-permute-done((bf16[320,256]{1,0:T(8,128)(2,1)S(1)}, bf16[320,256]{1,0:T(8,128)(2,1)S(1)}, u32[]{:S(2)}, u32[]{:S(2)}) %collective-permute-start.46) | collective-permute-done | bytes 163872 | tf_op jit(solution)/shard_map/ppermute | solution.py:170
  274.5 2.5 shard_map.94
  277.1 2.5 fusion.2
  (216 shorter events, 24.6 us)
Async XLA Ops:
  0.6 29.3 %collective-permute-start.3 = (bf16[768,768]{1,0:T(8,128)(2,1)}, bf16[768,768]{1,0:T(8,128)(2,1)S(1)}, u32[]{:S(2)}, u32[]{:S(2)}) collective-permute-start(bf16[768,768]{1,0:T(8,128)(2,1)} %bitcast.84), channel_id=1, source_target_pairs={{0,2},{1,3},{2,0},{3,1},{4,6},{5,7},{6,4},{7,5},{8,10},{9,11},{10,... | collective-permute-start | bytes 3538952 | tf_op jit(solution)/shard_map/ppermute | solution.py:170
  3.7 34.5 %collective-permute-start.4 = (bf16[768,768]{1,0:T(8,128)(2,1)}, bf16[768,768]{1,0:T(8,128)(2,1)}, u32[]{:S(2)}, u32[]{:S(2)}) collective-permute-start(bf16[768,768]{1,0:T(8,128)(2,1)} %bitcast.85), channel_id=1, source_target_pairs={{2,4},{3,5},{4,2},{5,3},{10,12},{11,13},{12,10},{13,11},{18,20},{1... | collective-permute-start | bytes 3538952 | tf_op jit(solution)/shard_map/ppermute | solution.py:170
  7.2 60.4 %collective-permute-start.18 = (bf16[1280,768]{1,0:T(8,128)(2,1)S(1)}, bf16[1280,768]{1,0:T(8,128)(2,1)}, u32[]{:S(2)}, u32[]{:S(2)}) collective-permute-start(bf16[1280,768]{1,0:T(8,128)(2,1)S(1)} %pad_maximum_fusion.refs_1_), channel_id=1, source_target_pairs={{24,16},{8,0},{25,17},{9,1},{26,18},{10,2},{27,19},{11,3},{28,20},... | collective-permute-start | bytes 5898248 | tf_op jit(solution)/shard_map/ppermute | solution.py:179
  8.7 87.3 %collective-permute-start.22 = (bf16[1280,768]{1,0:T(8,128)(2,1)S(1)}, bf16[1280,768]{1,0:T(8,128)(2,1)}, u32[]{:S(2)}, u32[]{:S(2)}) collective-permute-start(bf16[1280,768]{1,0:T(8,128)(2,1)S(1)} %pad_maximum_fusion.refs_1_), channel_id=1, source_target_pairs={{24,8},{16,0},{25,9},{17,1},{26,10},{18,2},{27,11},{19,3},{28,12},... | collective-permute-start | bytes 5898248 | tf_op jit(solution)/shard_map/ppermute | solution.py:179
  21.3 10.3 %collective-permute-start = (bf16[1280,128]{1,0:T(8,128)(2,1)}, bf16[1280,128]{1,0:T(8,128)(2,1)}, u32[]{:S(2)}, u32[]{:S(2)}) collective-permute-start(bf16[1280,128]{1,0:T(8,128)(2,1)} %pad_maximum_fusion.3), channel_id=1, source_target_pairs={{0,1},{1,0},{2,3},{3,2},{4,5},{5,4},{6,7},{7,6},{8,9},{9,8},{10,11... | collective-permute-start | bytes 983048 | tf_op jit(solution)/shard_map/ppermute | solution.py:175
  29.9 14.0 %collective-permute-start.6 = (bf16[768,768]{1,0:T(8,128)(2,1)S(1)}, bf16[768,768]{1,0:T(8,128)(2,1)}, u32[]{:S(2)}, u32[]{:S(2)}) collective-permute-start(bf16[768,768]{1,0:T(8,128)(2,1)S(1)} %collective-permute-done.3.refs_1_.refs_9_.refs_11_.refs_13_), channel_id=1, source_target_pairs={{2,4},{3,5},{4,2},{5,3},{10,12},{11,13},{12,10},{13,11},{18,20},{1... | collective-permute-start | bytes 3538952 | tf_op jit(solution)/shard_map/ppermute | solution.py:170
  34.3 6.3 %collective-permute-start.1 = (f32[128,768]{1,0:T(8,128)}, f32[128,768]{1,0:T(8,128)}, u32[]{:S(2)}, u32[]{:S(2)}) collective-permute-start(f32[128,768]{1,0:T(8,128)} %slice.41), channel_id=1, source_target_pairs={{0,1},{1,0},{2,3},{3,2},{4,5},{5,4},{6,7},{7,6},{8,9},{9,8},{10,11... | collective-permute-start | bytes 1179656 | tf_op jit(solution)/shard_map/ppermute | solution.py:175
  38.2 31.9 %collective-permute-start.5 = (bf16[768,768]{1,0:T(8,128)(2,1)}, bf16[768,768]{1,0:T(8,128)(2,1)S(1)}, u32[]{:S(2)}, u32[]{:S(2)}) collective-permute-start(bf16[768,768]{1,0:T(8,128)(2,1)} %collective-permute-done.4), channel_id=1, source_target_pairs={{2,0},{3,1},{4,6},{5,7},{10,8},{11,9},{12,14},{13,15},{18,16},{19,... | collective-permute-start | bytes 3538952 | tf_op jit(solution)/shard_map/ppermute | solution.py:170
  40.6 29.5 %copy-start.24 = (bf16[1280,256]{1,0:T(8,128)(2,1)}, bf16[1280,256]{1,0:T(8,128)(2,1)S(1)}, u32[]{:S(2)}) copy-start(bf16[1280,256]{1,0:T(8,128)(2,1)S(1)} %pad_maximum_fusion.1.refs_0_) | copy-start | bytes 1966084
  40.6 27.0 %copy-start.2 = (bf16[1,1,768,768]{3,2,1,0:T(8,128)(2,1)S(1)}, bf16[1,1,768,768]{3,2,1,0:T(8,128)(2,1)}, u32[]{:S(2)}) copy-start(bf16[1,1,768,768]{3,2,1,0:T(8,128)(2,1)} %param.13) | copy-start | bytes 3538948
  40.6 27.5 %copy-start.45 = (f32[256,768]{1,0:T(8,128)S(1)}, f32[256,768]{1,0:T(8,128)}, u32[]{:S(2)}) copy-start(f32[256,768]{1,0:T(8,128)} %copy-done.44) | copy-start | bytes 2359300
  40.6 27.0 %collective-permute-start.13 = (bf16[1280,256]{1,0:T(8,128)(2,1)S(1)}, bf16[1280,256]{1,0:T(8,128)(2,1)S(1)}, u32[]{:S(2)}, u32[]{:S(2)}) collective-permute-start(bf16[1280,256]{1,0:T(8,128)(2,1)S(1)} %pad_maximum_fusion.1.refs_0_), channel_id=1, source_target_pairs={{24,16},{8,0},{25,17},{9,1},{26,18},{10,2},{27,19},{11,3},{28,20},... | collective-permute-start | bytes 1966088 | tf_op jit(solution)/shard_map/ppermute | solution.py:179
  44.0 51.2 %collective-permute-start.7 = (bf16[768,768]{1,0:T(8,128)(2,1)}, bf16[768,768]{1,0:T(8,128)(2,1)S(1)}, u32[]{:S(2)}, u32[]{:S(2)}) collective-permute-start(bf16[768,768]{1,0:T(8,128)(2,1)} %collective-permute-done.6), channel_id=1, source_target_pairs={{2,0},{3,1},{4,6},{5,7},{10,8},{11,9},{12,14},{13,15},{18,16},{19,... | collective-permute-start | bytes 3538952 | tf_op jit(solution)/shard_map/ppermute | solution.py:170
  67.6 32.5 %copy-start.42 = (bf16[1280,256]{1,0:T(8,128)(2,1)}, bf16[1280,256]{1,0:T(8,128)(2,1)S(1)}, u32[]{:S(2)}) copy-start(bf16[1280,256]{1,0:T(8,128)(2,1)S(1)} %collective-permute-done.13) | copy-start | bytes 1966084
  67.6 32.0 %collective-permute-start.8 = (bf16[768,768]{1,0:T(8,128)(2,1)S(1)}, bf16[768,768]{1,0:T(8,128)(2,1)S(1)}, u32[]{:S(2)}, u32[]{:S(2)}) collective-permute-start(bf16[768,768]{1,0:T(8,128)(2,1)S(1)} %bitcast.86), channel_id=1, source_target_pairs={{0,1},{1,0},{2,3},{3,2},{4,5},{5,4},{6,7},{7,6},{8,9},{9,8},{10,11... | collective-permute-start | bytes 3538952 | tf_op jit(solution)/shard_map/ppermute | solution.py:175
  67.6 31.9 %collective-permute-start.2 = (bf16[768,768]{1,0:T(8,128)(2,1)S(1)}, bf16[768,768]{1,0:T(8,128)(2,1)S(1)}, u32[]{:S(2)}, u32[]{:S(2)}) collective-permute-start(bf16[768,768]{1,0:T(8,128)(2,1)S(1)} %convolution_convert_fusion.3), channel_id=1, source_target_pairs={{0,1},{1,0},{2,3},{3,2},{4,5},{5,4},{6,7},{7,6},{8,9},{9,8},{10,11... | collective-permute-start | bytes 3538952 | tf_op jit(solution)/shard_map/ppermute | solution.py:175
  70.1 25.2 %collective-permute-start.14 = (bf16[1280,256]{1,0:T(8,128)(2,1)S(1)}, bf16[1280,256]{1,0:T(8,128)(2,1)S(1)}, u32[]{:S(2)}, u32[]{:S(2)}) collective-permute-start(bf16[1280,256]{1,0:T(8,128)(2,1)S(1)} %pad_maximum_fusion.1.refs_0_), channel_id=1, source_target_pairs={{24,8},{16,0},{25,9},{17,1},{26,10},{18,2},{27,11},{19,3},{28,12},... | collective-permute-start | bytes 1966088 | tf_op jit(solution)/shard_map/ppermute | solution.py:179
  95.2 9.3 %collective-permute-start.19 = (bf16[768,768]{1,0:T(8,128)(2,1)S(1)}, bf16[768,768]{1,0:T(8,128)(2,1)S(1)}, u32[]{:S(2)}, u32[]{:S(2)}) collective-permute-start(bf16[768,768]{1,0:T(8,128)(2,1)S(1)} %convolution_convert_fusion.2), channel_id=1, source_target_pairs={{0,1},{1,0},{2,3},{3,2},{4,5},{5,4},{6,7},{7,6},{8,9},{9,8},{10,11... | collective-permute-start | bytes 3538952 | tf_op jit(solution)/shard_map/ppermute | solution.py:175
  95.4 61.5 %copy-start.38 = (bf16[1280,256]{1,0:T(8,128)(2,1)}, bf16[1280,256]{1,0:T(8,128)(2,1)S(1)}, u32[]{:S(2)}) copy-start(bf16[1280,256]{1,0:T(8,128)(2,1)S(1)} %collective-permute-done.14) | copy-start | bytes 1966084
  95.4 9.7 %collective-permute-start.9 = (bf16[768,768]{1,0:T(8,128)(2,1)S(1)}, bf16[768,768]{1,0:T(8,128)(2,1)S(1)}, u32[]{:S(2)}, u32[]{:S(2)}) collective-permute-start(bf16[768,768]{1,0:T(8,128)(2,1)S(1)} %copy-done.5), channel_id=1, source_target_pairs={{0,1},{1,0},{2,3},{3,2},{4,5},{5,4},{6,7},{7,6},{8,9},{9,8},{10,11... | collective-permute-start | bytes 3538952 | tf_op jit(solution)/shard_map/ppermute | solution.py:175
  95.9 47.8 %collective-permute-start.25 = (bf16[1280,768]{1,0:T(8,128)(2,1)}, bf16[1280,768]{1,0:T(8,128)(2,1)S(1)}, u32[]{:S(2)}, u32[]{:S(2)}) collective-permute-start(bf16[1280,768]{1,0:T(8,128)(2,1)} %collective-permute-done.22.refs_1_), channel_id=1, source_target_pairs={{0,8},{8,0},{1,9},{9,1},{2,10},{10,2},{3,11},{11,3},{4,12},{12,4},... | collective-permute-start | bytes 5898248 | tf_op jit(solution)/shard_map/ppermute | solution.py:179
  99.5 6.0 %collective-permute-start.10 = (bf16[768,768]{1,0:T(8,128)(2,1)S(1)}, bf16[768,768]{1,0:T(8,128)(2,1)S(1)}, u32[]{:S(2)}, u32[]{:S(2)}) collective-permute-start(bf16[768,768]{1,0:T(8,128)(2,1)S(1)} %broadcast_select_fusion.1.refs_2_.refs_10_.refs_12_.refs_14_), channel_id=1, source_target_pairs={{0,1},{1,0},{2,3},{3,2},{4,5},{5,4},{6,7},{7,6},{8,9},{9,8},{10,11... | collective-permute-start | bytes 3538952 | tf_op jit(solution)/shard_map/ppermute | solution.py:175
  99.6 8.3 %collective-permute-start.11 = (bf16[768,768]{1,0:T(8,128)(2,1)S(1)}, bf16[768,768]{1,0:T(8,128)(2,1)S(1)}, u32[]{:S(2)}, u32[]{:S(2)}) collective-permute-start(bf16[768,768]{1,0:T(8,128)(2,1)S(1)} %broadcast_select_fusion.refs_3_.refs_11_.refs_13_.refs_15_), channel_id=1, source_target_pairs={{0,1},{1,0},{2,3},{3,2},{4,5},{5,4},{6,7},{7,6},{8,9},{9,8},{10,11... | collective-permute-start | bytes 3538952 | tf_op jit(solution)/shard_map/ppermute | solution.py:175
  104.5 10.4 %collective-permute-start.16 = (f32[128,768]{1,0:T(8,128)S(1)}, f32[128,768]{1,0:T(8,128)S(1)}, u32[]{:S(2)}, u32[]{:S(2)}) collective-permute-start(f32[128,768]{1,0:T(8,128)S(1)} %slice.43), channel_id=1, source_target_pairs={{0,1},{1,0},{2,3},{3,2},{4,5},{5,4},{6,7},{7,6},{8,9},{9,8},{10,11... | collective-permute-start | bytes 1179656 | tf_op jit(solution)/shard_map/ppermute | solution.py:175
  105.0 41.5 %collective-permute-start.43 = (bf16[1280,128]{1,0:T(8,128)(2,1)S(1)}, bf16[1280,128]{1,0:T(8,128)(2,1)S(1)}, u32[]{:S(2)}, u32[]{:S(2)}) collective-permute-start(bf16[1280,128]{1,0:T(8,128)(2,1)S(1)} %pad_maximum_fusion.4), channel_id=1, source_target_pairs={{0,1},{1,0},{2,3},{3,2},{4,5},{5,4},{6,7},{7,6},{8,9},{9,8},{10,11... | collective-permute-start | bytes 983048 | tf_op jit(solution)/shard_map/ppermute | solution.py:175
  105.5 51.3 %collective-permute-start.15 = (bf16[1280,256]{1,0:T(8,128)(2,1)S(1)}, bf16[1280,256]{1,0:T(8,128)(2,1)S(1)}, u32[]{:S(2)}, u32[]{:S(2)}) collective-permute-start(bf16[1280,256]{1,0:T(8,128)(2,1)S(1)} %collective-permute-done.14), channel_id=1, source_target_pairs={{0,8},{8,0},{1,9},{9,1},{2,10},{10,2},{3,11},{11,3},{4,12},{12,4},... | collective-permute-start | bytes 1966088 | tf_op jit(solution)/shard_map/ppermute | solution.py:179
  108.0 51.4 %collective-permute-start.23 = (bf16[768,768]{1,0:T(8,128)(2,1)S(1)}, bf16[768,768]{1,0:T(8,128)(2,1)S(1)}, u32[]{:S(2)}, u32[]{:S(2)}) collective-permute-start(bf16[768,768]{1,0:T(8,128)(2,1)S(1)} %convolution_convert_fusion.1), channel_id=1, source_target_pairs={{0,1},{1,0},{2,3},{3,2},{4,5},{5,4},{6,7},{7,6},{8,9},{9,8},{10,11... | collective-permute-start | bytes 3538952 | tf_op jit(solution)/shard_map/ppermute | solution.py:175
  114.9 1.0 collective-permute-start.17
  120.2 26.3 %copy-start.35 = (f32[128,768]{1,0:T(8,128)}, f32[128,768]{1,0:T(8,128)S(1)}, u32[]{:S(2)}) copy-start(f32[128,768]{1,0:T(8,128)S(1)} %get-tuple-element.41) | copy-start | bytes 1179652
  120.2 26.3 %copy-start.36 = (bf16[128,768]{1,0:T(8,128)(2,1)}, bf16[128,768]{1,0:T(8,128)(2,1)S(1)}, u32[]{:S(2)}) copy-start(bf16[128,768]{1,0:T(8,128)(2,1)S(1)} %get-tuple-element.39) | copy-start | bytes 589828
  146.5 23.3 %collective-permute-start.26 = (bf16[768,768]{1,0:T(8,128)(2,1)}, bf16[768,768]{1,0:T(8,128)(2,1)}, u32[]{:S(2)}, u32[]{:S(2)}) collective-permute-start(bf16[768,768]{1,0:T(8,128)(2,1)} %convolution_convert_fusion), channel_id=1, source_target_pairs={{0,1},{1,0},{2,3},{3,2},{4,5},{5,4},{6,7},{7,6},{8,9},{9,8},{10,11... | collective-permute-start | bytes 3538952 | tf_op jit(solution)/shard_map/ppermute | solution.py:175
  158.5 9.1 %collective-permute-start.20 = (f32[128,768]{1,0:T(8,128)}, f32[128,768]{1,0:T(8,128)}, u32[]{:S(2)}, u32[]{:S(2)}) collective-permute-start(f32[128,768]{1,0:T(8,128)} %slice.45), channel_id=1, source_target_pairs={{0,1},{1,0},{2,3},{3,2},{4,5},{5,4},{6,7},{7,6},{8,9},{9,8},{10,11... | collective-permute-start | bytes 1179656 | tf_op jit(solution)/shard_map/ppermute | solution.py:175
  160.7 26.0 %collective-permute-start.12 = (bf16[128,768]{1,0:T(8,128)(2,1)S(1)}, bf16[128,768]{1,0:T(8,128)(2,1)}, u32[]{:S(2)}, u32[]{:S(2)}) collective-permute-start(bf16[128,768]{1,0:T(8,128)(2,1)S(1)} %get-tuple-element.54.refs_2_.refs_3_.refs_4_), channel_id=1, source_target_pairs={{0,1},{1,0},{2,3},{3,2},{4,5},{5,4},{6,7},{7,6},{8,9},{9,8},{10,11... | collective-permute-start | bytes 589832 | tf_op jit(solution)/shard_map/ppermute | solution.py:175
  161.3 12.0 %collective-permute-start.21 = (bf16[128,768]{1,0:T(8,128)(2,1)}, bf16[128,768]{1,0:T(8,128)(2,1)}, u32[]{:S(2)}, u32[]{:S(2)}) collective-permute-start(bf16[128,768]{1,0:T(8,128)(2,1)} %get-tuple-element.46), channel_id=1, source_target_pairs={{24,8},{25,9},{26,10},{27,11},{28,12},{29,13},{30,14},{31,15}} | collective-permute-start | bytes 589832 | tf_op jit(solution)/shard_map/ppermute | solution.py:179
  162.6 57.0 %collective-permute-start.44 = (bf16[320,256]{1,0:T(8,128)(2,1)}, bf16[320,256]{1,0:T(8,128)(2,1)}, u32[]{:S(2)}, u32[]{:S(2)}) collective-permute-start(bf16[320,256]{1,0:T(8,128)(2,1)} %get-tuple-element.58), channel_id=1, source_target_pairs={{0,2},{1,3},{2,0},{3,1},{4,6},{5,7},{6,4},{7,5},{8,10},{9,11},{10,... | collective-permute-start | bytes 491528 | tf_op jit(solution)/shard_map/ppermute | solution.py:170
  163.5 48.5 %all-to-all-start = ((bf16[8,32,768]{2,1,0:T(8,128)(2,1)}), bf16[8,32,768]{2,1,0:T(8,128)(2,1)}, u32[]{:S(2)}, u32[]{:S(2)}) async-start(bf16[8,32,768]{2,1,0:T(8,128)(2,1)} %bitcast.93), calls=%async_computation | async-start | bytes 786432 | tf_op jit(solution)/shard_map/all_to_all | solution.py:479
  167.6 6.9 %collective-permute-start.24 = (bf16[128,768]{1,0:T(8,128)(2,1)}, bf16[128,768]{1,0:T(8,128)(2,1)S(1)}, u32[]{:S(2)}, u32[]{:S(2)}) collective-permute-start(bf16[128,768]{1,0:T(8,128)(2,1)} %copy-done.36), channel_id=1, source_target_pairs={{16,8},{17,9},{18,10},{19,11},{20,12},{21,13},{22,14},{23,15}} | collective-permute-start | bytes 589832 | tf_op jit(solution)/shard_map/ppermute | solution.py:179
  169.8 18.7 %collective-permute-start.27 = (bf16[128,768]{1,0:T(8,128)(2,1)}, bf16[128,768]{1,0:T(8,128)(2,1)S(1)}, u32[]{:S(2)}, u32[]{:S(2)}) collective-permute-start(bf16[128,768]{1,0:T(8,128)(2,1)} %copy-done.36), channel_id=1, source_target_pairs={{16,0},{17,1},{18,2},{19,3},{20,4},{21,5},{22,6},{23,7}} | collective-permute-start | bytes 589832 | tf_op jit(solution)/shard_map/ppermute | solution.py:179
  173.3 16.8 %collective-permute-start.29 = (bf16[128,768]{1,0:T(8,128)(2,1)}, bf16[128,768]{1,0:T(8,128)(2,1)S(1)}, u32[]{:S(2)}, u32[]{:S(2)}) collective-permute-start(bf16[128,768]{1,0:T(8,128)(2,1)} %get-tuple-element.46), channel_id=1, source_target_pairs={{24,0},{25,1},{26,2},{27,3},{28,4},{29,5},{30,6},{31,7}} | collective-permute-start | bytes 589832 | tf_op jit(solution)/shard_map/ppermute | solution.py:179
  184.8 10.8 %collective-permute-start.32 = (bf16[128,768]{1,0:T(8,128)(2,1)S(1)}, bf16[128,768]{1,0:T(8,128)(2,1)S(1)}, u32[]{:S(2)}, u32[]{:S(2)}) collective-permute-start(bf16[128,768]{1,0:T(8,128)(2,1)S(1)} %get-tuple-element.43), channel_id=1, source_target_pairs={{8,0},{9,1},{10,2},{11,3},{12,4},{13,5},{14,6},{15,7}} | collective-permute-start | bytes 589832 | tf_op jit(solution)/shard_map/ppermute | solution.py:179
  189.6 12.0 %collective-permute-start.28 = (bf16[128,768]{1,0:T(8,128)(2,1)S(1)}, bf16[128,768]{1,0:T(8,128)(2,1)S(1)}, u32[]{:S(2)}, u32[]{:S(2)}) collective-permute-start(bf16[128,768]{1,0:T(8,128)(2,1)S(1)} %add.193.refs_2_), channel_id=1, source_target_pairs={{0,1},{1,0},{2,3},{3,2},{4,5},{5,4},{6,7},{7,6},{8,9},{9,8},{10,11... | collective-permute-start | bytes 589832 | tf_op jit(solution)/shard_map/ppermute | solution.py:175
  190.1 13.7 %collective-permute-start.30 = (bf16[128,768]{1,0:T(8,128)(2,1)S(1)}, bf16[128,768]{1,0:T(8,128)(2,1)S(1)}, u32[]{:S(2)}, u32[]{:S(2)}) collective-permute-start(bf16[128,768]{1,0:T(8,128)(2,1)S(1)} %add.194.refs_5_), channel_id=1, source_target_pairs={{0,1},{1,0},{2,3},{3,2},{4,5},{5,4},{6,7},{7,6},{8,9},{9,8},{10,11... | collective-permute-start | bytes 589832 | tf_op jit(solution)/shard_map/ppermute | solution.py:175
  190.3 15.0 %collective-permute-start.31 = (bf16[128,768]{1,0:T(8,128)(2,1)S(1)}, bf16[128,768]{1,0:T(8,128)(2,1)S(1)}, u32[]{:S(2)}, u32[]{:S(2)}) collective-permute-start(bf16[128,768]{1,0:T(8,128)(2,1)S(1)} %copy-done.33), channel_id=1, source_target_pairs={{0,1},{1,0},{2,3},{3,2},{4,5},{5,4},{6,7},{7,6},{8,9},{9,8},{10,11... | collective-permute-start | bytes 589832 | tf_op jit(solution)/shard_map/ppermute | solution.py:175
  195.6 14.1 %collective-permute-start.33 = (bf16[128,768]{1,0:T(8,128)(2,1)S(1)}, bf16[128,768]{1,0:T(8,128)(2,1)S(1)}, u32[]{:S(2)}, u32[]{:S(2)}) collective-permute-start(bf16[128,768]{1,0:T(8,128)(2,1)S(1)} %collective-permute-done.32.refs_2_.refs_10_), channel_id=1, source_target_pairs={{0,1},{1,0},{2,3},{3,2},{4,5},{5,4},{6,7},{7,6},{8,9},{9,8},{10,11... | collective-permute-start | bytes 589832 | tf_op jit(solution)/shard_map/ppermute | solution.py:175
  201.6 18.1 %collective-permute-start.45 = (bf16[320,256]{1,0:T(8,128)(2,1)S(1)}, bf16[320,256]{1,0:T(8,128)(2,1)S(1)}, u32[]{:S(2)}, u32[]{:S(2)}) collective-permute-start(bf16[320,256]{1,0:T(8,128)(2,1)S(1)} %copy-done.52), channel_id=1, source_target_pairs={{0,4},{1,5},{2,6},{3,7},{4,0},{5,1},{6,2},{7,3},{8,12},{9,13},{10,... | collective-permute-start | bytes 491528 | tf_op jit(solution)/shard_map/ppermute | solution.py:170
  203.8 16.5 %collective-permute-start.37 = (bf16[128,768]{1,0:T(8,128)(2,1)S(1)}, bf16[128,768]{1,0:T(8,128)(2,1)S(1)}, u32[]{:S(2)}, u32[]{:S(2)}) collective-permute-start(bf16[128,768]{1,0:T(8,128)(2,1)S(1)} %get-tuple-element.54.refs_2_.refs_3_.refs_4_), channel_id=1, source_target_pairs={{0,2},{1,3},{2,0},{3,1},{4,6},{5,7},{6,4},{7,5},{8,10},{9,11},{10,... | collective-permute-start | bytes 589832 | tf_op jit(solution)/shard_map/ppermute | solution.py:170
  205.4 18.6 %collective-permute-start.38 = (bf16[128,768]{1,0:T(8,128)(2,1)S(1)}, bf16[128,768]{1,0:T(8,128)(2,1)S(1)}, u32[]{:S(2)}, u32[]{:S(2)}) collective-permute-start(bf16[128,768]{1,0:T(8,128)(2,1)S(1)} %get-tuple-element.54.refs_2_.refs_3_.refs_4_), channel_id=1, source_target_pairs={{0,4},{1,5},{2,6},{3,7},{4,0},{5,1},{6,2},{7,3},{8,12},{9,13},{10,... | collective-permute-start | bytes 589832 | tf_op jit(solution)/shard_map/ppermute | solution.py:170
  209.7 56.7 %copy-start.51 = (bf16[320,256]{1,0:T(8,128)(2,1)S(1)}, bf16[320,256]{1,0:T(8,128)(2,1)}, u32[]{:S(2)}) copy-start(bf16[320,256]{1,0:T(8,128)(2,1)} %get-tuple-element.60) | copy-start | bytes 491524
  212.0 65.1 %all-to-all-start.1 = ((bf16[8,32,768]{2,1,0:T(8,128)(2,1)}), bf16[8,32,768]{2,1,0:T(8,128)(2,1)S(1)}, u32[]{:S(2)}, u32[]{:S(2)}) async-start(bf16[8,32,768]{2,1,0:T(8,128)(2,1)} %bitcast.34), calls=%async_computation.1 | async-start | bytes 786432 | tf_op jit(solution)/shard_map/all_to_all | solution.py:523
  215.8 16.2 %collective-permute-start.39 = (bf16[128,768]{1,0:T(8,128)(2,1)S(1)}, bf16[128,768]{1,0:T(8,128)(2,1)S(1)}, u32[]{:S(2)}, u32[]{:S(2)}) collective-permute-start(bf16[128,768]{1,0:T(8,128)(2,1)S(1)} %get-tuple-element.54.refs_2_.refs_3_.refs_4_), channel_id=1, source_target_pairs={{0,6},{1,7},{2,4},{3,5},{4,2},{5,3},{6,0},{7,1},{8,14},{9,15},{10,... | collective-permute-start | bytes 589832 | tf_op jit(solution)/shard_map/ppermute | solution.py:170
  219.6 16.2 %collective-permute-start.47 = (bf16[128,768]{1,0:T(8,128)(2,1)S(1)}, bf16[128,768]{1,0:T(8,128)(2,1)S(1)}, u32[]{:S(2)}, u32[]{:S(2)}) collective-permute-start(bf16[128,768]{1,0:T(8,128)(2,1)S(1)} %get-tuple-element.62.refs_5_), channel_id=1, source_target_pairs={{0,2},{1,3},{2,0},{3,1},{4,6},{5,7},{6,4},{7,5},{8,10},{9,11},{10,... | collective-permute-start | bytes 589832 | tf_op jit(solution)/shard_map/ppermute | solution.py:170
  219.6 31.4 %collective-permute-start.48 = (bf16[128,768]{1,0:T(8,128)(2,1)S(1)}, bf16[128,768]{1,0:T(8,128)(2,1)S(1)}, u32[]{:S(2)}, u32[]{:S(2)}) collective-permute-start(bf16[128,768]{1,0:T(8,128)(2,1)S(1)} %get-tuple-element.62.refs_5_), channel_id=1, source_target_pairs={{0,4},{1,5},{2,6},{3,7},{4,0},{5,1},{6,2},{7,3},{8,12},{9,13},{10,... | collective-permute-start | bytes 589832 | tf_op jit(solution)/shard_map/ppermute | solution.py:170
  220.3 30.8 %collective-permute-start.49 = (bf16[128,768]{1,0:T(8,128)(2,1)S(1)}, bf16[128,768]{1,0:T(8,128)(2,1)S(1)}, u32[]{:S(2)}, u32[]{:S(2)}) collective-permute-start(bf16[128,768]{1,0:T(8,128)(2,1)S(1)} %get-tuple-element.62.refs_5_), channel_id=1, source_target_pairs={{0,6},{1,7},{2,4},{3,5},{4,2},{5,3},{6,0},{7,1},{8,14},{9,15},{10,... | collective-permute-start | bytes 589832 | tf_op jit(solution)/shard_map/ppermute | solution.py:170
  224.0 27.0 %collective-permute-start.34 = (bf16[320,256]{1,0:T(8,128)(2,1)S(1)}, bf16[320,256]{1,0:T(8,128)(2,1)S(1)}, u32[]{:S(2)}, u32[]{:S(2)}) collective-permute-start(bf16[320,256]{1,0:T(8,128)(2,1)S(1)} %get-tuple-element.50), channel_id=1, source_target_pairs={{0,2},{1,3},{2,0},{3,1},{4,6},{5,7},{6,4},{7,5},{8,10},{9,11},{10,... | collective-permute-start | bytes 491528 | tf_op jit(solution)/shard_map/ppermute | solution.py:170
  232.0 33.8 %collective-permute-start.40 = (bf16[128,768]{1,0:T(8,128)(2,1)S(1)}, bf16[128,768]{1,0:T(8,128)(2,1)S(1)}, u32[]{:S(2)}, u32[]{:S(2)}) collective-permute-start(bf16[128,768]{1,0:T(8,128)(2,1)S(1)} %collective-permute-done.37.refs_5_), channel_id=1, source_target_pairs={{0,1},{1,0},{2,3},{3,2},{4,5},{5,4},{6,7},{7,6},{8,9},{9,8},{10,11... | collective-permute-start | bytes 589832 | tf_op jit(solution)/shard_map/ppermute | solution.py:175
  235.8 30.1 %collective-permute-start.41 = (bf16[128,768]{1,0:T(8,128)(2,1)S(1)}, bf16[128,768]{1,0:T(8,128)(2,1)S(1)}, u32[]{:S(2)}, u32[]{:S(2)}) collective-permute-start(bf16[128,768]{1,0:T(8,128)(2,1)S(1)} %collective-permute-done.38.refs_6_), channel_id=1, source_target_pairs={{0,1},{1,0},{2,3},{3,2},{4,5},{5,4},{6,7},{7,6},{8,9},{9,8},{10,11... | collective-permute-start | bytes 589832 | tf_op jit(solution)/shard_map/ppermute | solution.py:175
  251.0 14.3 %collective-permute-start.35 = (bf16[320,256]{1,0:T(8,128)(2,1)S(1)}, bf16[320,256]{1,0:T(8,128)(2,1)S(1)}, u32[]{:S(2)}, u32[]{:S(2)}) collective-permute-start(bf16[320,256]{1,0:T(8,128)(2,1)S(1)} %get-tuple-element.51), channel_id=1, source_target_pairs={{0,4},{1,5},{2,6},{3,7},{4,0},{5,1},{6,2},{7,3},{8,12},{9,13},{10,... | collective-permute-start | bytes 491528 | tf_op jit(solution)/shard_map/ppermute | solution.py:170
  251.1 15.3 %collective-permute-start.42 = (bf16[128,768]{1,0:T(8,128)(2,1)S(1)}, bf16[128,768]{1,0:T(8,128)(2,1)S(1)}, u32[]{:S(2)}, u32[]{:S(2)}) collective-permute-start(bf16[128,768]{1,0:T(8,128)(2,1)S(1)} %collective-permute-done.39.refs_7_), channel_id=1, source_target_pairs={{0,1},{1,0},{2,3},{3,2},{4,5},{5,4},{6,7},{7,6},{8,9},{9,8},{10,11... | collective-permute-start | bytes 589832 | tf_op jit(solution)/shard_map/ppermute | solution.py:175
  251.1 14.3 %collective-permute-start.36 = (bf16[320,256]{1,0:T(8,128)(2,1)S(1)}, bf16[320,256]{1,0:T(8,128)(2,1)S(1)}, u32[]{:S(2)}, u32[]{:S(2)}) collective-permute-start(bf16[320,256]{1,0:T(8,128)(2,1)S(1)} %get-tuple-element.52), channel_id=1, source_target_pairs={{0,6},{1,7},{2,4},{3,5},{4,2},{5,3},{6,0},{7,1},{8,14},{9,15},{10,... | collective-permute-start | bytes 491528 | tf_op jit(solution)/shard_map/ppermute | solution.py:170
  265.3 9.2 %collective-permute-start.50 = (bf16[128,768]{1,0:T(8,128)(2,1)S(1)}, bf16[128,768]{1,0:T(8,128)(2,1)S(1)}, u32[]{:S(2)}, u32[]{:S(2)}) collective-permute-start(bf16[128,768]{1,0:T(8,128)(2,1)S(1)} %get-tuple-element.62.refs_5_), channel_id=1, source_target_pairs={{0,1},{1,0},{2,3},{3,2},{4,5},{5,4},{6,7},{7,6},{8,9},{9,8},{10,11... | collective-permute-start | bytes 589832 | tf_op jit(solution)/shard_map/ppermute | solution.py:175
  265.3 9.2 %collective-permute-start.51 = (bf16[128,768]{1,0:T(8,128)(2,1)S(1)}, bf16[128,768]{1,0:T(8,128)(2,1)S(1)}, u32[]{:S(2)}, u32[]{:S(2)}) collective-permute-start(bf16[128,768]{1,0:T(8,128)(2,1)S(1)} %collective-permute-done.47.refs_6_), channel_id=1, source_target_pairs={{0,1},{1,0},{2,3},{3,2},{4,5},{5,4},{6,7},{7,6},{8,9},{9,8},{10,11... | collective-permute-start | bytes 589832 | tf_op jit(solution)/shard_map/ppermute | solution.py:175
  265.8 8.7 %collective-permute-start.52 = (bf16[128,768]{1,0:T(8,128)(2,1)S(1)}, bf16[128,768]{1,0:T(8,128)(2,1)S(1)}, u32[]{:S(2)}, u32[]{:S(2)}) collective-permute-start(bf16[128,768]{1,0:T(8,128)(2,1)S(1)} %collective-permute-done.48.refs_7_), channel_id=1, source_target_pairs={{0,1},{1,0},{2,3},{3,2},{4,5},{5,4},{6,7},{7,6},{8,9},{9,8},{10,11... | collective-permute-start | bytes 589832 | tf_op jit(solution)/shard_map/ppermute | solution.py:175
  265.9 8.6 %collective-permute-start.53 = (bf16[128,768]{1,0:T(8,128)(2,1)S(1)}, bf16[128,768]{1,0:T(8,128)(2,1)S(1)}, u32[]{:S(2)}, u32[]{:S(2)}) collective-permute-start(bf16[128,768]{1,0:T(8,128)(2,1)S(1)} %collective-permute-done.49.refs_8_), channel_id=1, source_target_pairs={{0,1},{1,0},{2,3},{3,2},{4,5},{5,4},{6,7},{7,6},{8,9},{9,8},{10,11... | collective-permute-start | bytes 589832 | tf_op jit(solution)/shard_map/ppermute | solution.py:175
  266.4 8.1 %collective-permute-start.46 = (bf16[320,256]{1,0:T(8,128)(2,1)S(1)}, bf16[320,256]{1,0:T(8,128)(2,1)S(1)}, u32[]{:S(2)}, u32[]{:S(2)}) collective-permute-start(bf16[320,256]{1,0:T(8,128)(2,1)S(1)} %copy-done.51), channel_id=1, source_target_pairs={{0,6},{1,7},{2,4},{3,5},{4,2},{5,3},{6,0},{7,1},{8,14},{9,15},{10,... | collective-permute-start | bytes 491528 | tf_op jit(solution)/shard_map/ppermute | solution.py:170
  (48 other events, 305.7 us)
where the time goes:
time: 283 us; the launch traced here: 280 us
  waiting for transfers between devices  123 us (43%)
  starting transfers between devices  66.3 us (23%)
  Pallas kernels  33.1 us (12%)
  matrix products  21.8 us (8%)
  local copies, waits for them, and re-layouts  19.6 us (7%)
  other arithmetic  13.9 us (5%)
    ppermute x17, waiting for transfers between devices, on_chips(): return lax.ppermute(value, 'expert', perm)  62.5 us
    ppermute x12, waiting for transfers between devices, between_layers(): return lax.ppermute(value, 'section', pairs)  60.6 us
    ppermute x17, starting transfers between devices, on_chips(): return lax.ppermute(value, 'expert', perm)  34.5 us
    pallas_call x4, Pallas kernels, call_rows(): pl.pallas_call(body, out_shape=[jax.ShapeDtypeStruct(shape, kind) for sha...  21.1 us
    ppermute x12, starting transfers between devices, between_layers(): return lax.ppermute(value, 'section', pairs)  19 us
    dot_general x8, matrix products, dot_first(): lax.dot_general(left, right, (((0,), (0,)), ((), ())), preferred_element_...  16.7 us
    pallas_call x3, Pallas kernels, spread(): pl.pallas_call(body, out_shape=outs, in_specs=[pl.BlockSpec(memory_space=...  7.89 us
  transfers between devices with their start and end apart: 56, of which 12 were waited for; matrix products, arithmetic and copies ran while one was open for 17% of the time, Pallas kernels for 12%

commit v1 on v0

--- a/solution.py
+++ b/solution.py
@@ -148,7 +148,8 @@
 CORES = 2
 CHIPS = 4
 LAYERS = 4
-ROOM = 24 * 2**20
+WIDE_ROOM = 24 * 2**20
+ROOM = 16 * 2**20
 
 
 def dot(left, right):
@@ -186,14 +187,21 @@
     outward = on_chips(across, [(1, 0), (2, 3)])
     far_outward = on_chips(far_across, [(1, 0), (2, 3)])
     second = jnp.where(middle, across, outward)
-    third = jnp.where(middle, far_across, far_outward)
-    held = [core, beside, second, third]
-    return held + [swap_cores(piece) for piece in held]
-
-
-def held_chips(chip, middle):
-    near, far = chip ^ 3, chip ^ 2
-    return [chip, chip ^ 1, jnp.where(middle, near, far), jnp.where(middle, far, near)]
+    held = [core, beside, second]
+    thirds = [far_across, far_outward]
+    return held + [swap_cores(piece) for piece in held], thirds + [
+        swap_cores(piece) for piece in thirds
+    ]
+
+
+def row_marks(route, weight, chip, core, middle):
+    count = CHIPS * CORES
+    place = lax.broadcasted_iota(jnp.int32, (1, 2 * count), 1)
+    step = (place % count) // CORES
+    turned = jnp.where(jnp.logical_and(step >= 2, middle), 5 - step, step)
+    expert = CORES * (chip ^ turned) + (core ^ (place % CORES))
+    marks = (route == expert).astype(jnp.float32)
+    return jnp.where(place < count, marks, weight)
 
 
 def across_chips(value, step):
@@ -233,17 +241,13 @@
     return (pair[0].astype(jnp.float32) + pair[1].astype(jnp.float32)).astype(jnp.bfloat16)
 
 
-def expert_ids(chips, core):
-    return jnp.stack(
-        [CORES * chip + core for chip in chips] + [CORES * chip + 1 - core for chip in chips]
-    ).astype(jnp.int32)
-
-
-def routed_product(rows, route, ids_ref, core_refs, transposed):
+def routed_product(rows, marks, core_refs, transposed, copies=None):
     dims = (((1,), (1 if transposed else 0,)), ((), ()))
     total = None
     for place, core_ref in enumerate(core_refs):
-        chosen = jnp.where(route == ids_ref[place], rows, jnp.zeros_like(rows))
+        if copies is not None:
+            copies[place].wait()
+        chosen = jnp.where(marks[:, place : place + 1] > 0.5, rows, jnp.zeros_like(rows))
         term = lax.dot_general(
             chosen, core_ref[...], dims, preferred_element_type=jnp.float32
         )
@@ -251,46 +255,61 @@
     return total
 
 
-def backward_rows(score, weight, slope, route, ids_ref, core_refs):
-    grad_hidden = (weight * score).astype(jnp.bfloat16)
+def backward_rows(score, slope, marks, core_refs):
+    count = len(core_refs)
+    grad_hidden = (marks[:, count : count + 1] * score).astype(jnp.bfloat16)
     grad_pre = (grad_hidden.astype(jnp.float32) * slope).astype(jnp.bfloat16)
-    grad_proj = routed_product(grad_pre, route, ids_ref, core_refs, True)
+    grad_proj = routed_product(grad_pre, marks, core_refs, True)
     return grad_pre, grad_proj.astype(jnp.bfloat16)
 
 
-def first_kernel(ids_ref, proj_ref, route_ref, weight_ref, own_ref, gram_ref, *refs):
-    count = len(refs) - 6
-    core_refs = refs[:count]
-    hidden_ref, scaled_ref, slope_ref, score_ref, grad_ref, chain_ref = refs[count:]
-    route = route_ref[...]
-    weight = weight_ref[...]
-    pre = routed_product(proj_ref[...], route, ids_ref, core_refs, False)
+def first_kernel(middle_ref, proj_ref, marks_ref, own_ref, gram_ref, *refs):
+    count = CHIPS * CORES
+    held, thirds = refs[: count - 2], refs[count - 2 : count + 2]
+    scaled_ref, slope_ref, score_ref, chain_ref = refs[count + 2 : count + 6]
+    core_refs, arrived = refs[count + 6 : -1], refs[-1]
+    middle = middle_ref[0] > 0
+    sources = paired(held, [thirds[:2], thirds[2:]])
+    copies = []
+    for place, (source, core_ref) in enumerate(zip(sources, core_refs)):
+        choices = source if isinstance(source, tuple) else (source,)
+        moves = [pltpu.make_async_copy(ref, core_ref, arrived.at[place]) for ref in choices]
+        copies.append(moves[0])
+        if len(moves) == 1:
+            moves[0].start()
+        else:
+            pl.when(middle)(moves[0].start)
+            pl.when(jnp.logical_not(middle))(moves[1].start)
+    marks = marks_ref[...]
+    pre = routed_product(proj_ref[...], marks, core_refs, False, copies)
     sigmoid = 1.0 / (1.0 + jnp.exp(-pre))
     hidden = (pre * sigmoid).astype(jnp.bfloat16)
     slope = sigmoid * (1.0 + pre * (1.0 - sigmoid))
+    weight = marks[:, count : count + 1]
     scaled = (weight * hidden.astype(jnp.float32)).astype(jnp.bfloat16)
     score = own_ref[...] + dot(scaled, gram_ref[...])
-    hidden_ref[...] = hidden
     scaled_ref[...] = scaled
     slope_ref[...] = slope
     score_ref[...] = score
-    grad_pre, grad_proj = backward_rows(score, weight, slope, route, ids_ref, core_refs)
-    grad_ref[...] = grad_pre
+    _, grad_proj = backward_rows(score, slope, marks, core_refs)
     chain_ref[...] = (scaled.astype(jnp.float32) + grad_proj.astype(jnp.float32)).astype(
         jnp.bfloat16
     )
 
 
-def turn_kernel(terms, ids_ref, route_ref, weight_ref, scaled_ref, slope_ref, score_ref, *refs):
+def paired(held, thirds):
+    own, other = [*held[:3], thirds[0]], [*held[3:], thirds[1]]
+    return [piece for pair in zip(own, other) for piece in pair]
+
+
+def turn_kernel(terms, marks_ref, scaled_ref, slope_ref, score_ref, late_ref, *refs):
     core_refs = refs[2 * terms : len(refs) - 4]
     next_ref, grad_ref, proj_ref, chain_ref = refs[len(refs) - 4 :]
-    score = score_ref[...]
+    score = score_ref[...] + late_ref[...]
     for term in range(terms):
         score = score + dot(refs[2 * term][...], refs[2 * term + 1][...])
     next_ref[...] = score
-    grad_pre, grad_proj = backward_rows(
-        score, weight_ref[...], slope_ref[...], route_ref[...], ids_ref, core_refs
-    )
+    grad_pre, grad_proj = backward_rows(score, slope_ref[...], marks_ref[...], core_refs)
     grad_ref[...] = grad_pre
     proj_ref[...] = grad_proj
     chain_ref[...] = (scaled_ref[...].astype(jnp.float32) + grad_proj.astype(jnp.float32)).astype(
@@ -298,51 +317,44 @@
     )
 
 
-def call_rows(body, outs, scalars, arrays, flops):
+def call_rows(body, outs, arrays, flops, scalars=()):
     in_bytes = sum(array.size * array.dtype.itemsize for array in arrays)
     return pl.pallas_call(
         body,
         out_shape=[jax.ShapeDtypeStruct(shape, kind) for shape, kind in outs],
-        in_specs=[pl.BlockSpec(memory_space=pltpu.SMEM)]
+        in_specs=[pl.BlockSpec(memory_space=pltpu.SMEM)] * len(scalars)
         + [pl.BlockSpec(memory_space=pltpu.VMEM)] * len(arrays),
         out_specs=[pl.BlockSpec(memory_space=pltpu.VMEM)] * len(outs),
         compiler_params=pltpu.CompilerParams(vmem_limit_bytes=ROOM),
         cost_estimate=pl.CostEstimate(flops=flops, bytes_accessed=in_bytes, transcendentals=0),
-    )(scalars, *arrays)
-
-
-def spread_kernel(terms, last, base_ref, *refs):
+    )(*scalars, *arrays)
+
+
+def spread_kernel(terms, base_ref, *refs):
     total = base_ref[...].astype(jnp.float32)
     for term in range(terms):
         half_ref, near_ref, far_ref = refs[3 * term : 3 * term + 3]
         values = jnp.concatenate([near_ref[...], far_ref[...]], axis=0)
         total = total + times_transposed(half_ref[...], values)
-    outs = refs[3 * terms :]
-    if not last:
-        outs[0][...] = total
-        return
     count = total.shape[0] // CHIPS
-    for step in range(CHIPS):
-        outs[step][...] = total[step * count : (step + 1) * count].astype(jnp.bfloat16)
-
-
-def spread(base, terms, last):
+    for step, out_ref in enumerate(refs[3 * terms :]):
+        out_ref[...] = total[step * count : (step + 1) * count].astype(jnp.bfloat16)
+
+
+def spread(base, terms):
     arrays = [base] + [array for term in terms for array in term]
     height, width = base.shape
-    if last:
-        outs = [jax.ShapeDtypeStruct((height // CHIPS, width), jnp.bfloat16)] * CHIPS
-    else:
-        outs = [jax.ShapeDtypeStruct((height, width), jnp.float32)]
 
     def body(*refs):
-        spread_kernel(len(terms), last, *refs)
+        spread_kernel(len(terms), *refs)
 
     return pl.pallas_call(
         body,
-        out_shape=outs,
+        name="spread",
+        out_shape=[jax.ShapeDtypeStruct((height // CHIPS, width), jnp.bfloat16)] * CHIPS,
         in_specs=[pl.BlockSpec(memory_space=pltpu.VMEM)] * len(arrays),
-        out_specs=[pl.BlockSpec(memory_space=pltpu.VMEM)] * len(outs),
-        compiler_params=pltpu.CompilerParams(vmem_limit_bytes=ROOM),
+        out_specs=[pl.BlockSpec(memory_space=pltpu.VMEM)] * CHIPS,
+        compiler_params=pltpu.CompilerParams(vmem_limit_bytes=WIDE_ROOM),
         cost_estimate=pl.CostEstimate(
             flops=2 * height * width * terms[0][0].shape[1] * len(terms),
             bytes_accessed=sum(array.size * array.dtype.itemsize for array in arrays),
@@ -401,11 +413,11 @@
     chip, core = here // CORES, here % CORES
     middle = jnp.logical_or(chip == 1, chip == 2)
     tokens = inputs[0].reshape(rows, channels)
-    weight = gate[0].reshape(rows, 1)
-    chosen = route[0].reshape(rows, 1)
-
-    pieces = gather_cores(cores[0, 0], middle)
-    ids = expert_ids(held_chips(chip, middle), core)
+
+    held, thirds = gather_cores(cores[0, 0], middle)
+    marks = row_marks(
+        route[0].reshape(rows, 1), gate[0].reshape(rows, 1), chip, core, middle
+    )
 
     down = [(3, 2), (1, 0)]
     two_down = [(3, 1), (2, 0)]
@@ -414,11 +426,12 @@
     half_down = between_layers(own_half, down)
     half_two = between_layers(own_half, two_down)
     half_cross = between_layers(half_two, crossed)
-    difference = tokens.astype(f32) - teacher[0].reshape(rows, channels).astype(f32)
-    difference = chip_columns(difference.astype(bf16).T, chip, core)
+    turned = lax.optimization_barrier(tokens.T)
+    wanted = lax.optimization_barrier(teacher[0].reshape(rows, channels).T)
+    difference = (turned.astype(f32) - wanted.astype(f32)).astype(bf16)
+    difference = chip_columns(difference, chip, core)
     step_down = between_layers(difference, down)
     step_two = between_layers(difference, two_down)
-    step_cross = between_layers(step_two, crossed)
 
     capacity = max(2, 2 * token_count // devices)
     slots = micro_count * capacity
@@ -434,7 +447,7 @@
     proj_slots = to_slots(projected)
     gram = gram_sum(own_gram)
     own_score = both_cores(dot_first(difference, own_half))
-    turned = chip_columns(tokens.T, chip, core)
+    turned = chip_columns(turned, chip, core)
     token_blocks = [
         turned[step * channels // devices : (step + 1) * channels // devices]
         for step in range(CHIPS)
@@ -445,15 +458,25 @@
 
     wide = (rows, ranks)
     product_flops = 2 * rows * ranks * ranks
-    _, scaled, slope, score, _, chain = call_rows(
+    scaled, slope, score, chain, *pieces = pl.pallas_call(
         first_kernel,
-        [(wide, bf16), (wide, bf16), (wide, f32), (wide, f32), (wide, bf16), (wide, bf16)],
-        ids,
-        [projected, chosen, weight, own_score, gram, *pieces],
-        product_flops * (2 * devices + 1),
-    )
-
-    def turn(score, terms):
+        name="first_turn",
+        out_shape=[jax.ShapeDtypeStruct(wide, kind) for kind in (bf16, f32, f32, bf16)]
+        + [pltpu.VMEM((ranks, ranks), bf16)] * devices,
+        in_specs=[pl.BlockSpec(memory_space=pltpu.SMEM)]
+        + [pl.BlockSpec(memory_space=pltpu.VMEM)] * 4
+        + [pl.BlockSpec(memory_space=pl.ANY)] * (devices + 2),
+        out_specs=[pl.BlockSpec(memory_space=pltpu.VMEM)] * (devices + 4),
+        scratch_shapes=[pltpu.SemaphoreType.DMA((devices,))],
+        compiler_params=pltpu.CompilerParams(vmem_limit_bytes=ROOM),
+        cost_estimate=pl.CostEstimate(
+            flops=product_flops * (2 * devices + 1),
+            bytes_accessed=2 * devices * ranks * ranks,
+            transcendentals=rows * ranks,
+        ),
+    )(middle.astype(jnp.int32).reshape(1), projected, marks, own_score, gram, *held, *thirds)
+
+    def turn(score, late, terms):
         arrays = [array for pair in terms for array in pair]
 
         def body(*refs):
@@ -462,25 +485,16 @@
         return call_rows(
             body,
             [(wide, f32), (wide, bf16), (wide, bf16), (wide, bf16)],
-            ids,
-            [chosen, weight, scaled, slope, score, *arrays, *pieces],
+            [marks, scaled, slope, score, late, *arrays, *pieces],
             product_flops * (devices + len(terms)),
         )
-
-    def with_swap(values):
-        return values, swap_cores(values)
 
     chain_first = chain
     first_down = between_layers(chain, [(3, 2)])
+    step_cross = between_layers(after(step_two, chain), crossed)
     first_two = between_layers(chain, [(3, 1)])
-    own_steps = after(difference, chain)
-    scaled_pair = with_swap(scaled)
-    spread_rows = spread(own_steps, [(own_half, *scaled_pair)], False)[0]
     proj_slots = lax.all_to_all(after(proj_slots, chain), "expert", 0, 0, tiled=True)
-    token_blocks = token_blocks[:1] + [
-        across_chips(after(token_blocks[step], chain), step) for step in range(1, CHIPS)
-    ]
-    score, _, _, chain = turn(score + down_score, [(first_down, down_gram)])
+    score, _, _, chain = turn(score, down_score, [(first_down, down_gram)])
 
     second_cross = between_layers(chain, [(2, 1)])
     second_two = between_layers(chain, [(2, 0)])
@@ -492,35 +506,47 @@
     late_score = both_cores(dot_first(late_steps, own_half))
     cross_product = gram_sum(cross_pair)
     score, _, _, chain = turn(
-        score + late_score, [(first_two, two_gram), (second_cross, cross_product)]
+        score, late_score, [(first_two, two_gram), (second_cross, cross_product)]
     )
 
     third_down = between_layers(chain, [(1, 0)])
-    two_values = with_swap(first_two + after(second_two, chain))
-    cross_values = with_swap(second_cross + after(first_three, chain))
-    down_values = with_swap(after(first_down, chain))
-    other_steps = step_down.astype(f32) + late_steps.astype(f32)
-    spread_rows = spread(
-        spread_rows + after(other_steps, chain),
-        [(half_two, *two_values), (half_cross, *cross_values), (half_down, *down_values)],
-        False,
-    )[0]
     scaled_rows = [scaled] + [across_chips(after(scaled, chain), step) for step in range(1, CHIPS)]
+    token_blocks = token_blocks[:1] + [
+        across_chips(after(token_blocks[step], chain), step) for step in range(1, CHIPS)
+    ]
+    steps_total = difference.astype(f32) + step_down.astype(f32)
+    steps_total = (steps_total + after(late_steps, chain).astype(f32)).astype(bf16)
     score, grad_pre, grad_proj, _ = turn(
-        score, [(second_two, two_gram), (first_three, cross_product), (third_down, down_gram)]
-    )
-
-    third_pair = with_swap(third_down)
-    mixed_blocks = list(spread(spread_rows, [(half_down, *third_pair)], True))
+        score,
+        jnp.zeros_like(score),
+        [(second_two, two_gram), (first_three, cross_product), (third_down, down_gram)],
+    )
+
+    def with_swap(values):
+        return values, swap_cores(values)
+
+    proj_rows = gather_rows(grad_proj)
+    scaled_pair = with_swap(after(scaled, chain))
+    two_pair = with_swap(first_two + after(second_two, chain))
+    cross_pair = with_swap(second_cross + after(first_three, chain))
+    down_pair = with_swap(first_down + third_down)
+    mixed_blocks = spread(
+        steps_total,
+        [
+            (own_half, *scaled_pair),
+            (half_two, *two_pair),
+            (half_cross, *cross_pair),
+            (half_down, *down_pair),
+        ],
+    )
     scaled_rows = [after(rows, mixed_blocks[0]) for rows in scaled_rows]
-    grad_slots = after(to_slots(grad_pre), mixed_blocks[0])
-    mixed_blocks = mixed_blocks[:1] + [
+    mixed_blocks = list(mixed_blocks[:1]) + [
         across_chips(mixed_blocks[step], step) for step in range(1, CHIPS)
     ]
     scaled_rows = scaled_rows + [scaled_pair[1]] + [swap_cores(rows) for rows in scaled_rows[1:]]
-    share = factor_rows(None, mixed_blocks, scaled_rows)
-    share = factor_rows(share, token_blocks, gather_rows(grad_proj))
-    grad_slots = lax.all_to_all(grad_slots, "expert", 0, 0, tiled=True)
+    share = factor_rows(None, token_blocks, proj_rows)
+    share = factor_rows(share, mixed_blocks, scaled_rows)
+    grad_slots = lax.all_to_all(to_slots(grad_pre), "expert", 0, 0, tiled=True)
     core_total = dot_first(proj_slots.reshape(-1, ranks), grad_slots.reshape(-1, ranks))
     return (share[None], core_total.astype(bf16)[None, None])
 

time: 283 us -> 274 us (0.968)
  waiting for transfers between devices: 123 us -> 88 us
  local copies, waits for them, and re-layouts: 19.6 us -> 31.1 us
  starting transfers between devices: 66.3 us -> 73.3 us
  other arithmetic: 13.9 us -> 19.6 us
    ppermute x12, waiting for transfers between devices: 60.6 us -> 22.6 us  [between_layers(): return lax.ppermute(value, 'section', pairs)]
    unnamed x112 -> x154, local copies, waits for them, and re-layouts: 5.62 us -> 22.7 us
    pallas_call x4 -> x3, Pallas kernels: 21.1 us -> 13.2 us  [call_rows(): pl.pallas_call(body, out_shape=[jax.ShapeDtypeStruct(shape, kind) for sha...]
    pallas_call x3 -> x2, Pallas kernels: 7.89 us -> 13 us  [the longest x1 8.59 us: gathered_plan(): pl.pallas_call(first_kernel, name='first_turn', out_shape=[jax.ShapeDtype...]
    ppermute x12, starting transfers between devices: 19 us -> 23.5 us  [between_layers(): return lax.ppermute(value, 'section', pairs)]
    ppermute x17, waiting for transfers between devices: 62.5 us -> 65.4 us  [on_chips(): return lax.ppermute(value, 'expert', perm)]
  transfers between devices with their start and end apart: 56 -> 56, of which waited for: 12 -> 11; matrix products, arithmetic and copies ran while one was open for 17% -> 18% of each run, Pallas kernels for 12% -> 11%
where the time goes in v1:
time: 274 us; the launch traced here: 268 us
  waiting for transfers between devices  88 us (32%)
  starting transfers between devices  73.3 us (27%)
  local copies, waits for them, and re-layouts  31.1 us (11%)
  Pallas kernels  30.7 us (11%)
  matrix products  23.9 us (9%)
  other arithmetic  19.6 us (7%)
    ppermute x17, waiting for transfers between devices, on_chips(): return lax.ppermute(value, 'expert', perm)  65.4 us
    ppermute x17, starting transfers between devices, on_chips(): return lax.ppermute(value, 'expert', perm)  34.7 us
    ppermute x12, starting transfers between devices, between_layers(): return lax.ppermute(value, 'section', pairs)  23.5 us
    unnamed x154, local copies, waits for them, and re-layouts  22.7 us
    ppermute x12, waiting for transfers between devices, between_layers(): return lax.ppermute(value, 'section', pairs)  22.6 us
    dot_general x8, matrix products, dot_first(): lax.dot_general(left, right, (((0,), (0,)), ((), ())), preferred_element_...  18.9 us
    pallas_call x3, Pallas kernels, call_rows(): pl.pallas_call(body, out_shape=[jax.ShapeDtypeStruct(shape, kind) for sha...  13.2 us
    pallas_call x1, Pallas kernels, gathered_plan(): pl.pallas_call(first_kernel, name='first_turn', out_shape=[jax.ShapeDtype...  8.59 us
  transfers between devices with their start and end apart: 56, of which 11 were waited for; matrix products, arithmetic and copies ran while one was open for 18% of the time, Pallas kernels for 11%

profile of v1, /device:TPU:0, one launch (start us, length us, event | category | flops | bytes accessed | tf_op | source)
XLA Modules:
  0.0 268.4 jit_solution(213873562457268594)
XLA Ops:
  0.7 1.5 copy.11
  4.4 3.1 %collective-permute-start.4 = (bf16[768,768]{1,0:T(8,128)(2,1)S(1)}, bf16[768,768]{1,0:T(8,128)(2,1)}, u32[]{:S(2)}, u32[]{:S(2)}) collective-permute-start(bf16[768,768]{1,0:T(8,128)(2,1)S(1)} %bitcast.46), channel_id=1, source_target_pairs={{0,2},{1,3},{2,0},{3,1},{4,6},{5,7},{6,4},{7,5},{8,10},{9,11},{10,... | collective-permute-start | bytes 3538952 | tf_op jit(solution)/shard_map/ppermute | solution.py:171
  7.5 1.6 dynamic-slice_bitcast_fusion.3
  9.2 2.8 %convolution_convert_fusion.3 = bf16[768,768]{1,0:T(8,128)(2,1)} fusion(bf16[1280,768]{1,0:T(8,128)(2,1)S(1)} %pad_maximum_fusion.refs_1_), kind=kOutput, calls=%fused_computation.11 | convolution fusion | flops 1510539264 | bytes 3145728 | tf_op jit(solution)/shard_map/dot_general | solution.py:160
  12.0 1.7 collective-permute-start.5
  14.7 1.4 collective-permute-start.14
  17.5 16.0 %collective-permute-done.4.refs_1_ = bf16[768,768]{1,0:T(8,128)(2,1)} collective-permute-done((bf16[768,768]{1,0:T(8,128)(2,1)S(1)}, bf16[768,768]{1,0:T(8,128)(2,1)}, u32[]{:S(2)}, u32[]{:S(2)}) %collective-permute-start.4) | collective-permute-done | bytes 1179680 | tf_op jit(solution)/shard_map/ppermute | solution.py:171
  33.5 1.7 collective-permute-start.10
  36.7 1.8 pad_maximum_fusion.3
  38.5 1.3 collective-permute-start.17
  39.8 1.3 collective-permute-start.23
  41.1 1.3 collective-permute-start.6
  43.1 3.0 %fusion.3.proj_ref = bf16[128,768]{1,0:T(8,128)(2,1)S(1)} fusion(bf16[128,2560]{1,0:T(8,128)(2,1)} %bitcast.53, bf16[1,2560,768]{2,1,0:T(8,128)(2,1)} %param.12), kind=kOutput, calls=%fused_computation.19 | convolution fusion | flops 503414784 | bytes 4784128 | tf_op jit(solution)/shard_map/dot_general | solution.py:156
  47.1 1.3 collective-permute-start.11
  48.4 1.8 fusion.15
  51.6 21.6 %collective-permute-done.6 = bf16[768,768]{1,0:T(8,128)(2,1)} collective-permute-done((bf16[768,768]{1,0:T(8,128)(2,1)}, bf16[768,768]{1,0:T(8,128)(2,1)}, u32[]{:S(2)}, u32[]{:S(2)}) %collective-permute-start.6) | collective-permute-done | bytes 1179680 | tf_op jit(solution)/shard_map/ppermute | solution.py:171
  73.9 1.5 broadcast_select_fusion.refs_2_
  77.0 10.1 %collective-permute-done.23.refs_4_ = bf16[1280,768]{1,0:T(8,128)(2,1)} collective-permute-done((bf16[1280,768]{1,0:T(8,128)(2,1)S(1)}, bf16[1280,768]{1,0:T(8,128)(2,1)}, u32[]{:S(2)}, u32[]{:S(2)}) %collective-permute-start.23) | collective-permute-done | bytes 1966112 | tf_op jit(solution)/shard_map/ppermute | solution.py:180
  87.0 5.5 %collective-permute-start.26 = (bf16[1280,768]{1,0:T(8,128)(2,1)}, bf16[1280,768]{1,0:T(8,128)(2,1)S(1)}, u32[]{:S(2)}, u32[]{:S(2)}) collective-permute-start(bf16[1280,768]{1,0:T(8,128)(2,1)} %collective-permute-done.23.refs_4_), channel_id=1, source_target_pairs={{0,8},{8,0},{1,9},{9,1},{2,10},{10,2},{3,11},{11,3},{4,12},{12,4},... | collective-permute-start | bytes 5898248 | tf_op jit(solution)/shard_map/ppermute | solution.py:180
  92.7 5.5 %collective-permute-done.11.refs_7_ = bf16[768,768]{1,0:T(8,128)(2,1)} collective-permute-done((bf16[768,768]{1,0:T(8,128)(2,1)}, bf16[768,768]{1,0:T(8,128)(2,1)}, u32[]{:S(2)}, u32[]{:S(2)}) %collective-permute-start.11) | collective-permute-done | bytes 1179680 | tf_op jit(solution)/shard_map/ppermute | solution.py:171
  98.2 3.3 %convolution_convert_fusion.2 = bf16[768,768]{1,0:T(8,128)(2,1)S(1)} fusion(bf16[1280,768]{1,0:T(8,128)(2,1)} %collective-permute-done.17.refs_10_, bf16[1280,768]{1,0:T(8,128)(2,1)S(1)} %pad_maximum_fusion.refs_1_), kind=kOutput, calls=%fused_computation.10 | convolution fusion | flops 1510539264 | bytes 5111808 | tf_op jit(solution)/shard_map/dot_general | solution.py:160
  103.1 1.9 add_convert_fusion.3.gram_ref
  106.1 1.6 collective-permute-start.19
  107.7 3.3 %convolution_convert_fusion.1 = bf16[768,768]{1,0:T(8,128)(2,1)S(1)} fusion(bf16[1280,768]{1,0:T(8,128)(2,1)} %collective-permute-done.23.refs_4_, bf16[1280,768]{1,0:T(8,128)(2,1)S(1)} %pad_maximum_fusion.refs_1_), kind=kOutput, calls=%fused_computation.9 | convolution fusion | flops 1510539264 | bytes 5111808 | tf_op jit(solution)/shard_map/dot_general | solution.py:160
  111.6 8.6 %first_turn.1 = (bf16[128,768]{1,0:T(8,128)(2,1)S(1)}, f32[128,768]{1,0:T(8,128)S(1)}, f32[128,768]{1,0:T(8,128)S(1)}, bf16[128,768]{1,0:T(8,128)(2,1)}, bf16[76...) custom-call(s32[1]{0:T(128)} %bitcast.2.middle_ref, ...), custom_call_target="tpu_custom_call" | custom-call | flops 2566914048 | bytes 9437184 | tf_op jit(solution)/shard_map/first_turn/pallas_call | solution.py:461
  120.2 6.2 %collective-permute-done.19 = bf16[1280,256]{1,0:T(8,128)(2,1)S(1)} collective-permute-done((bf16[1280,256]{1,0:T(8,128)(2,1)}, bf16[1280,256]{1,0:T(8,128)(2,1)S(1)}, u32[]{:S(2)}, u32[]{:S(2)}) %collective-permute-start.19) | collective-permute-done | bytes 655392 | tf_op jit(solution)/shard_map/ppermute | solution.py:180
  127.1 5.6 %collective-permute-start.20 = (bf16[1280,256]{1,0:T(8,128)(2,1)S(1)}, bf16[1280,256]{1,0:T(8,128)(2,1)S(1)}, u32[]{:S(2)}, u32[]{:S(2)}) collective-permute-start(bf16[1280,256]{1,0:T(8,128)(2,1)S(1)} %collective-permute-done.19), channel_id=1, source_target_pairs={{0,8},{8,0},{1,9},{9,1},{2,10},{10,2},{3,11},{11,3},{4,12},{12,4},... | collective-permute-start | bytes 1966088 | tf_op jit(solution)/shard_map/ppermute | solution.py:180
  133.0 3.8 %shard_map.86 = (f32[128,768]{1,0:T(8,128)S(1)}, bf16[128,768]{1,0:T(8,128)(2,1)}, bf16[128,768]{1,0:T(8,128)(2,1)}, bf16[128,768]{1,0:T(8,128)(2,1)S(1)}) custom-call(f32[128,16]{1,0:T(8,128)S(1)} %copy-done.23, bf16[128,768]{1,0:T(8,128)(2,1)S(1)} %get-tuple-element.72.refs_1_.refs_2_.refs_5_, f32[128,768]{1,0:T(8,128)S(1)} %get-tuple-element.41.refs_2_, ...), custom_call_target="tpu_custom_call" | custom-call | flops 1358954496 | bytes 12197888 | tf_op jit(solution)/shard_map/pallas_call | solution.py:322
  142.6 2.8 %convolution_convert_fusion = bf16[768,768]{1,0:T(8,128)(2,1)} fusion(bf16[1280,768]{1,0:T(8,128)(2,1)S(1)} %collective-permute-done.26.refs_7_, bf16[1280,768]{1,0:T(8,128)(2,1)S(1)} %pad_maximum_fusion.refs_1_), kind=kOutput, calls=%fused_computation.8 | convolution fusion | flops 1510539264 | bytes 5111808 | tf_op jit(solution)/shard_map/dot_general | solution.py:160
  145.5 3.7 %collective-permute-done.20 = bf16[1280,256]{1,0:T(8,128)(2,1)S(1)} collective-permute-done((bf16[1280,256]{1,0:T(8,128)(2,1)S(1)}, bf16[1280,256]{1,0:T(8,128)(2,1)S(1)}, u32[]{:S(2)}, u32[]{:S(2)}) %collective-permute-start.20) | collective-permute-done | bytes 655392 | tf_op jit(solution)/shard_map/ppermute | solution.py:180
  149.4 1.6 fusion.16
  151.0 1.8 slice.47
  153.8 1.3 add_convert_fusion.1.refs_6_
  155.1 1.3 collective-permute-start.22
  156.5 5.1 %all-to-all-start = ((bf16[8,32,768]{2,1,0:T(8,128)(2,1)}), bf16[8,32,768]{2,1,0:T(8,128)(2,1)}, u32[]{:S(2)}, u32[]{:S(2)}) async-start(bf16[8,32,768]{2,1,0:T(8,128)(2,1)} %bitcast.55), calls=%async_computation | async-start | bytes 786432 | tf_op jit(solution)/shard_map/all_to_all | solution.py:496
  162.3 1.3 collective-permute-start.31
  163.6 1.5 collective-permute-start.32
  166.4 2.1 add_convert_fusion.refs_8_
  169.1 1.3 copy-done.9
  170.4 1.3 copy-done.12
  171.7 1.3 copy-done.14
  172.9 1.3 copy-done.16
  174.2 1.3 copy-done.17
  177.5 5.0 %shard_map.87 = (f32[128,768]{1,0:T(8,128)S(1)}, bf16[128,768]{1,0:T(8,128)(2,1)}, bf16[128,768]{1,0:T(8,128)(2,1)}, bf16[128,768]{1,0:T(8,128)(2,1)S(1)}) custom-call(f32[128,16]{1,0:T(8,128)S(1)} %copy-done.24, bf16[128,768]{1,0:T(8,128)(2,1)S(1)} %get-tuple-element.72.refs_1_.refs_2_.refs_5_, f32[128,768]{1,0:T(8,128)S(1)} %copy-done.20, ...), custom_call_target="tpu_custom_call" | custom-call | flops 1509949440 | bytes 13574144 | tf_op jit(solution)/shard_map/pallas_call | solution.py:322
  182.5 1.4 collective-permute-start.33
  184.6 2.5 collective-permute-start.28
  187.1 1.9 collective-permute-start.29
  190.6 2.6 collective-permute-done.33.refs_9_
  193.2 2.4 collective-permute-start.48
  196.4 4.5 %shard_map.88 = (f32[128,768]{1,0:T(8,128)}, bf16[128,768]{1,0:T(8,128)(2,1)S(1)}, bf16[128,768]{1,0:T(8,128)(2,1)}, bf16[128,768]{1,0:T(8,128)(2,1)}) custom-call(f32[128,16]{1,0:T(8,128)S(1)} %copy-done.24, bf16[128,768]{1,0:T(8,128)(2,1)S(1)} %get-tuple-element.72.refs_1_.refs_2_.refs_5_, f32[128,768]{1,0:T(8,128)S(1)} %copy-done.20, ...), custom_call_target="tpu_custom_call" | custom-call | flops 1660944384 | bytes 14950400 | tf_op jit(solution)/shard_map/pallas_call | solution.py:322
  200.8 1.3 collective-permute-start.49
  204.5 1.8 collective-permute-start.50
  207.0 11.0 %collective-permute-start.34 = (bf16[128,768]{1,0:T(8,128)(2,1)}, bf16[128,768]{1,0:T(8,128)(2,1)}, u32[]{:S(2)}, u32[]{:S(2)}) collective-permute-start(bf16[128,768]{1,0:T(8,128)(2,1)} %get-tuple-element.63.refs_4_), channel_id=1, source_target_pairs={{0,2},{1,3},{2,0},{3,1},{4,6},{5,7},{6,4},{7,5},{8,10},{9,11},{10,... | collective-permute-start | bytes 589832 | tf_op jit(solution)/shard_map/ppermute | solution.py:171
  219.2 1.8 collective-permute-start.36
  221.2 4.2 %all-to-all-start.1 = ((bf16[8,32,768]{2,1,0:T(8,128)(2,1)}), bf16[8,32,768]{2,1,0:T(8,128)(2,1)}, u32[]{:S(2)}, u32[]{:S(2)}) async-start(bf16[8,32,768]{2,1,0:T(8,128)(2,1)} %bitcast.13), calls=%async_computation.1 | async-start | bytes 786432 | tf_op jit(solution)/shard_map/all_to_all | solution.py:549
  225.5 1.8 add_convert_fusion.4.refs_0_
  229.8 4.4 %spread.1 = (bf16[320,256]{1,0:T(8,128)(2,1)S(1)}, bf16[320,256]{1,0:T(8,128)(2,1)S(1)}, bf16[320,256]{1,0:T(8,128)(2,1)S(1)}, bf16[320,256]{1,0:T(8,128)(2,1)S(1)}) custom-call(bf16[1280,256]{1,0:T(8,128)(2,1)S(1)} %add_convert_fusion.4.refs_0_, bf16[1280,768]{1,0:T(8,128)(2,1)S(1)} %pad_maximum_fusion.refs_1_, ...), custom_call_target="tpu_custom_call" | custom-call | flops 2013265920 | bytes 10092544 | tf_op jit(solution)/shard_map/spread/pallas_call | solution.py:351
  234.2 6.4 %collective-permute-done.35.refs_6_ = bf16[128,768]{1,0:T(8,128)(2,1)} collective-permute-done((bf16[128,768]{1,0:T(8,128)(2,1)}, bf16[128,768]{1,0:T(8,128)(2,1)}, u32[]{:S(2)}, u32[]{:S(2)}) %collective-permute-start.35) | collective-permute-done | bytes 196640 | tf_op jit(solution)/shard_map/ppermute | solution.py:171
  241.3 8.0 %collective-permute-done.45.refs_2_ = bf16[320,256]{1,0:T(8,128)(2,1)S(1)} collective-permute-done((bf16[320,256]{1,0:T(8,128)(2,1)S(1)}, bf16[320,256]{1,0:T(8,128)(2,1)S(1)}, u32[]{:S(2)}, u32[]{:S(2)}) %collective-permute-start.45) | collective-permute-done | bytes 163872 | tf_op jit(solution)/shard_map/ppermute | solution.py:171
  249.9 1.9 collective-permute-start.47
  253.6 1.9 shard_map.89.refs_0_
  255.5 7.7 %collective-permute-done.46.refs_3_ = bf16[320,256]{1,0:T(8,128)(2,1)S(1)} collective-permute-done((bf16[320,256]{1,0:T(8,128)(2,1)S(1)}, bf16[320,256]{1,0:T(8,128)(2,1)S(1)}, u32[]{:S(2)}, u32[]{:S(2)}) %collective-permute-start.46) | collective-permute-done | bytes 163872 | tf_op jit(solution)/shard_map/ppermute | solution.py:171
  263.2 2.6 shard_map.90
  265.8 2.6 fusion.2
  (256 shorter events, 40.2 us)
Async XLA Ops:
  3.1 10.5 %collective-permute-start.1 = (bf16[1280,128]{1,0:T(8,128)(2,1)S(1)}, bf16[1280,128]{1,0:T(8,128)(2,1)S(1)}, u32[]{:S(2)}, u32[]{:S(2)}) collective-permute-start(bf16[1280,128]{1,0:T(8,128)(2,1)S(1)} %pad_maximum_fusion.4), channel_id=1, source_target_pairs={{0,1},{1,0},{2,3},{3,2},{4,5},{5,4},{6,7},{7,6},{8,9},{9,8},{10,11... | collective-permute-start | bytes 983048 | tf_op jit(solution)/shard_map/ppermute | solution.py:176
  4.4 29.1 %collective-permute-start.4 = (bf16[768,768]{1,0:T(8,128)(2,1)S(1)}, bf16[768,768]{1,0:T(8,128)(2,1)}, u32[]{:S(2)}, u32[]{:S(2)}) collective-permute-start(bf16[768,768]{1,0:T(8,128)(2,1)S(1)} %bitcast.46), channel_id=1, source_target_pairs={{0,2},{1,3},{2,0},{3,1},{4,6},{5,7},{6,4},{7,5},{8,10},{9,11},{10,... | collective-permute-start | bytes 3538952 | tf_op jit(solution)/shard_map/ppermute | solution.py:171
  12.0 27.8 %collective-permute-start.3 = (bf16[768,768]{1,0:T(8,128)(2,1)}, bf16[768,768]{1,0:T(8,128)(2,1)}, u32[]{:S(2)}, u32[]{:S(2)}) collective-permute-start(bf16[768,768]{1,0:T(8,128)(2,1)} %convolution_convert_fusion.3), channel_id=1, source_target_pairs={{0,1},{1,0},{2,3},{3,2},{4,5},{5,4},{6,7},{7,6},{8,9},{9,8},{10,11... | collective-permute-start | bytes 3538952 | tf_op jit(solution)/shard_map/ppermute | solution.py:176
  12.0 29.2 %collective-permute-start.5 = (bf16[768,768]{1,0:T(8,128)(2,1)S(1)}, bf16[768,768]{1,0:T(8,128)(2,1)}, u32[]{:S(2)}, u32[]{:S(2)}) collective-permute-start(bf16[768,768]{1,0:T(8,128)(2,1)S(1)} %bitcast.47), channel_id=1, source_target_pairs={{2,4},{3,5},{4,2},{5,3},{10,12},{11,13},{12,10},{13,11},{18,20},{1... | collective-permute-start | bytes 3538952 | tf_op jit(solution)/shard_map/ppermute | solution.py:171
  14.7 20.5 %copy-start.55 = (bf16[128,2560]{0,1:T(8,128)(2,1)S(1)}, bf16[128,2560]{0,1:T(8,128)(2,1)}, u32[]{:S(2)}) copy-start(bf16[128,2560]{0,1:T(8,128)(2,1)} %copy-done.54) | copy-start | bytes 1966084
  14.7 23.8 %collective-permute-start.14 = (bf16[1280,256]{1,0:T(8,128)(2,1)}, bf16[1280,256]{1,0:T(8,128)(2,1)}, u32[]{:S(2)}, u32[]{:S(2)}) collective-permute-start(bf16[1280,256]{1,0:T(8,128)(2,1)} %pad_maximum_fusion.2), channel_id=1, source_target_pairs={{24,16},{8,0},{25,17},{9,1},{26,18},{10,2},{27,19},{11,3},{28,20},... | collective-permute-start | bytes 1966088 | tf_op jit(solution)/shard_map/ppermute | solution.py:180
  16.9 19.2 %copy-start.75 = (s32[1,2,64]{2,1,0:T(2,128)S(1)}, s32[1,2,64]{2,1,0:T(2,128)}, u32[]{:S(2)}) copy-start(s32[1,2,64]{2,1,0:T(2,128)} %param.11) | copy-start | bytes 1540
  16.9 26.1 %copy-start.76 = (f32[1,2,64]{2,1,0:T(2,128)S(1)}, f32[1,2,64]{2,1,0:T(2,128)}, u32[]{:S(2)}) copy-start(f32[1,2,64]{2,1,0:T(2,128)} %param.9) | copy-start | bytes 1540
  17.0 21.5 %collective-permute-start.2 = (f32[128,768]{1,0:T(8,128)S(1)}, f32[128,768]{1,0:T(8,128)}, u32[]{:S(2)}, u32[]{:S(2)}) collective-permute-start(f32[128,768]{1,0:T(8,128)S(1)} %slice.43), channel_id=1, source_target_pairs={{0,1},{1,0},{2,3},{3,2},{4,5},{5,4},{6,7},{7,6},{8,9},{9,8},{10,11... | collective-permute-start | bytes 1179656 | tf_op jit(solution)/shard_map/ppermute | solution.py:176
  33.5 13.6 %collective-permute-start.10 = (bf16[768,768]{1,0:T(8,128)(2,1)}, bf16[768,768]{1,0:T(8,128)(2,1)}, u32[]{:S(2)}, u32[]{:S(2)}) collective-permute-start(bf16[768,768]{1,0:T(8,128)(2,1)} %collective-permute-done.4.refs_1_), channel_id=1, source_target_pairs={{2,4},{3,5},{4,2},{5,3},{10,12},{11,13},{12,10},{13,11},{18,20},{1... | collective-permute-start | bytes 3538952 | tf_op jit(solution)/shard_map/ppermute | solution.py:171
  38.5 12.6 %collective-permute-start.7 = (bf16[768,768]{1,0:T(8,128)(2,1)S(1)}, bf16[768,768]{1,0:T(8,128)(2,1)}, u32[]{:S(2)}, u32[]{:S(2)}) collective-permute-start(bf16[768,768]{1,0:T(8,128)(2,1)S(1)} %bitcast.48), channel_id=1, source_target_pairs={{0,1},{1,0},{2,3},{3,2},{4,5},{5,4},{6,7},{7,6},{8,9},{9,8},{10,11... | collective-permute-start | bytes 3538952 | tf_op jit(solution)/shard_map/ppermute | solution.py:176
  38.5 54.1 %collective-permute-start.17 = (bf16[1280,768]{1,0:T(8,128)(2,1)S(1)}, bf16[1280,768]{1,0:T(8,128)(2,1)}, u32[]{:S(2)}, u32[]{:S(2)}) collective-permute-start(bf16[1280,768]{1,0:T(8,128)(2,1)S(1)} %pad_maximum_fusion.refs_1_), channel_id=1, source_target_pairs={{24,16},{8,0},{25,17},{9,1},{26,18},{10,2},{27,19},{11,3},{28,20},... | collective-permute-start | bytes 5898248 | tf_op jit(solution)/shard_map/ppermute | solution.py:180
  39.8 47.2 %collective-permute-start.23 = (bf16[1280,768]{1,0:T(8,128)(2,1)S(1)}, bf16[1280,768]{1,0:T(8,128)(2,1)}, u32[]{:S(2)}, u32[]{:S(2)}) collective-permute-start(bf16[1280,768]{1,0:T(8,128)(2,1)S(1)} %pad_maximum_fusion.refs_1_), channel_id=1, source_target_pairs={{24,8},{16,0},{25,9},{17,1},{26,10},{18,2},{27,11},{19,3},{28,12},... | collective-permute-start | bytes 5898248 | tf_op jit(solution)/shard_map/ppermute | solution.py:180
  41.1 32.0 %collective-permute-start.6 = (bf16[768,768]{1,0:T(8,128)(2,1)}, bf16[768,768]{1,0:T(8,128)(2,1)}, u32[]{:S(2)}, u32[]{:S(2)}) collective-permute-start(bf16[768,768]{1,0:T(8,128)(2,1)} %collective-permute-done.5), channel_id=1, source_target_pairs={{2,0},{3,1},{4,6},{5,7},{10,8},{11,9},{12,14},{13,15},{18,16},{19,... | collective-permute-start | bytes 3538952 | tf_op jit(solution)/shard_map/ppermute | solution.py:171
  47.1 51.1 %collective-permute-start.11 = (bf16[768,768]{1,0:T(8,128)(2,1)}, bf16[768,768]{1,0:T(8,128)(2,1)}, u32[]{:S(2)}, u32[]{:S(2)}) collective-permute-start(bf16[768,768]{1,0:T(8,128)(2,1)} %collective-permute-done.10.refs_6_), channel_id=1, source_target_pairs={{2,0},{3,1},{4,6},{5,7},{10,8},{11,9},{12,14},{13,15},{18,16},{19,... | collective-permute-start | bytes 3538952 | tf_op jit(solution)/shard_map/ppermute | solution.py:171
  51.1 24.2 %collective-permute-start.15 = (f32[128,768]{1,0:T(8,128)}, f32[128,768]{1,0:T(8,128)}, u32[]{:S(2)}, u32[]{:S(2)}) collective-permute-start(f32[128,768]{1,0:T(8,128)} %slice.45), channel_id=1, source_target_pairs={{0,1},{1,0},{2,3},{3,2},{4,5},{5,4},{6,7},{7,6},{8,9},{9,8},{10,11... | collective-permute-start | bytes 1179656 | tf_op jit(solution)/shard_map/ppermute | solution.py:176
  73.1 28.4 %collective-permute-start.8 = (bf16[768,768]{1,0:T(8,128)(2,1)}, bf16[768,768]{1,0:T(8,128)(2,1)S(1)}, u32[]{:S(2)}, u32[]{:S(2)}) collective-permute-start(bf16[768,768]{1,0:T(8,128)(2,1)} %collective-permute-done.4.refs_1_), channel_id=1, source_target_pairs={{0,1},{1,0},{2,3},{3,2},{4,5},{5,4},{6,7},{7,6},{8,9},{9,8},{10,11... | collective-permute-start | bytes 3538952 | tf_op jit(solution)/shard_map/ppermute | solution.py:176
  75.3 30.8 %collective-permute-start.9 = (bf16[768,768]{1,0:T(8,128)(2,1)S(1)}, bf16[768,768]{1,0:T(8,128)(2,1)S(1)}, u32[]{:S(2)}, u32[]{:S(2)}) collective-permute-start(bf16[768,768]{1,0:T(8,128)(2,1)S(1)} %broadcast_select_fusion.refs_2_), channel_id=1, source_target_pairs={{0,1},{1,0},{2,3},{3,2},{4,5},{5,4},{6,7},{7,6},{8,9},{9,8},{10,11... | collective-permute-start | bytes 3538952 | tf_op jit(solution)/shard_map/ppermute | solution.py:176
  87.0 55.6 %collective-permute-start.26 = (bf16[1280,768]{1,0:T(8,128)(2,1)}, bf16[1280,768]{1,0:T(8,128)(2,1)S(1)}, u32[]{:S(2)}, u32[]{:S(2)}) collective-permute-start(bf16[1280,768]{1,0:T(8,128)(2,1)} %collective-permute-done.23.refs_4_), channel_id=1, source_target_pairs={{0,8},{8,0},{1,9},{9,1},{2,10},{10,2},{3,11},{11,3},{4,12},{12,4},... | collective-permute-start | bytes 5898248 | tf_op jit(solution)/shard_map/ppermute | solution.py:180
  92.6 18.4 %collective-permute-start.12 = (bf16[768,768]{1,0:T(8,128)(2,1)}, bf16[768,768]{1,0:T(8,128)(2,1)S(1)}, u32[]{:S(2)}, u32[]{:S(2)}) collective-permute-start(bf16[768,768]{1,0:T(8,128)(2,1)} %collective-permute-done.10.refs_6_), channel_id=1, source_target_pairs={{0,1},{1,0},{2,3},{3,2},{4,5},{5,4},{6,7},{7,6},{8,9},{9,8},{10,11... | collective-permute-start | bytes 3538952 | tf_op jit(solution)/shard_map/ppermute | solution.py:176
  98.2 12.9 %collective-permute-start.13 = (bf16[768,768]{1,0:T(8,128)(2,1)}, bf16[768,768]{1,0:T(8,128)(2,1)S(1)}, u32[]{:S(2)}, u32[]{:S(2)}) collective-permute-start(bf16[768,768]{1,0:T(8,128)(2,1)} %collective-permute-done.11.refs_7_), channel_id=1, source_target_pairs={{0,1},{1,0},{2,3},{3,2},{4,5},{5,4},{6,7},{7,6},{8,9},{9,8},{10,11... | collective-permute-start | bytes 3538952 | tf_op jit(solution)/shard_map/ppermute | solution.py:176
  102.6 24.5 %collective-permute-start.18 = (bf16[768,768]{1,0:T(8,128)(2,1)S(1)}, bf16[768,768]{1,0:T(8,128)(2,1)S(1)}, u32[]{:S(2)}, u32[]{:S(2)}) collective-permute-start(bf16[768,768]{1,0:T(8,128)(2,1)S(1)} %convolution_convert_fusion.2), channel_id=1, source_target_pairs={{0,1},{1,0},{2,3},{3,2},{4,5},{5,4},{6,7},{7,6},{8,9},{9,8},{10,11... | collective-permute-start | bytes 3538952 | tf_op jit(solution)/shard_map/ppermute | solution.py:176
  106.1 20.3 %collective-permute-start.19 = (bf16[1280,256]{1,0:T(8,128)(2,1)}, bf16[1280,256]{1,0:T(8,128)(2,1)S(1)}, u32[]{:S(2)}, u32[]{:S(2)}) collective-permute-start(bf16[1280,256]{1,0:T(8,128)(2,1)} %pad_maximum_fusion.2), channel_id=1, source_target_pairs={{24,8},{16,0},{25,9},{17,1},{26,10},{18,2},{27,11},{19,3},{28,12},... | collective-permute-start | bytes 1966088 | tf_op jit(solution)/shard_map/ppermute | solution.py:180
  111.0 41.8 %collective-permute-start = (bf16[1280,128]{1,0:T(8,128)(2,1)S(1)}, bf16[1280,128]{1,0:T(8,128)(2,1)S(1)}, u32[]{:S(2)}, u32[]{:S(2)}) collective-permute-start(bf16[1280,128]{1,0:T(8,128)(2,1)S(1)} %copy-done.73), channel_id=1, source_target_pairs={{0,1},{1,0},{2,3},{3,2},{4,5},{5,4},{6,7},{7,6},{8,9},{9,8},{10,11... | collective-permute-start | bytes 983048 | tf_op jit(solution)/shard_map/ppermute | solution.py:176
  111.1 42.7 %collective-permute-start.24 = (bf16[768,768]{1,0:T(8,128)(2,1)S(1)}, bf16[768,768]{1,0:T(8,128)(2,1)S(1)}, u32[]{:S(2)}, u32[]{:S(2)}) collective-permute-start(bf16[768,768]{1,0:T(8,128)(2,1)S(1)} %convolution_convert_fusion.1), channel_id=1, source_target_pairs={{0,1},{1,0},{2,3},{3,2},{4,5},{5,4},{6,7},{7,6},{8,9},{9,8},{10,11... | collective-permute-start | bytes 3538952 | tf_op jit(solution)/shard_map/ppermute | solution.py:176
  126.4 6.6 %collective-permute-start.16 = (bf16[128,768]{1,0:T(8,128)(2,1)}, bf16[128,768]{1,0:T(8,128)(2,1)S(1)}, u32[]{:S(2)}, u32[]{:S(2)}) collective-permute-start(bf16[128,768]{1,0:T(8,128)(2,1)} %get-tuple-element.62), channel_id=1, source_target_pairs={{24,16},{25,17},{26,18},{27,19},{28,20},{29,21},{30,22},{31,23}} | collective-permute-start | bytes 589832 | tf_op jit(solution)/shard_map/ppermute | solution.py:180
  127.1 22.1 %collective-permute-start.20 = (bf16[1280,256]{1,0:T(8,128)(2,1)S(1)}, bf16[1280,256]{1,0:T(8,128)(2,1)S(1)}, u32[]{:S(2)}, u32[]{:S(2)}) collective-permute-start(bf16[1280,256]{1,0:T(8,128)(2,1)S(1)} %collective-permute-done.19), channel_id=1, source_target_pairs={{0,8},{8,0},{1,9},{9,1},{2,10},{10,2},{3,11},{11,3},{4,12},{12,4},... | collective-permute-start | bytes 1966088 | tf_op jit(solution)/shard_map/ppermute | solution.py:180
  145.4 21.0 %collective-permute-start.27 = (bf16[768,768]{1,0:T(8,128)(2,1)}, bf16[768,768]{1,0:T(8,128)(2,1)}, u32[]{:S(2)}, u32[]{:S(2)}) collective-permute-start(bf16[768,768]{1,0:T(8,128)(2,1)} %convolution_convert_fusion), channel_id=1, source_target_pairs={{0,1},{1,0},{2,3},{3,2},{4,5},{5,4},{6,7},{7,6},{8,9},{9,8},{10,11... | collective-permute-start | bytes 3538952 | tf_op jit(solution)/shard_map/ppermute | solution.py:176
  152.8 10.8 %collective-permute-start.21 = (f32[128,768]{1,0:T(8,128)}, f32[128,768]{1,0:T(8,128)}, u32[]{:S(2)}, u32[]{:S(2)}) collective-permute-start(f32[128,768]{1,0:T(8,128)} %slice.47), channel_id=1, source_target_pairs={{0,1},{1,0},{2,3},{3,2},{4,5},{5,4},{6,7},{7,6},{8,9},{9,8},{10,11... | collective-permute-start | bytes 1179656 | tf_op jit(solution)/shard_map/ppermute | solution.py:176
  155.1 13.4 %collective-permute-start.22 = (bf16[128,768]{1,0:T(8,128)(2,1)}, bf16[128,768]{1,0:T(8,128)(2,1)}, u32[]{:S(2)}, u32[]{:S(2)}) collective-permute-start(bf16[128,768]{1,0:T(8,128)(2,1)} %get-tuple-element.62), channel_id=1, source_target_pairs={{24,8},{25,9},{26,10},{27,11},{28,12},{29,13},{30,14},{31,15}} | collective-permute-start | bytes 589832 | tf_op jit(solution)/shard_map/ppermute | solution.py:180
  156.5 64.7 %all-to-all-start = ((bf16[8,32,768]{2,1,0:T(8,128)(2,1)}), bf16[8,32,768]{2,1,0:T(8,128)(2,1)}, u32[]{:S(2)}, u32[]{:S(2)}) async-start(bf16[8,32,768]{2,1,0:T(8,128)(2,1)} %bitcast.55), calls=%async_computation | async-start | bytes 786432 | tf_op jit(solution)/shard_map/all_to_all | solution.py:496
  161.6 6.9 %collective-permute-start.25 = (bf16[128,768]{1,0:T(8,128)(2,1)}, bf16[128,768]{1,0:T(8,128)(2,1)S(1)}, u32[]{:S(2)}, u32[]{:S(2)}) collective-permute-start(bf16[128,768]{1,0:T(8,128)(2,1)} %copy-done.52), channel_id=1, source_target_pairs={{16,8},{17,9},{18,10},{19,11},{20,12},{21,13},{22,14},{23,15}} | collective-permute-start | bytes 589832 | tf_op jit(solution)/shard_map/ppermute | solution.py:180
  162.3 26.7 %collective-permute-start.31 = (bf16[128,768]{1,0:T(8,128)(2,1)}, bf16[128,768]{1,0:T(8,128)(2,1)S(1)}, u32[]{:S(2)}, u32[]{:S(2)}) collective-permute-start(bf16[128,768]{1,0:T(8,128)(2,1)} %copy-done.52), channel_id=1, source_target_pairs={{16,0},{17,1},{18,2},{19,3},{20,4},{21,5},{22,6},{23,7}} | collective-permute-start | bytes 589832 | tf_op jit(solution)/shard_map/ppermute | solution.py:180
  163.6 25.9 %collective-permute-start.32 = (bf16[128,768]{1,0:T(8,128)(2,1)}, bf16[128,768]{1,0:T(8,128)(2,1)S(1)}, u32[]{:S(2)}, u32[]{:S(2)}) collective-permute-start(bf16[128,768]{1,0:T(8,128)(2,1)} %get-tuple-element.62), channel_id=1, source_target_pairs={{24,0},{25,1},{26,2},{27,3},{28,4},{29,5},{30,6},{31,7}} | collective-permute-start | bytes 589832 | tf_op jit(solution)/shard_map/ppermute | solution.py:180
  182.5 10.7 %collective-permute-start.33 = (bf16[128,768]{1,0:T(8,128)(2,1)S(1)}, bf16[128,768]{1,0:T(8,128)(2,1)S(1)}, u32[]{:S(2)}, u32[]{:S(2)}) collective-permute-start(bf16[128,768]{1,0:T(8,128)(2,1)S(1)} %get-tuple-element.57), channel_id=1, source_target_pairs={{8,0},{9,1},{10,2},{11,3},{12,4},{13,5},{14,6},{15,7}} | collective-permute-start | bytes 589832 | tf_op jit(solution)/shard_map/ppermute | solution.py:180
  184.6 16.2 %collective-permute-start.28 = (bf16[320,256]{1,0:T(8,128)(2,1)S(1)}, bf16[320,256]{1,0:T(8,128)(2,1)S(1)}, u32[]{:S(2)}, u32[]{:S(2)}) collective-permute-start(bf16[320,256]{1,0:T(8,128)(2,1)S(1)} %get-tuple-element.58), channel_id=1, source_target_pairs={{0,2},{1,3},{2,0},{3,1},{4,6},{5,7},{6,4},{7,5},{8,10},{9,11},{10,... | collective-permute-start | bytes 491528 | tf_op jit(solution)/shard_map/ppermute | solution.py:171
  187.1 15.1 %collective-permute-start.29 = (bf16[320,256]{1,0:T(8,128)(2,1)S(1)}, bf16[320,256]{1,0:T(8,128)(2,1)S(1)}, u32[]{:S(2)}, u32[]{:S(2)}) collective-permute-start(bf16[320,256]{1,0:T(8,128)(2,1)S(1)} %get-tuple-element.59), channel_id=1, source_target_pairs={{0,4},{1,5},{2,6},{3,7},{4,0},{5,1},{6,2},{7,3},{8,12},{9,13},{10,... | collective-permute-start | bytes 491528 | tf_op jit(solution)/shard_map/ppermute | solution.py:171
  189.0 13.2 %collective-permute-start.30 = (bf16[320,256]{1,0:T(8,128)(2,1)S(1)}, bf16[320,256]{1,0:T(8,128)(2,1)S(1)}, u32[]{:S(2)}, u32[]{:S(2)}) collective-permute-start(bf16[320,256]{1,0:T(8,128)(2,1)S(1)} %get-tuple-element.60), channel_id=1, source_target_pairs={{0,6},{1,7},{2,4},{3,5},{4,2},{5,3},{6,0},{7,1},{8,14},{9,15},{10,... | collective-permute-start | bytes 491528 | tf_op jit(solution)/shard_map/ppermute | solution.py:171
  189.5 14.3 %collective-permute-start.41 = (bf16[128,768]{1,0:T(8,128)(2,1)S(1)}, bf16[128,768]{1,0:T(8,128)(2,1)S(1)}, u32[]{:S(2)}, u32[]{:S(2)}) collective-permute-start(bf16[128,768]{1,0:T(8,128)(2,1)S(1)} %get-tuple-element.72.refs_1_.refs_2_.refs_5_), channel_id=1, source_target_pairs={{0,1},{1,0},{2,3},{3,2},{4,5},{5,4},{6,7},{7,6},{8,9},{9,8},{10,11... | collective-permute-start | bytes 589832 | tf_op jit(solution)/shard_map/ppermute | solution.py:176
  193.2 26.0 %collective-permute-start.48 = (bf16[128,768]{1,0:T(8,128)(2,1)S(1)}, bf16[128,768]{1,0:T(8,128)(2,1)S(1)}, u32[]{:S(2)}, u32[]{:S(2)}) collective-permute-start(bf16[128,768]{1,0:T(8,128)(2,1)S(1)} %get-tuple-element.72.refs_1_.refs_2_.refs_5_), channel_id=1, source_target_pairs={{0,2},{1,3},{2,0},{3,1},{4,6},{5,7},{6,4},{7,5},{8,10},{9,11},{10,... | collective-permute-start | bytes 589832 | tf_op jit(solution)/shard_map/ppermute | solution.py:171
  200.8 24.6 %copy-start.63 = (bf16[320,128]{1,0:T(8,128)(2,1)S(1)}, bf16[320,128]{1,0:T(8,128)(2,1)}, u32[]{:S(2)}) copy-start(bf16[320,128]{1,0:T(8,128)(2,1)} %copy-done.62) | copy-start | bytes 245764
  200.8 24.6 %copy-start.65 = (bf16[320,128]{1,0:T(8,128)(2,1)S(1)}, bf16[320,128]{1,0:T(8,128)(2,1)}, u32[]{:S(2)}) copy-start(bf16[320,128]{1,0:T(8,128)(2,1)} %copy-done.64) | copy-start | bytes 245764
  200.8 20.2 %copy-start.46 = (bf16[320,256]{1,0:T(8,128)(2,1)}, bf16[320,256]{1,0:T(8,128)(2,1)S(1)}, u32[]{:S(2)}) copy-start(bf16[320,256]{1,0:T(8,128)(2,1)S(1)} %collective-permute-done.28.refs_1_) | copy-start | bytes 491524
  200.8 20.2 %collective-permute-start.49 = (bf16[128,768]{1,0:T(8,128)(2,1)S(1)}, bf16[128,768]{1,0:T(8,128)(2,1)S(1)}, u32[]{:S(2)}, u32[]{:S(2)}) collective-permute-start(bf16[128,768]{1,0:T(8,128)(2,1)S(1)} %get-tuple-element.72.refs_1_.refs_2_.refs_5_), channel_id=1, source_target_pairs={{0,4},{1,5},{2,6},{3,7},{4,0},{5,1},{6,2},{7,3},{8,12},{9,13},{10,... | collective-permute-start | bytes 589832 | tf_op jit(solution)/shard_map/ppermute | solution.py:171
  202.2 4.1 %collective-permute-start.42 = (bf16[128,768]{1,0:T(8,128)(2,1)S(1)}, bf16[128,768]{1,0:T(8,128)(2,1)S(1)}, u32[]{:S(2)}, u32[]{:S(2)}) collective-permute-start(bf16[128,768]{1,0:T(8,128)(2,1)S(1)} %add.203.refs_5_), channel_id=1, source_target_pairs={{0,1},{1,0},{2,3},{3,2},{4,5},{5,4},{6,7},{7,6},{8,9},{9,8},{10,11... | collective-permute-start | bytes 589832 | tf_op jit(solution)/shard_map/ppermute | solution.py:176
  202.2 15.8 %collective-permute-start.43 = (bf16[128,768]{1,0:T(8,128)(2,1)S(1)}, bf16[128,768]{1,0:T(8,128)(2,1)S(1)}, u32[]{:S(2)}, u32[]{:S(2)}) collective-permute-start(bf16[128,768]{1,0:T(8,128)(2,1)S(1)} %add.204.refs_8_), channel_id=1, source_target_pairs={{0,1},{1,0},{2,3},{3,2},{4,5},{5,4},{6,7},{7,6},{8,9},{9,8},{10,11... | collective-permute-start | bytes 589832 | tf_op jit(solution)/shard_map/ppermute | solution.py:176
  204.5 36.2 %collective-permute-start.50 = (bf16[128,768]{1,0:T(8,128)(2,1)S(1)}, bf16[128,768]{1,0:T(8,128)(2,1)}, u32[]{:S(2)}, u32[]{:S(2)}) collective-permute-start(bf16[128,768]{1,0:T(8,128)(2,1)S(1)} %get-tuple-element.72.refs_1_.refs_2_.refs_5_), channel_id=1, source_target_pairs={{0,6},{1,7},{2,4},{3,5},{4,2},{5,3},{6,0},{7,1},{8,14},{9,15},{10,... | collective-permute-start | bytes 589832 | tf_op jit(solution)/shard_map/ppermute | solution.py:171
  207.0 20.3 %collective-permute-start.34 = (bf16[128,768]{1,0:T(8,128)(2,1)}, bf16[128,768]{1,0:T(8,128)(2,1)}, u32[]{:S(2)}, u32[]{:S(2)}) collective-permute-start(bf16[128,768]{1,0:T(8,128)(2,1)} %get-tuple-element.63.refs_4_), channel_id=1, source_target_pairs={{0,2},{1,3},{2,0},{3,1},{4,6},{5,7},{6,4},{7,5},{8,10},{9,11},{10,... | collective-permute-start | bytes 589832 | tf_op jit(solution)/shard_map/ppermute | solution.py:171
  218.7 21.9 %collective-permute-start.35 = (bf16[128,768]{1,0:T(8,128)(2,1)}, bf16[128,768]{1,0:T(8,128)(2,1)}, u32[]{:S(2)}, u32[]{:S(2)}) collective-permute-start(bf16[128,768]{1,0:T(8,128)(2,1)} %get-tuple-element.63.refs_4_), channel_id=1, source_target_pairs={{0,4},{1,5},{2,6},{3,7},{4,0},{5,1},{6,2},{7,3},{8,12},{9,13},{10,... | collective-permute-start | bytes 589832 | tf_op jit(solution)/shard_map/ppermute | solution.py:171
  219.2 21.4 %collective-permute-start.36 = (bf16[128,768]{1,0:T(8,128)(2,1)}, bf16[128,768]{1,0:T(8,128)(2,1)}, u32[]{:S(2)}, u32[]{:S(2)}) collective-permute-start(bf16[128,768]{1,0:T(8,128)(2,1)} %get-tuple-element.63.refs_4_), channel_id=1, source_target_pairs={{0,6},{1,7},{2,4},{3,5},{4,2},{5,3},{6,0},{7,1},{8,14},{9,15},{10,... | collective-permute-start | bytes 589832 | tf_op jit(solution)/shard_map/ppermute | solution.py:171
  221.1 6.7 %collective-permute-start.44 = (bf16[128,768]{1,0:T(8,128)(2,1)}, bf16[128,768]{1,0:T(8,128)(2,1)}, u32[]{:S(2)}, u32[]{:S(2)}) collective-permute-start(bf16[128,768]{1,0:T(8,128)(2,1)} %add.205.refs_11_), channel_id=1, source_target_pairs={{0,1},{1,0},{2,3},{3,2},{4,5},{5,4},{6,7},{7,6},{8,9},{9,8},{10,11... | collective-permute-start | bytes 589832 | tf_op jit(solution)/shard_map/ppermute | solution.py:176
  221.2 30.6 %copy-start.47 = (bf16[320,256]{1,0:T(8,128)(2,1)S(1)}, bf16[320,256]{1,0:T(8,128)(2,1)}, u32[]{:S(2)}) copy-start(bf16[320,256]{1,0:T(8,128)(2,1)} %copy-done.46) | copy-start | bytes 491524
  221.2 44.6 %all-to-all-start.1 = ((bf16[8,32,768]{2,1,0:T(8,128)(2,1)}), bf16[8,32,768]{2,1,0:T(8,128)(2,1)}, u32[]{:S(2)}, u32[]{:S(2)}) async-start(bf16[8,32,768]{2,1,0:T(8,128)(2,1)} %bitcast.13), calls=%async_computation.1 | async-start | bytes 786432 | tf_op jit(solution)/shard_map/all_to_all | solution.py:549
  227.3 24.5 %copy-start.37 = (bf16[320,256]{1,0:T(8,128)(2,1)S(1)}, bf16[320,256]{1,0:T(8,128)(2,1)}, u32[]{:S(2)}) copy-start(bf16[320,256]{1,0:T(8,128)(2,1)} %get-tuple-element.85.refs_0_) | copy-start | bytes 491524
  227.3 13.9 %collective-permute-start.37 = (bf16[128,768]{1,0:T(8,128)(2,1)}, bf16[128,768]{1,0:T(8,128)(2,1)S(1)}, u32[]{:S(2)}, u32[]{:S(2)}) collective-permute-start(bf16[128,768]{1,0:T(8,128)(2,1)} %get-tuple-element.63.refs_4_), channel_id=1, source_target_pairs={{0,1},{1,0},{2,3},{3,2},{4,5},{5,4},{6,7},{7,6},{8,9},{9,8},{10,11... | collective-permute-start | bytes 589832 | tf_op jit(solution)/shard_map/ppermute | solution.py:176
  227.8 21.5 %collective-permute-start.38 = (bf16[128,768]{1,0:T(8,128)(2,1)}, bf16[128,768]{1,0:T(8,128)(2,1)S(1)}, u32[]{:S(2)}, u32[]{:S(2)}) collective-permute-start(bf16[128,768]{1,0:T(8,128)(2,1)} %collective-permute-done.34.refs_5_), channel_id=1, source_target_pairs={{0,1},{1,0},{2,3},{3,2},{4,5},{5,4},{6,7},{7,6},{8,9},{9,8},{10,11... | collective-permute-start | bytes 589832 | tf_op jit(solution)/shard_map/ppermute | solution.py:176
  240.6 9.2 %collective-permute-start.39 = (bf16[128,768]{1,0:T(8,128)(2,1)}, bf16[128,768]{1,0:T(8,128)(2,1)S(1)}, u32[]{:S(2)}, u32[]{:S(2)}) collective-permute-start(bf16[128,768]{1,0:T(8,128)(2,1)} %collective-permute-done.35.refs_6_), channel_id=1, source_target_pairs={{0,1},{1,0},{2,3},{3,2},{4,5},{5,4},{6,7},{7,6},{8,9},{9,8},{10,11... | collective-permute-start | bytes 589832 | tf_op jit(solution)/shard_map/ppermute | solution.py:176
  240.6 8.7 %collective-permute-start.45 = (bf16[320,256]{1,0:T(8,128)(2,1)S(1)}, bf16[320,256]{1,0:T(8,128)(2,1)S(1)}, u32[]{:S(2)}, u32[]{:S(2)}) collective-permute-start(bf16[320,256]{1,0:T(8,128)(2,1)S(1)} %get-tuple-element.69), channel_id=1, source_target_pairs={{0,2},{1,3},{2,0},{3,1},{4,6},{5,7},{6,4},{7,5},{8,10},{9,11},{10,... | collective-permute-start | bytes 491528 | tf_op jit(solution)/shard_map/ppermute | solution.py:171
  240.6 9.2 %collective-permute-start.40 = (bf16[128,768]{1,0:T(8,128)(2,1)}, bf16[128,768]{1,0:T(8,128)(2,1)S(1)}, u32[]{:S(2)}, u32[]{:S(2)}) collective-permute-start(bf16[128,768]{1,0:T(8,128)(2,1)} %collective-permute-done.36.refs_7_), channel_id=1, source_target_pairs={{0,1},{1,0},{2,3},{3,2},{4,5},{5,4},{6,7},{7,6},{8,9},{9,8},{10,11... | collective-permute-start | bytes 589832 | tf_op jit(solution)/shard_map/ppermute | solution.py:176
  241.2 22.0 %collective-permute-start.51 = (bf16[128,768]{1,0:T(8,128)(2,1)S(1)}, bf16[128,768]{1,0:T(8,128)(2,1)S(1)}, u32[]{:S(2)}, u32[]{:S(2)}) collective-permute-start(bf16[128,768]{1,0:T(8,128)(2,1)S(1)} %copy-done.41), channel_id=1, source_target_pairs={{0,1},{1,0},{2,3},{3,2},{4,5},{5,4},{6,7},{7,6},{8,9},{9,8},{10,11... | collective-permute-start | bytes 589832 | tf_op jit(solution)/shard_map/ppermute | solution.py:176
  249.3 13.9 %collective-permute-start.52 = (bf16[128,768]{1,0:T(8,128)(2,1)S(1)}, bf16[128,768]{1,0:T(8,128)(2,1)S(1)}, u32[]{:S(2)}, u32[]{:S(2)}) collective-permute-start(bf16[128,768]{1,0:T(8,128)(2,1)S(1)} %collective-permute-done.49.refs_7_), channel_id=1, source_target_pairs={{0,1},{1,0},{2,3},{3,2},{4,5},{5,4},{6,7},{7,6},{8,9},{9,8},{10,11... | collective-permute-start | bytes 589832 | tf_op jit(solution)/shard_map/ppermute | solution.py:176
  249.3 13.9 %collective-permute-start.53 = (bf16[128,768]{1,0:T(8,128)(2,1)}, bf16[128,768]{1,0:T(8,128)(2,1)S(1)}, u32[]{:S(2)}, u32[]{:S(2)}) collective-permute-start(bf16[128,768]{1,0:T(8,128)(2,1)} %collective-permute-done.50.refs_8_), channel_id=1, source_target_pairs={{0,1},{1,0},{2,3},{3,2},{4,5},{5,4},{6,7},{7,6},{8,9},{9,8},{10,11... | collective-permute-start | bytes 589832 | tf_op jit(solution)/shard_map/ppermute | solution.py:176
  249.9 13.4 %collective-permute-start.46 = (bf16[320,256]{1,0:T(8,128)(2,1)S(1)}, bf16[320,256]{1,0:T(8,128)(2,1)S(1)}, u32[]{:S(2)}, u32[]{:S(2)}) collective-permute-start(bf16[320,256]{1,0:T(8,128)(2,1)S(1)} %get-tuple-element.70), channel_id=1, source_target_pairs={{0,4},{1,5},{2,6},{3,7},{4,0},{5,1},{6,2},{7,3},{8,12},{9,13},{10,... | collective-permute-start | bytes 491528 | tf_op jit(solution)/shard_map/ppermute | solution.py:171
  249.9 13.4 %collective-permute-start.47 = (bf16[320,256]{1,0:T(8,128)(2,1)S(1)}, bf16[320,256]{1,0:T(8,128)(2,1)S(1)}, u32[]{:S(2)}, u32[]{:S(2)}) collective-permute-start(bf16[320,256]{1,0:T(8,128)(2,1)S(1)} %get-tuple-element.71), channel_id=1, source_target_pairs={{0,6},{1,7},{2,4},{3,5},{4,2},{5,3},{6,0},{7,1},{8,14},{9,15},{10,... | collective-permute-start | bytes 491528 | tf_op jit(solution)/shard_map/ppermute | solution.py:171
  (69 other events, 368.8 us)

commit v2 on v1

--- a/solution.py
+++ b/solution.py
@@ -302,10 +302,12 @@
     return [piece for pair in zip(own, other) for piece in pair]
 
 
-def turn_kernel(terms, marks_ref, scaled_ref, slope_ref, score_ref, late_ref, *refs):
+def turn_kernel(terms, late, marks_ref, scaled_ref, slope_ref, score_ref, *refs):
+    score = score_ref[...]
+    if late:
+        score, refs = score + refs[0][...], refs[1:]
     core_refs = refs[2 * terms : len(refs) - 4]
     next_ref, grad_ref, proj_ref, chain_ref = refs[len(refs) - 4 :]
-    score = score_ref[...] + late_ref[...]
     for term in range(terms):
         score = score + dot(refs[2 * term][...], refs[2 * term + 1][...])
     next_ref[...] = score
@@ -436,11 +438,22 @@
     capacity = max(2, 2 * token_count // devices)
     slots = micro_count * capacity
     micro = jnp.arange(rows, dtype=jnp.int32) // token_count
-    place = route[0].reshape(rows) * slots + micro * capacity + slot[0].reshape(rows)
+    expert = route[0].reshape(rows)
+    near = (expert % CORES ^ core) * CHIPS + (expert // CORES ^ chip)
+    place = near * slots + micro * capacity + slot[0].reshape(rows)
     picks = (jnp.arange(devices * slots, dtype=jnp.int32)[:, None] == place[None, :]).astype(bf16)
 
     def to_slots(values):
-        return dot(picks, values).astype(bf16).reshape(devices, slots, ranks)
+        held = dot(picks, values).astype(bf16)
+        half = CHIPS * slots
+        own, theirs = held[:half], swap_cores(held[half:])
+        return [
+            jnp.concatenate([part[step * slots : (step + 1) * slots] for part in (own, theirs)])
+            for step in range(CHIPS)
+        ]
+
+    def to_experts(parts):
+        return parts[:1] + [across_chips(parts[step], step) for step in range(1, CHIPS)]
 
     projected = dot(tokens, shared).astype(bf16)
     own_gram = gram_pair(own_half, own_half)
@@ -480,12 +493,12 @@
         arrays = [array for pair in terms for array in pair]
 
         def body(*refs):
-            turn_kernel(len(terms), *refs)
+            turn_kernel(len(terms), bool(late), *refs)
 
         return call_rows(
             body,
             [(wide, f32), (wide, bf16), (wide, bf16), (wide, bf16)],
-            [marks, scaled, slope, score, late, *arrays, *pieces],
+            [marks, scaled, slope, score, *late, *arrays, *pieces],
             product_flops * (devices + len(terms)),
         )
 
@@ -493,8 +506,8 @@
     first_down = between_layers(chain, [(3, 2)])
     step_cross = between_layers(after(step_two, chain), crossed)
     first_two = between_layers(chain, [(3, 1)])
-    proj_slots = lax.all_to_all(after(proj_slots, chain), "expert", 0, 0, tiled=True)
-    score, _, _, chain = turn(score, down_score, [(first_down, down_gram)])
+    proj_slots = to_experts([after(part, chain) for part in proj_slots])
+    score, _, _, chain = turn(score, [down_score], [(first_down, down_gram)])
 
     second_cross = between_layers(chain, [(2, 1)])
     second_two = between_layers(chain, [(2, 0)])
@@ -506,7 +519,7 @@
     late_score = both_cores(dot_first(late_steps, own_half))
     cross_product = gram_sum(cross_pair)
     score, _, _, chain = turn(
-        score, late_score, [(first_two, two_gram), (second_cross, cross_product)]
+        score, [late_score], [(first_two, two_gram), (second_cross, cross_product)]
     )
 
     third_down = between_layers(chain, [(1, 0)])
@@ -517,18 +530,18 @@
     steps_total = difference.astype(f32) + step_down.astype(f32)
     steps_total = (steps_total + after(late_steps, chain).astype(f32)).astype(bf16)
     score, grad_pre, grad_proj, _ = turn(
-        score,
-        jnp.zeros_like(score),
-        [(second_two, two_gram), (first_three, cross_product), (third_down, down_gram)],
+        score, [], [(second_two, two_gram), (first_three, cross_product), (third_down, down_gram)]
     )
 
     def with_swap(values):
         return values, swap_cores(values)
 
     proj_rows = gather_rows(grad_proj)
-    scaled_pair = with_swap(after(scaled, chain))
-    two_pair = with_swap(first_two + after(second_two, chain))
-    cross_pair = with_swap(second_cross + after(first_three, chain))
+    grad_slots = to_slots(grad_pre)
+    grad_slots = to_experts(grad_slots)
+    scaled_pair = with_swap(after(scaled, grad_proj))
+    two_pair = with_swap(first_two + after(second_two, grad_proj))
+    cross_pair = with_swap(second_cross + after(first_three, grad_proj))
     down_pair = with_swap(first_down + third_down)
     mixed_blocks = spread(
         steps_total,
@@ -545,10 +558,9 @@
     ]
     scaled_rows = scaled_rows + [scaled_pair[1]] + [swap_cores(rows) for rows in scaled_rows[1:]]
     share = factor_rows(None, token_blocks, proj_rows)
-    share = factor_rows(share, mixed_blocks, scaled_rows)
-    grad_slots = lax.all_to_all(to_slots(grad_pre), "expert", 0, 0, tiled=True)
-    core_total = dot_first(proj_slots.reshape(-1, ranks), grad_slots.reshape(-1, ranks))
-    return (share[None], core_total.astype(bf16)[None, None])
+    core_total = dot_first(jnp.concatenate(proj_slots), jnp.concatenate(grad_slots)).astype(bf16)
+    share = factor_rows(after(share, core_total), mixed_blocks, scaled_rows)
+    return (share[None], core_total[None, None])
 
 
 def solution(mesh):

time: 274 us -> 262 us (0.956); the launches traced: 268 us -> 261 us
  waiting for transfers between devices: 88 us -> 143 us
  local copies, waits for them, and re-layouts: 31.1 us -> 10.5 us
  starting transfers between devices: 73.3 us -> 57 us
  other arithmetic: 19.6 us -> 8.92 us
  matrix products: 23.9 us -> 15 us
  Pallas kernels: 30.7 us -> 24.9 us
    ppermute x17 -> x23, waiting for transfers between devices: 65.4 us -> 94.7 us  [on_chips(): return lax.ppermute(value, 'expert', perm)]
    ppermute x12, waiting for transfers between devices: 22.6 us -> 47.9 us  [between_layers(): return lax.ppermute(value, 'section', pairs)]
    unnamed x154 -> x44, local copies, waits for them, and re-layouts: 22.7 us -> 4.75 us
    all_to_all x2 -> x0, starting transfers between devices: 9.39 us -> none  [the longest x1 5.15 us: gathered_plan(): lax.all_to_all(after(proj_slots, chain), 'expert', 0, 0, tiled=True)]
    dot_general x8, matrix products: 18.9 us -> 13.8 us  [dot_first(): lax.dot_general(left, right, (((0,), (0,)), ((), ())), preferred_element_...]
    dot_general x3, matrix products: 4.99 us -> 1.17 us  [dot(): return jnp.dot(left, right, preferred_element_type=jnp.float32)]
    ppermute x12, starting transfers between devices: 23.5 us -> 20.2 us  [between_layers(): return lax.ppermute(value, 'section', pairs)]
    ppermute x17 -> x23, starting transfers between devices: 34.7 us -> 31.6 us  [on_chips(): return lax.ppermute(value, 'expert', perm)]
  transfers between devices with their start and end apart: 56 -> 62, of which waited for: 11 -> 19; matrix products, arithmetic and copies ran while one was open for 18% -> 11% of each run, Pallas kernels for 11% -> 9%
where the time goes in v2:
time: 262 us; the launch traced here: 261 us
  waiting for transfers between devices  143 us (55%)
  starting transfers between devices  57 us (22%)
  Pallas kernels  24.9 us (10%)
  matrix products  15 us (6%)
  local copies, waits for them, and re-layouts  10.5 us (4%)
  other arithmetic  8.92 us (3%)
    ppermute x23, waiting for transfers between devices, on_chips(): return lax.ppermute(value, 'expert', perm)  94.7 us
    ppermute x12, waiting for transfers between devices, between_layers(): return lax.ppermute(value, 'section', pairs)  47.9 us
    ppermute x23, starting transfers between devices, on_chips(): return lax.ppermute(value, 'expert', perm)  31.6 us
    ppermute x12, starting transfers between devices, between_layers(): return lax.ppermute(value, 'section', pairs)  20.2 us
    dot_general x8, matrix products, dot_first(): lax.dot_general(left, right, (((0,), (0,)), ((), ())), preferred_element_...  13.8 us
    pallas_call x3, Pallas kernels, call_rows(): pl.pallas_call(body, out_shape=[jax.ShapeDtypeStruct(shape, kind) for sha...  12.2 us
    pallas_call x1, Pallas kernels, gathered_plan(): pl.pallas_call(first_kernel, name='first_turn', out_shape=[jax.ShapeDtype...  8.19 us
    ppermute x27, starting transfers between devices, swap_cores(): lax.ppermute(value, 'expert', [(index, index ^ 1) for index in range(coun...  5.24 us
  transfers between devices with their start and end apart: 62, of which 19 were waited for; matrix products, arithmetic and copies ran while one was open for 11% of the time, Pallas kernels for 9%

profile of v2, /device:TPU:0, one launch (start us, length us, event | category | flops | bytes accessed | tf_op | source)
XLA Modules:
  0.0 260.8 jit_solution(5993720376759670452)
XLA Ops:
  0.6 3.1 %collective-permute-start.4 = (bf16[768,768]{1,0:T(8,128)(2,1)}, bf16[768,768]{1,0:T(8,128)(2,1)}, u32[]{:S(2)}, u32[]{:S(2)}) collective-permute-start(bf16[768,768]{1,0:T(8,128)(2,1)} %bitcast.38), channel_id=1, source_target_pairs={{0,2},{1,3},{2,0},{3,1},{4,6},{5,7},{6,4},{7,5},{8,10},{9,11},{10,... | collective-permute-start | bytes 3538952 | tf_op jit(solution)/shard_map/ppermute | solution.py:171
  3.7 1.7 collective-permute-start.5
  5.4 1.4 copy.11
  9.6 1.3 copy-done.1
  11.2 2.8 %convolution_convert_fusion.4 = bf16[768,768]{1,0:T(8,128)(2,1)} fusion(bf16[1280,768]{1,0:T(8,128)(2,1)S(1)} %pad_maximum_fusion.refs_1_), kind=kOutput, calls=%fused_computation.11 | convolution fusion | flops 1510539264 | bytes 3145728 | tf_op jit(solution)/shard_map/dot_general | solution.py:160
  17.2 0.9 pad_maximum_fusion.2
  18.8 1.3 collective-permute-start.14
  20.1 1.7 fusion.23
  21.8 0.9 copy-done.6
  23.5 6.5 %collective-permute-done.4.refs_1_ = bf16[768,768]{1,0:T(8,128)(2,1)} collective-permute-done((bf16[768,768]{1,0:T(8,128)(2,1)}, bf16[768,768]{1,0:T(8,128)(2,1)}, u32[]{:S(2)}, u32[]{:S(2)}) %collective-permute-start.4) | collective-permute-done | bytes 1179680 | tf_op jit(solution)/shard_map/ppermute | solution.py:171
  30.0 1.7 collective-permute-start.10
  31.9 5.7 %collective-permute-done.14 = bf16[1280,256]{1,0:T(8,128)(2,1)} collective-permute-done((bf16[1280,256]{1,0:T(8,128)(2,1)}, bf16[1280,256]{1,0:T(8,128)(2,1)}, u32[]{:S(2)}, u32[]{:S(2)}) %collective-permute-start.14) | collective-permute-done | bytes 655392 | tf_op jit(solution)/shard_map/ppermute | solution.py:180
  37.6 1.3 collective-permute-start.17
  38.9 1.3 collective-permute-start.23
  40.2 1.3 collective-permute-start.6
  41.6 0.9 fusion.25
  42.5 0.9 fusion.27
  43.4 1.3 collective-permute-start.11
  44.8 1.8 fusion.29
  46.8 25.2 %collective-permute-done.6 = bf16[768,768]{1,0:T(8,128)(2,1)S(1)} collective-permute-done((bf16[768,768]{1,0:T(8,128)(2,1)}, bf16[768,768]{1,0:T(8,128)(2,1)S(1)}, u32[]{:S(2)}, u32[]{:S(2)}) %collective-permute-start.6) | collective-permute-done | bytes 1179680 | tf_op jit(solution)/shard_map/ppermute | solution.py:171
  72.0 1.1 pad_maximum_fusion.1
  74.2 1.0 slice_add_fusion.2.own_ref
  75.3 9.4 %collective-permute-done.23.refs_4_ = bf16[1280,768]{1,0:T(8,128)(2,1)S(1)} collective-permute-done((bf16[1280,768]{1,0:T(8,128)(2,1)S(1)}, bf16[1280,768]{1,0:T(8,128)(2,1)S(1)}, u32[]{:S(2)}, u32[]{:S(2)}) %collective-permute-start.23) | collective-permute-done | bytes 1966112 | tf_op jit(solution)/shard_map/ppermute | solution.py:180
  84.7 4.4 %collective-permute-start.26 = (bf16[1280,768]{1,0:T(8,128)(2,1)S(1)}, bf16[1280,768]{1,0:T(8,128)(2,1)S(1)}, u32[]{:S(2)}, u32[]{:S(2)}) collective-permute-start(bf16[1280,768]{1,0:T(8,128)(2,1)S(1)} %collective-permute-done.23.refs_4_), channel_id=1, source_target_pairs={{0,8},{8,0},{1,9},{9,1},{2,10},{10,2},{3,11},{11,3},{4,12},{12,4},... | collective-permute-start | bytes 5898248 | tf_op jit(solution)/shard_map/ppermute | solution.py:180
  89.2 6.6 %collective-permute-done.11.refs_7_ = bf16[768,768]{1,0:T(8,128)(2,1)S(1)} collective-permute-done((bf16[768,768]{1,0:T(8,128)(2,1)}, bf16[768,768]{1,0:T(8,128)(2,1)S(1)}, u32[]{:S(2)}, u32[]{:S(2)}) %collective-permute-start.11) | collective-permute-done | bytes 1179680 | tf_op jit(solution)/shard_map/ppermute | solution.py:171
  95.7 1.7 convolution_convert_fusion.3
  98.1 1.9 add_convert_fusion.3.gram_ref
  100.0 1.5 collective-permute-start.19
  101.5 1.7 convolution_convert_fusion.2
  103.4 8.2 %first_turn.1 = (bf16[128,768]{1,0:T(8,128)(2,1)S(1)}, f32[128,768]{1,0:T(8,128)S(1)}, f32[128,768]{1,0:T(8,128)S(1)}, bf16[128,768]{1,0:T(8,128)(2,1)S(1)}, bf1...) custom-call(s32[1]{0:T(128)} %bitcast.2.middle_ref, ...), custom_call_target="tpu_custom_call" | custom-call | flops 2566914048 | bytes 9437184 | tf_op jit(solution)/shard_map/first_turn/pallas_call | solution.py:474
  112.2 6.7 %collective-permute-done.19 = bf16[1280,256]{1,0:T(8,128)(2,1)S(1)} collective-permute-done((bf16[1280,256]{1,0:T(8,128)(2,1)}, bf16[1280,256]{1,0:T(8,128)(2,1)S(1)}, u32[]{:S(2)}, u32[]{:S(2)}) %collective-permute-start.19) | collective-permute-done | bytes 655392 | tf_op jit(solution)/shard_map/ppermute | solution.py:180
  118.9 4.4 %collective-permute-start.20 = (bf16[1280,256]{1,0:T(8,128)(2,1)S(1)}, bf16[1280,256]{1,0:T(8,128)(2,1)S(1)}, u32[]{:S(2)}, u32[]{:S(2)}) collective-permute-start(bf16[1280,256]{1,0:T(8,128)(2,1)S(1)} %collective-permute-done.19), channel_id=1, source_target_pairs={{0,8},{8,0},{1,9},{9,1},{2,10},{10,2},{3,11},{11,3},{4,12},{12,4},... | collective-permute-start | bytes 1966088 | tf_op jit(solution)/shard_map/ppermute | solution.py:180
  123.6 3.8 %shard_map.86 = (f32[128,768]{1,0:T(8,128)S(1)}, bf16[128,768]{1,0:T(8,128)(2,1)}, bf16[128,768]{1,0:T(8,128)(2,1)}, bf16[128,768]{1,0:T(8,128)(2,1)S(1)}) custom-call(f32[128,16]{1,0:T(8,128)S(1)} %convert_select_fusion.marks_ref.refs_0_, bf16[128,768]{1,0:T(8,128)(2,1)S(1)} %get-tuple-element.84.refs_1_.refs_2_.refs_5_, ...), custom_call_target="tpu_custom_call" | custom-call | flops 1358954496 | bytes 12197888 | tf_op jit(solution)/shard_map/pallas_call | solution.py:324
  127.4 5.3 %collective-permute-done.26.refs_7_ = bf16[1280,768]{1,0:T(8,128)(2,1)S(1)} collective-permute-done((bf16[1280,768]{1,0:T(8,128)(2,1)S(1)}, bf16[1280,768]{1,0:T(8,128)(2,1)S(1)}, u32[]{:S(2)}, u32[]{:S(2)}) %collective-permute-start.26) | collective-permute-done | bytes 1966112 | tf_op jit(solution)/shard_map/ppermute | solution.py:180
  132.7 1.7 convolution_convert_fusion.1
  134.6 9.5 %collective-permute-done.20 = bf16[1280,256]{1,0:T(8,128)(2,1)S(1)} collective-permute-done((bf16[1280,256]{1,0:T(8,128)(2,1)S(1)}, bf16[1280,256]{1,0:T(8,128)(2,1)S(1)}, u32[]{:S(2)}, u32[]{:S(2)}) %collective-permute-start.20) | collective-permute-done | bytes 655392 | tf_op jit(solution)/shard_map/ppermute | solution.py:180
  146.1 2.5 collective-permute-start.44
  149.4 1.3 collective-permute-start.31
  150.7 1.5 collective-permute-start.32
  152.6 4.0 %shard_map.87 = (f32[128,768]{1,0:T(8,128)S(1)}, bf16[128,768]{1,0:T(8,128)(2,1)}, bf16[128,768]{1,0:T(8,128)(2,1)}, bf16[128,768]{1,0:T(8,128)(2,1)S(1)}) custom-call(f32[128,16]{1,0:T(8,128)S(1)} %convert_select_fusion.marks_ref.refs_0_, bf16[128,768]{1,0:T(8,128)(2,1)S(1)} %get-tuple-element.84.refs_1_.refs_2_.refs_5_, ...), custom_call_target="tpu_custom_call" | custom-call | flops 1509949440 | bytes 13574144 | tf_op jit(solution)/shard_map/pallas_call | solution.py:324
  156.6 1.3 collective-permute-start.33
  157.9 1.4 add_convert_fusion.4.refs_0_
  159.3 5.6 %collective-permute-done.31.refs_4_ = bf16[128,768]{1,0:T(8,128)(2,1)S(1)} collective-permute-done((bf16[128,768]{1,0:T(8,128)(2,1)S(1)}, bf16[128,768]{1,0:T(8,128)(2,1)S(1)}, u32[]{:S(2)}, u32[]{:S(2)}) %collective-permute-start.31) | collective-permute-done | bytes 196640 | tf_op jit(solution)/shard_map/ppermute | solution.py:180
  164.9 5.7 %collective-permute-done.33.refs_8_ = bf16[128,768]{1,0:T(8,128)(2,1)S(1)} collective-permute-done((bf16[128,768]{1,0:T(8,128)(2,1)S(1)}, bf16[128,768]{1,0:T(8,128)(2,1)S(1)}, u32[]{:S(2)}, u32[]{:S(2)}) %collective-permute-start.33) | collective-permute-done | bytes 196640 | tf_op jit(solution)/shard_map/ppermute | solution.py:180
  170.5 4.4 %shard_map.88 = (f32[128,768]{1,0:T(8,128)}, bf16[128,768]{1,0:T(8,128)(2,1)S(1)}, bf16[128,768]{1,0:T(8,128)(2,1)S(1)}, bf16[128,768]{1,0:T(8,128)(2,1)}) custom-call(f32[128,16]{1,0:T(8,128)S(1)} %convert_select_fusion.marks_ref.refs_0_, bf16[128,768]{1,0:T(8,128)(2,1)S(1)} %get-tuple-element.84.refs_1_.refs_2_.refs_5_, ...), custom_call_target="tpu_custom_call" | custom-call | flops 1660944384 | bytes 14557184 | tf_op jit(solution)/shard_map/pallas_call | solution.py:324
  177.0 3.5 %collective-permute-start.56 = (bf16[128,768]{1,0:T(8,128)(2,1)S(1)}, bf16[128,768]{1,0:T(8,128)(2,1)S(1)}, u32[]{:S(2)}, u32[]{:S(2)}) collective-permute-start(bf16[128,768]{1,0:T(8,128)(2,1)S(1)} %get-tuple-element.84.refs_1_.refs_2_.refs_5_), channel_id=1, source_target_pairs={{0,2},{1,3},{2,0},{3,1},{4,6},{5,7},{6,4},{7,5},{8,10},{9,11},{10,... | collective-permute-start | bytes 589832 | tf_op jit(solution)/shard_map/ppermute | solution.py:171
  180.5 2.7 %collective-permute-start.58 = (bf16[128,768]{1,0:T(8,128)(2,1)S(1)}, bf16[128,768]{1,0:T(8,128)(2,1)S(1)}, u32[]{:S(2)}, u32[]{:S(2)}) collective-permute-start(bf16[128,768]{1,0:T(8,128)(2,1)S(1)} %get-tuple-element.84.refs_1_.refs_2_.refs_5_), channel_id=1, source_target_pairs={{0,6},{1,7},{2,4},{3,5},{4,2},{5,3},{6,0},{7,1},{8,14},{9,15},{10,... | collective-permute-start | bytes 589832 | tf_op jit(solution)/shard_map/ppermute | solution.py:171
  184.0 2.2 spread.1
  186.3 1.0 collective-permute-start.29
  187.3 1.0 collective-permute-done.56.refs_6_
  188.3 1.2 collective-permute-start.43
  189.5 8.4 %collective-permute-done.57.refs_7_ = bf16[128,768]{1,0:T(8,128)(2,1)S(1)} collective-permute-done((bf16[128,768]{1,0:T(8,128)(2,1)S(1)}, bf16[128,768]{1,0:T(8,128)(2,1)S(1)}, u32[]{:S(2)}, u32[]{:S(2)}) %collective-permute-start.57) | collective-permute-done | bytes 196640 | tf_op jit(solution)/shard_map/ppermute | solution.py:171
  198.7 18.0 %collective-permute-done.43 = bf16[64,768]{1,0:T(8,128)(2,1)S(1)} collective-permute-done((bf16[64,768]{1,0:T(8,128)(2,1)S(1)}, bf16[64,768]{1,0:T(8,128)(2,1)S(1)}, u32[]{:S(2)}, u32[]{:S(2)}) %collective-permute-start.43) | collective-permute-done | bytes 98336 | tf_op jit(solution)/shard_map/ppermute | solution.py:171
  216.7 1.0 collective-permute-start.35
  217.7 3.4 %collective-permute-start.36 = (bf16[128,768]{1,0:T(8,128)(2,1)S(1)}, bf16[128,768]{1,0:T(8,128)(2,1)S(1)}, u32[]{:S(2)}, u32[]{:S(2)}) collective-permute-start(bf16[128,768]{1,0:T(8,128)(2,1)S(1)} %get-tuple-element.68.refs_4_), channel_id=1, source_target_pairs={{0,6},{1,7},{2,4},{3,5},{4,2},{5,3},{6,0},{7,1},{8,14},{9,15},{10,... | collective-permute-start | bytes 589832 | tf_op jit(solution)/shard_map/ppermute | solution.py:171
  221.1 1.1 collective-permute-start.47
  222.1 10.0 %collective-permute-done.46 = bf16[64,768]{1,0:T(8,128)(2,1)S(1)} collective-permute-done((bf16[64,768]{1,0:T(8,128)(2,1)S(1)}, bf16[64,768]{1,0:T(8,128)(2,1)S(1)}, u32[]{:S(2)}, u32[]{:S(2)}) %collective-permute-start.46) | collective-permute-done | bytes 98336 | tf_op jit(solution)/shard_map/ppermute | solution.py:171
  232.2 1.0 collective-permute-start.48
  233.2 3.0 %collective-permute-done.35.refs_6_ = bf16[128,768]{1,0:T(8,128)(2,1)S(1)} collective-permute-done((bf16[128,768]{1,0:T(8,128)(2,1)S(1)}, bf16[128,768]{1,0:T(8,128)(2,1)S(1)}, u32[]{:S(2)}, u32[]{:S(2)}) %collective-permute-start.35) | collective-permute-done | bytes 196640 | tf_op jit(solution)/shard_map/ppermute | solution.py:171
  236.2 7.3 %collective-permute-done.47 = bf16[64,768]{1,0:T(8,128)(2,1)S(1)} collective-permute-done((bf16[64,768]{1,0:T(8,128)(2,1)S(1)}, bf16[64,768]{1,0:T(8,128)(2,1)S(1)}, u32[]{:S(2)}, u32[]{:S(2)}) %collective-permute-start.47) | collective-permute-done | bytes 98336 | tf_op jit(solution)/shard_map/ppermute | solution.py:171
  244.5 3.1 %collective-permute-start.55 = (bf16[320,256]{1,0:T(8,128)(2,1)S(1)}, bf16[320,256]{1,0:T(8,128)(2,1)S(1)}, u32[]{:S(2)}, u32[]{:S(2)}) collective-permute-start(bf16[320,256]{1,0:T(8,128)(2,1)S(1)} %get-tuple-element.82), channel_id=1, source_target_pairs={{0,6},{1,7},{2,4},{3,5},{4,2},{5,3},{6,0},{7,1},{8,14},{9,15},{10,... | collective-permute-start | bytes 491528 | tf_op jit(solution)/shard_map/ppermute | solution.py:171
  248.2 1.5 convolution_convert_fusion
  250.4 8.7 %collective-permute-done.54.refs_3_ = bf16[320,256]{1,0:T(8,128)(2,1)S(1)} collective-permute-done((bf16[320,256]{1,0:T(8,128)(2,1)S(1)}, bf16[320,256]{1,0:T(8,128)(2,1)S(1)}, u32[]{:S(2)}, u32[]{:S(2)}) %collective-permute-start.54) | collective-permute-done | bytes 163872 | tf_op jit(solution)/shard_map/ppermute | solution.py:171
  259.1 1.6 shard_map.90
  (169 shorter events, 19.8 us)
Async XLA Ops:
  0.6 29.4 %collective-permute-start.4 = (bf16[768,768]{1,0:T(8,128)(2,1)}, bf16[768,768]{1,0:T(8,128)(2,1)}, u32[]{:S(2)}, u32[]{:S(2)}) collective-permute-start(bf16[768,768]{1,0:T(8,128)(2,1)} %bitcast.38), channel_id=1, source_target_pairs={{0,2},{1,3},{2,0},{3,1},{4,6},{5,7},{6,4},{7,5},{8,10},{9,11},{10,... | collective-permute-start | bytes 3538952 | tf_op jit(solution)/shard_map/ppermute | solution.py:171
  3.7 36.5 %collective-permute-start.5 = (bf16[768,768]{1,0:T(8,128)(2,1)}, bf16[768,768]{1,0:T(8,128)(2,1)}, u32[]{:S(2)}, u32[]{:S(2)}) collective-permute-start(bf16[768,768]{1,0:T(8,128)(2,1)} %bitcast.39), channel_id=1, source_target_pairs={{2,4},{3,5},{4,2},{5,3},{10,12},{11,13},{12,10},{13,11},{18,20},{1... | collective-permute-start | bytes 3538952 | tf_op jit(solution)/shard_map/ppermute | solution.py:171
  8.4 15.1 %collective-permute-start = (bf16[1280,128]{1,0:T(8,128)(2,1)}, bf16[1280,128]{1,0:T(8,128)(2,1)}, u32[]{:S(2)}, u32[]{:S(2)}) collective-permute-start(bf16[1280,128]{1,0:T(8,128)(2,1)} %pad_maximum_fusion.3), channel_id=1, source_target_pairs={{0,1},{1,0},{2,3},{3,2},{4,5},{5,4},{6,7},{7,6},{8,9},{9,8},{10,11... | collective-permute-start | bytes 983048 | tf_op jit(solution)/shard_map/ppermute | solution.py:176
  9.1 7.4 %collective-permute-start.1 = (bf16[1280,128]{1,0:T(8,128)(2,1)S(1)}, bf16[1280,128]{1,0:T(8,128)(2,1)S(1)}, u32[]{:S(2)}, u32[]{:S(2)}) collective-permute-start(bf16[1280,128]{1,0:T(8,128)(2,1)S(1)} %pad_maximum_fusion.4), channel_id=1, source_target_pairs={{0,1},{1,0},{2,3},{3,2},{4,5},{5,4},{6,7},{7,6},{8,9},{9,8},{10,11... | collective-permute-start | bytes 983048 | tf_op jit(solution)/shard_map/ppermute | solution.py:176
  14.0 24.9 %collective-permute-start.3 = (bf16[768,768]{1,0:T(8,128)(2,1)}, bf16[768,768]{1,0:T(8,128)(2,1)}, u32[]{:S(2)}, u32[]{:S(2)}) collective-permute-start(bf16[768,768]{1,0:T(8,128)(2,1)} %convolution_convert_fusion.4), channel_id=1, source_target_pairs={{0,1},{1,0},{2,3},{3,2},{4,5},{5,4},{6,7},{7,6},{8,9},{9,8},{10,11... | collective-permute-start | bytes 3538952 | tf_op jit(solution)/shard_map/ppermute | solution.py:176
  16.4 1.7 collective-permute-start.41
  18.8 18.8 %collective-permute-start.14 = (bf16[1280,256]{1,0:T(8,128)(2,1)}, bf16[1280,256]{1,0:T(8,128)(2,1)}, u32[]{:S(2)}, u32[]{:S(2)}) collective-permute-start(bf16[1280,256]{1,0:T(8,128)(2,1)} %pad_maximum_fusion.2), channel_id=1, source_target_pairs={{24,16},{8,0},{25,17},{9,1},{26,18},{10,2},{27,19},{11,3},{28,20},... | collective-permute-start | bytes 1966088 | tf_op jit(solution)/shard_map/ppermute | solution.py:180
  23.5 8.3 %collective-permute-start.2 = (f32[128,768]{1,0:T(8,128)}, f32[128,768]{1,0:T(8,128)}, u32[]{:S(2)}, u32[]{:S(2)}) collective-permute-start(f32[128,768]{1,0:T(8,128)} %slice.125), channel_id=1, source_target_pairs={{0,1},{1,0},{2,3},{3,2},{4,5},{5,4},{6,7},{7,6},{8,9},{9,8},{10,11... | collective-permute-start | bytes 1179656 | tf_op jit(solution)/shard_map/ppermute | solution.py:176
  30.0 13.4 %collective-permute-start.10 = (bf16[768,768]{1,0:T(8,128)(2,1)}, bf16[768,768]{1,0:T(8,128)(2,1)}, u32[]{:S(2)}, u32[]{:S(2)}) collective-permute-start(bf16[768,768]{1,0:T(8,128)(2,1)} %collective-permute-done.4.refs_1_), channel_id=1, source_target_pairs={{2,4},{3,5},{4,2},{5,3},{10,12},{11,13},{12,10},{13,11},{18,20},{1... | collective-permute-start | bytes 3538952 | tf_op jit(solution)/shard_map/ppermute | solution.py:171
  31.9 14.8 %collective-permute-start.7 = (bf16[768,768]{1,0:T(8,128)(2,1)S(1)}, bf16[768,768]{1,0:T(8,128)(2,1)S(1)}, u32[]{:S(2)}, u32[]{:S(2)}) collective-permute-start(bf16[768,768]{1,0:T(8,128)(2,1)S(1)} %bitcast.40), channel_id=1, source_target_pairs={{0,1},{1,0},{2,3},{3,2},{4,5},{5,4},{6,7},{7,6},{8,9},{9,8},{10,11... | collective-permute-start | bytes 3538952 | tf_op jit(solution)/shard_map/ppermute | solution.py:176
  37.6 51.5 %collective-permute-start.17 = (bf16[1280,768]{1,0:T(8,128)(2,1)S(1)}, bf16[1280,768]{1,0:T(8,128)(2,1)S(1)}, u32[]{:S(2)}, u32[]{:S(2)}) collective-permute-start(bf16[1280,768]{1,0:T(8,128)(2,1)S(1)} %pad_maximum_fusion.refs_1_), channel_id=1, source_target_pairs={{24,16},{8,0},{25,17},{9,1},{26,18},{10,2},{27,19},{11,3},{28,20},... | collective-permute-start | bytes 5898248 | tf_op jit(solution)/shard_map/ppermute | solution.py:180
  38.9 45.8 %collective-permute-start.23 = (bf16[1280,768]{1,0:T(8,128)(2,1)S(1)}, bf16[1280,768]{1,0:T(8,128)(2,1)S(1)}, u32[]{:S(2)}, u32[]{:S(2)}) collective-permute-start(bf16[1280,768]{1,0:T(8,128)(2,1)S(1)} %pad_maximum_fusion.refs_1_), channel_id=1, source_target_pairs={{24,8},{16,0},{25,9},{17,1},{26,10},{18,2},{27,11},{19,3},{28,12},... | collective-permute-start | bytes 5898248 | tf_op jit(solution)/shard_map/ppermute | solution.py:180
  40.2 31.7 %collective-permute-start.6 = (bf16[768,768]{1,0:T(8,128)(2,1)}, bf16[768,768]{1,0:T(8,128)(2,1)S(1)}, u32[]{:S(2)}, u32[]{:S(2)}) collective-permute-start(bf16[768,768]{1,0:T(8,128)(2,1)} %collective-permute-done.5), channel_id=1, source_target_pairs={{2,0},{3,1},{4,6},{5,7},{10,8},{11,9},{12,14},{13,15},{18,16},{19,... | collective-permute-start | bytes 3538952 | tf_op jit(solution)/shard_map/ppermute | solution.py:171
  43.4 52.3 %collective-permute-start.11 = (bf16[768,768]{1,0:T(8,128)(2,1)}, bf16[768,768]{1,0:T(8,128)(2,1)S(1)}, u32[]{:S(2)}, u32[]{:S(2)}) collective-permute-start(bf16[768,768]{1,0:T(8,128)(2,1)} %collective-permute-done.10.refs_6_), channel_id=1, source_target_pairs={{2,0},{3,1},{4,6},{5,7},{10,8},{11,9},{12,14},{13,15},{18,16},{19,... | collective-permute-start | bytes 3538952 | tf_op jit(solution)/shard_map/ppermute | solution.py:171
  44.8 27.2 %copy-start.13 = (bf16[320,128]{1,0:T(8,128)(2,1)S(1)}, bf16[320,128]{1,0:T(8,128)(2,1)}, u32[]{:S(2)}) copy-start(bf16[320,128]{1,0:T(8,128)(2,1)} %get-tuple-element.104) | copy-start | bytes 245764
  44.8 27.2 %copy-start.14 = (bf16[320,128]{1,0:T(8,128)(2,1)S(1)}, bf16[320,128]{1,0:T(8,128)(2,1)}, u32[]{:S(2)}) copy-start(bf16[320,128]{1,0:T(8,128)(2,1)} %get-tuple-element.109) | copy-start | bytes 245764
  46.7 26.5 %collective-permute-start.15 = (f32[128,768]{1,0:T(8,128)S(1)}, f32[128,768]{1,0:T(8,128)S(1)}, u32[]{:S(2)}, u32[]{:S(2)}) collective-permute-start(f32[128,768]{1,0:T(8,128)S(1)} %slice.127), channel_id=1, source_target_pairs={{0,1},{1,0},{2,3},{3,2},{4,5},{5,4},{6,7},{7,6},{8,9},{9,8},{10,11... | collective-permute-start | bytes 1179656 | tf_op jit(solution)/shard_map/ppermute | solution.py:176
  72.0 25.5 %collective-permute-start.8 = (bf16[768,768]{1,0:T(8,128)(2,1)}, bf16[768,768]{1,0:T(8,128)(2,1)S(1)}, u32[]{:S(2)}, u32[]{:S(2)}) collective-permute-start(bf16[768,768]{1,0:T(8,128)(2,1)} %collective-permute-done.4.refs_1_), channel_id=1, source_target_pairs={{0,1},{1,0},{2,3},{3,2},{4,5},{5,4},{6,7},{7,6},{8,9},{9,8},{10,11... | collective-permute-start | bytes 3538952 | tf_op jit(solution)/shard_map/ppermute | solution.py:176
  73.2 26.8 %collective-permute-start.9 = (bf16[768,768]{1,0:T(8,128)(2,1)S(1)}, bf16[768,768]{1,0:T(8,128)(2,1)S(1)}, u32[]{:S(2)}, u32[]{:S(2)}) collective-permute-start(bf16[768,768]{1,0:T(8,128)(2,1)S(1)} %broadcast_select_fusion.refs_2_), channel_id=1, source_target_pairs={{0,1},{1,0},{2,3},{3,2},{4,5},{5,4},{6,7},{7,6},{8,9},{9,8},{10,11... | collective-permute-start | bytes 3538952 | tf_op jit(solution)/shard_map/ppermute | solution.py:176
  84.7 48.0 %collective-permute-start.26 = (bf16[1280,768]{1,0:T(8,128)(2,1)S(1)}, bf16[1280,768]{1,0:T(8,128)(2,1)S(1)}, u32[]{:S(2)}, u32[]{:S(2)}) collective-permute-start(bf16[1280,768]{1,0:T(8,128)(2,1)S(1)} %collective-permute-done.23.refs_4_), channel_id=1, source_target_pairs={{0,8},{8,0},{1,9},{9,1},{2,10},{10,2},{3,11},{11,3},{4,12},{12,4},... | collective-permute-start | bytes 5898248 | tf_op jit(solution)/shard_map/ppermute | solution.py:180
  89.1 14.2 %collective-permute-start.12 = (bf16[768,768]{1,0:T(8,128)(2,1)}, bf16[768,768]{1,0:T(8,128)(2,1)S(1)}, u32[]{:S(2)}, u32[]{:S(2)}) collective-permute-start(bf16[768,768]{1,0:T(8,128)(2,1)} %collective-permute-done.10.refs_6_), channel_id=1, source_target_pairs={{0,1},{1,0},{2,3},{3,2},{4,5},{5,4},{6,7},{7,6},{8,9},{9,8},{10,11... | collective-permute-start | bytes 3538952 | tf_op jit(solution)/shard_map/ppermute | solution.py:176
  95.7 7.6 %collective-permute-start.13 = (bf16[768,768]{1,0:T(8,128)(2,1)S(1)}, bf16[768,768]{1,0:T(8,128)(2,1)S(1)}, u32[]{:S(2)}, u32[]{:S(2)}) collective-permute-start(bf16[768,768]{1,0:T(8,128)(2,1)S(1)} %collective-permute-done.11.refs_7_), channel_id=1, source_target_pairs={{0,1},{1,0},{2,3},{3,2},{4,5},{5,4},{6,7},{7,6},{8,9},{9,8},{10,11... | collective-permute-start | bytes 3538952 | tf_op jit(solution)/shard_map/ppermute | solution.py:176
  97.5 25.8 %collective-permute-start.18 = (bf16[768,768]{1,0:T(8,128)(2,1)S(1)}, bf16[768,768]{1,0:T(8,128)(2,1)S(1)}, u32[]{:S(2)}, u32[]{:S(2)}) collective-permute-start(bf16[768,768]{1,0:T(8,128)(2,1)S(1)} %convolution_convert_fusion.3), channel_id=1, source_target_pairs={{0,1},{1,0},{2,3},{3,2},{4,5},{5,4},{6,7},{7,6},{8,9},{9,8},{10,11... | collective-permute-start | bytes 3538952 | tf_op jit(solution)/shard_map/ppermute | solution.py:176
  100.0 18.9 %collective-permute-start.19 = (bf16[1280,256]{1,0:T(8,128)(2,1)}, bf16[1280,256]{1,0:T(8,128)(2,1)S(1)}, u32[]{:S(2)}, u32[]{:S(2)}) collective-permute-start(bf16[1280,256]{1,0:T(8,128)(2,1)} %pad_maximum_fusion.2), channel_id=1, source_target_pairs={{24,8},{16,0},{25,9},{17,1},{26,10},{18,2},{27,11},{19,3},{28,12},... | collective-permute-start | bytes 1966088 | tf_op jit(solution)/shard_map/ppermute | solution.py:180
  103.3 41.9 %collective-permute-start.24 = (bf16[768,768]{1,0:T(8,128)(2,1)S(1)}, bf16[768,768]{1,0:T(8,128)(2,1)S(1)}, u32[]{:S(2)}, u32[]{:S(2)}) collective-permute-start(bf16[768,768]{1,0:T(8,128)(2,1)S(1)} %convolution_convert_fusion.2), channel_id=1, source_target_pairs={{0,1},{1,0},{2,3},{3,2},{4,5},{5,4},{6,7},{7,6},{8,9},{9,8},{10,11... | collective-permute-start | bytes 3538952 | tf_op jit(solution)/shard_map/ppermute | solution.py:176
  111.6 12.0 %collective-permute-start.16 = (bf16[128,768]{1,0:T(8,128)(2,1)S(1)}, bf16[128,768]{1,0:T(8,128)(2,1)S(1)}, u32[]{:S(2)}, u32[]{:S(2)}) collective-permute-start(bf16[128,768]{1,0:T(8,128)(2,1)S(1)} %get-tuple-element.67), channel_id=1, source_target_pairs={{24,16},{25,17},{26,18},{27,19},{28,20},{29,21},{30,22},{31,23}} | collective-permute-start | bytes 589832 | tf_op jit(solution)/shard_map/ppermute | solution.py:180
  118.9 25.2 %collective-permute-start.20 = (bf16[1280,256]{1,0:T(8,128)(2,1)S(1)}, bf16[1280,256]{1,0:T(8,128)(2,1)S(1)}, u32[]{:S(2)}, u32[]{:S(2)}) collective-permute-start(bf16[1280,256]{1,0:T(8,128)(2,1)S(1)} %collective-permute-done.19), channel_id=1, source_target_pairs={{0,8},{8,0},{1,9},{9,1},{2,10},{10,2},{3,11},{11,3},{4,12},{12,4},... | collective-permute-start | bytes 1966088 | tf_op jit(solution)/shard_map/ppermute | solution.py:180
  134.5 16.2 %collective-permute-start.27 = (bf16[768,768]{1,0:T(8,128)(2,1)S(1)}, bf16[768,768]{1,0:T(8,128)(2,1)S(1)}, u32[]{:S(2)}, u32[]{:S(2)}) collective-permute-start(bf16[768,768]{1,0:T(8,128)(2,1)S(1)} %convolution_convert_fusion.1), channel_id=1, source_target_pairs={{0,1},{1,0},{2,3},{3,2},{4,5},{5,4},{6,7},{7,6},{8,9},{9,8},{10,11... | collective-permute-start | bytes 3538952 | tf_op jit(solution)/shard_map/ppermute | solution.py:176
  145.0 4.3 %collective-permute-start.21 = (f32[128,768]{1,0:T(8,128)S(1)}, f32[128,768]{1,0:T(8,128)S(1)}, u32[]{:S(2)}, u32[]{:S(2)}) collective-permute-start(f32[128,768]{1,0:T(8,128)S(1)} %slice.129), channel_id=1, source_target_pairs={{0,1},{1,0},{2,3},{3,2},{4,5},{5,4},{6,7},{7,6},{8,9},{9,8},{10,11... | collective-permute-start | bytes 1179656 | tf_op jit(solution)/shard_map/ppermute | solution.py:176
  145.4 7.1 %collective-permute-start.22 = (bf16[128,768]{1,0:T(8,128)(2,1)S(1)}, bf16[128,768]{1,0:T(8,128)(2,1)S(1)}, u32[]{:S(2)}, u32[]{:S(2)}) collective-permute-start(bf16[128,768]{1,0:T(8,128)(2,1)S(1)} %get-tuple-element.67), channel_id=1, source_target_pairs={{24,8},{25,9},{26,10},{27,11},{28,12},{29,13},{30,14},{31,15}} | collective-permute-start | bytes 589832 | tf_op jit(solution)/shard_map/ppermute | solution.py:180
  146.1 40.1 %collective-permute-start.44 = (bf16[64,768]{1,0:T(8,128)(2,1)S(1)}, bf16[64,768]{1,0:T(8,128)(2,1)S(1)}, u32[]{:S(2)}, u32[]{:S(2)}) collective-permute-start(bf16[64,768]{1,0:T(8,128)(2,1)S(1)} %get-tuple-element.72), channel_id=1, source_target_pairs={{0,6},{1,7},{2,4},{3,5},{4,2},{5,3},{6,0},{7,1},{8,14},{9,15},{10,... | collective-permute-start | bytes 294920 | tf_op jit(solution)/shard_map/ppermute | solution.py:171
  148.7 3.9 %collective-permute-start.25 = (bf16[128,768]{1,0:T(8,128)(2,1)S(1)}, bf16[128,768]{1,0:T(8,128)(2,1)S(1)}, u32[]{:S(2)}, u32[]{:S(2)}) collective-permute-start(bf16[128,768]{1,0:T(8,128)(2,1)S(1)} %get-tuple-element.59), channel_id=1, source_target_pairs={{16,8},{17,9},{18,10},{19,11},{20,12},{21,13},{22,14},{23,15}} | collective-permute-start | bytes 589832 | tf_op jit(solution)/shard_map/ppermute | solution.py:180
  149.4 15.5 %collective-permute-start.31 = (bf16[128,768]{1,0:T(8,128)(2,1)S(1)}, bf16[128,768]{1,0:T(8,128)(2,1)S(1)}, u32[]{:S(2)}, u32[]{:S(2)}) collective-permute-start(bf16[128,768]{1,0:T(8,128)(2,1)S(1)} %get-tuple-element.59), channel_id=1, source_target_pairs={{16,0},{17,1},{18,2},{19,3},{20,4},{21,5},{22,6},{23,7}} | collective-permute-start | bytes 589832 | tf_op jit(solution)/shard_map/ppermute | solution.py:180
  150.7 14.2 %collective-permute-start.32 = (bf16[128,768]{1,0:T(8,128)(2,1)S(1)}, bf16[128,768]{1,0:T(8,128)(2,1)S(1)}, u32[]{:S(2)}, u32[]{:S(2)}) collective-permute-start(bf16[128,768]{1,0:T(8,128)(2,1)S(1)} %get-tuple-element.67), channel_id=1, source_target_pairs={{24,0},{25,1},{26,2},{27,3},{28,4},{29,5},{30,6},{31,7}} | collective-permute-start | bytes 589832 | tf_op jit(solution)/shard_map/ppermute | solution.py:180
  156.6 13.9 %collective-permute-start.33 = (bf16[128,768]{1,0:T(8,128)(2,1)S(1)}, bf16[128,768]{1,0:T(8,128)(2,1)S(1)}, u32[]{:S(2)}, u32[]{:S(2)}) collective-permute-start(bf16[128,768]{1,0:T(8,128)(2,1)S(1)} %get-tuple-element.62), channel_id=1, source_target_pairs={{8,0},{9,1},{10,2},{11,3},{12,4},{13,5},{14,6},{15,7}} | collective-permute-start | bytes 589832 | tf_op jit(solution)/shard_map/ppermute | solution.py:180
  175.2 1.5 collective-permute-start.45
  175.3 1.7 collective-permute-start.49
  175.8 4.7 %collective-permute-start.50 = (bf16[128,768]{1,0:T(8,128)(2,1)S(1)}, bf16[128,768]{1,0:T(8,128)(2,1)S(1)}, u32[]{:S(2)}, u32[]{:S(2)}) collective-permute-start(bf16[128,768]{1,0:T(8,128)(2,1)S(1)} %add.229.refs_5_), channel_id=1, source_target_pairs={{0,1},{1,0},{2,3},{3,2},{4,5},{5,4},{6,7},{7,6},{8,9},{9,8},{10,11... | collective-permute-start | bytes 589832 | tf_op jit(solution)/shard_map/ppermute | solution.py:176
  176.0 4.5 %collective-permute-start.51 = (bf16[128,768]{1,0:T(8,128)(2,1)S(1)}, bf16[128,768]{1,0:T(8,128)(2,1)S(1)}, u32[]{:S(2)}, u32[]{:S(2)}) collective-permute-start(bf16[128,768]{1,0:T(8,128)(2,1)S(1)} %add.230.refs_8_), channel_id=1, source_target_pairs={{0,1},{1,0},{2,3},{3,2},{4,5},{5,4},{6,7},{7,6},{8,9},{9,8},{10,11... | collective-permute-start | bytes 589832 | tf_op jit(solution)/shard_map/ppermute | solution.py:176
  176.7 6.5 %collective-permute-start.52 = (bf16[128,768]{1,0:T(8,128)(2,1)S(1)}, bf16[128,768]{1,0:T(8,128)(2,1)S(1)}, u32[]{:S(2)}, u32[]{:S(2)}) collective-permute-start(bf16[128,768]{1,0:T(8,128)(2,1)S(1)} %add.231.refs_11_), channel_id=1, source_target_pairs={{0,1},{1,0},{2,3},{3,2},{4,5},{5,4},{6,7},{7,6},{8,9},{9,8},{10,11... | collective-permute-start | bytes 589832 | tf_op jit(solution)/shard_map/ppermute | solution.py:176
  177.0 11.3 %collective-permute-start.56 = (bf16[128,768]{1,0:T(8,128)(2,1)S(1)}, bf16[128,768]{1,0:T(8,128)(2,1)S(1)}, u32[]{:S(2)}, u32[]{:S(2)}) collective-permute-start(bf16[128,768]{1,0:T(8,128)(2,1)S(1)} %get-tuple-element.84.refs_1_.refs_2_.refs_5_), channel_id=1, source_target_pairs={{0,2},{1,3},{2,0},{3,1},{4,6},{5,7},{6,4},{7,5},{8,10},{9,11},{10,... | collective-permute-start | bytes 589832 | tf_op jit(solution)/shard_map/ppermute | solution.py:171
  180.5 17.4 %collective-permute-start.57 = (bf16[128,768]{1,0:T(8,128)(2,1)S(1)}, bf16[128,768]{1,0:T(8,128)(2,1)S(1)}, u32[]{:S(2)}, u32[]{:S(2)}) collective-permute-start(bf16[128,768]{1,0:T(8,128)(2,1)S(1)} %get-tuple-element.84.refs_1_.refs_2_.refs_5_), channel_id=1, source_target_pairs={{0,4},{1,5},{2,6},{3,7},{4,0},{5,1},{6,2},{7,3},{8,12},{9,13},{10,... | collective-permute-start | bytes 589832 | tf_op jit(solution)/shard_map/ppermute | solution.py:171
  180.5 17.4 %collective-permute-start.58 = (bf16[128,768]{1,0:T(8,128)(2,1)S(1)}, bf16[128,768]{1,0:T(8,128)(2,1)S(1)}, u32[]{:S(2)}, u32[]{:S(2)}) collective-permute-start(bf16[128,768]{1,0:T(8,128)(2,1)S(1)} %get-tuple-element.84.refs_1_.refs_2_.refs_5_), channel_id=1, source_target_pairs={{0,6},{1,7},{2,4},{3,5},{4,2},{5,3},{6,0},{7,1},{8,14},{9,15},{10,... | collective-permute-start | bytes 589832 | tf_op jit(solution)/shard_map/ppermute | solution.py:171
  183.2 34.5 %collective-permute-start.28 = (bf16[320,256]{1,0:T(8,128)(2,1)S(1)}, bf16[320,256]{1,0:T(8,128)(2,1)S(1)}, u32[]{:S(2)}, u32[]{:S(2)}) collective-permute-start(bf16[320,256]{1,0:T(8,128)(2,1)S(1)} %get-tuple-element.63), channel_id=1, source_target_pairs={{0,2},{1,3},{2,0},{3,1},{4,6},{5,7},{6,4},{7,5},{8,10},{9,11},{10,... | collective-permute-start | bytes 491528 | tf_op jit(solution)/shard_map/ppermute | solution.py:171
  186.3 34.8 %collective-permute-start.29 = (bf16[320,256]{1,0:T(8,128)(2,1)S(1)}, bf16[320,256]{1,0:T(8,128)(2,1)S(1)}, u32[]{:S(2)}, u32[]{:S(2)}) collective-permute-start(bf16[320,256]{1,0:T(8,128)(2,1)S(1)} %get-tuple-element.64), channel_id=1, source_target_pairs={{0,4},{1,5},{2,6},{3,7},{4,0},{5,1},{6,2},{7,3},{8,12},{9,13},{10,... | collective-permute-start | bytes 491528 | tf_op jit(solution)/shard_map/ppermute | solution.py:171
  188.3 28.3 %collective-permute-start.43 = (bf16[64,768]{1,0:T(8,128)(2,1)S(1)}, bf16[64,768]{1,0:T(8,128)(2,1)S(1)}, u32[]{:S(2)}, u32[]{:S(2)}) collective-permute-start(bf16[64,768]{1,0:T(8,128)(2,1)S(1)} %get-tuple-element.71), channel_id=1, source_target_pairs={{0,4},{1,5},{2,6},{3,7},{4,0},{5,1},{6,2},{7,3},{8,12},{9,13},{10,... | collective-permute-start | bytes 294920 | tf_op jit(solution)/shard_map/ppermute | solution.py:171
  198.0 18.7 %collective-permute-start.42 = (bf16[64,768]{1,0:T(8,128)(2,1)S(1)}, bf16[64,768]{1,0:T(8,128)(2,1)S(1)}, u32[]{:S(2)}, u32[]{:S(2)}) collective-permute-start(bf16[64,768]{1,0:T(8,128)(2,1)S(1)} %get-tuple-element.70), channel_id=1, source_target_pairs={{0,2},{1,3},{2,0},{3,1},{4,6},{5,7},{6,4},{7,5},{8,10},{9,11},{10,... | collective-permute-start | bytes 294920 | tf_op jit(solution)/shard_map/ppermute | solution.py:171
  198.0 23.1 %collective-permute-start.30 = (bf16[320,256]{1,0:T(8,128)(2,1)S(1)}, bf16[320,256]{1,0:T(8,128)(2,1)S(1)}, u32[]{:S(2)}, u32[]{:S(2)}) collective-permute-start(bf16[320,256]{1,0:T(8,128)(2,1)S(1)} %get-tuple-element.65), channel_id=1, source_target_pairs={{0,6},{1,7},{2,4},{3,5},{4,2},{5,3},{6,0},{7,1},{8,14},{9,15},{10,... | collective-permute-start | bytes 491528 | tf_op jit(solution)/shard_map/ppermute | solution.py:171
  216.7 16.5 %collective-permute-start.34 = (bf16[128,768]{1,0:T(8,128)(2,1)S(1)}, bf16[128,768]{1,0:T(8,128)(2,1)S(1)}, u32[]{:S(2)}, u32[]{:S(2)}) collective-permute-start(bf16[128,768]{1,0:T(8,128)(2,1)S(1)} %get-tuple-element.68.refs_4_), channel_id=1, source_target_pairs={{0,2},{1,3},{2,0},{3,1},{4,6},{5,7},{6,4},{7,5},{8,10},{9,11},{10,... | collective-permute-start | bytes 589832 | tf_op jit(solution)/shard_map/ppermute | solution.py:171
  216.7 19.5 %collective-permute-start.35 = (bf16[128,768]{1,0:T(8,128)(2,1)S(1)}, bf16[128,768]{1,0:T(8,128)(2,1)S(1)}, u32[]{:S(2)}, u32[]{:S(2)}) collective-permute-start(bf16[128,768]{1,0:T(8,128)(2,1)S(1)} %get-tuple-element.68.refs_4_), channel_id=1, source_target_pairs={{0,4},{1,5},{2,6},{3,7},{4,0},{5,1},{6,2},{7,3},{8,12},{9,13},{10,... | collective-permute-start | bytes 589832 | tf_op jit(solution)/shard_map/ppermute | solution.py:171
  217.7 18.5 %collective-permute-start.36 = (bf16[128,768]{1,0:T(8,128)(2,1)S(1)}, bf16[128,768]{1,0:T(8,128)(2,1)S(1)}, u32[]{:S(2)}, u32[]{:S(2)}) collective-permute-start(bf16[128,768]{1,0:T(8,128)(2,1)S(1)} %get-tuple-element.68.refs_4_), channel_id=1, source_target_pairs={{0,6},{1,7},{2,4},{3,5},{4,2},{5,3},{6,0},{7,1},{8,14},{9,15},{10,... | collective-permute-start | bytes 589832 | tf_op jit(solution)/shard_map/ppermute | solution.py:171
  221.1 11.1 %collective-permute-start.46 = (bf16[64,768]{1,0:T(8,128)(2,1)S(1)}, bf16[64,768]{1,0:T(8,128)(2,1)S(1)}, u32[]{:S(2)}, u32[]{:S(2)}) collective-permute-start(bf16[64,768]{1,0:T(8,128)(2,1)S(1)} %pad_maximum_fusion.9), channel_id=1, source_target_pairs={{0,2},{1,3},{2,0},{3,1},{4,6},{5,7},{6,4},{7,5},{8,10},{9,11},{10,... | collective-permute-start | bytes 294920 | tf_op jit(solution)/shard_map/ppermute | solution.py:171
  221.1 22.4 %collective-permute-start.47 = (bf16[64,768]{1,0:T(8,128)(2,1)S(1)}, bf16[64,768]{1,0:T(8,128)(2,1)S(1)}, u32[]{:S(2)}, u32[]{:S(2)}) collective-permute-start(bf16[64,768]{1,0:T(8,128)(2,1)S(1)} %pad_maximum_fusion.10), channel_id=1, source_target_pairs={{0,4},{1,5},{2,6},{3,7},{4,0},{5,1},{6,2},{7,3},{8,12},{9,13},{10,... | collective-permute-start | bytes 294920 | tf_op jit(solution)/shard_map/ppermute | solution.py:171
  232.2 11.4 %collective-permute-start.48 = (bf16[64,768]{1,0:T(8,128)(2,1)S(1)}, bf16[64,768]{1,0:T(8,128)(2,1)S(1)}, u32[]{:S(2)}, u32[]{:S(2)}) collective-permute-start(bf16[64,768]{1,0:T(8,128)(2,1)S(1)} %pad_maximum_fusion.11), channel_id=1, source_target_pairs={{0,6},{1,7},{2,4},{3,5},{4,2},{5,3},{6,0},{7,1},{8,14},{9,15},{10,... | collective-permute-start | bytes 294920 | tf_op jit(solution)/shard_map/ppermute | solution.py:171
  233.2 10.9 %collective-permute-start.37 = (bf16[128,768]{1,0:T(8,128)(2,1)S(1)}, bf16[128,768]{1,0:T(8,128)(2,1)S(1)}, u32[]{:S(2)}, u32[]{:S(2)}) collective-permute-start(bf16[128,768]{1,0:T(8,128)(2,1)S(1)} %get-tuple-element.68.refs_4_), channel_id=1, source_target_pairs={{0,1},{1,0},{2,3},{3,2},{4,5},{5,4},{6,7},{7,6},{8,9},{9,8},{10,11... | collective-permute-start | bytes 589832 | tf_op jit(solution)/shard_map/ppermute | solution.py:176
  236.2 8.3 %collective-permute-start.53 = (bf16[320,256]{1,0:T(8,128)(2,1)S(1)}, bf16[320,256]{1,0:T(8,128)(2,1)S(1)}, u32[]{:S(2)}, u32[]{:S(2)}) collective-permute-start(bf16[320,256]{1,0:T(8,128)(2,1)S(1)} %get-tuple-element.80), channel_id=1, source_target_pairs={{0,2},{1,3},{2,0},{3,1},{4,6},{5,7},{6,4},{7,5},{8,10},{9,11},{10,... | collective-permute-start | bytes 491528 | tf_op jit(solution)/shard_map/ppermute | solution.py:171
  236.2 11.4 %collective-permute-start.38 = (bf16[128,768]{1,0:T(8,128)(2,1)S(1)}, bf16[128,768]{1,0:T(8,128)(2,1)S(1)}, u32[]{:S(2)}, u32[]{:S(2)}) collective-permute-start(bf16[128,768]{1,0:T(8,128)(2,1)S(1)} %collective-permute-done.34.refs_5_), channel_id=1, source_target_pairs={{0,1},{1,0},{2,3},{3,2},{4,5},{5,4},{6,7},{7,6},{8,9},{9,8},{10,11... | collective-permute-start | bytes 589832 | tf_op jit(solution)/shard_map/ppermute | solution.py:176
  243.5 4.1 %collective-permute-start.39 = (bf16[128,768]{1,0:T(8,128)(2,1)S(1)}, bf16[128,768]{1,0:T(8,128)(2,1)S(1)}, u32[]{:S(2)}, u32[]{:S(2)}) collective-permute-start(bf16[128,768]{1,0:T(8,128)(2,1)S(1)} %collective-permute-done.35.refs_6_), channel_id=1, source_target_pairs={{0,1},{1,0},{2,3},{3,2},{4,5},{5,4},{6,7},{7,6},{8,9},{9,8},{10,11... | collective-permute-start | bytes 589832 | tf_op jit(solution)/shard_map/ppermute | solution.py:176
  243.5 4.6 %collective-permute-start.40 = (bf16[128,768]{1,0:T(8,128)(2,1)S(1)}, bf16[128,768]{1,0:T(8,128)(2,1)S(1)}, u32[]{:S(2)}, u32[]{:S(2)}) collective-permute-start(bf16[128,768]{1,0:T(8,128)(2,1)S(1)} %collective-permute-done.36.refs_7_), channel_id=1, source_target_pairs={{0,1},{1,0},{2,3},{3,2},{4,5},{5,4},{6,7},{7,6},{8,9},{9,8},{10,11... | collective-permute-start | bytes 589832 | tf_op jit(solution)/shard_map/ppermute | solution.py:176
  244.1 15.1 %collective-permute-start.54 = (bf16[320,256]{1,0:T(8,128)(2,1)S(1)}, bf16[320,256]{1,0:T(8,128)(2,1)S(1)}, u32[]{:S(2)}, u32[]{:S(2)}) collective-permute-start(bf16[320,256]{1,0:T(8,128)(2,1)S(1)} %get-tuple-element.81), channel_id=1, source_target_pairs={{0,4},{1,5},{2,6},{3,7},{4,0},{5,1},{6,2},{7,3},{8,12},{9,13},{10,... | collective-permute-start | bytes 491528 | tf_op jit(solution)/shard_map/ppermute | solution.py:171
  244.5 14.7 %collective-permute-start.55 = (bf16[320,256]{1,0:T(8,128)(2,1)S(1)}, bf16[320,256]{1,0:T(8,128)(2,1)S(1)}, u32[]{:S(2)}, u32[]{:S(2)}) collective-permute-start(bf16[320,256]{1,0:T(8,128)(2,1)S(1)} %get-tuple-element.82), channel_id=1, source_target_pairs={{0,6},{1,7},{2,4},{3,5},{4,2},{5,3},{6,0},{7,1},{8,14},{9,15},{10,... | collective-permute-start | bytes 491528 | tf_op jit(solution)/shard_map/ppermute | solution.py:171
  247.6 11.5 %collective-permute-start.59 = (bf16[128,768]{1,0:T(8,128)(2,1)S(1)}, bf16[128,768]{1,0:T(8,128)(2,1)S(1)}, u32[]{:S(2)}, u32[]{:S(2)}) collective-permute-start(bf16[128,768]{1,0:T(8,128)(2,1)S(1)} %collective-permute-done.56.refs_6_), channel_id=1, source_target_pairs={{0,1},{1,0},{2,3},{3,2},{4,5},{5,4},{6,7},{7,6},{8,9},{9,8},{10,11... | collective-permute-start | bytes 589832 | tf_op jit(solution)/shard_map/ppermute | solution.py:176
  247.6 11.5 %collective-permute-start.60 = (bf16[128,768]{1,0:T(8,128)(2,1)S(1)}, bf16[128,768]{1,0:T(8,128)(2,1)S(1)}, u32[]{:S(2)}, u32[]{:S(2)}) collective-permute-start(bf16[128,768]{1,0:T(8,128)(2,1)S(1)} %collective-permute-done.57.refs_7_), channel_id=1, source_target_pairs={{0,1},{1,0},{2,3},{3,2},{4,5},{5,4},{6,7},{7,6},{8,9},{9,8},{10,11... | collective-permute-start | bytes 589832 | tf_op jit(solution)/shard_map/ppermute | solution.py:176
  248.1 11.0 %collective-permute-start.61 = (bf16[128,768]{1,0:T(8,128)(2,1)S(1)}, bf16[128,768]{1,0:T(8,128)(2,1)S(1)}, u32[]{:S(2)}, u32[]{:S(2)}) collective-permute-start(bf16[128,768]{1,0:T(8,128)(2,1)S(1)} %collective-permute-done.58.refs_8_), channel_id=1, source_target_pairs={{0,1},{1,0},{2,3},{3,2},{4,5},{5,4},{6,7},{7,6},{8,9},{9,8},{10,11... | collective-permute-start | bytes 589832 | tf_op jit(solution)/shard_map/ppermute | solution.py:176
  (19 other events, 126.7 us)

commit v3 on v2

--- a/solution.py
+++ b/solution.py
@@ -180,18 +180,16 @@
     return lax.ppermute(value, "section", pairs)
 
 
-def gather_cores(core, middle):
+def gather_cores(core):
     beside = on_chips(core, [(0, 1), (1, 0), (2, 3), (3, 2)])
     across = on_chips(core, [(1, 2), (2, 1)])
     far_across = on_chips(beside, [(1, 2), (2, 1)])
     outward = on_chips(across, [(1, 0), (2, 3)])
     far_outward = on_chips(far_across, [(1, 0), (2, 3)])
-    second = jnp.where(middle, across, outward)
-    held = [core, beside, second]
-    thirds = [far_across, far_outward]
-    return held + [swap_cores(piece) for piece in held], thirds + [
-        swap_cores(piece) for piece in thirds
-    ]
+    held, swapped = [core, beside], [swap_cores(piece) for piece in (core, beside)]
+    near = [(across, outward), (far_across, far_outward)]
+    far = [tuple(swap_cores(piece) for piece in pair) for pair in near]
+    return [piece for both in zip(held + near, swapped + far) for piece in both]
 
 
 def row_marks(route, weight, chip, core, middle):
@@ -241,13 +239,14 @@
     return (pair[0].astype(jnp.float32) + pair[1].astype(jnp.float32)).astype(jnp.bfloat16)
 
 
-def routed_product(rows, marks, core_refs, transposed, copies=None):
+def routed_product(rows, marks, start, core_refs, transposed, copies=None):
     dims = (((1,), (1 if transposed else 0,)), ((), ()))
     total = None
     for place, core_ref in enumerate(core_refs):
         if copies is not None:
             copies[place].wait()
-        chosen = jnp.where(marks[:, place : place + 1] > 0.5, rows, jnp.zeros_like(rows))
+        mark = marks[:, start + place : start + place + 1]
+        chosen = jnp.where(mark > 0.5, rows, jnp.zeros_like(rows))
         term = lax.dot_general(
             chosen, core_ref[...], dims, preferred_element_type=jnp.float32
         )
@@ -259,34 +258,49 @@
     count = len(core_refs)
     grad_hidden = (marks[:, count : count + 1] * score).astype(jnp.bfloat16)
     grad_pre = (grad_hidden.astype(jnp.float32) * slope).astype(jnp.bfloat16)
-    grad_proj = routed_product(grad_pre, marks, core_refs, True)
+    grad_proj = routed_product(grad_pre, marks, 0, core_refs, True)
     return grad_pre, grad_proj.astype(jnp.bfloat16)
 
 
-def first_kernel(middle_ref, proj_ref, marks_ref, own_ref, gram_ref, *refs):
-    count = CHIPS * CORES
-    held, thirds = refs[: count - 2], refs[count - 2 : count + 2]
-    scaled_ref, slope_ref, score_ref, chain_ref = refs[count + 2 : count + 6]
-    core_refs, arrived = refs[count + 6 : -1], refs[-1]
-    middle = middle_ref[0] > 0
-    sources = paired(held, [thirds[:2], thirds[2:]])
+def fetch(middle, sources, targets, arrived):
     copies = []
-    for place, (source, core_ref) in enumerate(zip(sources, core_refs)):
+    for place, (source, target) in enumerate(zip(sources, targets)):
         choices = source if isinstance(source, tuple) else (source,)
-        moves = [pltpu.make_async_copy(ref, core_ref, arrived.at[place]) for ref in choices]
+        moves = [pltpu.make_async_copy(ref, target, arrived.at[place]) for ref in choices]
         copies.append(moves[0])
         if len(moves) == 1:
             moves[0].start()
         else:
             pl.when(middle)(moves[0].start)
             pl.when(jnp.logical_not(middle))(moves[1].start)
+    return copies
+
+
+def early_kernel(middle_ref, proj_ref, marks_ref, *refs):
+    sources = [*refs[:4], (refs[4], refs[5]), (refs[6], refs[7])]
+    part_ref, core_refs, arrived = refs[8], refs[9:-1], refs[-1]
+    copies = fetch(middle_ref[0] > 0, sources, core_refs, arrived)
+    part_ref[...] = routed_product(proj_ref[...], marks_ref[...], 0, core_refs, False, copies)
+
+
+def first_kernel(middle_ref, proj_ref, marks_ref, part_ref, *refs):
+    early = CHIPS * CORES - 2
+    held, refs = refs[:early], refs[early:]
+    sources = [(refs[0], refs[1]), (refs[2], refs[3]), refs[4], refs[5]]
+    scaled_ref, slope_ref, score_ref, chain_ref, near_ref, far_ref = refs[6:12]
+    own_ref, gram_ref, arrived = refs[12:]
+    last = [near_ref, far_ref]
+    copies = fetch(middle_ref[0] > 0, sources, [*last, own_ref, gram_ref], arrived)
+    core_refs, count = [*held, *last], early + 2
     marks = marks_ref[...]
-    pre = routed_product(proj_ref[...], marks, core_refs, False, copies)
+    pre = part_ref[...] + routed_product(proj_ref[...], marks, early, last, False, copies)
     sigmoid = 1.0 / (1.0 + jnp.exp(-pre))
     hidden = (pre * sigmoid).astype(jnp.bfloat16)
     slope = sigmoid * (1.0 + pre * (1.0 - sigmoid))
     weight = marks[:, count : count + 1]
     scaled = (weight * hidden.astype(jnp.float32)).astype(jnp.bfloat16)
+    copies[2].wait()
+    copies[3].wait()
     score = own_ref[...] + dot(scaled, gram_ref[...])
     scaled_ref[...] = scaled
     slope_ref[...] = slope
@@ -295,11 +309,6 @@
     chain_ref[...] = (scaled.astype(jnp.float32) + grad_proj.astype(jnp.float32)).astype(
         jnp.bfloat16
     )
-
-
-def paired(held, thirds):
-    own, other = [*held[:3], thirds[0]], [*held[3:], thirds[1]]
-    return [piece for pair in zip(own, other) for piece in pair]
 
 
 def turn_kernel(terms, late, marks_ref, scaled_ref, slope_ref, score_ref, *refs):
@@ -416,7 +425,7 @@
     middle = jnp.logical_or(chip == 1, chip == 2)
     tokens = inputs[0].reshape(rows, channels)
 
-    held, thirds = gather_cores(cores[0, 0], middle)
+    travelled = gather_cores(cores[0, 0])
     marks = row_marks(
         route[0].reshape(rows, 1), gate[0].reshape(rows, 1), chip, core, middle
     )
@@ -455,6 +464,7 @@
     def to_experts(parts):
         return parts[:1] + [across_chips(parts[step], step) for step in range(1, CHIPS)]
 
+    step_cross = between_layers(step_two, crossed)
     projected = dot(tokens, shared).astype(bf16)
     own_gram = gram_pair(own_half, own_half)
     proj_slots = to_slots(projected)
@@ -471,23 +481,44 @@
 
     wide = (rows, ranks)
     product_flops = 2 * rows * ranks * ranks
-    scaled, slope, score, chain, *pieces = pl.pallas_call(
+    flag = middle.astype(jnp.int32).reshape(1)
+    block = pltpu.VMEM((ranks, ranks), bf16)
+
+    def core_call(body, sources, outs, arrays, scratch, products):
+        flat = [ref for source in sources for ref in (source if type(source) is tuple else [source])]
+        return pl.pallas_call(
+            body,
+            out_shape=outs,
+            in_specs=[pl.BlockSpec(memory_space=pltpu.SMEM)]
+            + [pl.BlockSpec(memory_space=pltpu.VMEM)] * len(arrays)
+            + [pl.BlockSpec(memory_space=pl.ANY)] * len(flat),
+            out_specs=[pl.BlockSpec(memory_space=pltpu.VMEM)] * len(outs),
+            scratch_shapes=scratch + [pltpu.SemaphoreType.DMA((len(sources),))],
+            compiler_params=pltpu.CompilerParams(vmem_limit_bytes=ROOM),
+            cost_estimate=pl.CostEstimate(
+                flops=product_flops * products,
+                bytes_accessed=2 * len(sources) * ranks * ranks,
+                transcendentals=0,
+            ),
+        )(flag, *arrays, *flat)
+
+    part, *held = core_call(
+        early_kernel,
+        travelled[:-2],
+        [jax.ShapeDtypeStruct(wide, f32)] + [block] * (devices - 2),
+        [projected, marks],
+        [],
+        devices - 2,
+    )
+    scaled, slope, score, chain, *last = core_call(
         first_kernel,
-        name="first_turn",
-        out_shape=[jax.ShapeDtypeStruct(wide, kind) for kind in (bf16, f32, f32, bf16)]
-        + [pltpu.VMEM((ranks, ranks), bf16)] * devices,
-        in_specs=[pl.BlockSpec(memory_space=pltpu.SMEM)]
-        + [pl.BlockSpec(memory_space=pltpu.VMEM)] * 4
-        + [pl.BlockSpec(memory_space=pl.ANY)] * (devices + 2),
-        out_specs=[pl.BlockSpec(memory_space=pltpu.VMEM)] * (devices + 4),
-        scratch_shapes=[pltpu.SemaphoreType.DMA((devices,))],
-        compiler_params=pltpu.CompilerParams(vmem_limit_bytes=ROOM),
-        cost_estimate=pl.CostEstimate(
-            flops=product_flops * (2 * devices + 1),
-            bytes_accessed=2 * devices * ranks * ranks,
-            transcendentals=rows * ranks,
-        ),
-    )(middle.astype(jnp.int32).reshape(1), projected, marks, own_score, gram, *held, *thirds)
+        [*travelled[-2:], own_score, gram],
+        [jax.ShapeDtypeStruct(wide, kind) for kind in (bf16, f32, f32, bf16)] + [block] * 2,
+        [projected, marks, part, *held],
+        [pltpu.VMEM(wide, f32), pltpu.VMEM((ranks, ranks), bf16)],
+        devices + 3,
+    )
+    pieces = [*held, *last]
 
     def turn(score, late, terms):
         arrays = [array for pair in terms for array in pair]
@@ -504,14 +535,17 @@
 
     chain_first = chain
     first_down = between_layers(chain, [(3, 2)])
-    step_cross = between_layers(after(step_two, chain), crossed)
     first_two = between_layers(chain, [(3, 1)])
-    proj_slots = to_experts([after(part, chain) for part in proj_slots])
+    scaled_rows = [scaled] + [across_chips(after(scaled, chain), step) for step in range(1, CHIPS)]
+    token_blocks = token_blocks[:1] + [
+        across_chips(after(token_blocks[step], chain), step) for step in range(1, CHIPS)
+    ]
     score, _, _, chain = turn(score, [down_score], [(first_down, down_gram)])
 
     second_cross = between_layers(chain, [(2, 1)])
     second_two = between_layers(chain, [(2, 0)])
     first_three = between_layers(after(chain_first, chain), [(3, 0)])
+    proj_slots = to_experts([after(part, chain) for part in proj_slots])
     half_cross = after(half_cross, chain)
     step_cross = after(step_cross, chain)
     cross_pair = gram_pair(half_cross, own_half)
@@ -523,10 +557,6 @@
     )
 
     third_down = between_layers(chain, [(1, 0)])
-    scaled_rows = [scaled] + [across_chips(after(scaled, chain), step) for step in range(1, CHIPS)]
-    token_blocks = token_blocks[:1] + [
-        across_chips(after(token_blocks[step], chain), step) for step in range(1, CHIPS)
-    ]
     steps_total = difference.astype(f32) + step_down.astype(f32)
     steps_total = (steps_total + after(late_steps, chain).astype(f32)).astype(bf16)
     score, grad_pre, grad_proj, _ = turn(
@@ -537,8 +567,6 @@
         return values, swap_cores(values)
 
     proj_rows = gather_rows(grad_proj)
-    grad_slots = to_slots(grad_pre)
-    grad_slots = to_experts(grad_slots)
     scaled_pair = with_swap(after(scaled, grad_proj))
     two_pair = with_swap(first_two + after(second_two, grad_proj))
     cross_pair = with_swap(second_cross + after(first_three, grad_proj))
@@ -552,10 +580,13 @@
             (half_down, *down_pair),
         ],
     )
-    scaled_rows = [after(rows, mixed_blocks[0]) for rows in scaled_rows]
+    mixed_first = mixed_blocks[0]
+    scaled_rows = [after(rows, mixed_first) for rows in scaled_rows]
     mixed_blocks = list(mixed_blocks[:1]) + [
         across_chips(mixed_blocks[step], step) for step in range(1, CHIPS)
     ]
+    grad_slots = to_slots(after(grad_pre, mixed_first))
+    grad_slots = to_experts(grad_slots)
     scaled_rows = scaled_rows + [scaled_pair[1]] + [swap_cores(rows) for rows in scaled_rows[1:]]
     share = factor_rows(None, token_blocks, proj_rows)
     core_total = dot_first(jnp.concatenate(proj_slots), jnp.concatenate(grad_slots)).astype(bf16)

time: 262 us -> 275 us (1.050)
  starting transfers between devices: 57 us -> 70.4 us
  waiting for transfers between devices: 143 us -> 138 us
  matrix products: 15 us -> 18.1 us
    ppermute x23, waiting for transfers between devices: 94.7 us -> 60.5 us  [on_chips(): return lax.ppermute(value, 'expert', perm)]
    ppermute x12, waiting for transfers between devices: 47.9 us -> 75 us  [between_layers(): return lax.ppermute(value, 'section', pairs)]
    ppermute x23, starting transfers between devices: 31.6 us -> 41.7 us  [on_chips(): return lax.ppermute(value, 'expert', perm)]
    dot_general x8, matrix products: 13.8 us -> 16.9 us  [dot_first(): lax.dot_general(left, right, (((0,), (0,)), ((), ())), preferred_element_...]
    ppermute x27 -> x28, starting transfers between devices: 5.24 us -> 6.53 us  [swap_cores(): lax.ppermute(value, 'expert', [(index, index ^ 1) for index in range(coun...]
    pallas_call x1 -> x2, Pallas kernels: 8.19 us -> 8.1 us  [core_call(): pl.pallas_call(body, out_shape=outs, in_specs=[pl.BlockSpec(memory_space=...]
  transfers between devices with their start and end apart: 62 -> 63, of which waited for: 19 -> 17; matrix products, arithmetic and copies ran while one was open for 11% -> 12% of each run, Pallas kernels for 9% -> 9%
where the time goes in v3:
time: 275 us; the launch traced here: 274 us
  waiting for transfers between devices  138 us (50%)
  starting transfers between devices  70.4 us (26%)
  Pallas kernels  26.9 us (10%)
  matrix products  18.1 us (7%)
  local copies, waits for them, and re-layouts  11.7 us (4%)
  other arithmetic  7.79 us (3%)
    ppermute x12, waiting for transfers between devices, between_layers(): return lax.ppermute(value, 'section', pairs)  75 us
    ppermute x23, waiting for transfers between devices, on_chips(): return lax.ppermute(value, 'expert', perm)  60.5 us
    ppermute x23, starting transfers between devices, on_chips(): return lax.ppermute(value, 'expert', perm)  41.7 us
    ppermute x12, starting transfers between devices, between_layers(): return lax.ppermute(value, 'section', pairs)  22.3 us
    dot_general x8, matrix products, dot_first(): lax.dot_general(left, right, (((0,), (0,)), ((), ())), preferred_element_...  16.9 us
    pallas_call x3, Pallas kernels, call_rows(): pl.pallas_call(body, out_shape=[jax.ShapeDtypeStruct(shape, kind) for sha...  12.2 us
    pallas_call x2, Pallas kernels, core_call(): pl.pallas_call(body, out_shape=outs, in_specs=[pl.BlockSpec(memory_space=...  8.1 us
    ppermute x28, starting transfers between devices, swap_cores(): lax.ppermute(value, 'expert', [(index, index ^ 1) for index in range(coun...  6.53 us
  transfers between devices with their start and end apart: 63, of which 17 were waited for; matrix products, arithmetic and copies ran while one was open for 12% of the time, Pallas kernels for 9%

profile of v3, /device:TPU:0, one launch (start us, length us, event | category | flops | bytes accessed | tf_op | source)
XLA Modules:
  0.0 274.1 jit_solution(9652943647287294621)
XLA Ops:
  1.2 2.6 collective-permute-start.2
  3.8 1.7 collective-permute-start.4
  5.5 1.4 copy.11
  6.9 1.7 copy.12
  13.0 1.6 dynamic-slice_bitcast_fusion.3
  15.5 1.0 pad_maximum_fusion.2
  16.6 1.3 collective-permute-start.18
  17.9 1.7 fusion.23
  19.6 0.9 copy-done.10
  20.9 2.8 %convolution_convert_fusion.4 = bf16[768,768]{1,0:T(8,128)(2,1)} fusion(bf16[1280,768]{1,0:T(8,128)(2,1)S(1)} %pad_maximum_fusion.refs_1_), kind=kOutput, calls=%fused_computation.11 | convolution fusion | flops 1510539264 | bytes 3145728 | tf_op jit(solution)/shard_map/dot_general | solution.py:160
  23.9 11.6 %collective-permute-done.18 = bf16[1280,256]{1,0:T(8,128)(2,1)S(1)} collective-permute-done((bf16[1280,256]{1,0:T(8,128)(2,1)S(1)}, bf16[1280,256]{1,0:T(8,128)(2,1)S(1)}, u32[]{:S(2)}, u32[]{:S(2)}) %collective-permute-start.18) | collective-permute-done | bytes 655392 | tf_op jit(solution)/shard_map/ppermute | solution.py:180
  35.5 1.3 collective-permute-start.21
  36.8 1.8 collective-permute-start.8
  38.6 1.3 collective-permute-start.27
  39.9 1.3 collective-permute-start.5
  41.2 1.8 fusion.29
  43.0 0.9 copy-done.3
  44.8 1.3 constant_dynamic-slice_fusion.15
  46.9 1.3 collective-permute-start.9
  48.3 33.4 %collective-permute-done.21.refs_10_ = bf16[1280,768]{1,0:T(8,128)(2,1)} collective-permute-done((bf16[1280,768]{1,0:T(8,128)(2,1)S(1)}, bf16[1280,768]{1,0:T(8,128)(2,1)}, u32[]{:S(2)}, u32[]{:S(2)}) %collective-permute-start.21) | collective-permute-done | bytes 1966112 | tf_op jit(solution)/shard_map/ppermute | solution.py:180
  82.4 2.4 collective-permute-done.27.refs_4_
  84.8 5.5 %collective-permute-start.30 = (bf16[1280,768]{1,0:T(8,128)(2,1)}, bf16[1280,768]{1,0:T(8,128)(2,1)S(1)}, u32[]{:S(2)}, u32[]{:S(2)}) collective-permute-start(bf16[1280,768]{1,0:T(8,128)(2,1)} %collective-permute-done.27.refs_4_), channel_id=1, source_target_pairs={{0,8},{8,0},{1,9},{9,1},{2,10},{10,2},{3,11},{11,3},{4,12},{12,4},... | collective-permute-start | bytes 5898248 | tf_op jit(solution)/shard_map/ppermute | solution.py:180
  90.4 6.0 %collective-permute-done.9.refs_7_ = bf16[768,768]{1,0:T(8,128)(2,1)S(1)} collective-permute-done((bf16[768,768]{1,0:T(8,128)(2,1)}, bf16[768,768]{1,0:T(8,128)(2,1)S(1)}, u32[]{:S(2)}, u32[]{:S(2)}) %collective-permute-start.9) | collective-permute-done | bytes 1179680 | tf_op jit(solution)/shard_map/ppermute | solution.py:171
  96.4 3.3 %convolution_convert_fusion.3 = bf16[768,768]{1,0:T(8,128)(2,1)S(1)} fusion(bf16[1280,768]{1,0:T(8,128)(2,1)} %collective-permute-done.21.refs_10_, bf16[1280,768]{1,0:T(8,128)(2,1)S(1)} %pad_maximum_fusion.refs_1_), kind=kOutput, calls=%fused_computation.10 | convolution fusion | flops 1510539264 | bytes 5111808 | tf_op jit(solution)/shard_map/dot_general | solution.py:160
  100.3 1.9 add_convert_fusion.3.refs_11_
  102.2 1.3 collective-permute-start.23
  103.5 1.0 slice_add_fusion.1.refs_4_
  104.6 3.4 %convolution_convert_fusion.2 = bf16[768,768]{1,0:T(8,128)(2,1)S(1)} fusion(bf16[1280,768]{1,0:T(8,128)(2,1)} %collective-permute-done.27.refs_4_, bf16[1280,768]{1,0:T(8,128)(2,1)S(1)} %pad_maximum_fusion.refs_1_), kind=kOutput, calls=%fused_computation.9 | convolution fusion | flops 1510539264 | bytes 5111808 | tf_op jit(solution)/shard_map/dot_general | solution.py:160
  108.0 3.3 %shard_map.86 = (f32[128,768]{1,0:T(8,128)S(1)}, bf16[768,768]{1,0:T(8,128)(2,1)S(1)}, bf16[768,768]{1,0:T(8,128)(2,1)S(1)}, bf16[768,768]{1,0:T(8,128)(2,1)S(1)...) custom-call(s32[1]{0:T(128)} %bitcast.2.middle_ref, ...), custom_call_target="tpu_custom_call" | custom-call | flops 905969664 | bytes 7077888 | tf_op jit(solution)/shard_map/pallas_call | solution.py:489
  111.3 10.6 %collective-permute-done.23 = bf16[1280,256]{1,0:T(8,128)(2,1)S(1)} collective-permute-done((bf16[1280,256]{1,0:T(8,128)(2,1)S(1)}, bf16[1280,256]{1,0:T(8,128)(2,1)S(1)}, u32[]{:S(2)}, u32[]{:S(2)}) %collective-permute-start.23) | collective-permute-done | bytes 655392 | tf_op jit(solution)/shard_map/ppermute | solution.py:180
  121.9 5.5 %collective-permute-start.24 = (bf16[1280,256]{1,0:T(8,128)(2,1)S(1)}, bf16[1280,256]{1,0:T(8,128)(2,1)S(1)}, u32[]{:S(2)}, u32[]{:S(2)}) collective-permute-start(bf16[1280,256]{1,0:T(8,128)(2,1)S(1)} %collective-permute-done.23), channel_id=1, source_target_pairs={{0,8},{8,0},{1,9},{9,1},{2,10},{10,2},{3,11},{11,3},{4,12},{12,4},... | collective-permute-start | bytes 1966088 | tf_op jit(solution)/shard_map/ppermute | solution.py:180
  127.7 4.8 %shard_map.87 = (bf16[128,768]{1,0:T(8,128)(2,1)S(1)}, f32[128,768]{1,0:T(8,128)S(1)}, f32[128,768]{1,0:T(8,128)S(1)}, bf16[128,768]{1,0:T(8,128)(2,1)S(1)}, bf1...) custom-call(s32[1]{0:T(128)} %bitcast.2.middle_ref, bf16[128,768]{1,0:T(8,128)(2,1)S(1)} %fusion.2.proj_ref, ...), custom_call_target="tpu_custom_call" | custom-call | flops 1660944384 | bytes 4718592 | tf_op jit(solution)/shard_map/pallas_call | solution.py:489
  133.5 3.8 %shard_map.88 = (f32[128,768]{1,0:T(8,128)S(1)}, bf16[128,768]{1,0:T(8,128)(2,1)}, bf16[128,768]{1,0:T(8,128)(2,1)}, bf16[128,768]{1,0:T(8,128)(2,1)S(1)}) custom-call(f32[128,16]{1,0:T(8,128)S(1)} %convert_select_fusion.marks_ref.refs_0_, bf16[128,768]{1,0:T(8,128)(2,1)S(1)} %get-tuple-element.86.refs_1_.refs_2_.refs_5_, ...), custom_call_target="tpu_custom_call" | custom-call | flops 1358954496 | bytes 12197888 | tf_op jit(solution)/shard_map/pallas_call | solution.py:333
  137.3 1.7 convolution_convert_fusion.1
  139.0 6.9 %collective-permute-done.24 = bf16[1280,256]{1,0:T(8,128)(2,1)S(1)} collective-permute-done((bf16[1280,256]{1,0:T(8,128)(2,1)S(1)}, bf16[1280,256]{1,0:T(8,128)(2,1)S(1)}, u32[]{:S(2)}, u32[]{:S(2)}) %collective-permute-start.24) | collective-permute-done | bytes 655392 | tf_op jit(solution)/shard_map/ppermute | solution.py:180
  149.1 1.3 collective-permute-start.32
  150.4 1.5 collective-permute-start.33
  152.3 4.0 %shard_map.89 = (f32[128,768]{1,0:T(8,128)S(1)}, bf16[128,768]{1,0:T(8,128)(2,1)}, bf16[128,768]{1,0:T(8,128)(2,1)}, bf16[128,768]{1,0:T(8,128)(2,1)S(1)}) custom-call(f32[128,16]{1,0:T(8,128)S(1)} %convert_select_fusion.marks_ref.refs_0_, bf16[128,768]{1,0:T(8,128)(2,1)S(1)} %get-tuple-element.86.refs_1_.refs_2_.refs_5_, ...), custom_call_target="tpu_custom_call" | custom-call | flops 1509949440 | bytes 13574144 | tf_op jit(solution)/shard_map/pallas_call | solution.py:333
  156.4 1.3 collective-permute-start.34
  157.7 4.0 %collective-permute-start.57 = (bf16[128,768]{1,0:T(8,128)(2,1)S(1)}, bf16[128,768]{1,0:T(8,128)(2,1)S(1)}, u32[]{:S(2)}, u32[]{:S(2)}) collective-permute-start(bf16[128,768]{1,0:T(8,128)(2,1)S(1)} %get-tuple-element.86.refs_1_.refs_2_.refs_5_), channel_id=1, source_target_pairs={{0,2},{1,3},{2,0},{3,1},{4,6},{5,7},{6,4},{7,5},{8,10},{9,11},{10,... | collective-permute-start | bytes 589832 | tf_op jit(solution)/shard_map/ppermute | solution.py:171
  161.7 2.8 %collective-permute-done.32.refs_4_ = bf16[128,768]{1,0:T(8,128)(2,1)S(1)} collective-permute-done((bf16[128,768]{1,0:T(8,128)(2,1)S(1)}, bf16[128,768]{1,0:T(8,128)(2,1)S(1)}, u32[]{:S(2)}, u32[]{:S(2)}) %collective-permute-start.32) | collective-permute-done | bytes 196640 | tf_op jit(solution)/shard_map/ppermute | solution.py:180
  164.5 7.5 %collective-permute-done.34.refs_8_ = bf16[128,768]{1,0:T(8,128)(2,1)S(1)} collective-permute-done((bf16[128,768]{1,0:T(8,128)(2,1)S(1)}, bf16[128,768]{1,0:T(8,128)(2,1)S(1)}, u32[]{:S(2)}, u32[]{:S(2)}) %collective-permute-start.34) | collective-permute-done | bytes 196640 | tf_op jit(solution)/shard_map/ppermute | solution.py:180
  172.0 4.4 %shard_map.90 = (f32[128,768]{1,0:T(8,128)}, bf16[128,768]{1,0:T(8,128)(2,1)S(1)}, bf16[128,768]{1,0:T(8,128)(2,1)S(1)}, bf16[128,768]{1,0:T(8,128)(2,1)}) custom-call(f32[128,16]{1,0:T(8,128)S(1)} %convert_select_fusion.marks_ref.refs_0_, bf16[128,768]{1,0:T(8,128)(2,1)S(1)} %get-tuple-element.86.refs_1_.refs_2_.refs_5_, ...), custom_call_target="tpu_custom_call" | custom-call | flops 1660944384 | bytes 14557184 | tf_op jit(solution)/shard_map/pallas_call | solution.py:333
  177.7 1.2 add_convert_fusion.4.refs_0_
  179.0 4.9 %collective-permute-start.58 = (bf16[128,768]{1,0:T(8,128)(2,1)S(1)}, bf16[128,768]{1,0:T(8,128)(2,1)S(1)}, u32[]{:S(2)}, u32[]{:S(2)}) collective-permute-start(bf16[128,768]{1,0:T(8,128)(2,1)S(1)} %get-tuple-element.86.refs_1_.refs_2_.refs_5_), channel_id=1, source_target_pairs={{0,4},{1,5},{2,6},{3,7},{4,0},{5,1},{6,2},{7,3},{8,12},{9,13},{10,... | collective-permute-start | bytes 589832 | tf_op jit(solution)/shard_map/ppermute | solution.py:171
  183.9 1.5 collective-permute-start.59
  185.3 2.9 %collective-permute-start.16 = (bf16[320,256]{1,0:T(8,128)(2,1)S(1)}, bf16[320,256]{1,0:T(8,128)(2,1)S(1)}, u32[]{:S(2)}, u32[]{:S(2)}) collective-permute-start(bf16[320,256]{1,0:T(8,128)(2,1)S(1)} %get-tuple-element.55), channel_id=1, source_target_pairs={{0,4},{1,5},{2,6},{3,7},{4,0},{5,1},{6,2},{7,3},{8,12},{9,13},{10,... | collective-permute-start | bytes 491528 | tf_op jit(solution)/shard_map/ppermute | solution.py:171
  188.2 4.4 %spread.1 = (bf16[320,256]{1,0:T(8,128)(2,1)S(1)}, bf16[320,256]{1,0:T(8,128)(2,1)S(1)}, bf16[320,256]{1,0:T(8,128)(2,1)S(1)}, bf16[320,256]{1,0:T(8,128)(2,1)S(1)}) custom-call(bf16[1280,256]{1,0:T(8,128)(2,1)S(1)} %add_convert_fusion.4.refs_0_, bf16[1280,768]{1,0:T(8,128)(2,1)S(1)} %pad_maximum_fusion.refs_1_, ...), custom_call_target="tpu_custom_call" | custom-call | flops 2013265920 | bytes 10092544 | tf_op jit(solution)/shard_map/spread/pallas_call | solution.py:362
  193.0 7.7 %collective-permute-done.58.refs_7_ = bf16[128,768]{1,0:T(8,128)(2,1)S(1)} collective-permute-done((bf16[128,768]{1,0:T(8,128)(2,1)S(1)}, bf16[128,768]{1,0:T(8,128)(2,1)S(1)}, u32[]{:S(2)}, u32[]{:S(2)}) %collective-permute-start.58) | collective-permute-done | bytes 196640 | tf_op jit(solution)/shard_map/ppermute | solution.py:171
  200.8 1.4 collective-permute-done.50
  202.2 3.9 %collective-permute-start.17 = (bf16[320,256]{1,0:T(8,128)(2,1)S(1)}, bf16[320,256]{1,0:T(8,128)(2,1)S(1)}, u32[]{:S(2)}, u32[]{:S(2)}) collective-permute-start(bf16[320,256]{1,0:T(8,128)(2,1)S(1)} %get-tuple-element.56), channel_id=1, source_target_pairs={{0,6},{1,7},{2,4},{3,5},{4,2},{5,3},{6,0},{7,1},{8,14},{9,15},{10,... | collective-permute-start | bytes 491528 | tf_op jit(solution)/shard_map/ppermute | solution.py:171
  206.1 15.1 %collective-permute-done.16.refs_2_ = bf16[320,256]{1,0:T(8,128)(2,1)S(1)} collective-permute-done((bf16[320,256]{1,0:T(8,128)(2,1)S(1)}, bf16[320,256]{1,0:T(8,128)(2,1)S(1)}, u32[]{:S(2)}, u32[]{:S(2)}) %collective-permute-start.16) | collective-permute-done | bytes 163872 | tf_op jit(solution)/shard_map/ppermute | solution.py:171
  221.8 3.7 %collective-permute-done.36.refs_6_ = bf16[128,768]{1,0:T(8,128)(2,1)S(1)} collective-permute-done((bf16[128,768]{1,0:T(8,128)(2,1)S(1)}, bf16[128,768]{1,0:T(8,128)(2,1)S(1)}, u32[]{:S(2)}, u32[]{:S(2)}) %collective-permute-start.36) | collective-permute-done | bytes 196640 | tf_op jit(solution)/shard_map/ppermute | solution.py:171
  226.0 1.5 collective-permute-start.45
  227.5 9.1 %collective-permute-start.44 = (bf16[64,768]{1,0:T(8,128)(2,1)S(1)}, bf16[64,768]{1,0:T(8,128)(2,1)S(1)}, u32[]{:S(2)}, u32[]{:S(2)}) collective-permute-start(bf16[64,768]{1,0:T(8,128)(2,1)S(1)} %get-tuple-element.72), channel_id=1, source_target_pairs={{0,4},{1,5},{2,6},{3,7},{4,0},{5,1},{6,2},{7,3},{8,12},{9,13},{10,... | collective-permute-start | bytes 294920 | tf_op jit(solution)/shard_map/ppermute | solution.py:171
  236.7 2.0 collective-permute-start.54
  239.5 8.3 %collective-permute-done.51 = bf16[64,768]{1,0:T(8,128)(2,1)S(1)} collective-permute-done((bf16[64,768]{1,0:T(8,128)(2,1)S(1)}, bf16[64,768]{1,0:T(8,128)(2,1)S(1)}, u32[]{:S(2)}, u32[]{:S(2)}) %collective-permute-start.51) | collective-permute-done | bytes 98336 | tf_op jit(solution)/shard_map/ppermute | solution.py:171
  248.3 7.0 %collective-permute-done.52 = bf16[64,768]{1,0:T(8,128)(2,1)S(1)} collective-permute-done((bf16[64,768]{1,0:T(8,128)(2,1)S(1)}, bf16[64,768]{1,0:T(8,128)(2,1)S(1)}, u32[]{:S(2)}, u32[]{:S(2)}) %collective-permute-start.52) | collective-permute-done | bytes 98336 | tf_op jit(solution)/shard_map/ppermute | solution.py:171
  255.3 1.1 collective-permute-start.53
  256.4 6.3 %collective-permute-done.53 = bf16[64,768]{1,0:T(8,128)(2,1)S(1)} collective-permute-done((bf16[64,768]{1,0:T(8,128)(2,1)S(1)}, bf16[64,768]{1,0:T(8,128)(2,1)S(1)}, u32[]{:S(2)}, u32[]{:S(2)}) %collective-permute-start.53) | collective-permute-done | bytes 98336 | tf_op jit(solution)/shard_map/ppermute | solution.py:171
  262.7 1.3 collective-permute-start.56
  264.6 1.5 convolution_convert_fusion
  266.1 6.3 %collective-permute-done.55.refs_3_ = bf16[320,256]{1,0:T(8,128)(2,1)S(1)} collective-permute-done((bf16[320,256]{1,0:T(8,128)(2,1)S(1)}, bf16[320,256]{1,0:T(8,128)(2,1)S(1)}, u32[]{:S(2)}, u32[]{:S(2)}) %collective-permute-start.55) | collective-permute-done | bytes 163872 | tf_op jit(solution)/shard_map/ppermute | solution.py:171
  272.5 1.6 shard_map.92
  (179 shorter events, 19.2 us)
Async XLA Ops:
  0.6 37.9 %collective-permute-start.1 = (bf16[768,768]{1,0:T(8,128)(2,1)}, bf16[768,768]{1,0:T(8,128)(2,1)S(1)}, u32[]{:S(2)}, u32[]{:S(2)}) collective-permute-start(bf16[768,768]{1,0:T(8,128)(2,1)} %bitcast.38), channel_id=1, source_target_pairs={{0,1},{1,0},{2,3},{3,2},{4,5},{5,4},{6,7},{7,6},{8,9},{9,8},{10,11... | collective-permute-start | bytes 3538952 | tf_op jit(solution)/shard_map/ppermute | solution.py:176
  1.2 35.6 %collective-permute-start.2 = (bf16[768,768]{1,0:T(8,128)(2,1)}, bf16[768,768]{1,0:T(8,128)(2,1)}, u32[]{:S(2)}, u32[]{:S(2)}) collective-permute-start(bf16[768,768]{1,0:T(8,128)(2,1)} %bitcast.39), channel_id=1, source_target_pairs={{0,2},{1,3},{2,0},{3,1},{4,6},{5,7},{6,4},{7,5},{8,10},{9,11},{10,... | collective-permute-start | bytes 3538952 | tf_op jit(solution)/shard_map/ppermute | solution.py:171
  3.8 36.1 %collective-permute-start.4 = (bf16[768,768]{1,0:T(8,128)(2,1)}, bf16[768,768]{1,0:T(8,128)(2,1)}, u32[]{:S(2)}, u32[]{:S(2)}) collective-permute-start(bf16[768,768]{1,0:T(8,128)(2,1)} %bitcast.40), channel_id=1, source_target_pairs={{2,4},{3,5},{4,2},{5,3},{10,12},{11,13},{12,10},{13,11},{18,20},{1... | collective-permute-start | bytes 3538952 | tf_op jit(solution)/shard_map/ppermute | solution.py:171
  10.3 4.4 %collective-permute-start.12 = (bf16[1280,128]{1,0:T(8,128)(2,1)}, bf16[1280,128]{1,0:T(8,128)(2,1)}, u32[]{:S(2)}, u32[]{:S(2)}) collective-permute-start(bf16[1280,128]{1,0:T(8,128)(2,1)} %pad_maximum_fusion.4), channel_id=1, source_target_pairs={{0,1},{1,0},{2,3},{3,2},{4,5},{5,4},{6,7},{7,6},{8,9},{9,8},{10,11... | collective-permute-start | bytes 983048 | tf_op jit(solution)/shard_map/ppermute | solution.py:176
  12.8 7.7 %collective-permute-start.42 = (bf16[128,768]{1,0:T(8,128)(2,1)S(1)}, bf16[128,768]{1,0:T(8,128)(2,1)S(1)}, u32[]{:S(2)}, u32[]{:S(2)}) collective-permute-start(bf16[128,768]{1,0:T(8,128)(2,1)S(1)} %slice.133), channel_id=1, source_target_pairs={{0,1},{1,0},{2,3},{3,2},{4,5},{5,4},{6,7},{7,6},{8,9},{9,8},{10,11... | collective-permute-start | bytes 589832 | tf_op jit(solution)/shard_map/ppermute | solution.py:176
  16.6 18.9 %collective-permute-start.18 = (bf16[1280,256]{1,0:T(8,128)(2,1)S(1)}, bf16[1280,256]{1,0:T(8,128)(2,1)S(1)}, u32[]{:S(2)}, u32[]{:S(2)}) collective-permute-start(bf16[1280,256]{1,0:T(8,128)(2,1)S(1)} %pad_maximum_fusion.2), channel_id=1, source_target_pairs={{24,16},{8,0},{25,17},{9,1},{26,18},{10,2},{27,19},{11,3},{28,20},... | collective-permute-start | bytes 1966088 | tf_op jit(solution)/shard_map/ppermute | solution.py:180
  20.5 3.2 %collective-permute-start.13 = (f32[128,768]{1,0:T(8,128)S(1)}, f32[128,768]{1,0:T(8,128)S(1)}, u32[]{:S(2)}, u32[]{:S(2)}) collective-permute-start(f32[128,768]{1,0:T(8,128)S(1)} %slice.125), channel_id=1, source_target_pairs={{0,1},{1,0},{2,3},{3,2},{4,5},{5,4},{6,7},{7,6},{8,9},{9,8},{10,11... | collective-permute-start | bytes 1179656 | tf_op jit(solution)/shard_map/ppermute | solution.py:176
  23.7 21.0 %collective-permute-start.14 = (bf16[768,768]{1,0:T(8,128)(2,1)}, bf16[768,768]{1,0:T(8,128)(2,1)}, u32[]{:S(2)}, u32[]{:S(2)}) collective-permute-start(bf16[768,768]{1,0:T(8,128)(2,1)} %convolution_convert_fusion.4), channel_id=1, source_target_pairs={{0,1},{1,0},{2,3},{3,2},{4,5},{5,4},{6,7},{7,6},{8,9},{9,8},{10,11... | collective-permute-start | bytes 3538952 | tf_op jit(solution)/shard_map/ppermute | solution.py:176
  35.5 46.2 %collective-permute-start.21 = (bf16[1280,768]{1,0:T(8,128)(2,1)S(1)}, bf16[1280,768]{1,0:T(8,128)(2,1)}, u32[]{:S(2)}, u32[]{:S(2)}) collective-permute-start(bf16[1280,768]{1,0:T(8,128)(2,1)S(1)} %pad_maximum_fusion.refs_1_), channel_id=1, source_target_pairs={{24,16},{8,0},{25,17},{9,1},{26,18},{10,2},{27,19},{11,3},{28,20},... | collective-permute-start | bytes 5898248 | tf_op jit(solution)/shard_map/ppermute | solution.py:180
  36.8 10.1 %collective-permute-start.8 = (bf16[768,768]{1,0:T(8,128)(2,1)}, bf16[768,768]{1,0:T(8,128)(2,1)}, u32[]{:S(2)}, u32[]{:S(2)}) collective-permute-start(bf16[768,768]{1,0:T(8,128)(2,1)} %collective-permute-done.2.refs_2_), channel_id=1, source_target_pairs={{2,4},{3,5},{4,2},{5,3},{10,12},{11,13},{12,10},{13,11},{18,20},{1... | collective-permute-start | bytes 3538952 | tf_op jit(solution)/shard_map/ppermute | solution.py:171
  38.6 46.2 %collective-permute-start.27 = (bf16[1280,768]{1,0:T(8,128)(2,1)S(1)}, bf16[1280,768]{1,0:T(8,128)(2,1)}, u32[]{:S(2)}, u32[]{:S(2)}) collective-permute-start(bf16[1280,768]{1,0:T(8,128)(2,1)S(1)} %pad_maximum_fusion.refs_1_), channel_id=1, source_target_pairs={{24,8},{16,0},{25,9},{17,1},{26,10},{18,2},{27,11},{19,3},{28,12},... | collective-permute-start | bytes 5898248 | tf_op jit(solution)/shard_map/ppermute | solution.py:180
  39.9 41.8 %collective-permute-start.5 = (bf16[768,768]{1,0:T(8,128)(2,1)}, bf16[768,768]{1,0:T(8,128)(2,1)}, u32[]{:S(2)}, u32[]{:S(2)}) collective-permute-start(bf16[768,768]{1,0:T(8,128)(2,1)} %collective-permute-done.4.refs_4_), channel_id=1, source_target_pairs={{2,0},{3,1},{4,6},{5,7},{10,8},{11,9},{12,14},{13,15},{18,16},{19,... | collective-permute-start | bytes 3538952 | tf_op jit(solution)/shard_map/ppermute | solution.py:171
  44.7 2.1 collective-permute-start.19
  44.8 36.9 %copy-start.21 = (bf16[128,768]{1,0:T(8,128)(2,1)S(1)}, bf16[128,768]{1,0:T(8,128)(2,1)}, u32[]{:S(2)}) copy-start(bf16[128,768]{1,0:T(8,128)(2,1)} %copy-done.20) | copy-start | bytes 589828
  46.7 43.6 %collective-permute-start.3 = (bf16[768,768]{1,0:T(8,128)(2,1)}, bf16[768,768]{1,0:T(8,128)(2,1)S(1)}, u32[]{:S(2)}, u32[]{:S(2)}) collective-permute-start(bf16[768,768]{1,0:T(8,128)(2,1)} %collective-permute-done.2.refs_2_), channel_id=1, source_target_pairs={{0,1},{1,0},{2,3},{3,2},{4,5},{5,4},{6,7},{7,6},{8,9},{9,8},{10,11... | collective-permute-start | bytes 3538952 | tf_op jit(solution)/shard_map/ppermute | solution.py:176
  46.9 49.5 %collective-permute-start.9 = (bf16[768,768]{1,0:T(8,128)(2,1)}, bf16[768,768]{1,0:T(8,128)(2,1)S(1)}, u32[]{:S(2)}, u32[]{:S(2)}) collective-permute-start(bf16[768,768]{1,0:T(8,128)(2,1)} %collective-permute-done.8.refs_6_), channel_id=1, source_target_pairs={{2,0},{3,1},{4,6},{5,7},{10,8},{11,9},{12,14},{13,15},{18,16},{19,... | collective-permute-start | bytes 3538952 | tf_op jit(solution)/shard_map/ppermute | solution.py:171
  81.7 18.0 %collective-permute-start.6 = (bf16[768,768]{1,0:T(8,128)(2,1)}, bf16[768,768]{1,0:T(8,128)(2,1)S(1)}, u32[]{:S(2)}, u32[]{:S(2)}) collective-permute-start(bf16[768,768]{1,0:T(8,128)(2,1)} %collective-permute-done.4.refs_4_), channel_id=1, source_target_pairs={{0,1},{1,0},{2,3},{3,2},{4,5},{5,4},{6,7},{7,6},{8,9},{9,8},{10,11... | collective-permute-start | bytes 3538952 | tf_op jit(solution)/shard_map/ppermute | solution.py:176
  81.7 20.5 %collective-permute-start.7 = (bf16[768,768]{1,0:T(8,128)(2,1)}, bf16[768,768]{1,0:T(8,128)(2,1)S(1)}, u32[]{:S(2)}, u32[]{:S(2)}) collective-permute-start(bf16[768,768]{1,0:T(8,128)(2,1)} %collective-permute-done.5.refs_5_), channel_id=1, source_target_pairs={{0,1},{1,0},{2,3},{3,2},{4,5},{5,4},{6,7},{7,6},{8,9},{9,8},{10,11... | collective-permute-start | bytes 3538952 | tf_op jit(solution)/shard_map/ppermute | solution.py:176
  84.8 52.5 %collective-permute-start.30 = (bf16[1280,768]{1,0:T(8,128)(2,1)}, bf16[1280,768]{1,0:T(8,128)(2,1)S(1)}, u32[]{:S(2)}, u32[]{:S(2)}) collective-permute-start(bf16[1280,768]{1,0:T(8,128)(2,1)} %collective-permute-done.27.refs_4_), channel_id=1, source_target_pairs={{0,8},{8,0},{1,9},{9,1},{2,10},{10,2},{3,11},{11,3},{4,12},{12,4},... | collective-permute-start | bytes 5898248 | tf_op jit(solution)/shard_map/ppermute | solution.py:180
  90.3 31.5 %collective-permute-start.10 = (bf16[768,768]{1,0:T(8,128)(2,1)}, bf16[768,768]{1,0:T(8,128)(2,1)S(1)}, u32[]{:S(2)}, u32[]{:S(2)}) collective-permute-start(bf16[768,768]{1,0:T(8,128)(2,1)} %collective-permute-done.8.refs_6_), channel_id=1, source_target_pairs={{0,1},{1,0},{2,3},{3,2},{4,5},{5,4},{6,7},{7,6},{8,9},{9,8},{10,11... | collective-permute-start | bytes 3538952 | tf_op jit(solution)/shard_map/ppermute | solution.py:176
  96.4 31.0 %collective-permute-start.11 = (bf16[768,768]{1,0:T(8,128)(2,1)S(1)}, bf16[768,768]{1,0:T(8,128)(2,1)S(1)}, u32[]{:S(2)}, u32[]{:S(2)}) collective-permute-start(bf16[768,768]{1,0:T(8,128)(2,1)S(1)} %collective-permute-done.9.refs_7_), channel_id=1, source_target_pairs={{0,1},{1,0},{2,3},{3,2},{4,5},{5,4},{6,7},{7,6},{8,9},{9,8},{10,11... | collective-permute-start | bytes 3538952 | tf_op jit(solution)/shard_map/ppermute | solution.py:176
  99.7 32.8 %collective-permute-start.22 = (bf16[768,768]{1,0:T(8,128)(2,1)S(1)}, bf16[768,768]{1,0:T(8,128)(2,1)S(1)}, u32[]{:S(2)}, u32[]{:S(2)}) collective-permute-start(bf16[768,768]{1,0:T(8,128)(2,1)S(1)} %convolution_convert_fusion.3), channel_id=1, source_target_pairs={{0,1},{1,0},{2,3},{3,2},{4,5},{5,4},{6,7},{7,6},{8,9},{9,8},{10,11... | collective-permute-start | bytes 3538952 | tf_op jit(solution)/shard_map/ppermute | solution.py:176
  102.2 19.6 %collective-permute-start.23 = (bf16[1280,256]{1,0:T(8,128)(2,1)S(1)}, bf16[1280,256]{1,0:T(8,128)(2,1)S(1)}, u32[]{:S(2)}, u32[]{:S(2)}) collective-permute-start(bf16[1280,256]{1,0:T(8,128)(2,1)S(1)} %copy-done.17), channel_id=1, source_target_pairs={{24,8},{16,0},{25,9},{17,1},{26,10},{18,2},{27,11},{19,3},{28,12},... | collective-permute-start | bytes 1966088 | tf_op jit(solution)/shard_map/ppermute | solution.py:180
  121.9 25.5 %collective-permute-start = (bf16[1280,128]{1,0:T(8,128)(2,1)S(1)}, bf16[1280,128]{1,0:T(8,128)(2,1)S(1)}, u32[]{:S(2)}, u32[]{:S(2)}) collective-permute-start(bf16[1280,128]{1,0:T(8,128)(2,1)S(1)} %pad_maximum_fusion.3), channel_id=1, source_target_pairs={{0,1},{1,0},{2,3},{3,2},{4,5},{5,4},{6,7},{7,6},{8,9},{9,8},{10,11... | collective-permute-start | bytes 983048 | tf_op jit(solution)/shard_map/ppermute | solution.py:176
  121.9 24.0 %collective-permute-start.24 = (bf16[1280,256]{1,0:T(8,128)(2,1)S(1)}, bf16[1280,256]{1,0:T(8,128)(2,1)S(1)}, u32[]{:S(2)}, u32[]{:S(2)}) collective-permute-start(bf16[1280,256]{1,0:T(8,128)(2,1)S(1)} %collective-permute-done.23), channel_id=1, source_target_pairs={{0,8},{8,0},{1,9},{9,1},{2,10},{10,2},{3,11},{11,3},{4,12},{12,4},... | collective-permute-start | bytes 1966088 | tf_op jit(solution)/shard_map/ppermute | solution.py:180
  127.4 20.1 %collective-permute-start.28 = (bf16[768,768]{1,0:T(8,128)(2,1)S(1)}, bf16[768,768]{1,0:T(8,128)(2,1)S(1)}, u32[]{:S(2)}, u32[]{:S(2)}) collective-permute-start(bf16[768,768]{1,0:T(8,128)(2,1)S(1)} %convolution_convert_fusion.2), channel_id=1, source_target_pairs={{0,1},{1,0},{2,3},{3,2},{4,5},{5,4},{6,7},{7,6},{8,9},{9,8},{10,11... | collective-permute-start | bytes 3538952 | tf_op jit(solution)/shard_map/ppermute | solution.py:176
  132.5 1.0 collective-permute-start.20
  145.9 6.1 %collective-permute-start.31 = (bf16[768,768]{1,0:T(8,128)(2,1)S(1)}, bf16[768,768]{1,0:T(8,128)(2,1)S(1)}, u32[]{:S(2)}, u32[]{:S(2)}) collective-permute-start(bf16[768,768]{1,0:T(8,128)(2,1)S(1)} %convolution_convert_fusion.1), channel_id=1, source_target_pairs={{0,1},{1,0},{2,3},{3,2},{4,5},{5,4},{6,7},{7,6},{8,9},{9,8},{10,11... | collective-permute-start | bytes 3538952 | tf_op jit(solution)/shard_map/ppermute | solution.py:176
  146.8 3.6 %collective-permute-start.25 = (f32[128,768]{1,0:T(8,128)S(1)}, f32[128,768]{1,0:T(8,128)S(1)}, u32[]{:S(2)}, u32[]{:S(2)}) collective-permute-start(f32[128,768]{1,0:T(8,128)S(1)} %slice.131), channel_id=1, source_target_pairs={{0,1},{1,0},{2,3},{3,2},{4,5},{5,4},{6,7},{7,6},{8,9},{9,8},{10,11... | collective-permute-start | bytes 1179656 | tf_op jit(solution)/shard_map/ppermute | solution.py:176
  147.8 4.6 %collective-permute-start.26 = (bf16[128,768]{1,0:T(8,128)(2,1)S(1)}, bf16[128,768]{1,0:T(8,128)(2,1)S(1)}, u32[]{:S(2)}, u32[]{:S(2)}) collective-permute-start(bf16[128,768]{1,0:T(8,128)(2,1)S(1)} %get-tuple-element.67), channel_id=1, source_target_pairs={{24,8},{25,9},{26,10},{27,11},{28,12},{29,13},{30,14},{31,15}} | collective-permute-start | bytes 589832 | tf_op jit(solution)/shard_map/ppermute | solution.py:180
  148.4 3.9 %collective-permute-start.29 = (bf16[128,768]{1,0:T(8,128)(2,1)S(1)}, bf16[128,768]{1,0:T(8,128)(2,1)S(1)}, u32[]{:S(2)}, u32[]{:S(2)}) collective-permute-start(bf16[128,768]{1,0:T(8,128)(2,1)S(1)} %get-tuple-element.63), channel_id=1, source_target_pairs={{16,8},{17,9},{18,10},{19,11},{20,12},{21,13},{22,14},{23,15}} | collective-permute-start | bytes 589832 | tf_op jit(solution)/shard_map/ppermute | solution.py:180
  149.1 15.4 %collective-permute-start.32 = (bf16[128,768]{1,0:T(8,128)(2,1)S(1)}, bf16[128,768]{1,0:T(8,128)(2,1)S(1)}, u32[]{:S(2)}, u32[]{:S(2)}) collective-permute-start(bf16[128,768]{1,0:T(8,128)(2,1)S(1)} %get-tuple-element.63), channel_id=1, source_target_pairs={{16,0},{17,1},{18,2},{19,3},{20,4},{21,5},{22,6},{23,7}} | collective-permute-start | bytes 589832 | tf_op jit(solution)/shard_map/ppermute | solution.py:180
  150.4 14.1 %collective-permute-start.33 = (bf16[128,768]{1,0:T(8,128)(2,1)S(1)}, bf16[128,768]{1,0:T(8,128)(2,1)S(1)}, u32[]{:S(2)}, u32[]{:S(2)}) collective-permute-start(bf16[128,768]{1,0:T(8,128)(2,1)S(1)} %get-tuple-element.67), channel_id=1, source_target_pairs={{24,0},{25,1},{26,2},{27,3},{28,4},{29,5},{30,6},{31,7}} | collective-permute-start | bytes 589832 | tf_op jit(solution)/shard_map/ppermute | solution.py:180
  156.4 15.6 %collective-permute-start.34 = (bf16[128,768]{1,0:T(8,128)(2,1)S(1)}, bf16[128,768]{1,0:T(8,128)(2,1)S(1)}, u32[]{:S(2)}, u32[]{:S(2)}) collective-permute-start(bf16[128,768]{1,0:T(8,128)(2,1)S(1)} %get-tuple-element.68), channel_id=1, source_target_pairs={{8,0},{9,1},{10,2},{11,3},{12,4},{13,5},{14,6},{15,7}} | collective-permute-start | bytes 589832 | tf_op jit(solution)/shard_map/ppermute | solution.py:180
  157.7 35.2 %collective-permute-start.57 = (bf16[128,768]{1,0:T(8,128)(2,1)S(1)}, bf16[128,768]{1,0:T(8,128)(2,1)S(1)}, u32[]{:S(2)}, u32[]{:S(2)}) collective-permute-start(bf16[128,768]{1,0:T(8,128)(2,1)S(1)} %get-tuple-element.86.refs_1_.refs_2_.refs_5_), channel_id=1, source_target_pairs={{0,2},{1,3},{2,0},{3,1},{4,6},{5,7},{6,4},{7,5},{8,10},{9,11},{10,... | collective-permute-start | bytes 589832 | tf_op jit(solution)/shard_map/ppermute | solution.py:171
  176.3 2.6 collective-permute-start.46
  176.4 7.4 %collective-permute-start.47 = (bf16[128,768]{1,0:T(8,128)(2,1)S(1)}, bf16[128,768]{1,0:T(8,128)(2,1)S(1)}, u32[]{:S(2)}, u32[]{:S(2)}) collective-permute-start(bf16[128,768]{1,0:T(8,128)(2,1)S(1)} %add.229.refs_5_), channel_id=1, source_target_pairs={{0,1},{1,0},{2,3},{3,2},{4,5},{5,4},{6,7},{7,6},{8,9},{9,8},{10,11... | collective-permute-start | bytes 589832 | tf_op jit(solution)/shard_map/ppermute | solution.py:176
  177.0 8.3 %collective-permute-start.48 = (bf16[128,768]{1,0:T(8,128)(2,1)S(1)}, bf16[128,768]{1,0:T(8,128)(2,1)S(1)}, u32[]{:S(2)}, u32[]{:S(2)}) collective-permute-start(bf16[128,768]{1,0:T(8,128)(2,1)S(1)} %add.230.refs_8_), channel_id=1, source_target_pairs={{0,1},{1,0},{2,3},{3,2},{4,5},{5,4},{6,7},{7,6},{8,9},{9,8},{10,11... | collective-permute-start | bytes 589832 | tf_op jit(solution)/shard_map/ppermute | solution.py:176
  177.2 8.2 %collective-permute-start.49 = (bf16[128,768]{1,0:T(8,128)(2,1)S(1)}, bf16[128,768]{1,0:T(8,128)(2,1)S(1)}, u32[]{:S(2)}, u32[]{:S(2)}) collective-permute-start(bf16[128,768]{1,0:T(8,128)(2,1)S(1)} %add.231.refs_11_), channel_id=1, source_target_pairs={{0,1},{1,0},{2,3},{3,2},{4,5},{5,4},{6,7},{7,6},{8,9},{9,8},{10,11... | collective-permute-start | bytes 589832 | tf_op jit(solution)/shard_map/ppermute | solution.py:176
  179.0 21.8 %collective-permute-start.58 = (bf16[128,768]{1,0:T(8,128)(2,1)S(1)}, bf16[128,768]{1,0:T(8,128)(2,1)S(1)}, u32[]{:S(2)}, u32[]{:S(2)}) collective-permute-start(bf16[128,768]{1,0:T(8,128)(2,1)S(1)} %get-tuple-element.86.refs_1_.refs_2_.refs_5_), channel_id=1, source_target_pairs={{0,4},{1,5},{2,6},{3,7},{4,0},{5,1},{6,2},{7,3},{8,12},{9,13},{10,... | collective-permute-start | bytes 589832 | tf_op jit(solution)/shard_map/ppermute | solution.py:171
  183.9 16.9 %collective-permute-start.59 = (bf16[128,768]{1,0:T(8,128)(2,1)S(1)}, bf16[128,768]{1,0:T(8,128)(2,1)S(1)}, u32[]{:S(2)}, u32[]{:S(2)}) collective-permute-start(bf16[128,768]{1,0:T(8,128)(2,1)S(1)} %get-tuple-element.86.refs_1_.refs_2_.refs_5_), channel_id=1, source_target_pairs={{0,6},{1,7},{2,4},{3,5},{4,2},{5,3},{6,0},{7,1},{8,14},{9,15},{10,... | collective-permute-start | bytes 589832 | tf_op jit(solution)/shard_map/ppermute | solution.py:171
  185.3 16.9 %collective-permute-start.15 = (bf16[320,256]{1,0:T(8,128)(2,1)S(1)}, bf16[320,256]{1,0:T(8,128)(2,1)S(1)}, u32[]{:S(2)}, u32[]{:S(2)}) collective-permute-start(bf16[320,256]{1,0:T(8,128)(2,1)S(1)} %get-tuple-element.54), channel_id=1, source_target_pairs={{0,2},{1,3},{2,0},{3,1},{4,6},{5,7},{6,4},{7,5},{8,10},{9,11},{10,... | collective-permute-start | bytes 491528 | tf_op jit(solution)/shard_map/ppermute | solution.py:171
  185.3 35.9 %collective-permute-start.16 = (bf16[320,256]{1,0:T(8,128)(2,1)S(1)}, bf16[320,256]{1,0:T(8,128)(2,1)S(1)}, u32[]{:S(2)}, u32[]{:S(2)}) collective-permute-start(bf16[320,256]{1,0:T(8,128)(2,1)S(1)} %get-tuple-element.55), channel_id=1, source_target_pairs={{0,4},{1,5},{2,6},{3,7},{4,0},{5,1},{6,2},{7,3},{8,12},{9,13},{10,... | collective-permute-start | bytes 491528 | tf_op jit(solution)/shard_map/ppermute | solution.py:171
  192.9 28.4 %collective-permute-start.35 = (bf16[128,768]{1,0:T(8,128)(2,1)S(1)}, bf16[128,768]{1,0:T(8,128)(2,1)S(1)}, u32[]{:S(2)}, u32[]{:S(2)}) collective-permute-start(bf16[128,768]{1,0:T(8,128)(2,1)S(1)} %get-tuple-element.69.refs_4_), channel_id=1, source_target_pairs={{0,2},{1,3},{2,0},{3,1},{4,6},{5,7},{6,4},{7,5},{8,10},{9,11},{10,... | collective-permute-start | bytes 589832 | tf_op jit(solution)/shard_map/ppermute | solution.py:171
  200.7 24.7 %collective-permute-start.36 = (bf16[128,768]{1,0:T(8,128)(2,1)S(1)}, bf16[128,768]{1,0:T(8,128)(2,1)S(1)}, u32[]{:S(2)}, u32[]{:S(2)}) collective-permute-start(bf16[128,768]{1,0:T(8,128)(2,1)S(1)} %get-tuple-element.69.refs_4_), channel_id=1, source_target_pairs={{0,4},{1,5},{2,6},{3,7},{4,0},{5,1},{6,2},{7,3},{8,12},{9,13},{10,... | collective-permute-start | bytes 589832 | tf_op jit(solution)/shard_map/ppermute | solution.py:171
  200.7 1.4 collective-permute-start.50
  202.2 23.3 %collective-permute-start.37 = (bf16[128,768]{1,0:T(8,128)(2,1)S(1)}, bf16[128,768]{1,0:T(8,128)(2,1)S(1)}, u32[]{:S(2)}, u32[]{:S(2)}) collective-permute-start(bf16[128,768]{1,0:T(8,128)(2,1)S(1)} %get-tuple-element.69.refs_4_), channel_id=1, source_target_pairs={{0,6},{1,7},{2,4},{3,5},{4,2},{5,3},{6,0},{7,1},{8,14},{9,15},{10,... | collective-permute-start | bytes 589832 | tf_op jit(solution)/shard_map/ppermute | solution.py:171
  202.2 23.8 %collective-permute-start.17 = (bf16[320,256]{1,0:T(8,128)(2,1)S(1)}, bf16[320,256]{1,0:T(8,128)(2,1)S(1)}, u32[]{:S(2)}, u32[]{:S(2)}) collective-permute-start(bf16[320,256]{1,0:T(8,128)(2,1)S(1)} %get-tuple-element.56), channel_id=1, source_target_pairs={{0,6},{1,7},{2,4},{3,5},{4,2},{5,3},{6,0},{7,1},{8,14},{9,15},{10,... | collective-permute-start | bytes 491528 | tf_op jit(solution)/shard_map/ppermute | solution.py:171
  221.3 6.3 %collective-permute-start.38 = (bf16[128,768]{1,0:T(8,128)(2,1)S(1)}, bf16[128,768]{1,0:T(8,128)(2,1)S(1)}, u32[]{:S(2)}, u32[]{:S(2)}) collective-permute-start(bf16[128,768]{1,0:T(8,128)(2,1)S(1)} %get-tuple-element.69.refs_4_), channel_id=1, source_target_pairs={{0,1},{1,0},{2,3},{3,2},{4,5},{5,4},{6,7},{7,6},{8,9},{9,8},{10,11... | collective-permute-start | bytes 589832 | tf_op jit(solution)/shard_map/ppermute | solution.py:176
  221.3 15.4 %collective-permute-start.39 = (bf16[128,768]{1,0:T(8,128)(2,1)S(1)}, bf16[128,768]{1,0:T(8,128)(2,1)S(1)}, u32[]{:S(2)}, u32[]{:S(2)}) collective-permute-start(bf16[128,768]{1,0:T(8,128)(2,1)S(1)} %collective-permute-done.35.refs_5_), channel_id=1, source_target_pairs={{0,1},{1,0},{2,3},{3,2},{4,5},{5,4},{6,7},{7,6},{8,9},{9,8},{10,11... | collective-permute-start | bytes 589832 | tf_op jit(solution)/shard_map/ppermute | solution.py:176
  225.5 11.2 %collective-permute-start.40 = (bf16[128,768]{1,0:T(8,128)(2,1)S(1)}, bf16[128,768]{1,0:T(8,128)(2,1)S(1)}, u32[]{:S(2)}, u32[]{:S(2)}) collective-permute-start(bf16[128,768]{1,0:T(8,128)(2,1)S(1)} %collective-permute-done.36.refs_6_), channel_id=1, source_target_pairs={{0,1},{1,0},{2,3},{3,2},{4,5},{5,4},{6,7},{7,6},{8,9},{9,8},{10,11... | collective-permute-start | bytes 589832 | tf_op jit(solution)/shard_map/ppermute | solution.py:176
  225.5 13.2 %collective-permute-start.41 = (bf16[128,768]{1,0:T(8,128)(2,1)S(1)}, bf16[128,768]{1,0:T(8,128)(2,1)S(1)}, u32[]{:S(2)}, u32[]{:S(2)}) collective-permute-start(bf16[128,768]{1,0:T(8,128)(2,1)S(1)} %collective-permute-done.37.refs_7_), channel_id=1, source_target_pairs={{0,1},{1,0},{2,3},{3,2},{4,5},{5,4},{6,7},{7,6},{8,9},{9,8},{10,11... | collective-permute-start | bytes 589832 | tf_op jit(solution)/shard_map/ppermute | solution.py:176
  226.0 36.7 %collective-permute-start.45 = (bf16[64,768]{1,0:T(8,128)(2,1)S(1)}, bf16[64,768]{1,0:T(8,128)(2,1)S(1)}, u32[]{:S(2)}, u32[]{:S(2)}) collective-permute-start(bf16[64,768]{1,0:T(8,128)(2,1)S(1)} %get-tuple-element.73), channel_id=1, source_target_pairs={{0,6},{1,7},{2,4},{3,5},{4,2},{5,3},{6,0},{7,1},{8,14},{9,15},{10,... | collective-permute-start | bytes 294920 | tf_op jit(solution)/shard_map/ppermute | solution.py:171
  227.5 36.5 %collective-permute-start.44 = (bf16[64,768]{1,0:T(8,128)(2,1)S(1)}, bf16[64,768]{1,0:T(8,128)(2,1)S(1)}, u32[]{:S(2)}, u32[]{:S(2)}) collective-permute-start(bf16[64,768]{1,0:T(8,128)(2,1)S(1)} %get-tuple-element.72), channel_id=1, source_target_pairs={{0,4},{1,5},{2,6},{3,7},{4,0},{5,1},{6,2},{7,3},{8,12},{9,13},{10,... | collective-permute-start | bytes 294920 | tf_op jit(solution)/shard_map/ppermute | solution.py:171
  236.7 27.3 %collective-permute-start.43 = (bf16[64,768]{1,0:T(8,128)(2,1)S(1)}, bf16[64,768]{1,0:T(8,128)(2,1)S(1)}, u32[]{:S(2)}, u32[]{:S(2)}) collective-permute-start(bf16[64,768]{1,0:T(8,128)(2,1)S(1)} %get-tuple-element.71), channel_id=1, source_target_pairs={{0,2},{1,3},{2,0},{3,1},{4,6},{5,7},{6,4},{7,5},{8,10},{9,11},{10,... | collective-permute-start | bytes 294920 | tf_op jit(solution)/shard_map/ppermute | solution.py:171
  236.7 27.8 %collective-permute-start.54 = (bf16[320,256]{1,0:T(8,128)(2,1)S(1)}, bf16[320,256]{1,0:T(8,128)(2,1)S(1)}, u32[]{:S(2)}, u32[]{:S(2)}) collective-permute-start(bf16[320,256]{1,0:T(8,128)(2,1)S(1)} %get-tuple-element.82), channel_id=1, source_target_pairs={{0,2},{1,3},{2,0},{3,1},{4,6},{5,7},{6,4},{7,5},{8,10},{9,11},{10,... | collective-permute-start | bytes 491528 | tf_op jit(solution)/shard_map/ppermute | solution.py:171
  238.7 9.1 %collective-permute-start.51 = (bf16[64,768]{1,0:T(8,128)(2,1)S(1)}, bf16[64,768]{1,0:T(8,128)(2,1)S(1)}, u32[]{:S(2)}, u32[]{:S(2)}) collective-permute-start(bf16[64,768]{1,0:T(8,128)(2,1)S(1)} %pad_maximum_fusion.9), channel_id=1, source_target_pairs={{0,2},{1,3},{2,0},{3,1},{4,6},{5,7},{6,4},{7,5},{8,10},{9,11},{10,... | collective-permute-start | bytes 294920 | tf_op jit(solution)/shard_map/ppermute | solution.py:171
  247.8 7.5 %collective-permute-start.52 = (bf16[64,768]{1,0:T(8,128)(2,1)S(1)}, bf16[64,768]{1,0:T(8,128)(2,1)S(1)}, u32[]{:S(2)}, u32[]{:S(2)}) collective-permute-start(bf16[64,768]{1,0:T(8,128)(2,1)S(1)} %pad_maximum_fusion.10), channel_id=1, source_target_pairs={{0,4},{1,5},{2,6},{3,7},{4,0},{5,1},{6,2},{7,3},{8,12},{9,13},{10,... | collective-permute-start | bytes 294920 | tf_op jit(solution)/shard_map/ppermute | solution.py:171
  255.3 7.4 %collective-permute-start.53 = (bf16[64,768]{1,0:T(8,128)(2,1)S(1)}, bf16[64,768]{1,0:T(8,128)(2,1)S(1)}, u32[]{:S(2)}, u32[]{:S(2)}) collective-permute-start(bf16[64,768]{1,0:T(8,128)(2,1)S(1)} %pad_maximum_fusion.11), channel_id=1, source_target_pairs={{0,6},{1,7},{2,4},{3,5},{4,2},{5,3},{6,0},{7,1},{8,14},{9,15},{10,... | collective-permute-start | bytes 294920 | tf_op jit(solution)/shard_map/ppermute | solution.py:171
  262.7 9.8 %collective-permute-start.55 = (bf16[320,256]{1,0:T(8,128)(2,1)S(1)}, bf16[320,256]{1,0:T(8,128)(2,1)S(1)}, u32[]{:S(2)}, u32[]{:S(2)}) collective-permute-start(bf16[320,256]{1,0:T(8,128)(2,1)S(1)} %get-tuple-element.83), channel_id=1, source_target_pairs={{0,4},{1,5},{2,6},{3,7},{4,0},{5,1},{6,2},{7,3},{8,12},{9,13},{10,... | collective-permute-start | bytes 491528 | tf_op jit(solution)/shard_map/ppermute | solution.py:171
  262.7 9.8 %collective-permute-start.56 = (bf16[320,256]{1,0:T(8,128)(2,1)S(1)}, bf16[320,256]{1,0:T(8,128)(2,1)S(1)}, u32[]{:S(2)}, u32[]{:S(2)}) collective-permute-start(bf16[320,256]{1,0:T(8,128)(2,1)S(1)} %get-tuple-element.84), channel_id=1, source_target_pairs={{0,6},{1,7},{2,4},{3,5},{4,2},{5,3},{6,0},{7,1},{8,14},{9,15},{10,... | collective-permute-start | bytes 491528 | tf_op jit(solution)/shard_map/ppermute | solution.py:171
  264.0 8.5 %collective-permute-start.60 = (bf16[128,768]{1,0:T(8,128)(2,1)S(1)}, bf16[128,768]{1,0:T(8,128)(2,1)S(1)}, u32[]{:S(2)}, u32[]{:S(2)}) collective-permute-start(bf16[128,768]{1,0:T(8,128)(2,1)S(1)} %collective-permute-done.57.refs_6_), channel_id=1, source_target_pairs={{0,1},{1,0},{2,3},{3,2},{4,5},{5,4},{6,7},{7,6},{8,9},{9,8},{10,11... | collective-permute-start | bytes 589832 | tf_op jit(solution)/shard_map/ppermute | solution.py:176
  264.0 8.5 %collective-permute-start.61 = (bf16[128,768]{1,0:T(8,128)(2,1)S(1)}, bf16[128,768]{1,0:T(8,128)(2,1)S(1)}, u32[]{:S(2)}, u32[]{:S(2)}) collective-permute-start(bf16[128,768]{1,0:T(8,128)(2,1)S(1)} %collective-permute-done.58.refs_7_), channel_id=1, source_target_pairs={{0,1},{1,0},{2,3},{3,2},{4,5},{5,4},{6,7},{7,6},{8,9},{9,8},{10,11... | collective-permute-start | bytes 589832 | tf_op jit(solution)/shard_map/ppermute | solution.py:176
  264.5 8.0 %collective-permute-start.62 = (bf16[128,768]{1,0:T(8,128)(2,1)S(1)}, bf16[128,768]{1,0:T(8,128)(2,1)S(1)}, u32[]{:S(2)}, u32[]{:S(2)}) collective-permute-start(bf16[128,768]{1,0:T(8,128)(2,1)S(1)} %collective-permute-done.59.refs_8_), channel_id=1, source_target_pairs={{0,1},{1,0},{2,3},{3,2},{4,5},{5,4},{6,7},{7,6},{8,9},{9,8},{10,11... | collective-permute-start | bytes 589832 | tf_op jit(solution)/shard_map/ppermute | solution.py:176
  (24 other events, 132.8 us)

commit v4 on v3

--- a/solution.py
+++ b/solution.py
@@ -148,7 +148,6 @@
 CORES = 2
 CHIPS = 4
 LAYERS = 4
-WIDE_ROOM = 24 * 2**20
 ROOM = 16 * 2**20
 
 
@@ -347,14 +346,28 @@
         half_ref, near_ref, far_ref = refs[3 * term : 3 * term + 3]
         values = jnp.concatenate([near_ref[...], far_ref[...]], axis=0)
         total = total + times_transposed(half_ref[...], values)
-    count = total.shape[0] // CHIPS
+    block = total.astype(jnp.bfloat16)
     for step, out_ref in enumerate(refs[3 * terms :]):
-        out_ref[...] = total[step * count : (step + 1) * count].astype(jnp.bfloat16)
+
+        @pl.when(pl.program_id(0) == step)
+        def _():
+            out_ref[...] = block
 
 
 def spread(base, terms):
     arrays = [base] + [array for term in terms for array in term]
     height, width = base.shape
+    count = height // CHIPS
+
+    def rows(columns):
+        return pl.BlockSpec((count, columns), lambda step: (step, 0))
+
+    def whole(array):
+        return pl.BlockSpec(array.shape, lambda step: (0, 0))
+
+    specs = [rows(width)]
+    for half, near, far in terms:
+        specs += [rows(half.shape[1]), whole(near), whole(far)]
 
     def body(*refs):
         spread_kernel(len(terms), *refs)
@@ -362,10 +375,11 @@
     return pl.pallas_call(
         body,
         name="spread",
-        out_shape=[jax.ShapeDtypeStruct((height // CHIPS, width), jnp.bfloat16)] * CHIPS,
-        in_specs=[pl.BlockSpec(memory_space=pltpu.VMEM)] * len(arrays),
-        out_specs=[pl.BlockSpec(memory_space=pltpu.VMEM)] * CHIPS,
-        compiler_params=pltpu.CompilerParams(vmem_limit_bytes=WIDE_ROOM),
+        grid=(CHIPS,),
+        out_shape=[jax.ShapeDtypeStruct((count, width), jnp.bfloat16)] * CHIPS,
+        in_specs=specs,
+        out_specs=[pl.BlockSpec((count, width), lambda step: (0, 0))] * CHIPS,
+        compiler_params=pltpu.CompilerParams(vmem_limit_bytes=ROOM),
         cost_estimate=pl.CostEstimate(
             flops=2 * height * width * terms[0][0].shape[1] * len(terms),
             bytes_accessed=sum(array.size * array.dtype.itemsize for array in arrays),
@@ -432,11 +446,12 @@
 
     down = [(3, 2), (1, 0)]
     two_down = [(3, 1), (2, 0)]
-    crossed = [(0, 1), (1, 0)]
+    two_cross, down_cross = [(0, 1)], [(2, 0)]
     own_half = chip_blocks(shared, chip, core)
     half_down = between_layers(own_half, down)
     half_two = between_layers(own_half, two_down)
-    half_cross = between_layers(half_two, crossed)
+    half_cross = between_layers(half_two, two_cross)
+    half_late = between_layers(half_down, down_cross)
     turned = lax.optimization_barrier(tokens.T)
     wanted = lax.optimization_barrier(teacher[0].reshape(rows, channels).T)
     difference = (turned.astype(f32) - wanted.astype(f32)).astype(bf16)
@@ -464,7 +479,8 @@
     def to_experts(parts):
         return parts[:1] + [across_chips(parts[step], step) for step in range(1, CHIPS)]
 
-    step_cross = between_layers(step_two, crossed)
+    step_cross = between_layers(step_two, two_cross)
+    step_late = between_layers(step_down, down_cross)
     projected = dot(tokens, shared).astype(bf16)
     own_gram = gram_pair(own_half, own_half)
     proj_slots = to_slots(projected)
@@ -557,10 +573,17 @@
     )
 
     third_down = between_layers(chain, [(1, 0)])
+    half_late, step_late = after(half_late, chain), after(step_late, chain)
+    late_pair = gram_pair(half_late, own_half)
+    last_score = both_cores(dot_first(step_late, own_half))
     steps_total = difference.astype(f32) + step_down.astype(f32)
-    steps_total = (steps_total + after(late_steps, chain).astype(f32)).astype(bf16)
+    steps_total = steps_total + after(late_steps, chain).astype(f32)
+    steps_total = (steps_total + step_late.astype(f32)).astype(bf16)
+    late_product = gram_sum(late_pair)
     score, grad_pre, grad_proj, _ = turn(
-        score, [], [(second_two, two_gram), (first_three, cross_product), (third_down, down_gram)]
+        score,
+        [last_score],
+        [(second_two, two_gram), (first_three, late_product), (third_down, down_gram)],
     )
 
     def with_swap(values):
@@ -569,7 +592,8 @@
     proj_rows = gather_rows(grad_proj)
     scaled_pair = with_swap(after(scaled, grad_proj))
     two_pair = with_swap(first_two + after(second_two, grad_proj))
-    cross_pair = with_swap(second_cross + after(first_three, grad_proj))
+    cross_pair = with_swap(after(second_cross, grad_proj))
+    late_pair = with_swap(after(first_three, grad_proj))
     down_pair = with_swap(first_down + third_down)
     mixed_blocks = spread(
         steps_total,
@@ -577,6 +601,7 @@
             (own_half, *scaled_pair),
             (half_two, *two_pair),
             (half_cross, *cross_pair),
+            (half_late, *late_pair),
             (half_down, *down_pair),
         ],
     )

time: 275 us -> 311 us (1.13)
  waiting for transfers between devices: 138 us -> 179 us
  starting transfers between devices: 70.4 us -> 66.7 us
    ppermute x12 -> x14, waiting for transfers between devices: 75 us -> 114 us  [between_layers(): return lax.ppermute(value, 'section', pairs)]
    ppermute x23, starting transfers between devices: 41.7 us -> 38.4 us  [on_chips(): return lax.ppermute(value, 'expert', perm)]
    ppermute x12 -> x14, starting transfers between devices: 22.3 us -> 21.2 us  [between_layers(): return lax.ppermute(value, 'section', pairs)]
    dot_general x8 -> x10, matrix products: 16.9 us -> 16.3 us  [dot_first(): lax.dot_general(left, right, (((0,), (0,)), ((), ())), preferred_element_...]
    ppermute x28 -> x31, starting transfers between devices: 6.53 us -> 7.05 us  [swap_cores(): lax.ppermute(value, 'expert', [(index, index ^ 1) for index in range(coun...]
  transfers between devices with their start and end apart: 63 -> 68, of which waited for: 17 -> 21; matrix products, arithmetic and copies ran while one was open for 12% -> 10% of each run, Pallas kernels for 9% -> 9%
where the time goes in v4:
time: 311 us; the launch traced here: 310 us
  waiting for transfers between devices  179 us (58%)
  starting transfers between devices  66.7 us (21%)
  Pallas kernels  28.2 us (9%)
  matrix products  18.2 us (6%)
  local copies, waits for them, and re-layouts  9.33 us (3%)
  other arithmetic  6.88 us (2%)
    ppermute x14, waiting for transfers between devices, between_layers(): return lax.ppermute(value, 'section', pairs)  114 us
    ppermute x23, waiting for transfers between devices, on_chips(): return lax.ppermute(value, 'expert', perm)  62.8 us
    ppermute x23, starting transfers between devices, on_chips(): return lax.ppermute(value, 'expert', perm)  38.4 us
    ppermute x14, starting transfers between devices, between_layers(): return lax.ppermute(value, 'section', pairs)  21.2 us
    dot_general x10, matrix products, dot_first(): lax.dot_general(left, right, (((0,), (0,)), ((), ())), preferred_element_...  16.3 us
    pallas_call x3, Pallas kernels, call_rows(): pl.pallas_call(body, out_shape=[jax.ShapeDtypeStruct(shape, kind) for sha...  12.2 us
    pallas_call x2, Pallas kernels, core_call(): pl.pallas_call(body, out_shape=outs, in_specs=[pl.BlockSpec(memory_space=...  8.7 us
    ppermute x31, starting transfers between devices, swap_cores(): lax.ppermute(value, 'expert', [(index, index ^ 1) for index in range(coun...  7.05 us
  transfers between devices with their start and end apart: 68, of which 21 were waited for; matrix products, arithmetic and copies ran while one was open for 10% of the time, Pallas kernels for 9%

profile of v4, /device:TPU:0, one launch (start us, length us, event | category | flops | bytes accessed | tf_op | source)
XLA Modules:
  0.0 309.8 jit_solution(3360476634072959801)
XLA Ops:
  1.5 5.9 %collective-permute-start.2 = (bf16[768,768]{1,0:T(8,128)(2,1)}, bf16[768,768]{1,0:T(8,128)(2,1)}, u32[]{:S(2)}, u32[]{:S(2)}) collective-permute-start(bf16[768,768]{1,0:T(8,128)(2,1)} %bitcast.43), channel_id=1, source_target_pairs={{0,2},{1,3},{2,0},{3,1},{4,6},{5,7},{6,4},{7,5},{8,10},{9,11},{10,... | collective-permute-start | bytes 3538952 | tf_op jit(solution)/shard_map/ppermute | solution.py:170
  7.4 1.4 copy.11
  10.3 1.1 copy-done.1
  11.8 1.3 collective-permute-start.18
  15.2 1.7 convolution_convert_fusion.5
  17.1 13.7 %collective-permute-done.18 = bf16[1280,256]{1,0:T(8,128)(2,1)S(1)} collective-permute-done((bf16[1280,256]{1,0:T(8,128)(2,1)S(1)}, bf16[1280,256]{1,0:T(8,128)(2,1)S(1)}, u32[]{:S(2)}, u32[]{:S(2)}) %collective-permute-start.18) | collective-permute-done | bytes 655392 | tf_op jit(solution)/shard_map/ppermute | solution.py:179
  30.8 1.3 collective-permute-start.27
  32.1 1.3 collective-permute-done.2.refs_2_
  33.4 1.8 collective-permute-start.8
  36.7 1.4 collective-permute-start.21
  40.0 1.3 collective-permute-start.5
  42.4 1.8 pad_maximum_fusion.3
  44.6 1.3 collective-permute-start.9
  47.0 30.3 %collective-permute-done.27.refs_4_ = bf16[1280,768]{1,0:T(8,128)(2,1)} collective-permute-done((bf16[1280,768]{1,0:T(8,128)(2,1)S(1)}, bf16[1280,768]{1,0:T(8,128)(2,1)}, u32[]{:S(2)}, u32[]{:S(2)}) %collective-permute-start.27) | collective-permute-done | bytes 1966112 | tf_op jit(solution)/shard_map/ppermute | solution.py:179
  79.9 1.2 slice_add_fusion.3.refs_10_
  81.1 1.5 collective-permute-done.21.refs_13_
  82.6 1.5 collective-permute-start.30
  84.1 11.5 %collective-permute-done.9.refs_7_ = bf16[768,768]{1,0:T(8,128)(2,1)} collective-permute-done((bf16[768,768]{1,0:T(8,128)(2,1)}, bf16[768,768]{1,0:T(8,128)(2,1)}, u32[]{:S(2)}, u32[]{:S(2)}) %collective-permute-start.9) | collective-permute-done | bytes 1179680 | tf_op jit(solution)/shard_map/ppermute | solution.py:170
  95.7 3.3 %convolution_convert_fusion.4 = bf16[768,768]{1,0:T(8,128)(2,1)S(1)} fusion(bf16[1280,768]{1,0:T(8,128)(2,1)} %collective-permute-done.21.refs_13_, bf16[1280,768]{1,0:T(8,128)(2,1)S(1)} %pad_maximum_fusion.refs_1_), kind=kOutput, calls=%fused_computation.12 | convolution fusion | flops 1510539264 | bytes 5111808 | tf_op jit(solution)/shard_map/dot_general | solution.py:159
  100.0 1.3 collective-permute-start.23
  102.4 3.4 %convolution_convert_fusion.3 = bf16[768,768]{1,0:T(8,128)(2,1)S(1)} fusion(bf16[1280,768]{1,0:T(8,128)(2,1)} %collective-permute-done.27.refs_4_, bf16[1280,768]{1,0:T(8,128)(2,1)S(1)} %pad_maximum_fusion.refs_1_), kind=kOutput, calls=%fused_computation.11 | convolution fusion | flops 1510539264 | bytes 5111808 | tf_op jit(solution)/shard_map/dot_general | solution.py:159
  105.8 3.5 %shard_map.86 = (f32[128,768]{1,0:T(8,128)S(1)}, bf16[768,768]{1,0:T(8,128)(2,1)S(1)}, bf16[768,768]{1,0:T(8,128)(2,1)S(1)}, bf16[768,768]{1,0:T(8,128)(2,1)S(1)...) custom-call(s32[1]{0:T(128)} %bitcast.2.middle_ref, ...), custom_call_target="tpu_custom_call" | custom-call | flops 905969664 | bytes 7077888 | tf_op jit(solution)/shard_map/pallas_call | solution.py:505
  109.4 10.0 %collective-permute-done.23 = bf16[1280,256]{1,0:T(8,128)(2,1)S(1)} collective-permute-done((bf16[1280,256]{1,0:T(8,128)(2,1)S(1)}, bf16[1280,256]{1,0:T(8,128)(2,1)S(1)}, u32[]{:S(2)}, u32[]{:S(2)}) %collective-permute-start.23) | collective-permute-done | bytes 655392 | tf_op jit(solution)/shard_map/ppermute | solution.py:179
  119.8 5.8 %collective-permute-start.24 = (bf16[1280,256]{1,0:T(8,128)(2,1)S(1)}, bf16[1280,256]{1,0:T(8,128)(2,1)S(1)}, u32[]{:S(2)}, u32[]{:S(2)}) collective-permute-start(bf16[1280,256]{1,0:T(8,128)(2,1)S(1)} %collective-permute-done.23), channel_id=1, source_target_pairs={{0,8},{1,9},{2,10},{3,11},{4,12},{5,13},{6,14},{7,15}} | collective-permute-start | bytes 1966088 | tf_op jit(solution)/shard_map/ppermute | solution.py:179
  125.7 5.2 %shard_map.87 = (bf16[128,768]{1,0:T(8,128)(2,1)S(1)}, f32[128,768]{1,0:T(8,128)S(1)}, f32[128,768]{1,0:T(8,128)S(1)}, bf16[128,768]{1,0:T(8,128)(2,1)S(1)}, bf1...) custom-call(s32[1]{0:T(128)} %bitcast.2.middle_ref, bf16[128,768]{1,0:T(8,128)(2,1)S(1)} %fusion.2.proj_ref, ...), custom_call_target="tpu_custom_call" | custom-call | flops 1660944384 | bytes 4718592 | tf_op jit(solution)/shard_map/pallas_call | solution.py:505
  131.9 3.7 %shard_map.88 = (f32[128,768]{1,0:T(8,128)S(1)}, bf16[128,768]{1,0:T(8,128)(2,1)}, bf16[128,768]{1,0:T(8,128)(2,1)}, bf16[128,768]{1,0:T(8,128)(2,1)S(1)}) custom-call(f32[128,16]{1,0:T(8,128)S(1)} %convert_select_fusion.marks_ref.refs_0_, bf16[128,768]{1,0:T(8,128)(2,1)S(1)} %get-tuple-element.92.refs_1_.refs_2_.refs_5_, ...), custom_call_target="tpu_custom_call" | custom-call | flops 1358954496 | bytes 12197888 | tf_op jit(solution)/shard_map/pallas_call | solution.py:332
  135.7 1.3 collective-permute-start.36
  137.0 1.8 convolution_convert_fusion.2
  138.7 1.1 collective-permute-done.24
  141.4 1.3 collective-permute-start.32
  145.2 4.0 %shard_map.89 = (f32[128,768]{1,0:T(8,128)S(1)}, bf16[128,768]{1,0:T(8,128)(2,1)}, bf16[128,768]{1,0:T(8,128)(2,1)}, bf16[128,768]{1,0:T(8,128)(2,1)S(1)}) custom-call(f32[128,16]{1,0:T(8,128)S(1)} %convert_select_fusion.marks_ref.refs_0_, bf16[128,768]{1,0:T(8,128)(2,1)S(1)} %get-tuple-element.92.refs_1_.refs_2_.refs_5_, ...), custom_call_target="tpu_custom_call" | custom-call | flops 1509949440 | bytes 13574144 | tf_op jit(solution)/shard_map/pallas_call | solution.py:332
  149.2 35.2 %collective-permute-done.36.refs_10_ = bf16[1280,768]{1,0:T(8,128)(2,1)S(1)} collective-permute-done((bf16[1280,768]{1,0:T(8,128)(2,1)}, bf16[1280,768]{1,0:T(8,128)(2,1)S(1)}, u32[]{:S(2)}, u32[]{:S(2)}) %collective-permute-start.36) | collective-permute-done | bytes 1966112 | tf_op jit(solution)/shard_map/ppermute | solution.py:179
  184.5 1.8 convolution_convert_fusion.1
  186.4 11.9 %collective-permute-done.32 = bf16[1280,256]{1,0:T(8,128)(2,1)S(1)} collective-permute-done((bf16[1280,256]{1,0:T(8,128)(2,1)S(1)}, bf16[1280,256]{1,0:T(8,128)(2,1)S(1)}, u32[]{:S(2)}, u32[]{:S(2)}) %collective-permute-start.32) | collective-permute-done | bytes 655392 | tf_op jit(solution)/shard_map/ppermute | solution.py:179
  199.3 1.3 collective-permute-start.38
  200.6 1.3 collective-permute-start.34
  201.9 1.3 collective-permute-start.35
  203.2 5.2 %collective-permute-done.38.refs_9_ = bf16[128,768]{1,0:T(8,128)(2,1)S(1)} collective-permute-done((bf16[128,768]{1,0:T(8,128)(2,1)S(1)}, bf16[128,768]{1,0:T(8,128)(2,1)S(1)}, u32[]{:S(2)}, u32[]{:S(2)}) %collective-permute-start.38) | collective-permute-done | bytes 196640 | tf_op jit(solution)/shard_map/ppermute | solution.py:179
  209.0 3.1 %collective-permute-done.35.refs_7_.refs_11_ = bf16[128,768]{1,0:T(8,128)(2,1)S(1)} collective-permute-done((bf16[128,768]{1,0:T(8,128)(2,1)S(1)}, bf16[128,768]{1,0:T(8,128)(2,1)S(1)}, u32[]{:S(2)}, u32[]{:S(2)}) %collective-permute-start.35) | collective-permute-done | bytes 196640 | tf_op jit(solution)/shard_map/ppermute | solution.py:179
  212.1 1.9 collective-permute-done.34.refs_5_
  214.0 4.4 %shard_map.90 = (f32[128,768]{1,0:T(8,128)}, bf16[128,768]{1,0:T(8,128)(2,1)S(1)}, bf16[128,768]{1,0:T(8,128)(2,1)S(1)}, bf16[128,768]{1,0:T(8,128)(2,1)}) custom-call(f32[128,16]{1,0:T(8,128)S(1)} %convert_select_fusion.marks_ref.refs_0_, bf16[128,768]{1,0:T(8,128)(2,1)S(1)} %get-tuple-element.92.refs_1_.refs_2_.refs_5_, ...), custom_call_target="tpu_custom_call" | custom-call | flops 1660944384 | bytes 14950400 | tf_op jit(solution)/shard_map/pallas_call | solution.py:332
  219.9 2.3 collective-permute-start.64
  222.2 2.2 collective-permute-start.62
  224.4 2.7 collective-permute-start.16
  227.1 5.1 %spread.1 = (bf16[320,256]{1,0:T(8,128)(2,1)S(1)}, bf16[320,256]{1,0:T(8,128)(2,1)S(1)}, bf16[320,256]{1,0:T(8,128)(2,1)S(1)}, bf16[320,256]{1,0:T(8,128)(2,1)S(1)}) custom-call(bf16[1280,256]{1,0:T(8,128)(2,1)S(1)} %add_convert_fusion.5.refs_0_, bf16[1280,768]{1,0:T(8,128)(2,1)S(1)} %pad_maximum_fusion.refs_1_, ...), custom_call_target="tpu_custom_call" | custom-call | flops 2516582400 | bytes 12451840 | tf_op jit(solution)/shard_map/spread/pallas_call | solution.py:375
  232.2 1.7 collective-permute-start.41
  233.9 5.5 %collective-permute-done.63.refs_7_ = bf16[128,768]{1,0:T(8,128)(2,1)S(1)} collective-permute-done((bf16[128,768]{1,0:T(8,128)(2,1)S(1)}, bf16[128,768]{1,0:T(8,128)(2,1)S(1)}, u32[]{:S(2)}, u32[]{:S(2)}) %collective-permute-start.63) | collective-permute-done | bytes 196640 | tf_op jit(solution)/shard_map/ppermute | solution.py:170
  239.8 1.4 collective-permute-done.55
  241.2 2.8 collective-permute-start.39
  244.0 1.7 collective-permute-start.17
  245.7 9.2 %collective-permute-done.16.refs_2_ = bf16[320,256]{1,0:T(8,128)(2,1)S(1)} collective-permute-done((bf16[320,256]{1,0:T(8,128)(2,1)S(1)}, bf16[320,256]{1,0:T(8,128)(2,1)S(1)}, u32[]{:S(2)}, u32[]{:S(2)}) %collective-permute-start.16) | collective-permute-done | bytes 163872 | tf_op jit(solution)/shard_map/ppermute | solution.py:170
  255.4 11.4 %collective-permute-done.40.refs_6_ = bf16[128,768]{1,0:T(8,128)(2,1)S(1)} collective-permute-done((bf16[128,768]{1,0:T(8,128)(2,1)S(1)}, bf16[128,768]{1,0:T(8,128)(2,1)S(1)}, u32[]{:S(2)}, u32[]{:S(2)}) %collective-permute-start.40) | collective-permute-done | bytes 196640 | tf_op jit(solution)/shard_map/ppermute | solution.py:170
  267.4 2.6 collective-permute-start.47
  270.8 1.6 collective-permute-start.49
  272.4 1.1 collective-permute-start.59
  275.1 7.6 %collective-permute-done.56 = bf16[64,768]{1,0:T(8,128)(2,1)S(1)} collective-permute-done((bf16[64,768]{1,0:T(8,128)(2,1)S(1)}, bf16[64,768]{1,0:T(8,128)(2,1)S(1)}, u32[]{:S(2)}, u32[]{:S(2)}) %collective-permute-start.56) | collective-permute-done | bytes 98336 | tf_op jit(solution)/shard_map/ppermute | solution.py:170
  282.8 1.7 collective-permute-start.57
  284.5 5.5 %collective-permute-done.57 = bf16[64,768]{1,0:T(8,128)(2,1)S(1)} collective-permute-done((bf16[64,768]{1,0:T(8,128)(2,1)S(1)}, bf16[64,768]{1,0:T(8,128)(2,1)S(1)}, u32[]{:S(2)}, u32[]{:S(2)}) %collective-permute-start.57) | collective-permute-done | bytes 98336 | tf_op jit(solution)/shard_map/ppermute | solution.py:170
  290.0 2.9 collective-permute-start.58
  292.9 4.3 %collective-permute-done.58 = bf16[64,768]{1,0:T(8,128)(2,1)S(1)} collective-permute-done((bf16[64,768]{1,0:T(8,128)(2,1)S(1)}, bf16[64,768]{1,0:T(8,128)(2,1)S(1)}, u32[]{:S(2)}, u32[]{:S(2)}) %collective-permute-start.58) | collective-permute-done | bytes 98336 | tf_op jit(solution)/shard_map/ppermute | solution.py:170
  297.3 2.4 collective-permute-start.61
  300.2 1.5 convolution_convert_fusion
  301.8 6.3 %collective-permute-done.60.refs_3_ = bf16[320,256]{1,0:T(8,128)(2,1)S(1)} collective-permute-done((bf16[320,256]{1,0:T(8,128)(2,1)S(1)}, bf16[320,256]{1,0:T(8,128)(2,1)S(1)}, u32[]{:S(2)}, u32[]{:S(2)}) %collective-permute-start.60) | collective-permute-done | bytes 163872 | tf_op jit(solution)/shard_map/ppermute | solution.py:170
  308.1 1.6 shard_map.92
  (207 shorter events, 28.5 us)
Async XLA Ops:
  0.6 36.1 %collective-permute-start.4 = (bf16[768,768]{1,0:T(8,128)(2,1)}, bf16[768,768]{1,0:T(8,128)(2,1)S(1)}, u32[]{:S(2)}, u32[]{:S(2)}) collective-permute-start(bf16[768,768]{1,0:T(8,128)(2,1)} %bitcast.42), channel_id=1, source_target_pairs={{2,4},{3,5},{4,2},{5,3},{10,12},{11,13},{12,10},{13,11},{18,20},{1... | collective-permute-start | bytes 3538952 | tf_op jit(solution)/shard_map/ppermute | solution.py:170
  1.5 31.9 %collective-permute-start.2 = (bf16[768,768]{1,0:T(8,128)(2,1)}, bf16[768,768]{1,0:T(8,128)(2,1)}, u32[]{:S(2)}, u32[]{:S(2)}) collective-permute-start(bf16[768,768]{1,0:T(8,128)(2,1)} %bitcast.43), channel_id=1, source_target_pairs={{0,2},{1,3},{2,0},{3,1},{4,6},{5,7},{6,4},{7,5},{8,10},{9,11},{10,... | collective-permute-start | bytes 3538952 | tf_op jit(solution)/shard_map/ppermute | solution.py:170
  7.4 30.8 %collective-permute-start.1 = (bf16[768,768]{1,0:T(8,128)(2,1)}, bf16[768,768]{1,0:T(8,128)(2,1)}, u32[]{:S(2)}, u32[]{:S(2)}) collective-permute-start(bf16[768,768]{1,0:T(8,128)(2,1)} %bitcast.44), channel_id=1, source_target_pairs={{0,1},{1,0},{2,3},{3,2},{4,5},{5,4},{6,7},{7,6},{8,9},{9,8},{10,11... | collective-permute-start | bytes 3538952 | tf_op jit(solution)/shard_map/ppermute | solution.py:175
  11.8 19.0 %collective-permute-start.18 = (bf16[1280,256]{1,0:T(8,128)(2,1)S(1)}, bf16[1280,256]{1,0:T(8,128)(2,1)S(1)}, u32[]{:S(2)}, u32[]{:S(2)}) collective-permute-start(bf16[1280,256]{1,0:T(8,128)(2,1)S(1)} %pad_maximum_fusion.2), channel_id=1, source_target_pairs={{24,16},{8,0},{25,17},{9,1},{26,18},{10,2},{27,19},{11,3},{28,20},... | collective-permute-start | bytes 1966088 | tf_op jit(solution)/shard_map/ppermute | solution.py:179
  14.7 2.3 collective-permute-start.13
  17.0 22.0 %collective-permute-start.14 = (bf16[768,768]{1,0:T(8,128)(2,1)S(1)}, bf16[768,768]{1,0:T(8,128)(2,1)S(1)}, u32[]{:S(2)}, u32[]{:S(2)}) collective-permute-start(bf16[768,768]{1,0:T(8,128)(2,1)S(1)} %convolution_convert_fusion.5), channel_id=1, source_target_pairs={{0,1},{1,0},{2,3},{3,2},{4,5},{5,4},{6,7},{7,6},{8,9},{9,8},{10,11... | collective-permute-start | bytes 3538952 | tf_op jit(solution)/shard_map/ppermute | solution.py:175
  30.8 46.5 %collective-permute-start.27 = (bf16[1280,768]{1,0:T(8,128)(2,1)S(1)}, bf16[1280,768]{1,0:T(8,128)(2,1)}, u32[]{:S(2)}, u32[]{:S(2)}) collective-permute-start(bf16[1280,768]{1,0:T(8,128)(2,1)S(1)} %pad_maximum_fusion.refs_1_), channel_id=1, source_target_pairs={{24,8},{16,0},{25,9},{17,1},{26,10},{18,2},{27,11},{19,3},{28,12},... | collective-permute-start | bytes 5898248 | tf_op jit(solution)/shard_map/ppermute | solution.py:179
  33.4 11.2 %collective-permute-start.8 = (bf16[768,768]{1,0:T(8,128)(2,1)}, bf16[768,768]{1,0:T(8,128)(2,1)}, u32[]{:S(2)}, u32[]{:S(2)}) collective-permute-start(bf16[768,768]{1,0:T(8,128)(2,1)} %collective-permute-done.2.refs_2_), channel_id=1, source_target_pairs={{2,4},{3,5},{4,2},{5,3},{10,12},{11,13},{12,10},{13,11},{18,20},{1... | collective-permute-start | bytes 3538952 | tf_op jit(solution)/shard_map/ppermute | solution.py:170
  36.7 45.8 %collective-permute-start.21 = (bf16[1280,768]{1,0:T(8,128)(2,1)S(1)}, bf16[1280,768]{1,0:T(8,128)(2,1)}, u32[]{:S(2)}, u32[]{:S(2)}) collective-permute-start(bf16[1280,768]{1,0:T(8,128)(2,1)S(1)} %pad_maximum_fusion.refs_1_), channel_id=1, source_target_pairs={{24,16},{8,0},{25,17},{9,1},{26,18},{10,2},{27,19},{11,3},{28,20},... | collective-permute-start | bytes 5898248 | tf_op jit(solution)/shard_map/ppermute | solution.py:179
  38.2 6.0 %collective-permute-start.19 = (f32[128,768]{1,0:T(8,128)}, f32[128,768]{1,0:T(8,128)}, u32[]{:S(2)}, u32[]{:S(2)}) collective-permute-start(f32[128,768]{1,0:T(8,128)} %slice.137), channel_id=1, source_target_pairs={{0,1},{1,0},{2,3},{3,2},{4,5},{5,4},{6,7},{7,6},{8,9},{9,8},{10,11... | collective-permute-start | bytes 1179656 | tf_op jit(solution)/shard_map/ppermute | solution.py:175
  40.0 39.2 %collective-permute-start.5 = (bf16[768,768]{1,0:T(8,128)(2,1)S(1)}, bf16[768,768]{1,0:T(8,128)(2,1)}, u32[]{:S(2)}, u32[]{:S(2)}) collective-permute-start(bf16[768,768]{1,0:T(8,128)(2,1)S(1)} %collective-permute-done.4.refs_4_), channel_id=1, source_target_pairs={{2,0},{3,1},{4,6},{5,7},{10,8},{11,9},{12,14},{13,15},{18,16},{19,... | collective-permute-start | bytes 3538952 | tf_op jit(solution)/shard_map/ppermute | solution.py:170
  44.1 39.9 %collective-permute-start.6 = (bf16[768,768]{1,0:T(8,128)(2,1)S(1)}, bf16[768,768]{1,0:T(8,128)(2,1)}, u32[]{:S(2)}, u32[]{:S(2)}) collective-permute-start(bf16[768,768]{1,0:T(8,128)(2,1)S(1)} %collective-permute-done.4.refs_4_), channel_id=1, source_target_pairs={{0,1},{1,0},{2,3},{3,2},{4,5},{5,4},{6,7},{7,6},{8,9},{9,8},{10,11... | collective-permute-start | bytes 3538952 | tf_op jit(solution)/shard_map/ppermute | solution.py:175
  44.6 51.0 %collective-permute-start.9 = (bf16[768,768]{1,0:T(8,128)(2,1)}, bf16[768,768]{1,0:T(8,128)(2,1)}, u32[]{:S(2)}, u32[]{:S(2)}) collective-permute-start(bf16[768,768]{1,0:T(8,128)(2,1)} %collective-permute-done.8.refs_6_), channel_id=1, source_target_pairs={{2,0},{3,1},{4,6},{5,7},{10,8},{11,9},{12,14},{13,15},{18,16},{19,... | collective-permute-start | bytes 3538952 | tf_op jit(solution)/shard_map/ppermute | solution.py:170
  77.3 21.7 %collective-permute-start.3 = (bf16[768,768]{1,0:T(8,128)(2,1)}, bf16[768,768]{1,0:T(8,128)(2,1)}, u32[]{:S(2)}, u32[]{:S(2)}) collective-permute-start(bf16[768,768]{1,0:T(8,128)(2,1)} %collective-permute-done.2.refs_2_), channel_id=1, source_target_pairs={{0,1},{1,0},{2,3},{3,2},{4,5},{5,4},{6,7},{7,6},{8,9},{9,8},{10,11... | collective-permute-start | bytes 3538952 | tf_op jit(solution)/shard_map/ppermute | solution.py:175
  79.2 20.6 %collective-permute-start.7 = (bf16[768,768]{1,0:T(8,128)(2,1)}, bf16[768,768]{1,0:T(8,128)(2,1)S(1)}, u32[]{:S(2)}, u32[]{:S(2)}) collective-permute-start(bf16[768,768]{1,0:T(8,128)(2,1)} %collective-permute-done.5.refs_5_), channel_id=1, source_target_pairs={{0,1},{1,0},{2,3},{3,2},{4,5},{5,4},{6,7},{7,6},{8,9},{9,8},{10,11... | collective-permute-start | bytes 3538952 | tf_op jit(solution)/shard_map/ppermute | solution.py:175
  82.6 53.1 %collective-permute-start.30 = (bf16[1280,768]{1,0:T(8,128)(2,1)}, bf16[1280,768]{1,0:T(8,128)(2,1)S(1)}, u32[]{:S(2)}, u32[]{:S(2)}) collective-permute-start(bf16[1280,768]{1,0:T(8,128)(2,1)} %collective-permute-done.27.refs_4_), channel_id=1, source_target_pairs={{0,8},{1,9},{2,10},{3,11},{4,12},{5,13},{6,14},{7,15}} | collective-permute-start | bytes 5898248 | tf_op jit(solution)/shard_map/ppermute | solution.py:179
  84.0 35.3 %collective-permute-start.10 = (bf16[768,768]{1,0:T(8,128)(2,1)}, bf16[768,768]{1,0:T(8,128)(2,1)S(1)}, u32[]{:S(2)}, u32[]{:S(2)}) collective-permute-start(bf16[768,768]{1,0:T(8,128)(2,1)} %collective-permute-done.8.refs_6_), channel_id=1, source_target_pairs={{0,1},{1,0},{2,3},{3,2},{4,5},{5,4},{6,7},{7,6},{8,9},{9,8},{10,11... | collective-permute-start | bytes 3538952 | tf_op jit(solution)/shard_map/ppermute | solution.py:175
  95.6 24.2 %collective-permute-start.11 = (bf16[768,768]{1,0:T(8,128)(2,1)}, bf16[768,768]{1,0:T(8,128)(2,1)S(1)}, u32[]{:S(2)}, u32[]{:S(2)}) collective-permute-start(bf16[768,768]{1,0:T(8,128)(2,1)} %collective-permute-done.9.refs_7_), channel_id=1, source_target_pairs={{0,1},{1,0},{2,3},{3,2},{4,5},{5,4},{6,7},{7,6},{8,9},{9,8},{10,11... | collective-permute-start | bytes 3538952 | tf_op jit(solution)/shard_map/ppermute | solution.py:175
  99.0 31.8 %collective-permute-start.22 = (bf16[768,768]{1,0:T(8,128)(2,1)S(1)}, bf16[768,768]{1,0:T(8,128)(2,1)S(1)}, u32[]{:S(2)}, u32[]{:S(2)}) collective-permute-start(bf16[768,768]{1,0:T(8,128)(2,1)S(1)} %convolution_convert_fusion.4), channel_id=1, source_target_pairs={{0,1},{1,0},{2,3},{3,2},{4,5},{5,4},{6,7},{7,6},{8,9},{9,8},{10,11... | collective-permute-start | bytes 3538952 | tf_op jit(solution)/shard_map/ppermute | solution.py:175
  100.0 19.3 %collective-permute-start.23 = (bf16[1280,256]{1,0:T(8,128)(2,1)S(1)}, bf16[1280,256]{1,0:T(8,128)(2,1)S(1)}, u32[]{:S(2)}, u32[]{:S(2)}) collective-permute-start(bf16[1280,256]{1,0:T(8,128)(2,1)S(1)} %copy-done.22), channel_id=1, source_target_pairs={{24,8},{16,0},{25,9},{17,1},{26,10},{18,2},{27,11},{19,3},{28,12},... | collective-permute-start | bytes 1966088 | tf_op jit(solution)/shard_map/ppermute | solution.py:179
  119.3 21.5 %collective-permute-start.46 = (bf16[128,768]{1,0:T(8,128)(2,1)S(1)}, bf16[128,768]{1,0:T(8,128)(2,1)S(1)}, u32[]{:S(2)}, u32[]{:S(2)}) collective-permute-start(bf16[128,768]{1,0:T(8,128)(2,1)S(1)} %slice.143), channel_id=1, source_target_pairs={{0,1},{1,0},{2,3},{3,2},{4,5},{5,4},{6,7},{7,6},{8,9},{9,8},{10,11... | collective-permute-start | bytes 589832 | tf_op jit(solution)/shard_map/ppermute | solution.py:175
  119.3 79.8 %collective-permute-start = (bf16[1280,128]{1,0:T(8,128)(2,1)S(1)}, bf16[1280,128]{1,0:T(8,128)(2,1)S(1)}, u32[]{:S(2)}, u32[]{:S(2)}) collective-permute-start(bf16[1280,128]{1,0:T(8,128)(2,1)S(1)} %copy-done.28), channel_id=1, source_target_pairs={{0,1},{1,0},{2,3},{3,2},{4,5},{5,4},{6,7},{7,6},{8,9},{9,8},{10,11... | collective-permute-start | bytes 983048 | tf_op jit(solution)/shard_map/ppermute | solution.py:175
  119.8 20.0 %collective-permute-start.24 = (bf16[1280,256]{1,0:T(8,128)(2,1)S(1)}, bf16[1280,256]{1,0:T(8,128)(2,1)S(1)}, u32[]{:S(2)}, u32[]{:S(2)}) collective-permute-start(bf16[1280,256]{1,0:T(8,128)(2,1)S(1)} %collective-permute-done.23), channel_id=1, source_target_pairs={{0,8},{1,9},{2,10},{3,11},{4,12},{5,13},{6,14},{7,15}} | collective-permute-start | bytes 1966088 | tf_op jit(solution)/shard_map/ppermute | solution.py:179
  131.8 9.5 %collective-permute-start.28 = (bf16[768,768]{1,0:T(8,128)(2,1)S(1)}, bf16[768,768]{1,0:T(8,128)(2,1)S(1)}, u32[]{:S(2)}, u32[]{:S(2)}) collective-permute-start(bf16[768,768]{1,0:T(8,128)(2,1)S(1)} %convolution_convert_fusion.3), channel_id=1, source_target_pairs={{0,1},{1,0},{2,3},{3,2},{4,5},{5,4},{6,7},{7,6},{8,9},{9,8},{10,11... | collective-permute-start | bytes 3538952 | tf_op jit(solution)/shard_map/ppermute | solution.py:175
  135.7 48.8 %collective-permute-start.36 = (bf16[1280,768]{1,0:T(8,128)(2,1)}, bf16[1280,768]{1,0:T(8,128)(2,1)S(1)}, u32[]{:S(2)}, u32[]{:S(2)}) collective-permute-start(bf16[1280,768]{1,0:T(8,128)(2,1)} %collective-permute-done.21.refs_13_), channel_id=1, source_target_pairs={{16,0},{17,1},{18,2},{19,3},{20,4},{21,5},{22,6},{23,7}} | collective-permute-start | bytes 5898248 | tf_op jit(solution)/shard_map/ppermute | solution.py:179
  139.8 4.1 %collective-permute-start.31 = (bf16[768,768]{1,0:T(8,128)(2,1)S(1)}, bf16[768,768]{1,0:T(8,128)(2,1)S(1)}, u32[]{:S(2)}, u32[]{:S(2)}) collective-permute-start(bf16[768,768]{1,0:T(8,128)(2,1)S(1)} %convolution_convert_fusion.2), channel_id=1, source_target_pairs={{0,1},{1,0},{2,3},{3,2},{4,5},{5,4},{6,7},{7,6},{8,9},{9,8},{10,11... | collective-permute-start | bytes 3538952 | tf_op jit(solution)/shard_map/ppermute | solution.py:175
  140.8 2.5 collective-permute-start.25
  141.4 56.9 %collective-permute-start.32 = (bf16[1280,256]{1,0:T(8,128)(2,1)S(1)}, bf16[1280,256]{1,0:T(8,128)(2,1)S(1)}, u32[]{:S(2)}, u32[]{:S(2)}) collective-permute-start(bf16[1280,256]{1,0:T(8,128)(2,1)S(1)} %copy-done.8), channel_id=1, source_target_pairs={{16,0},{17,1},{18,2},{19,3},{20,4},{21,5},{22,6},{23,7}} | collective-permute-start | bytes 1966088 | tf_op jit(solution)/shard_map/ppermute | solution.py:179
  143.2 1.9 collective-permute-start.26
  186.2 22.4 %collective-permute-start.37 = (bf16[768,768]{1,0:T(8,128)(2,1)S(1)}, bf16[768,768]{1,0:T(8,128)(2,1)S(1)}, u32[]{:S(2)}, u32[]{:S(2)}) collective-permute-start(bf16[768,768]{1,0:T(8,128)(2,1)S(1)} %convolution_convert_fusion.1), channel_id=1, source_target_pairs={{0,1},{1,0},{2,3},{3,2},{4,5},{5,4},{6,7},{7,6},{8,9},{9,8},{10,11... | collective-permute-start | bytes 3538952 | tf_op jit(solution)/shard_map/ppermute | solution.py:175
  199.1 9.5 %collective-permute-start.33 = (f32[128,768]{1,0:T(8,128)S(1)}, f32[128,768]{1,0:T(8,128)S(1)}, u32[]{:S(2)}, u32[]{:S(2)}) collective-permute-start(f32[128,768]{1,0:T(8,128)S(1)} %slice.141), channel_id=1, source_target_pairs={{0,1},{1,0},{2,3},{3,2},{4,5},{5,4},{6,7},{7,6},{8,9},{9,8},{10,11... | collective-permute-start | bytes 1179656 | tf_op jit(solution)/shard_map/ppermute | solution.py:175
  199.3 9.2 %collective-permute-start.38 = (bf16[128,768]{1,0:T(8,128)(2,1)S(1)}, bf16[128,768]{1,0:T(8,128)(2,1)S(1)}, u32[]{:S(2)}, u32[]{:S(2)}) collective-permute-start(bf16[128,768]{1,0:T(8,128)(2,1)S(1)} %get-tuple-element.70), channel_id=1, source_target_pairs={{8,0},{9,1},{10,2},{11,3},{12,4},{13,5},{14,6},{15,7}} | collective-permute-start | bytes 589832 | tf_op jit(solution)/shard_map/ppermute | solution.py:179
  200.6 13.4 %collective-permute-start.34 = (bf16[128,768]{1,0:T(8,128)(2,1)S(1)}, bf16[128,768]{1,0:T(8,128)(2,1)S(1)}, u32[]{:S(2)}, u32[]{:S(2)}) collective-permute-start(bf16[128,768]{1,0:T(8,128)(2,1)S(1)} %get-tuple-element.66), channel_id=1, source_target_pairs={{16,0},{17,1},{18,2},{19,3},{20,4},{21,5},{22,6},{23,7}} | collective-permute-start | bytes 589832 | tf_op jit(solution)/shard_map/ppermute | solution.py:179
  201.9 10.2 %collective-permute-start.35 = (bf16[128,768]{1,0:T(8,128)(2,1)S(1)}, bf16[128,768]{1,0:T(8,128)(2,1)S(1)}, u32[]{:S(2)}, u32[]{:S(2)}) collective-permute-start(bf16[128,768]{1,0:T(8,128)(2,1)S(1)} %get-tuple-element.72), channel_id=1, source_target_pairs={{24,0},{25,1},{26,2},{27,3},{28,4},{29,5},{30,6},{31,7}} | collective-permute-start | bytes 589832 | tf_op jit(solution)/shard_map/ppermute | solution.py:179
  208.5 11.4 %collective-permute-start.54 = (bf16[128,768]{1,0:T(8,128)(2,1)S(1)}, bf16[128,768]{1,0:T(8,128)(2,1)S(1)}, u32[]{:S(2)}, u32[]{:S(2)}) collective-permute-start(bf16[128,768]{1,0:T(8,128)(2,1)S(1)} %add.239.refs_14_), channel_id=1, source_target_pairs={{0,1},{1,0},{2,3},{3,2},{4,5},{5,4},{6,7},{7,6},{8,9},{9,8},{10,11... | collective-permute-start | bytes 589832 | tf_op jit(solution)/shard_map/ppermute | solution.py:175
  218.4 3.8 %collective-permute-start.50 = (bf16[128,768]{1,0:T(8,128)(2,1)S(1)}, bf16[128,768]{1,0:T(8,128)(2,1)S(1)}, u32[]{:S(2)}, u32[]{:S(2)}) collective-permute-start(bf16[128,768]{1,0:T(8,128)(2,1)S(1)} %get-tuple-element.92.refs_1_.refs_2_.refs_5_), channel_id=1, source_target_pairs={{0,1},{1,0},{2,3},{3,2},{4,5},{5,4},{6,7},{7,6},{8,9},{9,8},{10,11... | collective-permute-start | bytes 589832 | tf_op jit(solution)/shard_map/ppermute | solution.py:175
  218.4 3.7 %collective-permute-start.51 = (bf16[128,768]{1,0:T(8,128)(2,1)S(1)}, bf16[128,768]{1,0:T(8,128)(2,1)S(1)}, u32[]{:S(2)}, u32[]{:S(2)}) collective-permute-start(bf16[128,768]{1,0:T(8,128)(2,1)S(1)} %add.238.refs_5_), channel_id=1, source_target_pairs={{0,1},{1,0},{2,3},{3,2},{4,5},{5,4},{6,7},{7,6},{8,9},{9,8},{10,11... | collective-permute-start | bytes 589832 | tf_op jit(solution)/shard_map/ppermute | solution.py:175
  219.0 5.3 %collective-permute-start.52 = (bf16[128,768]{1,0:T(8,128)(2,1)S(1)}, bf16[128,768]{1,0:T(8,128)(2,1)S(1)}, u32[]{:S(2)}, u32[]{:S(2)}) collective-permute-start(bf16[128,768]{1,0:T(8,128)(2,1)S(1)} %collective-permute-done.29.refs_7_.refs_8_), channel_id=1, source_target_pairs={{0,1},{1,0},{2,3},{3,2},{4,5},{5,4},{6,7},{7,6},{8,9},{9,8},{10,11... | collective-permute-start | bytes 589832 | tf_op jit(solution)/shard_map/ppermute | solution.py:175
  219.1 5.3 %collective-permute-start.53 = (bf16[128,768]{1,0:T(8,128)(2,1)S(1)}, bf16[128,768]{1,0:T(8,128)(2,1)S(1)}, u32[]{:S(2)}, u32[]{:S(2)}) collective-permute-start(bf16[128,768]{1,0:T(8,128)(2,1)S(1)} %collective-permute-done.35.refs_7_.refs_11_), channel_id=1, source_target_pairs={{0,1},{1,0},{2,3},{3,2},{4,5},{5,4},{6,7},{7,6},{8,9},{9,8},{10,11... | collective-permute-start | bytes 589832 | tf_op jit(solution)/shard_map/ppermute | solution.py:175
  219.9 12.3 %collective-permute-start.64 = (bf16[128,768]{1,0:T(8,128)(2,1)S(1)}, bf16[128,768]{1,0:T(8,128)(2,1)S(1)}, u32[]{:S(2)}, u32[]{:S(2)}) collective-permute-start(bf16[128,768]{1,0:T(8,128)(2,1)S(1)} %get-tuple-element.92.refs_1_.refs_2_.refs_5_), channel_id=1, source_target_pairs={{0,6},{1,7},{2,4},{3,5},{4,2},{5,3},{6,0},{7,1},{8,14},{9,15},{10,... | collective-permute-start | bytes 589832 | tf_op jit(solution)/shard_map/ppermute | solution.py:170
  222.2 17.3 %collective-permute-start.63 = (bf16[128,768]{1,0:T(8,128)(2,1)S(1)}, bf16[128,768]{1,0:T(8,128)(2,1)S(1)}, u32[]{:S(2)}, u32[]{:S(2)}) collective-permute-start(bf16[128,768]{1,0:T(8,128)(2,1)S(1)} %get-tuple-element.92.refs_1_.refs_2_.refs_5_), channel_id=1, source_target_pairs={{0,4},{1,5},{2,6},{3,7},{4,0},{5,1},{6,2},{7,3},{8,12},{9,13},{10,... | collective-permute-start | bytes 589832 | tf_op jit(solution)/shard_map/ppermute | solution.py:170
  222.2 17.3 %collective-permute-start.62 = (bf16[128,768]{1,0:T(8,128)(2,1)S(1)}, bf16[128,768]{1,0:T(8,128)(2,1)S(1)}, u32[]{:S(2)}, u32[]{:S(2)}) collective-permute-start(bf16[128,768]{1,0:T(8,128)(2,1)S(1)} %get-tuple-element.92.refs_1_.refs_2_.refs_5_), channel_id=1, source_target_pairs={{0,2},{1,3},{2,0},{3,1},{4,6},{5,7},{6,4},{7,5},{8,10},{9,11},{10,... | collective-permute-start | bytes 589832 | tf_op jit(solution)/shard_map/ppermute | solution.py:170
  224.4 19.7 %collective-permute-start.15 = (bf16[320,256]{1,0:T(8,128)(2,1)S(1)}, bf16[320,256]{1,0:T(8,128)(2,1)S(1)}, u32[]{:S(2)}, u32[]{:S(2)}) collective-permute-start(bf16[320,256]{1,0:T(8,128)(2,1)S(1)} %get-tuple-element.57), channel_id=1, source_target_pairs={{0,2},{1,3},{2,0},{3,1},{4,6},{5,7},{6,4},{7,5},{8,10},{9,11},{10,... | collective-permute-start | bytes 491528 | tf_op jit(solution)/shard_map/ppermute | solution.py:170
  224.4 30.5 %collective-permute-start.16 = (bf16[320,256]{1,0:T(8,128)(2,1)S(1)}, bf16[320,256]{1,0:T(8,128)(2,1)S(1)}, u32[]{:S(2)}, u32[]{:S(2)}) collective-permute-start(bf16[320,256]{1,0:T(8,128)(2,1)S(1)} %get-tuple-element.58), channel_id=1, source_target_pairs={{0,4},{1,5},{2,6},{3,7},{4,0},{5,1},{6,2},{7,3},{8,12},{9,13},{10,... | collective-permute-start | bytes 491528 | tf_op jit(solution)/shard_map/ppermute | solution.py:170
  232.2 22.7 %collective-permute-start.41 = (bf16[128,768]{1,0:T(8,128)(2,1)S(1)}, bf16[128,768]{1,0:T(8,128)(2,1)S(1)}, u32[]{:S(2)}, u32[]{:S(2)}) collective-permute-start(bf16[128,768]{1,0:T(8,128)(2,1)S(1)} %get-tuple-element.74.refs_4_), channel_id=1, source_target_pairs={{0,6},{1,7},{2,4},{3,5},{4,2},{5,3},{6,0},{7,1},{8,14},{9,15},{10,... | collective-permute-start | bytes 589832 | tf_op jit(solution)/shard_map/ppermute | solution.py:170
  239.5 27.4 %collective-permute-start.40 = (bf16[128,768]{1,0:T(8,128)(2,1)S(1)}, bf16[128,768]{1,0:T(8,128)(2,1)S(1)}, u32[]{:S(2)}, u32[]{:S(2)}) collective-permute-start(bf16[128,768]{1,0:T(8,128)(2,1)S(1)} %get-tuple-element.74.refs_4_), channel_id=1, source_target_pairs={{0,4},{1,5},{2,6},{3,7},{4,0},{5,1},{6,2},{7,3},{8,12},{9,13},{10,... | collective-permute-start | bytes 589832 | tf_op jit(solution)/shard_map/ppermute | solution.py:170
  241.2 25.6 %collective-permute-start.39 = (bf16[128,768]{1,0:T(8,128)(2,1)S(1)}, bf16[128,768]{1,0:T(8,128)(2,1)S(1)}, u32[]{:S(2)}, u32[]{:S(2)}) collective-permute-start(bf16[128,768]{1,0:T(8,128)(2,1)S(1)} %get-tuple-element.74.refs_4_), channel_id=1, source_target_pairs={{0,2},{1,3},{2,0},{3,1},{4,6},{5,7},{6,4},{7,5},{8,10},{9,11},{10,... | collective-permute-start | bytes 589832 | tf_op jit(solution)/shard_map/ppermute | solution.py:170
  244.0 23.3 %collective-permute-start.17 = (bf16[320,256]{1,0:T(8,128)(2,1)S(1)}, bf16[320,256]{1,0:T(8,128)(2,1)S(1)}, u32[]{:S(2)}, u32[]{:S(2)}) collective-permute-start(bf16[320,256]{1,0:T(8,128)(2,1)S(1)} %get-tuple-element.59), channel_id=1, source_target_pairs={{0,6},{1,7},{2,4},{3,5},{4,2},{5,3},{6,0},{7,1},{8,14},{9,15},{10,... | collective-permute-start | bytes 491528 | tf_op jit(solution)/shard_map/ppermute | solution.py:170
  254.9 15.1 %collective-permute-start.42 = (bf16[128,768]{1,0:T(8,128)(2,1)S(1)}, bf16[128,768]{1,0:T(8,128)(2,1)S(1)}, u32[]{:S(2)}, u32[]{:S(2)}) collective-permute-start(bf16[128,768]{1,0:T(8,128)(2,1)S(1)} %get-tuple-element.74.refs_4_), channel_id=1, source_target_pairs={{0,1},{1,0},{2,3},{3,2},{4,5},{5,4},{6,7},{7,6},{8,9},{9,8},{10,11... | collective-permute-start | bytes 589832 | tf_op jit(solution)/shard_map/ppermute | solution.py:175
  254.9 15.9 %collective-permute-start.45 = (bf16[128,768]{1,0:T(8,128)(2,1)S(1)}, bf16[128,768]{1,0:T(8,128)(2,1)S(1)}, u32[]{:S(2)}, u32[]{:S(2)}) collective-permute-start(bf16[128,768]{1,0:T(8,128)(2,1)S(1)} %collective-permute-done.41.refs_7_), channel_id=1, source_target_pairs={{0,1},{1,0},{2,3},{3,2},{4,5},{5,4},{6,7},{7,6},{8,9},{9,8},{10,11... | collective-permute-start | bytes 589832 | tf_op jit(solution)/shard_map/ppermute | solution.py:175
  266.8 5.6 %collective-permute-start.44 = (bf16[128,768]{1,0:T(8,128)(2,1)S(1)}, bf16[128,768]{1,0:T(8,128)(2,1)S(1)}, u32[]{:S(2)}, u32[]{:S(2)}) collective-permute-start(bf16[128,768]{1,0:T(8,128)(2,1)S(1)} %collective-permute-done.40.refs_6_), channel_id=1, source_target_pairs={{0,1},{1,0},{2,3},{3,2},{4,5},{5,4},{6,7},{7,6},{8,9},{9,8},{10,11... | collective-permute-start | bytes 589832 | tf_op jit(solution)/shard_map/ppermute | solution.py:175
  266.8 6.7 %collective-permute-start.43 = (bf16[128,768]{1,0:T(8,128)(2,1)S(1)}, bf16[128,768]{1,0:T(8,128)(2,1)S(1)}, u32[]{:S(2)}, u32[]{:S(2)}) collective-permute-start(bf16[128,768]{1,0:T(8,128)(2,1)S(1)} %collective-permute-done.39.refs_5_), channel_id=1, source_target_pairs={{0,1},{1,0},{2,3},{3,2},{4,5},{5,4},{6,7},{7,6},{8,9},{9,8},{10,11... | collective-permute-start | bytes 589832 | tf_op jit(solution)/shard_map/ppermute | solution.py:175
  267.4 29.9 %collective-permute-start.47 = (bf16[64,768]{1,0:T(8,128)(2,1)S(1)}, bf16[64,768]{1,0:T(8,128)(2,1)S(1)}, u32[]{:S(2)}, u32[]{:S(2)}) collective-permute-start(bf16[64,768]{1,0:T(8,128)(2,1)S(1)} %get-tuple-element.76), channel_id=1, source_target_pairs={{0,2},{1,3},{2,0},{3,1},{4,6},{5,7},{6,4},{7,5},{8,10},{9,11},{10,... | collective-permute-start | bytes 294920 | tf_op jit(solution)/shard_map/ppermute | solution.py:170
  270.0 29.6 %collective-permute-start.48 = (bf16[64,768]{1,0:T(8,128)(2,1)S(1)}, bf16[64,768]{1,0:T(8,128)(2,1)S(1)}, u32[]{:S(2)}, u32[]{:S(2)}) collective-permute-start(bf16[64,768]{1,0:T(8,128)(2,1)S(1)} %get-tuple-element.77), channel_id=1, source_target_pairs={{0,4},{1,5},{2,6},{3,7},{4,0},{5,1},{6,2},{7,3},{8,12},{9,13},{10,... | collective-permute-start | bytes 294920 | tf_op jit(solution)/shard_map/ppermute | solution.py:170
  270.8 28.9 %collective-permute-start.49 = (bf16[64,768]{1,0:T(8,128)(2,1)S(1)}, bf16[64,768]{1,0:T(8,128)(2,1)S(1)}, u32[]{:S(2)}, u32[]{:S(2)}) collective-permute-start(bf16[64,768]{1,0:T(8,128)(2,1)S(1)} %get-tuple-element.78), channel_id=1, source_target_pairs={{0,6},{1,7},{2,4},{3,5},{4,2},{5,3},{6,0},{7,1},{8,14},{9,15},{10,... | collective-permute-start | bytes 294920 | tf_op jit(solution)/shard_map/ppermute | solution.py:170
  272.4 27.8 %collective-permute-start.59 = (bf16[320,256]{1,0:T(8,128)(2,1)S(1)}, bf16[320,256]{1,0:T(8,128)(2,1)S(1)}, u32[]{:S(2)}, u32[]{:S(2)}) collective-permute-start(bf16[320,256]{1,0:T(8,128)(2,1)S(1)} %get-tuple-element.88), channel_id=1, source_target_pairs={{0,2},{1,3},{2,0},{3,1},{4,6},{5,7},{6,4},{7,5},{8,10},{9,11},{10,... | collective-permute-start | bytes 491528 | tf_op jit(solution)/shard_map/ppermute | solution.py:170
  273.5 9.3 %collective-permute-start.56 = (bf16[64,768]{1,0:T(8,128)(2,1)S(1)}, bf16[64,768]{1,0:T(8,128)(2,1)S(1)}, u32[]{:S(2)}, u32[]{:S(2)}) collective-permute-start(bf16[64,768]{1,0:T(8,128)(2,1)S(1)} %pad_maximum_fusion.9), channel_id=1, source_target_pairs={{0,2},{1,3},{2,0},{3,1},{4,6},{5,7},{6,4},{7,5},{8,10},{9,11},{10,... | collective-permute-start | bytes 294920 | tf_op jit(solution)/shard_map/ppermute | solution.py:170
  282.8 7.2 %collective-permute-start.57 = (bf16[64,768]{1,0:T(8,128)(2,1)S(1)}, bf16[64,768]{1,0:T(8,128)(2,1)S(1)}, u32[]{:S(2)}, u32[]{:S(2)}) collective-permute-start(bf16[64,768]{1,0:T(8,128)(2,1)S(1)} %pad_maximum_fusion.10), channel_id=1, source_target_pairs={{0,4},{1,5},{2,6},{3,7},{4,0},{5,1},{6,2},{7,3},{8,12},{9,13},{10,... | collective-permute-start | bytes 294920 | tf_op jit(solution)/shard_map/ppermute | solution.py:170
  290.0 7.2 %collective-permute-start.58 = (bf16[64,768]{1,0:T(8,128)(2,1)S(1)}, bf16[64,768]{1,0:T(8,128)(2,1)S(1)}, u32[]{:S(2)}, u32[]{:S(2)}) collective-permute-start(bf16[64,768]{1,0:T(8,128)(2,1)S(1)} %pad_maximum_fusion.11), channel_id=1, source_target_pairs={{0,6},{1,7},{2,4},{3,5},{4,2},{5,3},{6,0},{7,1},{8,14},{9,15},{10,... | collective-permute-start | bytes 294920 | tf_op jit(solution)/shard_map/ppermute | solution.py:170
  297.2 10.9 %collective-permute-start.60 = (bf16[320,256]{1,0:T(8,128)(2,1)S(1)}, bf16[320,256]{1,0:T(8,128)(2,1)S(1)}, u32[]{:S(2)}, u32[]{:S(2)}) collective-permute-start(bf16[320,256]{1,0:T(8,128)(2,1)S(1)} %get-tuple-element.89), channel_id=1, source_target_pairs={{0,4},{1,5},{2,6},{3,7},{4,0},{5,1},{6,2},{7,3},{8,12},{9,13},{10,... | collective-permute-start | bytes 491528 | tf_op jit(solution)/shard_map/ppermute | solution.py:170
  297.3 10.8 %collective-permute-start.61 = (bf16[320,256]{1,0:T(8,128)(2,1)S(1)}, bf16[320,256]{1,0:T(8,128)(2,1)S(1)}, u32[]{:S(2)}, u32[]{:S(2)}) collective-permute-start(bf16[320,256]{1,0:T(8,128)(2,1)S(1)} %get-tuple-element.90), channel_id=1, source_target_pairs={{0,6},{1,7},{2,4},{3,5},{4,2},{5,3},{6,0},{7,1},{8,14},{9,15},{10,... | collective-permute-start | bytes 491528 | tf_op jit(solution)/shard_map/ppermute | solution.py:170
  299.6 8.5 %collective-permute-start.65 = (bf16[128,768]{1,0:T(8,128)(2,1)S(1)}, bf16[128,768]{1,0:T(8,128)(2,1)S(1)}, u32[]{:S(2)}, u32[]{:S(2)}) collective-permute-start(bf16[128,768]{1,0:T(8,128)(2,1)S(1)} %collective-permute-done.62.refs_6_), channel_id=1, source_target_pairs={{0,1},{1,0},{2,3},{3,2},{4,5},{5,4},{6,7},{7,6},{8,9},{9,8},{10,11... | collective-permute-start | bytes 589832 | tf_op jit(solution)/shard_map/ppermute | solution.py:175
  299.6 8.5 %collective-permute-start.66 = (bf16[128,768]{1,0:T(8,128)(2,1)S(1)}, bf16[128,768]{1,0:T(8,128)(2,1)S(1)}, u32[]{:S(2)}, u32[]{:S(2)}) collective-permute-start(bf16[128,768]{1,0:T(8,128)(2,1)S(1)} %collective-permute-done.63.refs_7_), channel_id=1, source_target_pairs={{0,1},{1,0},{2,3},{3,2},{4,5},{5,4},{6,7},{7,6},{8,9},{9,8},{10,11... | collective-permute-start | bytes 589832 | tf_op jit(solution)/shard_map/ppermute | solution.py:175
  300.2 8.0 %collective-permute-start.67 = (bf16[128,768]{1,0:T(8,128)(2,1)S(1)}, bf16[128,768]{1,0:T(8,128)(2,1)S(1)}, u32[]{:S(2)}, u32[]{:S(2)}) collective-permute-start(bf16[128,768]{1,0:T(8,128)(2,1)S(1)} %collective-permute-done.64.refs_8_), channel_id=1, source_target_pairs={{0,1},{1,0},{2,3},{3,2},{4,5},{5,4},{6,7},{7,6},{8,9},{9,8},{10,11... | collective-permute-start | bytes 589832 | tf_op jit(solution)/shard_map/ppermute | solution.py:175
  (36 other events, 272.0 us)

commit v5 on v4

--- a/solution.py
+++ b/solution.py
@@ -347,17 +347,44 @@
         values = jnp.concatenate([near_ref[...], far_ref[...]], axis=0)
         total = total + times_transposed(half_ref[...], values)
     block = total.astype(jnp.bfloat16)
-    for step, out_ref in enumerate(refs[3 * terms :]):
+    slot_refs, outs = refs[3 * terms : 3 * terms + 2], refs[3 * terms + 2 :]
+    count, width = block.shape
+    for step, out_ref in enumerate(outs):
 
         @pl.when(pl.program_id(0) == step)
         def _():
-            out_ref[...] = block
-
-
-def spread(base, terms):
-    arrays = [base] + [array for term in terms for array in term]
+            out_ref[:count, :] = block
+            for part, (row, column, slots) in enumerate(slot_tiles(slot_refs[0], width)):
+                slot_ref = slot_refs[part % CORES]
+                out_ref[pl.ds(count + row, slots), :] = slot_ref[
+                    step * slots : (step + 1) * slots, column : column + width
+                ]
+
+
+def slot_tiles(slot_ref, width):
+    slots = slot_ref.shape[0] // CHIPS
+    groups = slot_ref.shape[1] // width
+    return [
+        ((CORES * group + side) * slots, group * width, slots)
+        for group in range(groups)
+        for side in range(CORES)
+    ]
+
+
+def under_block(block, own, theirs, step):
+    width = block.shape[1]
+    parts = [
+        (own, theirs)[part % CORES][step * slots : (step + 1) * slots, column : column + width]
+        for part, (_, column, slots) in enumerate(slot_tiles(own, width))
+    ]
+    return jnp.concatenate([block, *parts], axis=0)
+
+
+def spread(base, terms, own_slots, their_slots):
+    arrays = [base] + [array for term in terms for array in term] + [own_slots, their_slots]
     height, width = base.shape
     count = height // CHIPS
+    tall = count + CORES * own_slots.size // (CHIPS * width)
 
     def rows(columns):
         return pl.BlockSpec((count, columns), lambda step: (step, 0))
@@ -368,6 +395,7 @@
     specs = [rows(width)]
     for half, near, far in terms:
         specs += [rows(half.shape[1]), whole(near), whole(far)]
+    specs += [whole(own_slots), whole(their_slots)]
 
     def body(*refs):
         spread_kernel(len(terms), *refs)
@@ -376,9 +404,9 @@
         body,
         name="spread",
         grid=(CHIPS,),
-        out_shape=[jax.ShapeDtypeStruct((count, width), jnp.bfloat16)] * CHIPS,
+        out_shape=[jax.ShapeDtypeStruct((tall, width), jnp.bfloat16)] * CHIPS,
         in_specs=specs,
-        out_specs=[pl.BlockSpec((count, width), lambda step: (0, 0))] * CHIPS,
+        out_specs=[pl.BlockSpec((tall, width), lambda step: (0, 0))] * CHIPS,
         compiler_params=pltpu.CompilerParams(vmem_limit_bytes=ROOM),
         cost_estimate=pl.CostEstimate(
             flops=2 * height * width * terms[0][0].shape[1] * len(terms),
@@ -388,35 +416,53 @@
     )(*arrays)
 
 
-def pair_products(block_ref, near_ref, far_ref):
-    return dot(block_ref[...], jnp.concatenate([near_ref[...], far_ref[...]], axis=0))
-
-
-def factor_kernel(start, *refs):
-    total_ref = refs[-1]
-    total = refs[0][...] if start else None
-    refs = refs[1:-1] if start else refs[:-1]
+def pair_products(block_ref, count, near_ref, far_ref):
+    return dot(block_ref[:count, :], jnp.concatenate([near_ref[...], far_ref[...]], axis=0))
+
+
+def block_products(count, refs):
+    total = None
     for step in range(CHIPS):
-        term = pair_products(refs[step], refs[CHIPS + step], refs[2 * CHIPS + step])
+        term = pair_products(refs[step], count, refs[CHIPS + step], refs[2 * CHIPS + step])
         total = term if total is None else total + term
-    total_ref[...] = total
-
-
-def factor_rows(total, blocks, pieces):
-    arrays = ([] if total is None else [total]) + blocks + pieces
-    count, ranks = blocks[0].shape[0], pieces[0].shape[1]
-
-    def body(*refs):
-        factor_kernel(total is not None, *refs)
-
+    return total
+
+
+def token_kernel(*refs):
+    refs[-1][...] = block_products(refs[-1].shape[0], refs[:-1])
+
+
+def last_kernel(*refs):
+    token_refs, refs = refs[:CHIPS], refs[CHIPS:]
+    total_ref, product_refs = refs[0], refs[1:-2]
+    share_ref, core_ref = refs[-2:]
+    count = share_ref.shape[0]
+    share_ref[...] = total_ref[...] + block_products(count, product_refs)
+    width = token_refs[0].shape[1]
+    slots = (token_refs[0].shape[0] - count) * width // core_ref.shape[0]
+
+    def group(block_refs, column):
+        start = count + column * slots
+        return jnp.concatenate([ref[start : start + slots, :] for ref in block_refs], axis=0)
+
+    groups = core_ref.shape[0] // width
+    for left in range(groups):
+        for right in range(groups):
+            product = dot_first(group(token_refs, left), group(product_refs[:CHIPS], right))
+            core_ref[
+                left * width : (left + 1) * width, right * width : (right + 1) * width
+            ] = product.astype(jnp.bfloat16)
+
+
+def block_call(body, outs, arrays, flops):
     return pl.pallas_call(
         body,
-        out_shape=jax.ShapeDtypeStruct((count, ranks), jnp.float32),
+        out_shape=outs,
         in_specs=[pl.BlockSpec(memory_space=pltpu.VMEM)] * len(arrays),
-        out_specs=pl.BlockSpec(memory_space=pltpu.VMEM),
+        out_specs=[pl.BlockSpec(memory_space=pltpu.VMEM)] * len(outs),
         compiler_params=pltpu.CompilerParams(vmem_limit_bytes=ROOM),
         cost_estimate=pl.CostEstimate(
-            flops=2 * count * ranks * len(pieces) * pieces[0].shape[0],
+            flops=flops,
             bytes_accessed=sum(array.size * array.dtype.itemsize for array in arrays),
             transcendentals=0,
         ),
@@ -470,14 +516,7 @@
     def to_slots(values):
         held = dot(picks, values).astype(bf16)
         half = CHIPS * slots
-        own, theirs = held[:half], swap_cores(held[half:])
-        return [
-            jnp.concatenate([part[step * slots : (step + 1) * slots] for part in (own, theirs)])
-            for step in range(CHIPS)
-        ]
-
-    def to_experts(parts):
-        return parts[:1] + [across_chips(parts[step], step) for step in range(1, CHIPS)]
+        return held[:half], swap_cores(held[half:])
 
     step_cross = between_layers(step_two, two_cross)
     step_late = between_layers(step_down, down_cross)
@@ -488,7 +527,11 @@
     own_score = both_cores(dot_first(difference, own_half))
     turned = chip_columns(turned, chip, core)
     token_blocks = [
-        turned[step * channels // devices : (step + 1) * channels // devices]
+        under_block(
+            turned[step * channels // devices : (step + 1) * channels // devices],
+            *proj_slots,
+            step,
+        )
         for step in range(CHIPS)
     ]
     down_gram = gram_sum(gram_pair(half_down, own_half))
@@ -561,7 +604,6 @@
     second_cross = between_layers(chain, [(2, 1)])
     second_two = between_layers(chain, [(2, 0)])
     first_three = between_layers(after(chain_first, chain), [(3, 0)])
-    proj_slots = to_experts([after(part, chain) for part in proj_slots])
     half_cross = after(half_cross, chain)
     step_cross = after(step_cross, chain)
     cross_pair = gram_pair(half_cross, own_half)
@@ -590,6 +632,7 @@
         return values, swap_cores(values)
 
     proj_rows = gather_rows(grad_proj)
+    grad_slots = to_slots(grad_pre)
     scaled_pair = with_swap(after(scaled, grad_proj))
     two_pair = with_swap(first_two + after(second_two, grad_proj))
     cross_pair = with_swap(after(second_cross, grad_proj))
@@ -604,19 +647,24 @@
             (half_late, *late_pair),
             (half_down, *down_pair),
         ],
+        *grad_slots,
     )
     mixed_first = mixed_blocks[0]
     scaled_rows = [after(rows, mixed_first) for rows in scaled_rows]
     mixed_blocks = list(mixed_blocks[:1]) + [
         across_chips(mixed_blocks[step], step) for step in range(1, CHIPS)
     ]
-    grad_slots = to_slots(after(grad_pre, mixed_first))
-    grad_slots = to_experts(grad_slots)
     scaled_rows = scaled_rows + [scaled_pair[1]] + [swap_cores(rows) for rows in scaled_rows[1:]]
-    share = factor_rows(None, token_blocks, proj_rows)
-    core_total = dot_first(jnp.concatenate(proj_slots), jnp.concatenate(grad_slots)).astype(bf16)
-    share = factor_rows(after(share, core_total), mixed_blocks, scaled_rows)
-    return (share[None], core_total[None, None])
+    share = jax.ShapeDtypeStruct((channels // devices, ranks), f32)
+    share_flops = 2 * channels * rows * ranks
+    token_share = block_call(token_kernel, [share], token_blocks + proj_rows, share_flops)
+    factor_share, core_total = block_call(
+        last_kernel,
+        [share, jax.ShapeDtypeStruct((ranks, ranks), bf16)],
+        [*token_blocks, *token_share, *mixed_blocks, *scaled_rows],
+        share_flops,
+    )
+    return (factor_share[None], core_total[None, None])
 
 
 def solution(mesh):
@@ -633,7 +681,9 @@
 
     def per_device(*arrays):
         local_experts = arrays[-1].shape[1]
-        if (mesh.shape["section"], mesh.shape["expert"]) == drawn_for and local_experts == 1:
+        ranks, width = arrays[-1].shape[-1], CORES * arrays[3].shape[1] * arrays[3].shape[2]
+        fits = local_experts == 1 and ranks % width == 0
+        if (mesh.shape["section"], mesh.shape["expert"]) == drawn_for and fits:
             return gathered_plan(*arrays)
         return general_plan(*arrays)
 

time: 311 us -> 291 us (0.936)
  waiting for transfers between devices: 179 us -> 163 us
  starting transfers between devices: 66.7 us -> 54.5 us
    ppermute x14, waiting for transfers between devices: 114 us -> 98.1 us  [between_layers(): return lax.ppermute(value, 'section', pairs)]
    ppermute x23 -> x17, starting transfers between devices: 38.4 us -> 25.8 us  [on_chips(): return lax.ppermute(value, 'expert', perm)]
    ppermute x23 -> x17, waiting for transfers between devices: 62.8 us -> 63.5 us  [on_chips(): return lax.ppermute(value, 'expert', perm)]
    dot_general x10 -> x9, matrix products: 16.3 us -> 16.9 us  [dot_first(): lax.dot_general(left, right, (((0,), (0,)), ((), ())), preferred_element_...]
  transfers between devices with their start and end apart: 68 -> 62, of which waited for: 21 -> 19; matrix products, arithmetic and copies ran while one was open for 10% -> 11% of each run, Pallas kernels for 9% -> 9%
where the time goes in v5:
time: 291 us; the launch traced here: 288 us
  waiting for transfers between devices  163 us (56%)
  starting transfers between devices  54.5 us (19%)
  Pallas kernels  28.5 us (10%)
  matrix products  20.4 us (7%)
  local copies, waits for them, and re-layouts  10.7 us (4%)
  other arithmetic  8.58 us (3%)
    ppermute x14, waiting for transfers between devices, between_layers(): return lax.ppermute(value, 'section', pairs)  98.1 us
    ppermute x17, waiting for transfers between devices, on_chips(): return lax.ppermute(value, 'expert', perm)  63.5 us
    ppermute x17, starting transfers between devices, on_chips(): return lax.ppermute(value, 'expert', perm)  25.8 us
    ppermute x14, starting transfers between devices, between_layers(): return lax.ppermute(value, 'section', pairs)  22.3 us
    dot_general x9, matrix products, dot_first(): lax.dot_general(left, right, (((0,), (0,)), ((), ())), preferred_element_...  16.9 us
    pallas_call x3, Pallas kernels, call_rows(): pl.pallas_call(body, out_shape=[jax.ShapeDtypeStruct(shape, kind) for sha...  12.2 us
    pallas_call x2, Pallas kernels, core_call(): pl.pallas_call(body, out_shape=outs, in_specs=[pl.BlockSpec(memory_space=...  8.38 us
    ppermute x31, starting transfers between devices, swap_cores(): lax.ppermute(value, 'expert', [(index, index ^ 1) for index in range(coun...  6.48 us
  transfers between devices with their start and end apart: 62, of which 19 were waited for; matrix products, arithmetic and copies ran while one was open for 11% of the time, Pallas kernels for 9%

profile of v5, /device:TPU:0, one launch (start us, length us, event | category | flops | bytes accessed | tf_op | source)
XLA Modules:
  0.0 287.8 jit_solution(444930372946984500)
XLA Ops:
  2.2 3.0 %fusion.2.proj_ref = bf16[128,768]{1,0:T(8,128)(2,1)S(1)} fusion(bf16[128,2560]{1,0:T(8,128)(2,1)} %bitcast.47, bf16[1,2560,768]{2,1,0:T(8,128)(2,1)} %param.12), kind=kOutput, calls=%fused_computation.18 | convolution fusion | flops 503414784 | bytes 4784128 | tf_op jit(solution)/shard_map/dot_general | solution.py:155
  10.5 3.0 %collective-permute-start.3 = (bf16[768,768]{1,0:T(8,128)(2,1)S(1)}, bf16[768,768]{1,0:T(8,128)(2,1)}, u32[]{:S(2)}, u32[]{:S(2)}) collective-permute-start(bf16[768,768]{1,0:T(8,128)(2,1)S(1)} %bitcast.41), channel_id=1, source_target_pairs={{0,2},{1,3},{2,0},{3,1},{4,6},{5,7},{6,4},{7,5},{8,10},{9,11},{10,... | collective-permute-start | bytes 3538952 | tf_op jit(solution)/shard_map/ppermute | solution.py:170
  13.5 1.6 dynamic-slice_bitcast_fusion.3
  15.4 1.3 collective-permute-start.19
  18.3 1.3 collective-permute-start.24
  19.6 1.3 collective-permute-start.28
  21.0 12.8 %collective-permute-done.19 = bf16[1280,256]{1,0:T(8,128)(2,1)} collective-permute-done((bf16[1280,256]{1,0:T(8,128)(2,1)S(1)}, bf16[1280,256]{1,0:T(8,128)(2,1)}, u32[]{:S(2)}, u32[]{:S(2)}) %collective-permute-start.19) | collective-permute-done | bytes 655392 | tf_op jit(solution)/shard_map/ppermute | solution.py:179
  33.8 2.8 convolution_convert_fusion.4
  36.5 1.3 collective-permute-done.24
  37.8 2.0 collective-permute-done.3.refs_2_
  39.8 1.8 collective-permute-start.9
  41.6 1.0 copy-done.1
  42.6 1.3 collective-permute-start.22
  43.9 1.8 fusion.17
  45.7 0.9 slice.201
  47.6 1.3 collective-permute-done.20
  48.8 1.3 collective-permute-start.6
  50.1 1.3 collective-permute-start.10
  51.5 1.3 pad_maximum_fusion.1
  52.8 26.8 %collective-permute-done.28.refs_4_ = bf16[1280,768]{1,0:T(8,128)(2,1)} collective-permute-done((bf16[1280,768]{1,0:T(8,128)(2,1)S(1)}, bf16[1280,768]{1,0:T(8,128)(2,1)}, u32[]{:S(2)}, u32[]{:S(2)}) %collective-permute-start.28) | collective-permute-done | bytes 1966112 | tf_op jit(solution)/shard_map/ppermute | solution.py:179
  79.6 0.8 constant_dynamic-update-slice_fusion.22
  80.5 8.5 %collective-permute-done.22.refs_13_ = bf16[1280,768]{1,0:T(8,128)(2,1)} collective-permute-done((bf16[1280,768]{1,0:T(8,128)(2,1)S(1)}, bf16[1280,768]{1,0:T(8,128)(2,1)}, u32[]{:S(2)}, u32[]{:S(2)}) %collective-permute-start.22) | collective-permute-done | bytes 1966112 | tf_op jit(solution)/shard_map/ppermute | solution.py:179
  89.0 1.5 collective-permute-start.31
  91.0 18.7 %collective-permute-done.10.refs_7_ = bf16[768,768]{1,0:T(8,128)(2,1)S(1)} collective-permute-done((bf16[768,768]{1,0:T(8,128)(2,1)}, bf16[768,768]{1,0:T(8,128)(2,1)S(1)}, u32[]{:S(2)}, u32[]{:S(2)}) %collective-permute-start.10) | collective-permute-done | bytes 1179680 | tf_op jit(solution)/shard_map/ppermute | solution.py:170
  109.7 3.3 %convolution_convert_fusion.3 = bf16[768,768]{1,0:T(8,128)(2,1)S(1)} fusion(bf16[1280,768]{1,0:T(8,128)(2,1)} %collective-permute-done.22.refs_13_, bf16[1280,768]{1,0:T(8,128)(2,1)S(1)} %pad_maximum_fusion.refs_1_), kind=kOutput, calls=%fused_computation.11 | convolution fusion | flops 1510539264 | bytes 5111808 | tf_op jit(solution)/shard_map/dot_general | solution.py:159
  113.6 1.9 add_convert_fusion.4.refs_11_
  115.5 1.1 slice_add_fusion.2.refs_4_
  116.6 3.4 %convolution_convert_fusion.2 = bf16[768,768]{1,0:T(8,128)(2,1)S(1)} fusion(bf16[1280,768]{1,0:T(8,128)(2,1)} %collective-permute-done.28.refs_4_, bf16[1280,768]{1,0:T(8,128)(2,1)S(1)} %pad_maximum_fusion.refs_1_), kind=kOutput, calls=%fused_computation.10 | convolution fusion | flops 1510539264 | bytes 5111808 | tf_op jit(solution)/shard_map/dot_general | solution.py:159
  120.1 6.7 %collective-permute-start.25 = (bf16[1280,256]{1,0:T(8,128)(2,1)S(1)}, bf16[1280,256]{1,0:T(8,128)(2,1)S(1)}, u32[]{:S(2)}, u32[]{:S(2)}) collective-permute-start(bf16[1280,256]{1,0:T(8,128)(2,1)S(1)} %copy-done.18), channel_id=1, source_target_pairs={{0,8},{1,9},{2,10},{3,11},{4,12},{5,13},{6,14},{7,15}} | collective-permute-start | bytes 1966088 | tf_op jit(solution)/shard_map/ppermute | solution.py:179
  126.8 3.5 %shard_map.86 = (f32[128,768]{1,0:T(8,128)S(1)}, bf16[768,768]{1,0:T(8,128)(2,1)S(1)}, bf16[768,768]{1,0:T(8,128)(2,1)S(1)}, bf16[768,768]{1,0:T(8,128)(2,1)S(1)...) custom-call(s32[1]{0:T(128)} %bitcast.3.middle_ref, ...), custom_call_target="tpu_custom_call" | custom-call | flops 905969664 | bytes 7077888 | tf_op jit(solution)/shard_map/pallas_call | solution.py:548
  130.4 1.3 collective-permute-start.37
  131.7 4.8 %shard_map.87 = (bf16[128,768]{1,0:T(8,128)(2,1)S(1)}, f32[128,768]{1,0:T(8,128)S(1)}, f32[128,768]{1,0:T(8,128)S(1)}, bf16[128,768]{1,0:T(8,128)(2,1)S(1)}, bf1...) custom-call(s32[1]{0:T(128)} %bitcast.3.middle_ref, bf16[128,768]{1,0:T(8,128)(2,1)S(1)} %fusion.2.proj_ref, ...), custom_call_target="tpu_custom_call" | custom-call | flops 1660944384 | bytes 4718592 | tf_op jit(solution)/shard_map/pallas_call | solution.py:548
  137.6 3.8 %shard_map.88 = (f32[128,768]{1,0:T(8,128)S(1)}, bf16[128,768]{1,0:T(8,128)(2,1)}, bf16[128,768]{1,0:T(8,128)(2,1)}, bf16[128,768]{1,0:T(8,128)(2,1)S(1)}) custom-call(f32[128,16]{1,0:T(8,128)S(1)} %convert_select_fusion.marks_ref.refs_0_, bf16[128,768]{1,0:T(8,128)(2,1)S(1)} %get-tuple-element.82.refs_1_.refs_2_.refs_9_, ...), custom_call_target="tpu_custom_call" | custom-call | flops 1358954496 | bytes 12197888 | tf_op jit(solution)/shard_map/pallas_call | solution.py:332
  141.3 1.8 convolution_convert_fusion.1
  143.1 2.7 collective-permute-done.25
  147.3 1.3 collective-permute-start.33
  149.6 0.9 collective-permute-start.30
  150.9 4.0 %shard_map.89 = (f32[128,768]{1,0:T(8,128)S(1)}, bf16[128,768]{1,0:T(8,128)(2,1)}, bf16[128,768]{1,0:T(8,128)(2,1)}, bf16[128,768]{1,0:T(8,128)(2,1)S(1)}) custom-call(f32[128,16]{1,0:T(8,128)S(1)} %convert_select_fusion.marks_ref.refs_0_, bf16[128,768]{1,0:T(8,128)(2,1)S(1)} %get-tuple-element.82.refs_1_.refs_2_.refs_9_, ...), custom_call_target="tpu_custom_call" | custom-call | flops 1509949440 | bytes 13574144 | tf_op jit(solution)/shard_map/pallas_call | solution.py:332
  154.9 23.3 %collective-permute-done.37.refs_10_ = bf16[1280,768]{1,0:T(8,128)(2,1)S(1)} collective-permute-done((bf16[1280,768]{1,0:T(8,128)(2,1)}, bf16[1280,768]{1,0:T(8,128)(2,1)S(1)}, u32[]{:S(2)}, u32[]{:S(2)}) %collective-permute-start.37) | collective-permute-done | bytes 1966112 | tf_op jit(solution)/shard_map/ppermute | solution.py:179
  178.2 1.8 convolution_convert_fusion
  180.1 0.8 constant_dynamic-update-slice_fusion.20
  180.8 10.9 %collective-permute-done.33 = bf16[1280,256]{1,0:T(8,128)(2,1)S(1)} collective-permute-done((bf16[1280,256]{1,0:T(8,128)(2,1)}, bf16[1280,256]{1,0:T(8,128)(2,1)S(1)}, u32[]{:S(2)}, u32[]{:S(2)}) %collective-permute-start.33) | collective-permute-done | bytes 655392 | tf_op jit(solution)/shard_map/ppermute | solution.py:179
  192.6 1.3 collective-permute-start.39
  193.9 0.8 constant_dynamic-update-slice_fusion.18
  194.7 2.9 %collective-permute-start.58 = (bf16[128,768]{1,0:T(8,128)(2,1)S(1)}, bf16[128,768]{1,0:T(8,128)(2,1)S(1)}, u32[]{:S(2)}, u32[]{:S(2)}) collective-permute-start(bf16[128,768]{1,0:T(8,128)(2,1)S(1)} %get-tuple-element.82.refs_1_.refs_2_.refs_9_), channel_id=1, source_target_pairs={{0,6},{1,7},{2,4},{3,5},{4,2},{5,3},{6,0},{7,1},{8,14},{9,15},{10,... | collective-permute-start | bytes 589832 | tf_op jit(solution)/shard_map/ppermute | solution.py:170
  197.6 4.2 %collective-permute-done.39.refs_9_ = bf16[128,768]{1,0:T(8,128)(2,1)S(1)} collective-permute-done((bf16[128,768]{1,0:T(8,128)(2,1)S(1)}, bf16[128,768]{1,0:T(8,128)(2,1)S(1)}, u32[]{:S(2)}, u32[]{:S(2)}) %collective-permute-start.39) | collective-permute-done | bytes 196640 | tf_op jit(solution)/shard_map/ppermute | solution.py:179
  201.9 1.3 collective-permute-start.35
  203.2 1.6 collective-permute-start.36
  205.1 7.5 %collective-permute-done.36.refs_7_.refs_11_ = bf16[128,768]{1,0:T(8,128)(2,1)S(1)} collective-permute-done((bf16[128,768]{1,0:T(8,128)(2,1)S(1)}, bf16[128,768]{1,0:T(8,128)(2,1)S(1)}, u32[]{:S(2)}, u32[]{:S(2)}) %collective-permute-start.36) | collective-permute-done | bytes 196640 | tf_op jit(solution)/shard_map/ppermute | solution.py:179
  212.5 1.7 collective-permute-start.16
  214.4 4.4 %shard_map.90 = (f32[128,768]{1,0:T(8,128)}, bf16[128,768]{1,0:T(8,128)(2,1)S(1)}, bf16[128,768]{1,0:T(8,128)(2,1)S(1)}, bf16[128,768]{1,0:T(8,128)(2,1)}) custom-call(f32[128,16]{1,0:T(8,128)S(1)} %convert_select_fusion.marks_ref.refs_0_, bf16[128,768]{1,0:T(8,128)(2,1)S(1)} %get-tuple-element.82.refs_1_.refs_2_.refs_9_, ...), custom_call_target="tpu_custom_call" | custom-call | flops 1660944384 | bytes 14950400 | tf_op jit(solution)/shard_map/pallas_call | solution.py:332
  219.8 3.3 %collective-permute-start.17 = (bf16[512,256]{1,0:T(8,128)(2,1)S(1)}, bf16[512,256]{1,0:T(8,128)(2,1)S(1)}, u32[]{:S(2)}, u32[]{:S(2)}) collective-permute-start(bf16[512,256]{1,0:T(8,128)(2,1)S(1)} %get-tuple-element.54), channel_id=1, source_target_pairs={{0,4},{1,5},{2,6},{3,7},{4,0},{5,1},{6,2},{7,3},{8,12},{9,13},{10,... | collective-permute-start | bytes 786440 | tf_op jit(solution)/shard_map/ppermute | solution.py:170
  223.0 0.9 collective-permute-start.18
  224.6 1.4 add_convert_fusion.5.refs_0_
  226.0 3.0 %collective-permute-start.42 = (bf16[128,768]{1,0:T(8,128)(2,1)S(1)}, bf16[128,768]{1,0:T(8,128)(2,1)S(1)}, u32[]{:S(2)}, u32[]{:S(2)}) collective-permute-start(bf16[128,768]{1,0:T(8,128)(2,1)S(1)} %get-tuple-element.70.refs_4_), channel_id=1, source_target_pairs={{0,6},{1,7},{2,4},{3,5},{4,2},{5,3},{6,0},{7,1},{8,14},{9,15},{10,... | collective-permute-start | bytes 589832 | tf_op jit(solution)/shard_map/ppermute | solution.py:170
  229.0 1.5 collective-permute-start.40
  230.5 5.1 %spread.1 = (bf16[512,256]{1,0:T(8,128)(2,1)S(1)}, bf16[512,256]{1,0:T(8,128)(2,1)S(1)}, bf16[512,256]{1,0:T(8,128)(2,1)S(1)}, bf16[512,256]{1,0:T(8,128)(2,1)S(1)}) custom-call(bf16[1280,256]{1,0:T(8,128)(2,1)S(1)} %add_convert_fusion.5.refs_0_, bf16[1280,768]{1,0:T(8,128)(2,1)S(1)} %pad_maximum_fusion.refs_1_, ...), custom_call_target="tpu_custom_call" | custom-call | flops 2516582400 | bytes 12845056 | tf_op jit(solution)/shard_map/spread/pallas_call | solution.py:403
  235.6 14.3 %collective-permute-done.17.refs_2_ = bf16[512,256]{1,0:T(8,128)(2,1)S(1)} collective-permute-done((bf16[512,256]{1,0:T(8,128)(2,1)S(1)}, bf16[512,256]{1,0:T(8,128)(2,1)S(1)}, u32[]{:S(2)}, u32[]{:S(2)}) %collective-permute-start.17) | collective-permute-done | bytes 262176 | tf_op jit(solution)/shard_map/ppermute | solution.py:170
  250.5 13.2 %collective-permute-done.41.refs_6_ = bf16[128,768]{1,0:T(8,128)(2,1)S(1)} collective-permute-done((bf16[128,768]{1,0:T(8,128)(2,1)S(1)}, bf16[128,768]{1,0:T(8,128)(2,1)S(1)}, u32[]{:S(2)}, u32[]{:S(2)}) %collective-permute-start.41) | collective-permute-done | bytes 196640 | tf_op jit(solution)/shard_map/ppermute | solution.py:170
  264.2 2.9 %collective-permute-start.54 = (bf16[512,256]{1,0:T(8,128)(2,1)S(1)}, bf16[512,256]{1,0:T(8,128)(2,1)S(1)}, u32[]{:S(2)}, u32[]{:S(2)}) collective-permute-start(bf16[512,256]{1,0:T(8,128)(2,1)S(1)} %get-tuple-element.79), channel_id=1, source_target_pairs={{0,4},{1,5},{2,6},{3,7},{4,0},{5,1},{6,2},{7,3},{8,12},{9,13},{10,... | collective-permute-start | bytes 786440 | tf_op jit(solution)/shard_map/ppermute | solution.py:170
  267.1 1.5 collective-permute-start.55
  270.3 7.2 %collective-permute-done.53.refs_6_ = bf16[512,256]{1,0:T(8,128)(2,1)S(1)} collective-permute-done((bf16[512,256]{1,0:T(8,128)(2,1)S(1)}, bf16[512,256]{1,0:T(8,128)(2,1)S(1)}, u32[]{:S(2)}, u32[]{:S(2)}) %collective-permute-start.53) | collective-permute-done | bytes 262176 | tf_op jit(solution)/shard_map/ppermute | solution.py:170
  277.5 8.1 %collective-permute-done.54.refs_7_ = bf16[512,256]{1,0:T(8,128)(2,1)S(1)} collective-permute-done((bf16[512,256]{1,0:T(8,128)(2,1)S(1)}, bf16[512,256]{1,0:T(8,128)(2,1)S(1)}, u32[]{:S(2)}, u32[]{:S(2)}) %collective-permute-start.54) | collective-permute-done | bytes 262176 | tf_op jit(solution)/shard_map/ppermute | solution.py:170
  285.6 2.2 shard_map.92
  (168 shorter events, 20.4 us)
Async XLA Ops:
  6.2 11.3 %collective-permute-start.1 = (bf16[128,768]{1,0:T(8,128)(2,1)}, bf16[128,768]{1,0:T(8,128)(2,1)}, u32[]{:S(2)}, u32[]{:S(2)}) collective-permute-start(bf16[128,768]{1,0:T(8,128)(2,1)} %slice.171), channel_id=1, source_target_pairs={{0,1},{1,0},{2,3},{3,2},{4,5},{5,4},{6,7},{7,6},{8,9},{9,8},{10,11... | collective-permute-start | bytes 589832 | tf_op jit(solution)/shard_map/ppermute | solution.py:175
  8.6 9.7 %collective-permute-start = (bf16[1280,128]{1,0:T(8,128)(2,1)}, bf16[1280,128]{1,0:T(8,128)(2,1)}, u32[]{:S(2)}, u32[]{:S(2)}) collective-permute-start(bf16[1280,128]{1,0:T(8,128)(2,1)} %pad_maximum_fusion.3), channel_id=1, source_target_pairs={{0,1},{1,0},{2,3},{3,2},{4,5},{5,4},{6,7},{7,6},{8,9},{9,8},{10,11... | collective-permute-start | bytes 983048 | tf_op jit(solution)/shard_map/ppermute | solution.py:175
  9.3 6.0 %collective-permute-start.13 = (bf16[1280,128]{1,0:T(8,128)(2,1)S(1)}, bf16[1280,128]{1,0:T(8,128)(2,1)S(1)}, u32[]{:S(2)}, u32[]{:S(2)}) collective-permute-start(bf16[1280,128]{1,0:T(8,128)(2,1)S(1)} %pad_maximum_fusion.4), channel_id=1, source_target_pairs={{0,1},{1,0},{2,3},{3,2},{4,5},{5,4},{6,7},{7,6},{8,9},{9,8},{10,11... | collective-permute-start | bytes 983048 | tf_op jit(solution)/shard_map/ppermute | solution.py:175
  10.5 29.3 %collective-permute-start.3 = (bf16[768,768]{1,0:T(8,128)(2,1)S(1)}, bf16[768,768]{1,0:T(8,128)(2,1)}, u32[]{:S(2)}, u32[]{:S(2)}) collective-permute-start(bf16[768,768]{1,0:T(8,128)(2,1)S(1)} %bitcast.41), channel_id=1, source_target_pairs={{0,2},{1,3},{2,0},{3,1},{4,6},{5,7},{6,4},{7,5},{8,10},{9,11},{10,... | collective-permute-start | bytes 3538952 | tf_op jit(solution)/shard_map/ppermute | solution.py:170
  15.4 18.4 %collective-permute-start.19 = (bf16[1280,256]{1,0:T(8,128)(2,1)S(1)}, bf16[1280,256]{1,0:T(8,128)(2,1)}, u32[]{:S(2)}, u32[]{:S(2)}) collective-permute-start(bf16[1280,256]{1,0:T(8,128)(2,1)S(1)} %pad_maximum_fusion.2), channel_id=1, source_target_pairs={{24,16},{8,0},{25,17},{9,1},{26,18},{10,2},{27,19},{11,3},{28,20},... | collective-permute-start | bytes 1966088 | tf_op jit(solution)/shard_map/ppermute | solution.py:179
  17.5 2.1 collective-permute-start.14
  17.6 24.0 %collective-permute-start.5 = (bf16[768,768]{1,0:T(8,128)(2,1)S(1)}, bf16[768,768]{1,0:T(8,128)(2,1)S(1)}, u32[]{:S(2)}, u32[]{:S(2)}) collective-permute-start(bf16[768,768]{1,0:T(8,128)(2,1)S(1)} %bitcast.42), channel_id=1, source_target_pairs={{2,4},{3,5},{4,2},{5,3},{10,12},{11,13},{12,10},{13,11},{18,20},{1... | collective-permute-start | bytes 3538952 | tf_op jit(solution)/shard_map/ppermute | solution.py:170
  18.3 19.5 %collective-permute-start.24 = (bf16[1280,256]{1,0:T(8,128)(2,1)S(1)}, bf16[1280,256]{1,0:T(8,128)(2,1)S(1)}, u32[]{:S(2)}, u32[]{:S(2)}) collective-permute-start(bf16[1280,256]{1,0:T(8,128)(2,1)S(1)} %pad_maximum_fusion.2), channel_id=1, source_target_pairs={{24,8},{16,0},{25,9},{17,1},{26,10},{18,2},{27,11},{19,3},{28,12},... | collective-permute-start | bytes 1966088 | tf_op jit(solution)/shard_map/ppermute | solution.py:179
  19.6 59.9 %collective-permute-start.28 = (bf16[1280,768]{1,0:T(8,128)(2,1)S(1)}, bf16[1280,768]{1,0:T(8,128)(2,1)}, u32[]{:S(2)}, u32[]{:S(2)}) collective-permute-start(bf16[1280,768]{1,0:T(8,128)(2,1)S(1)} %pad_maximum_fusion.refs_1_), channel_id=1, source_target_pairs={{24,8},{16,0},{25,9},{17,1},{26,10},{18,2},{27,11},{19,3},{28,12},... | collective-permute-start | bytes 5898248 | tf_op jit(solution)/shard_map/ppermute | solution.py:179
  33.8 12.8 %collective-permute-start.2 = (bf16[768,768]{1,0:T(8,128)(2,1)S(1)}, bf16[768,768]{1,0:T(8,128)(2,1)}, u32[]{:S(2)}, u32[]{:S(2)}) collective-permute-start(bf16[768,768]{1,0:T(8,128)(2,1)S(1)} %bitcast.43), channel_id=1, source_target_pairs={{0,1},{1,0},{2,3},{3,2},{4,5},{5,4},{6,7},{7,6},{8,9},{9,8},{10,11... | collective-permute-start | bytes 3538952 | tf_op jit(solution)/shard_map/ppermute | solution.py:175
  37.8 9.2 %collective-permute-start.15 = (bf16[768,768]{1,0:T(8,128)(2,1)}, bf16[768,768]{1,0:T(8,128)(2,1)}, u32[]{:S(2)}, u32[]{:S(2)}) collective-permute-start(bf16[768,768]{1,0:T(8,128)(2,1)} %convolution_convert_fusion.4), channel_id=1, source_target_pairs={{0,1},{1,0},{2,3},{3,2},{4,5},{5,4},{6,7},{7,6},{8,9},{9,8},{10,11... | collective-permute-start | bytes 3538952 | tf_op jit(solution)/shard_map/ppermute | solution.py:175
  39.8 10.3 %collective-permute-start.9 = (bf16[768,768]{1,0:T(8,128)(2,1)}, bf16[768,768]{1,0:T(8,128)(2,1)}, u32[]{:S(2)}, u32[]{:S(2)}) collective-permute-start(bf16[768,768]{1,0:T(8,128)(2,1)} %collective-permute-done.3.refs_2_), channel_id=1, source_target_pairs={{2,4},{3,5},{4,2},{5,3},{10,12},{11,13},{12,10},{13,11},{18,20},{1... | collective-permute-start | bytes 3538952 | tf_op jit(solution)/shard_map/ppermute | solution.py:170
  42.6 46.4 %collective-permute-start.22 = (bf16[1280,768]{1,0:T(8,128)(2,1)S(1)}, bf16[1280,768]{1,0:T(8,128)(2,1)}, u32[]{:S(2)}, u32[]{:S(2)}) collective-permute-start(bf16[1280,768]{1,0:T(8,128)(2,1)S(1)} %pad_maximum_fusion.refs_1_), channel_id=1, source_target_pairs={{24,16},{8,0},{25,17},{9,1},{26,18},{10,2},{27,19},{11,3},{28,20},... | collective-permute-start | bytes 5898248 | tf_op jit(solution)/shard_map/ppermute | solution.py:179
  46.8 2.1 collective-permute-start.20
  47.0 43.4 %collective-permute-start.7 = (bf16[768,768]{1,0:T(8,128)(2,1)}, bf16[768,768]{1,0:T(8,128)(2,1)S(1)}, u32[]{:S(2)}, u32[]{:S(2)}) collective-permute-start(bf16[768,768]{1,0:T(8,128)(2,1)} %copy-done.1), channel_id=1, source_target_pairs={{0,1},{1,0},{2,3},{3,2},{4,5},{5,4},{6,7},{7,6},{8,9},{9,8},{10,11... | collective-permute-start | bytes 3538952 | tf_op jit(solution)/shard_map/ppermute | solution.py:175
  48.8 41.7 %collective-permute-start.6 = (bf16[768,768]{1,0:T(8,128)(2,1)}, bf16[768,768]{1,0:T(8,128)(2,1)S(1)}, u32[]{:S(2)}, u32[]{:S(2)}) collective-permute-start(bf16[768,768]{1,0:T(8,128)(2,1)} %copy-done.1), channel_id=1, source_target_pairs={{2,0},{3,1},{4,6},{5,7},{10,8},{11,9},{12,14},{13,15},{18,16},{19,... | collective-permute-start | bytes 3538952 | tf_op jit(solution)/shard_map/ppermute | solution.py:170
  50.1 59.6 %collective-permute-start.10 = (bf16[768,768]{1,0:T(8,128)(2,1)}, bf16[768,768]{1,0:T(8,128)(2,1)S(1)}, u32[]{:S(2)}, u32[]{:S(2)}) collective-permute-start(bf16[768,768]{1,0:T(8,128)(2,1)} %collective-permute-done.9.refs_6_), channel_id=1, source_target_pairs={{2,0},{3,1},{4,6},{5,7},{10,8},{11,9},{12,14},{13,15},{18,16},{19,... | collective-permute-start | bytes 3538952 | tf_op jit(solution)/shard_map/ppermute | solution.py:170
  51.4 29.0 %copy-start.11 = (f32[256,768]{1,0:T(8,128)S(1)}, f32[256,768]{1,0:T(8,128)}, u32[]{:S(2)}) copy-start(f32[256,768]{1,0:T(8,128)} %copy-done.10) | copy-start | bytes 2359300
  51.5 29.0 %copy-start.20 = (f32[128,768]{1,0:T(8,128)S(1)}, f32[128,768]{1,0:T(8,128)}, u32[]{:S(2)}) copy-start(f32[128,768]{1,0:T(8,128)} %copy-done.19) | copy-start | bytes 1179652
  79.6 33.4 %collective-permute-start.4 = (bf16[768,768]{1,0:T(8,128)(2,1)}, bf16[768,768]{1,0:T(8,128)(2,1)S(1)}, u32[]{:S(2)}, u32[]{:S(2)}) collective-permute-start(bf16[768,768]{1,0:T(8,128)(2,1)} %collective-permute-done.3.refs_2_), channel_id=1, source_target_pairs={{0,1},{1,0},{2,3},{3,2},{4,5},{5,4},{6,7},{7,6},{8,9},{9,8},{10,11... | collective-permute-start | bytes 3538952 | tf_op jit(solution)/shard_map/ppermute | solution.py:175
  89.0 52.4 %collective-permute-start.31 = (bf16[1280,768]{1,0:T(8,128)(2,1)}, bf16[1280,768]{1,0:T(8,128)(2,1)S(1)}, u32[]{:S(2)}, u32[]{:S(2)}) collective-permute-start(bf16[1280,768]{1,0:T(8,128)(2,1)} %collective-permute-done.28.refs_4_), channel_id=1, source_target_pairs={{0,8},{1,9},{2,10},{3,11},{4,12},{5,13},{6,14},{7,15}} | collective-permute-start | bytes 5898248 | tf_op jit(solution)/shard_map/ppermute | solution.py:179
  90.4 39.9 %collective-permute-start.11 = (bf16[768,768]{1,0:T(8,128)(2,1)}, bf16[768,768]{1,0:T(8,128)(2,1)S(1)}, u32[]{:S(2)}, u32[]{:S(2)}) collective-permute-start(bf16[768,768]{1,0:T(8,128)(2,1)} %collective-permute-done.9.refs_6_), channel_id=1, source_target_pairs={{0,1},{1,0},{2,3},{3,2},{4,5},{5,4},{6,7},{7,6},{8,9},{9,8},{10,11... | collective-permute-start | bytes 3538952 | tf_op jit(solution)/shard_map/ppermute | solution.py:175
  90.5 29.5 %collective-permute-start.8 = (bf16[768,768]{1,0:T(8,128)(2,1)S(1)}, bf16[768,768]{1,0:T(8,128)(2,1)S(1)}, u32[]{:S(2)}, u32[]{:S(2)}) collective-permute-start(bf16[768,768]{1,0:T(8,128)(2,1)S(1)} %collective-permute-done.6.refs_5_), channel_id=1, source_target_pairs={{0,1},{1,0},{2,3},{3,2},{4,5},{5,4},{6,7},{7,6},{8,9},{9,8},{10,11... | collective-permute-start | bytes 3538952 | tf_op jit(solution)/shard_map/ppermute | solution.py:175
  109.7 20.7 %collective-permute-start.12 = (bf16[768,768]{1,0:T(8,128)(2,1)S(1)}, bf16[768,768]{1,0:T(8,128)(2,1)S(1)}, u32[]{:S(2)}, u32[]{:S(2)}) collective-permute-start(bf16[768,768]{1,0:T(8,128)(2,1)S(1)} %collective-permute-done.10.refs_7_), channel_id=1, source_target_pairs={{0,1},{1,0},{2,3},{3,2},{4,5},{5,4},{6,7},{7,6},{8,9},{9,8},{10,11... | collective-permute-start | bytes 3538952 | tf_op jit(solution)/shard_map/ppermute | solution.py:175
  113.0 23.5 %collective-permute-start.23 = (bf16[768,768]{1,0:T(8,128)(2,1)S(1)}, bf16[768,768]{1,0:T(8,128)(2,1)S(1)}, u32[]{:S(2)}, u32[]{:S(2)}) collective-permute-start(bf16[768,768]{1,0:T(8,128)(2,1)S(1)} %convolution_convert_fusion.3), channel_id=1, source_target_pairs={{0,1},{1,0},{2,3},{3,2},{4,5},{5,4},{6,7},{7,6},{8,9},{9,8},{10,11... | collective-permute-start | bytes 3538952 | tf_op jit(solution)/shard_map/ppermute | solution.py:175
  120.1 25.7 %collective-permute-start.25 = (bf16[1280,256]{1,0:T(8,128)(2,1)S(1)}, bf16[1280,256]{1,0:T(8,128)(2,1)S(1)}, u32[]{:S(2)}, u32[]{:S(2)}) collective-permute-start(bf16[1280,256]{1,0:T(8,128)(2,1)S(1)} %copy-done.18), channel_id=1, source_target_pairs={{0,8},{1,9},{2,10},{3,11},{4,12},{5,13},{6,14},{7,15}} | collective-permute-start | bytes 1966088 | tf_op jit(solution)/shard_map/ppermute | solution.py:179
  130.3 18.2 %collective-permute-start.29 = (bf16[768,768]{1,0:T(8,128)(2,1)S(1)}, bf16[768,768]{1,0:T(8,128)(2,1)S(1)}, u32[]{:S(2)}, u32[]{:S(2)}) collective-permute-start(bf16[768,768]{1,0:T(8,128)(2,1)S(1)} %convolution_convert_fusion.2), channel_id=1, source_target_pairs={{0,1},{1,0},{2,3},{3,2},{4,5},{5,4},{6,7},{7,6},{8,9},{9,8},{10,11... | collective-permute-start | bytes 3538952 | tf_op jit(solution)/shard_map/ppermute | solution.py:175
  130.4 47.8 %collective-permute-start.37 = (bf16[1280,768]{1,0:T(8,128)(2,1)}, bf16[1280,768]{1,0:T(8,128)(2,1)S(1)}, u32[]{:S(2)}, u32[]{:S(2)}) collective-permute-start(bf16[1280,768]{1,0:T(8,128)(2,1)} %collective-permute-done.22.refs_13_), channel_id=1, source_target_pairs={{16,0},{17,1},{18,2},{19,3},{20,4},{21,5},{22,6},{23,7}} | collective-permute-start | bytes 5898248 | tf_op jit(solution)/shard_map/ppermute | solution.py:179
  136.6 1.0 collective-permute-start.21
  145.8 4.7 %collective-permute-start.32 = (bf16[768,768]{1,0:T(8,128)(2,1)S(1)}, bf16[768,768]{1,0:T(8,128)(2,1)S(1)}, u32[]{:S(2)}, u32[]{:S(2)}) collective-permute-start(bf16[768,768]{1,0:T(8,128)(2,1)S(1)} %convolution_convert_fusion.1), channel_id=1, source_target_pairs={{0,1},{1,0},{2,3},{3,2},{4,5},{5,4},{6,7},{7,6},{8,9},{9,8},{10,11... | collective-permute-start | bytes 3538952 | tf_op jit(solution)/shard_map/ppermute | solution.py:175
  146.7 2.9 collective-permute-start.26
  147.3 44.5 %collective-permute-start.33 = (bf16[1280,256]{1,0:T(8,128)(2,1)}, bf16[1280,256]{1,0:T(8,128)(2,1)S(1)}, u32[]{:S(2)}, u32[]{:S(2)}) collective-permute-start(bf16[1280,256]{1,0:T(8,128)(2,1)} %collective-permute-done.19), channel_id=1, source_target_pairs={{16,0},{17,1},{18,2},{19,3},{20,4},{21,5},{22,6},{23,7}} | collective-permute-start | bytes 1966088 | tf_op jit(solution)/shard_map/ppermute | solution.py:179
  148.9 2.0 collective-permute-start.27
  149.6 1.3 collective-permute-start.30
  180.0 23.2 %collective-permute-start.38 = (bf16[768,768]{1,0:T(8,128)(2,1)S(1)}, bf16[768,768]{1,0:T(8,128)(2,1)S(1)}, u32[]{:S(2)}, u32[]{:S(2)}) collective-permute-start(bf16[768,768]{1,0:T(8,128)(2,1)S(1)} %convolution_convert_fusion), channel_id=1, source_target_pairs={{0,1},{1,0},{2,3},{3,2},{4,5},{5,4},{6,7},{7,6},{8,9},{9,8},{10,11... | collective-permute-start | bytes 3538952 | tf_op jit(solution)/shard_map/ppermute | solution.py:175
  192.5 9.3 %collective-permute-start.34 = (f32[128,768]{1,0:T(8,128)S(1)}, f32[128,768]{1,0:T(8,128)S(1)}, u32[]{:S(2)}, u32[]{:S(2)}) collective-permute-start(f32[128,768]{1,0:T(8,128)S(1)} %slice.205), channel_id=1, source_target_pairs={{0,1},{1,0},{2,3},{3,2},{4,5},{5,4},{6,7},{7,6},{8,9},{9,8},{10,11... | collective-permute-start | bytes 1179656 | tf_op jit(solution)/shard_map/ppermute | solution.py:175
  192.6 9.2 %collective-permute-start.39 = (bf16[128,768]{1,0:T(8,128)(2,1)S(1)}, bf16[128,768]{1,0:T(8,128)(2,1)S(1)}, u32[]{:S(2)}, u32[]{:S(2)}) collective-permute-start(bf16[128,768]{1,0:T(8,128)(2,1)S(1)} %get-tuple-element.66), channel_id=1, source_target_pairs={{8,0},{9,1},{10,2},{11,3},{12,4},{13,5},{14,6},{15,7}} | collective-permute-start | bytes 589832 | tf_op jit(solution)/shard_map/ppermute | solution.py:179
  194.7 24.4 %collective-permute-start.58 = (bf16[128,768]{1,0:T(8,128)(2,1)S(1)}, bf16[128,768]{1,0:T(8,128)(2,1)S(1)}, u32[]{:S(2)}, u32[]{:S(2)}) collective-permute-start(bf16[128,768]{1,0:T(8,128)(2,1)S(1)} %get-tuple-element.82.refs_1_.refs_2_.refs_9_), channel_id=1, source_target_pairs={{0,6},{1,7},{2,4},{3,5},{4,2},{5,3},{6,0},{7,1},{8,14},{9,15},{10,... | collective-permute-start | bytes 589832 | tf_op jit(solution)/shard_map/ppermute | solution.py:170
  197.6 22.0 %collective-permute-start.57 = (bf16[128,768]{1,0:T(8,128)(2,1)S(1)}, bf16[128,768]{1,0:T(8,128)(2,1)S(1)}, u32[]{:S(2)}, u32[]{:S(2)}) collective-permute-start(bf16[128,768]{1,0:T(8,128)(2,1)S(1)} %get-tuple-element.82.refs_1_.refs_2_.refs_9_), channel_id=1, source_target_pairs={{0,4},{1,5},{2,6},{3,7},{4,0},{5,1},{6,2},{7,3},{8,12},{9,13},{10,... | collective-permute-start | bytes 589832 | tf_op jit(solution)/shard_map/ppermute | solution.py:170
  201.8 18.0 %collective-permute-start.56 = (bf16[128,768]{1,0:T(8,128)(2,1)S(1)}, bf16[128,768]{1,0:T(8,128)(2,1)S(1)}, u32[]{:S(2)}, u32[]{:S(2)}) collective-permute-start(bf16[128,768]{1,0:T(8,128)(2,1)S(1)} %get-tuple-element.82.refs_1_.refs_2_.refs_9_), channel_id=1, source_target_pairs={{0,2},{1,3},{2,0},{3,1},{4,6},{5,7},{6,4},{7,5},{8,10},{9,11},{10,... | collective-permute-start | bytes 589832 | tf_op jit(solution)/shard_map/ppermute | solution.py:170
  201.9 12.5 %collective-permute-start.35 = (bf16[128,768]{1,0:T(8,128)(2,1)S(1)}, bf16[128,768]{1,0:T(8,128)(2,1)S(1)}, u32[]{:S(2)}, u32[]{:S(2)}) collective-permute-start(bf16[128,768]{1,0:T(8,128)(2,1)S(1)} %get-tuple-element.62), channel_id=1, source_target_pairs={{16,0},{17,1},{18,2},{19,3},{20,4},{21,5},{22,6},{23,7}} | collective-permute-start | bytes 589832 | tf_op jit(solution)/shard_map/ppermute | solution.py:179
  203.2 9.3 %collective-permute-start.36 = (bf16[128,768]{1,0:T(8,128)(2,1)S(1)}, bf16[128,768]{1,0:T(8,128)(2,1)S(1)}, u32[]{:S(2)}, u32[]{:S(2)}) collective-permute-start(bf16[128,768]{1,0:T(8,128)(2,1)S(1)} %get-tuple-element.68), channel_id=1, source_target_pairs={{24,0},{25,1},{26,2},{27,3},{28,4},{29,5},{30,6},{31,7}} | collective-permute-start | bytes 589832 | tf_op jit(solution)/shard_map/ppermute | solution.py:179
  212.5 10.5 %collective-permute-start.16 = (bf16[512,256]{1,0:T(8,128)(2,1)S(1)}, bf16[512,256]{1,0:T(8,128)(2,1)S(1)}, u32[]{:S(2)}, u32[]{:S(2)}) collective-permute-start(bf16[512,256]{1,0:T(8,128)(2,1)S(1)} %get-tuple-element.53), channel_id=1, source_target_pairs={{0,2},{1,3},{2,0},{3,1},{4,6},{5,7},{6,4},{7,5},{8,10},{9,11},{10,... | collective-permute-start | bytes 786440 | tf_op jit(solution)/shard_map/ppermute | solution.py:170
  214.4 9.6 %collective-permute-start.51 = (bf16[128,768]{1,0:T(8,128)(2,1)S(1)}, bf16[128,768]{1,0:T(8,128)(2,1)S(1)}, u32[]{:S(2)}, u32[]{:S(2)}) collective-permute-start(bf16[128,768]{1,0:T(8,128)(2,1)S(1)} %add.239.refs_14_), channel_id=1, source_target_pairs={{0,1},{1,0},{2,3},{3,2},{4,5},{5,4},{6,7},{7,6},{8,9},{9,8},{10,11... | collective-permute-start | bytes 589832 | tf_op jit(solution)/shard_map/ppermute | solution.py:175
  219.1 4.9 %collective-permute-start.52 = (bf16[128,768]{1,0:T(8,128)(2,1)S(1)}, bf16[128,768]{1,0:T(8,128)(2,1)S(1)}, u32[]{:S(2)}, u32[]{:S(2)}) collective-permute-start(bf16[128,768]{1,0:T(8,128)(2,1)S(1)} %get-tuple-element.112), channel_id=1, source_target_pairs={{0,1},{1,0},{2,3},{3,2},{4,5},{5,4},{6,7},{7,6},{8,9},{9,8},{10,11... | collective-permute-start | bytes 589832 | tf_op jit(solution)/shard_map/ppermute | solution.py:175
  219.6 4.8 %collective-permute-start.47 = (bf16[128,768]{1,0:T(8,128)(2,1)S(1)}, bf16[128,768]{1,0:T(8,128)(2,1)S(1)}, u32[]{:S(2)}, u32[]{:S(2)}) collective-permute-start(bf16[128,768]{1,0:T(8,128)(2,1)S(1)} %get-tuple-element.82.refs_1_.refs_2_.refs_9_), channel_id=1, source_target_pairs={{0,1},{1,0},{2,3},{3,2},{4,5},{5,4},{6,7},{7,6},{8,9},{9,8},{10,11... | collective-permute-start | bytes 589832 | tf_op jit(solution)/shard_map/ppermute | solution.py:175
  219.8 30.1 %collective-permute-start.17 = (bf16[512,256]{1,0:T(8,128)(2,1)S(1)}, bf16[512,256]{1,0:T(8,128)(2,1)S(1)}, u32[]{:S(2)}, u32[]{:S(2)}) collective-permute-start(bf16[512,256]{1,0:T(8,128)(2,1)S(1)} %get-tuple-element.54), channel_id=1, source_target_pairs={{0,4},{1,5},{2,6},{3,7},{4,0},{5,1},{6,2},{7,3},{8,12},{9,13},{10,... | collective-permute-start | bytes 786440 | tf_op jit(solution)/shard_map/ppermute | solution.py:170
  223.0 26.9 %collective-permute-start.18 = (bf16[512,256]{1,0:T(8,128)(2,1)S(1)}, bf16[512,256]{1,0:T(8,128)(2,1)S(1)}, u32[]{:S(2)}, u32[]{:S(2)}) collective-permute-start(bf16[512,256]{1,0:T(8,128)(2,1)S(1)} %get-tuple-element.55), channel_id=1, source_target_pairs={{0,6},{1,7},{2,4},{3,5},{4,2},{5,3},{6,0},{7,1},{8,14},{9,15},{10,... | collective-permute-start | bytes 786440 | tf_op jit(solution)/shard_map/ppermute | solution.py:170
  224.0 2.0 collective-permute-start.48
  224.0 5.0 %collective-permute-start.49 = (bf16[128,768]{1,0:T(8,128)(2,1)S(1)}, bf16[128,768]{1,0:T(8,128)(2,1)S(1)}, u32[]{:S(2)}, u32[]{:S(2)}) collective-permute-start(bf16[128,768]{1,0:T(8,128)(2,1)S(1)} %collective-permute-done.30.refs_7_.refs_8_), channel_id=1, source_target_pairs={{0,1},{1,0},{2,3},{3,2},{4,5},{5,4},{6,7},{7,6},{8,9},{9,8},{10,11... | collective-permute-start | bytes 589832 | tf_op jit(solution)/shard_map/ppermute | solution.py:175
  224.5 4.5 %collective-permute-start.50 = (bf16[128,768]{1,0:T(8,128)(2,1)S(1)}, bf16[128,768]{1,0:T(8,128)(2,1)S(1)}, u32[]{:S(2)}, u32[]{:S(2)}) collective-permute-start(bf16[128,768]{1,0:T(8,128)(2,1)S(1)} %collective-permute-done.36.refs_7_.refs_11_), channel_id=1, source_target_pairs={{0,1},{1,0},{2,3},{3,2},{4,5},{5,4},{6,7},{7,6},{8,9},{9,8},{10,11... | collective-permute-start | bytes 589832 | tf_op jit(solution)/shard_map/ppermute | solution.py:175
  226.0 24.4 %collective-permute-start.42 = (bf16[128,768]{1,0:T(8,128)(2,1)S(1)}, bf16[128,768]{1,0:T(8,128)(2,1)S(1)}, u32[]{:S(2)}, u32[]{:S(2)}) collective-permute-start(bf16[128,768]{1,0:T(8,128)(2,1)S(1)} %get-tuple-element.70.refs_4_), channel_id=1, source_target_pairs={{0,6},{1,7},{2,4},{3,5},{4,2},{5,3},{6,0},{7,1},{8,14},{9,15},{10,... | collective-permute-start | bytes 589832 | tf_op jit(solution)/shard_map/ppermute | solution.py:170
  229.0 34.7 %collective-permute-start.41 = (bf16[128,768]{1,0:T(8,128)(2,1)S(1)}, bf16[128,768]{1,0:T(8,128)(2,1)S(1)}, u32[]{:S(2)}, u32[]{:S(2)}) collective-permute-start(bf16[128,768]{1,0:T(8,128)(2,1)S(1)} %get-tuple-element.70.refs_4_), channel_id=1, source_target_pairs={{0,4},{1,5},{2,6},{3,7},{4,0},{5,1},{6,2},{7,3},{8,12},{9,13},{10,... | collective-permute-start | bytes 589832 | tf_op jit(solution)/shard_map/ppermute | solution.py:170
  229.0 34.7 %collective-permute-start.40 = (bf16[128,768]{1,0:T(8,128)(2,1)S(1)}, bf16[128,768]{1,0:T(8,128)(2,1)S(1)}, u32[]{:S(2)}, u32[]{:S(2)}) collective-permute-start(bf16[128,768]{1,0:T(8,128)(2,1)S(1)} %get-tuple-element.70.refs_4_), channel_id=1, source_target_pairs={{0,2},{1,3},{2,0},{3,1},{4,6},{5,7},{6,4},{7,5},{8,10},{9,11},{10,... | collective-permute-start | bytes 589832 | tf_op jit(solution)/shard_map/ppermute | solution.py:170
  249.9 14.3 %collective-permute-start.43 = (bf16[128,768]{1,0:T(8,128)(2,1)S(1)}, bf16[128,768]{1,0:T(8,128)(2,1)S(1)}, u32[]{:S(2)}, u32[]{:S(2)}) collective-permute-start(bf16[128,768]{1,0:T(8,128)(2,1)S(1)} %get-tuple-element.70.refs_4_), channel_id=1, source_target_pairs={{0,1},{1,0},{2,3},{3,2},{4,5},{5,4},{6,7},{7,6},{8,9},{9,8},{10,11... | collective-permute-start | bytes 589832 | tf_op jit(solution)/shard_map/ppermute | solution.py:175
  249.9 14.3 %collective-permute-start.59 = (bf16[128,768]{1,0:T(8,128)(2,1)S(1)}, bf16[128,768]{1,0:T(8,128)(2,1)S(1)}, u32[]{:S(2)}, u32[]{:S(2)}) collective-permute-start(bf16[128,768]{1,0:T(8,128)(2,1)S(1)} %collective-permute-done.56.refs_10_), channel_id=1, source_target_pairs={{0,1},{1,0},{2,3},{3,2},{4,5},{5,4},{6,7},{7,6},{8,9},{9,8},{10,11... | collective-permute-start | bytes 589832 | tf_op jit(solution)/shard_map/ppermute | solution.py:175
  250.4 16.7 %collective-permute-start.46 = (bf16[128,768]{1,0:T(8,128)(2,1)S(1)}, bf16[128,768]{1,0:T(8,128)(2,1)S(1)}, u32[]{:S(2)}, u32[]{:S(2)}) collective-permute-start(bf16[128,768]{1,0:T(8,128)(2,1)S(1)} %collective-permute-done.42.refs_7_), channel_id=1, source_target_pairs={{0,1},{1,0},{2,3},{3,2},{4,5},{5,4},{6,7},{7,6},{8,9},{9,8},{10,11... | collective-permute-start | bytes 589832 | tf_op jit(solution)/shard_map/ppermute | solution.py:175
  263.7 4.9 %collective-permute-start.45 = (bf16[128,768]{1,0:T(8,128)(2,1)S(1)}, bf16[128,768]{1,0:T(8,128)(2,1)S(1)}, u32[]{:S(2)}, u32[]{:S(2)}) collective-permute-start(bf16[128,768]{1,0:T(8,128)(2,1)S(1)} %collective-permute-done.41.refs_6_), channel_id=1, source_target_pairs={{0,1},{1,0},{2,3},{3,2},{4,5},{5,4},{6,7},{7,6},{8,9},{9,8},{10,11... | collective-permute-start | bytes 589832 | tf_op jit(solution)/shard_map/ppermute | solution.py:175
  263.7 4.9 %collective-permute-start.44 = (bf16[128,768]{1,0:T(8,128)(2,1)S(1)}, bf16[128,768]{1,0:T(8,128)(2,1)S(1)}, u32[]{:S(2)}, u32[]{:S(2)}) collective-permute-start(bf16[128,768]{1,0:T(8,128)(2,1)S(1)} %collective-permute-done.40.refs_5_), channel_id=1, source_target_pairs={{0,1},{1,0},{2,3},{3,2},{4,5},{5,4},{6,7},{7,6},{8,9},{9,8},{10,11... | collective-permute-start | bytes 589832 | tf_op jit(solution)/shard_map/ppermute | solution.py:175
  264.2 13.3 %collective-permute-start.53 = (bf16[512,256]{1,0:T(8,128)(2,1)S(1)}, bf16[512,256]{1,0:T(8,128)(2,1)S(1)}, u32[]{:S(2)}, u32[]{:S(2)}) collective-permute-start(bf16[512,256]{1,0:T(8,128)(2,1)S(1)} %get-tuple-element.78), channel_id=1, source_target_pairs={{0,2},{1,3},{2,0},{3,1},{4,6},{5,7},{6,4},{7,5},{8,10},{9,11},{10,... | collective-permute-start | bytes 786440 | tf_op jit(solution)/shard_map/ppermute | solution.py:170
  264.2 21.4 %collective-permute-start.54 = (bf16[512,256]{1,0:T(8,128)(2,1)S(1)}, bf16[512,256]{1,0:T(8,128)(2,1)S(1)}, u32[]{:S(2)}, u32[]{:S(2)}) collective-permute-start(bf16[512,256]{1,0:T(8,128)(2,1)S(1)} %get-tuple-element.79), channel_id=1, source_target_pairs={{0,4},{1,5},{2,6},{3,7},{4,0},{5,1},{6,2},{7,3},{8,12},{9,13},{10,... | collective-permute-start | bytes 786440 | tf_op jit(solution)/shard_map/ppermute | solution.py:170
  267.1 18.5 %collective-permute-start.55 = (bf16[512,256]{1,0:T(8,128)(2,1)S(1)}, bf16[512,256]{1,0:T(8,128)(2,1)S(1)}, u32[]{:S(2)}, u32[]{:S(2)}) collective-permute-start(bf16[512,256]{1,0:T(8,128)(2,1)S(1)} %get-tuple-element.80), channel_id=1, source_target_pairs={{0,6},{1,7},{2,4},{3,5},{4,2},{5,3},{6,0},{7,1},{8,14},{9,15},{10,... | collective-permute-start | bytes 786440 | tf_op jit(solution)/shard_map/ppermute | solution.py:170
  268.6 1.4 collective-permute-start.60
  268.6 1.7 collective-permute-start.61
  (20 other events, 112.0 us)

commit v6 on v5

--- a/solution.py
+++ b/solution.py
@@ -182,11 +182,14 @@
 def gather_cores(core):
     beside = on_chips(core, [(0, 1), (1, 0), (2, 3), (3, 2)])
     across = on_chips(core, [(1, 2), (2, 1)])
-    far_across = on_chips(beside, [(1, 2), (2, 1)])
+    half = core.shape[0] // 2
+    far_a = on_chips(beside[:half], [(1, 2), (2, 1)])
+    far_b = on_chips(beside[half:], [(1, 2), (2, 1)])
     outward = on_chips(across, [(1, 0), (2, 3)])
-    far_outward = on_chips(far_across, [(1, 0), (2, 3)])
+    last_a = on_chips(far_a, [(1, 0), (2, 3)])
+    last_b = on_chips(far_b, [(1, 0), (2, 3)])
     held, swapped = [core, beside], [swap_cores(piece) for piece in (core, beside)]
-    near = [(across, outward), (far_across, far_outward)]
+    near = [(across, outward), (far_a, last_a, far_b, last_b)]
     far = [tuple(swap_cores(piece) for piece in pair) for pair in near]
     return [piece for both in zip(held + near, swapped + far) for piece in both]
 
@@ -243,7 +246,8 @@
     total = None
     for place, core_ref in enumerate(core_refs):
         if copies is not None:
-            copies[place].wait()
+            for move in copies[place]:
+                move.wait()
         mark = marks[:, start + place : start + place + 1]
         chosen = jnp.where(mark > 0.5, rows, jnp.zeros_like(rows))
         term = lax.dot_general(
@@ -262,16 +266,26 @@
 
 
 def fetch(middle, sources, targets, arrived):
-    copies = []
-    for place, (source, target) in enumerate(zip(sources, targets)):
-        choices = source if isinstance(source, tuple) else (source,)
-        moves = [pltpu.make_async_copy(ref, target, arrived.at[place]) for ref in choices]
-        copies.append(moves[0])
-        if len(moves) == 1:
-            moves[0].start()
-        else:
-            pl.when(middle)(moves[0].start)
-            pl.when(jnp.logical_not(middle))(moves[1].start)
+    copies, count = [], 0
+    for source, target in zip(sources, targets):
+        if not isinstance(source, tuple):
+            move = pltpu.make_async_copy(source, target, arrived.at[count])
+            move.start()
+            copies.append([move])
+            count += 1
+            continue
+        moves = []
+        for place in range(0, len(source), 2):
+            inner, outer = source[place : place + 2]
+            part = target.at[pl.ds(place // 2 * inner.shape[0], inner.shape[0]), :]
+            move = pltpu.make_async_copy(inner, part, arrived.at[count])
+            pl.when(middle)(move.start)
+            pl.when(jnp.logical_not(middle))(
+                pltpu.make_async_copy(outer, part, arrived.at[count]).start
+            )
+            moves.append(move)
+            count += 1
+        copies.append(moves)
     return copies
 
 
@@ -285,9 +299,9 @@
 def first_kernel(middle_ref, proj_ref, marks_ref, part_ref, *refs):
     early = CHIPS * CORES - 2
     held, refs = refs[:early], refs[early:]
-    sources = [(refs[0], refs[1]), (refs[2], refs[3]), refs[4], refs[5]]
-    scaled_ref, slope_ref, score_ref, chain_ref, near_ref, far_ref = refs[6:12]
-    own_ref, gram_ref, arrived = refs[12:]
+    sources = [tuple(refs[:4]), tuple(refs[4:8]), refs[8], refs[9]]
+    scaled_ref, slope_ref, score_ref, chain_ref, near_ref, far_ref = refs[10:16]
+    own_ref, gram_ref, arrived = refs[16:]
     last = [near_ref, far_ref]
     copies = fetch(middle_ref[0] > 0, sources, [*last, own_ref, gram_ref], arrived)
     core_refs, count = [*held, *last], early + 2
@@ -298,8 +312,8 @@
     slope = sigmoid * (1.0 + pre * (1.0 - sigmoid))
     weight = marks[:, count : count + 1]
     scaled = (weight * hidden.astype(jnp.float32)).astype(jnp.bfloat16)
-    copies[2].wait()
-    copies[3].wait()
+    for move in copies[2] + copies[3]:
+        move.wait()
     score = own_ref[...] + dot(scaled, gram_ref[...])
     scaled_ref[...] = scaled
     slope_ref[...] = slope
@@ -534,7 +548,8 @@
         )
         for step in range(CHIPS)
     ]
-    down_gram = gram_sum(gram_pair(half_down, own_half))
+    down_pair = gram_pair(half_down, own_half)
+    down_gram = gram_sum(down_pair)
     two_gram = gram_sum(gram_pair(half_two, own_half))
     down_score = both_cores(dot_first(step_down, own_half))
 
@@ -552,7 +567,7 @@
             + [pl.BlockSpec(memory_space=pltpu.VMEM)] * len(arrays)
             + [pl.BlockSpec(memory_space=pl.ANY)] * len(flat),
             out_specs=[pl.BlockSpec(memory_space=pltpu.VMEM)] * len(outs),
-            scratch_shapes=scratch + [pltpu.SemaphoreType.DMA((len(sources),))],
+            scratch_shapes=scratch + [pltpu.SemaphoreType.DMA((len(flat),))],
             compiler_params=pltpu.CompilerParams(vmem_limit_bytes=ROOM),
             cost_estimate=pl.CostEstimate(
                 flops=product_flops * products,

time: 291 us -> 296 us (1.017)
  starting transfers between devices: 54.5 us -> 60.1 us
    ppermute x17 -> x19, waiting for transfers between devices: 63.5 us -> 79.4 us  [on_chips(): return lax.ppermute(value, 'expert', perm)]
    ppermute x14, waiting for transfers between devices: 98.1 us -> 83.3 us  [between_layers(): return lax.ppermute(value, 'section', pairs)]
    ppermute x17 -> x19, starting transfers between devices: 25.8 us -> 29 us  [on_chips(): return lax.ppermute(value, 'expert', perm)]
    ppermute x31 -> x33, starting transfers between devices: 6.48 us -> 8.02 us  [swap_cores(): lax.ppermute(value, 'expert', [(index, index ^ 1) for index in range(coun...]
  transfers between devices with their start and end apart: 62 -> 66, of which waited for: 19 -> 20; matrix products, arithmetic and copies ran while one was open for 11% -> 11% of each run, Pallas kernels for 9% -> 9%
where the time goes in v6:
time: 296 us; the launch traced here: 293 us
  waiting for transfers between devices  164 us (55%)
  starting transfers between devices  60.1 us (20%)
  Pallas kernels  28.6 us (10%)
  matrix products  19.3 us (7%)
  local copies, waits for them, and re-layouts  11.3 us (4%)
  other arithmetic  7.74 us (3%)
    ppermute x14, waiting for transfers between devices, between_layers(): return lax.ppermute(value, 'section', pairs)  83.3 us
    ppermute x19, waiting for transfers between devices, on_chips(): return lax.ppermute(value, 'expert', perm)  79.4 us
    ppermute x19, starting transfers between devices, on_chips(): return lax.ppermute(value, 'expert', perm)  29 us
    ppermute x14, starting transfers between devices, between_layers(): return lax.ppermute(value, 'section', pairs)  23.1 us
    dot_general x9, matrix products, dot_first(): lax.dot_general(left, right, (((0,), (0,)), ((), ())), preferred_element_...  15.8 us
    pallas_call x3, Pallas kernels, call_rows(): pl.pallas_call(body, out_shape=[jax.ShapeDtypeStruct(shape, kind) for sha...  12.1 us
    pallas_call x2, Pallas kernels, core_call(): pl.pallas_call(body, out_shape=outs, in_specs=[pl.BlockSpec(memory_space=...  8.51 us
    ppermute x33, starting transfers between devices, swap_cores(): lax.ppermute(value, 'expert', [(index, index ^ 1) for index in range(coun...  8.02 us
  transfers between devices with their start and end apart: 66, of which 20 were waited for; matrix products, arithmetic and copies ran while one was open for 11% of the time, Pallas kernels for 9%

profile of v6, /device:TPU:0, one launch (start us, length us, event | category | flops | bytes accessed | tf_op | source)
XLA Modules:
  0.0 292.6 jit_solution(12085547456474620342)
XLA Ops:
  2.2 3.0 %fusion.2.proj_ref = bf16[128,768]{1,0:T(8,128)(2,1)S(1)} fusion(bf16[128,2560]{1,0:T(8,128)(2,1)} %bitcast.47, bf16[1,2560,768]{2,1,0:T(8,128)(2,1)} %param.12), kind=kOutput, calls=%fused_computation.18 | convolution fusion | flops 503414784 | bytes 4784128 | tf_op jit(solution)/shard_map/dot_general | solution.py:155
  9.0 0.9 copy-done
  10.6 1.6 dynamic-slice_bitcast_fusion.3
  13.6 1.3 collective-permute-start.23
  14.9 1.3 collective-permute-start.28
  16.2 5.4 %collective-permute-start.3 = (bf16[768,768]{1,0:T(8,128)(2,1)S(1)}, bf16[768,768]{1,0:T(8,128)(2,1)S(1)}, u32[]{:S(2)}, u32[]{:S(2)}) collective-permute-start(bf16[768,768]{1,0:T(8,128)(2,1)S(1)} %bitcast.42), channel_id=1, source_target_pairs={{0,2},{1,3},{2,0},{3,1},{4,6},{5,7},{6,4},{7,5},{8,10},{9,11},{10,... | collective-permute-start | bytes 3538952 | tf_op jit(solution)/shard_map/ppermute | solution.py:170
  21.8 2.8 convolution_convert_fusion.4
  24.6 8.2 %collective-permute-done.23 = bf16[1280,256]{1,0:T(8,128)(2,1)S(1)} collective-permute-done((bf16[1280,256]{1,0:T(8,128)(2,1)S(1)}, bf16[1280,256]{1,0:T(8,128)(2,1)S(1)}, u32[]{:S(2)}, u32[]{:S(2)}) %collective-permute-start.23) | collective-permute-done | bytes 655392 | tf_op jit(solution)/shard_map/ppermute | solution.py:179
  32.8 1.3 collective-permute-done.28
  34.1 1.3 collective-permute-start.32
  35.4 1.3 collective-permute-start.26
  37.5 0.9 slice.211
  38.3 9.9 %collective-permute-done.3.refs_2_ = bf16[768,768]{1,0:T(8,128)(2,1)S(1)} collective-permute-done((bf16[768,768]{1,0:T(8,128)(2,1)S(1)}, bf16[768,768]{1,0:T(8,128)(2,1)S(1)}, u32[]{:S(2)}, u32[]{:S(2)}) %collective-permute-start.3) | collective-permute-done | bytes 1179680 | tf_op jit(solution)/shard_map/ppermute | solution.py:170
  48.2 1.1 fusion.16
  49.3 1.0 copy-done.4
  50.3 1.5 collective-permute-start.11
  52.5 1.5 collective-permute-start.9
  54.1 1.3 collective-permute-start.6
  55.4 1.3 pad_maximum_fusion.1
  56.8 23.7 %collective-permute-done.32.refs_4_ = bf16[1280,768]{1,0:T(8,128)(2,1)} collective-permute-done((bf16[1280,768]{1,0:T(8,128)(2,1)S(1)}, bf16[1280,768]{1,0:T(8,128)(2,1)}, u32[]{:S(2)}, u32[]{:S(2)}) %collective-permute-start.32) | collective-permute-done | bytes 1966112 | tf_op jit(solution)/shard_map/ppermute | solution.py:179
  80.5 1.3 collective-permute-start.12
  83.3 1.1 slice_add_fusion.3.refs_14_
  84.3 14.5 %collective-permute-done.6.refs_5_ = bf16[768,768]{1,0:T(8,128)(2,1)S(1)} collective-permute-done((bf16[768,768]{1,0:T(8,128)(2,1)}, bf16[768,768]{1,0:T(8,128)(2,1)S(1)}, u32[]{:S(2)}, u32[]{:S(2)}) %collective-permute-start.6) | collective-permute-done | bytes 1179680 | tf_op jit(solution)/shard_map/ppermute | solution.py:170
  98.8 1.3 collective-permute-start.10
  100.1 4.6 %collective-permute-start.35 = (bf16[1280,768]{1,0:T(8,128)(2,1)}, bf16[1280,768]{1,0:T(8,128)(2,1)S(1)}, u32[]{:S(2)}, u32[]{:S(2)}) collective-permute-start(bf16[1280,768]{1,0:T(8,128)(2,1)} %collective-permute-done.32.refs_4_), channel_id=1, source_target_pairs={{0,8},{1,9},{2,10},{3,11},{4,12},{5,13},{6,14},{7,15}} | collective-permute-start | bytes 5898248 | tf_op jit(solution)/shard_map/ppermute | solution.py:179
  104.7 6.7 %collective-permute-done.12.refs_9_ = bf16[384,768]{1,0:T(8,128)(2,1)S(1)} collective-permute-done((bf16[384,768]{1,0:T(8,128)(2,1)}, bf16[384,768]{1,0:T(8,128)(2,1)S(1)}, u32[]{:S(2)}, u32[]{:S(2)}) %collective-permute-start.12) | collective-permute-done | bytes 589856 | tf_op jit(solution)/shard_map/ppermute | solution.py:170
  111.4 3.3 %convolution_convert_fusion.3 = bf16[768,768]{1,0:T(8,128)(2,1)S(1)} fusion(bf16[1280,768]{1,0:T(8,128)(2,1)} %collective-permute-done.26.refs_13_, bf16[1280,768]{1,0:T(8,128)(2,1)S(1)} %pad_maximum_fusion.refs_1_), kind=kOutput, calls=%fused_computation.11 | convolution fusion | flops 1510539264 | bytes 5111808 | tf_op jit(solution)/shard_map/dot_general | solution.py:159
  115.3 1.9 add_convert_fusion.4.refs_15_
  117.2 5.3 %collective-permute-done.10.refs_7_ = bf16[384,768]{1,0:T(8,128)(2,1)S(1)} collective-permute-done((bf16[384,768]{1,0:T(8,128)(2,1)}, bf16[384,768]{1,0:T(8,128)(2,1)S(1)}, u32[]{:S(2)}, u32[]{:S(2)}) %collective-permute-start.10) | collective-permute-done | bytes 589856 | tf_op jit(solution)/shard_map/ppermute | solution.py:170
  123.1 1.1 slice_add_fusion.2.refs_4_
  124.2 3.4 %convolution_convert_fusion.2 = bf16[768,768]{1,0:T(8,128)(2,1)S(1)} fusion(bf16[1280,768]{1,0:T(8,128)(2,1)} %collective-permute-done.32.refs_4_, bf16[1280,768]{1,0:T(8,128)(2,1)S(1)} %pad_maximum_fusion.refs_1_), kind=kOutput, calls=%fused_computation.10 | convolution fusion | flops 1510539264 | bytes 5111808 | tf_op jit(solution)/shard_map/dot_general | solution.py:159
  127.6 4.3 %collective-permute-start.29 = (bf16[1280,256]{1,0:T(8,128)(2,1)S(1)}, bf16[1280,256]{1,0:T(8,128)(2,1)S(1)}, u32[]{:S(2)}, u32[]{:S(2)}) collective-permute-start(bf16[1280,256]{1,0:T(8,128)(2,1)S(1)} %copy-done.25), channel_id=1, source_target_pairs={{0,8},{1,9},{2,10},{3,11},{4,12},{5,13},{6,14},{7,15}} | collective-permute-start | bytes 1966088 | tf_op jit(solution)/shard_map/ppermute | solution.py:179
  132.0 3.6 %shard_map.86 = (f32[128,768]{1,0:T(8,128)S(1)}, bf16[768,768]{1,0:T(8,128)(2,1)S(1)}, bf16[768,768]{1,0:T(8,128)(2,1)S(1)}, bf16[768,768]{1,0:T(8,128)(2,1)S(1)...) custom-call(s32[1]{0:T(128)} %bitcast.3.middle_ref, ...), custom_call_target="tpu_custom_call" | custom-call | flops 905969664 | bytes 7077888 | tf_op jit(solution)/shard_map/pallas_call | solution.py:563
  135.7 1.3 collective-permute-start.41
  137.0 4.9 %shard_map.87 = (bf16[128,768]{1,0:T(8,128)(2,1)S(1)}, f32[128,768]{1,0:T(8,128)S(1)}, f32[128,768]{1,0:T(8,128)S(1)}, bf16[128,768]{1,0:T(8,128)(2,1)S(1)}, bf1...) custom-call(s32[1]{0:T(128)} %bitcast.3.middle_ref, bf16[128,768]{1,0:T(8,128)(2,1)S(1)} %fusion.2.proj_ref, ...), custom_call_target="tpu_custom_call" | custom-call | flops 1660944384 | bytes 4718592 | tf_op jit(solution)/shard_map/pallas_call | solution.py:563
  142.0 0.9 collective-permute-start.25
  143.2 3.7 %shard_map.88 = (f32[128,768]{1,0:T(8,128)S(1)}, bf16[128,768]{1,0:T(8,128)(2,1)}, bf16[128,768]{1,0:T(8,128)(2,1)}, bf16[128,768]{1,0:T(8,128)(2,1)S(1)}) custom-call(f32[128,16]{1,0:T(8,128)S(1)} %convert_select_fusion.marks_ref.refs_0_, bf16[128,768]{1,0:T(8,128)(2,1)S(1)} %get-tuple-element.82.refs_1_.refs_2_.refs_9_, ...), custom_call_target="tpu_custom_call" | custom-call | flops 1358954496 | bytes 12197888 | tf_op jit(solution)/shard_map/pallas_call | solution.py:346
  146.9 11.1 %collective-permute-done.29 = bf16[1280,256]{1,0:T(8,128)(2,1)S(1)} collective-permute-done((bf16[1280,256]{1,0:T(8,128)(2,1)S(1)}, bf16[1280,256]{1,0:T(8,128)(2,1)S(1)}, u32[]{:S(2)}, u32[]{:S(2)}) %collective-permute-start.29) | collective-permute-done | bytes 655392 | tf_op jit(solution)/shard_map/ppermute | solution.py:179
  158.0 1.8 convolution_convert_fusion.1
  161.3 1.3 collective-permute-start.37
  164.7 4.0 %shard_map.89 = (f32[128,768]{1,0:T(8,128)S(1)}, bf16[128,768]{1,0:T(8,128)(2,1)}, bf16[128,768]{1,0:T(8,128)(2,1)}, bf16[128,768]{1,0:T(8,128)(2,1)S(1)}) custom-call(f32[128,16]{1,0:T(8,128)S(1)} %convert_select_fusion.marks_ref.refs_0_, bf16[128,768]{1,0:T(8,128)(2,1)S(1)} %get-tuple-element.82.refs_1_.refs_2_.refs_9_, ...), custom_call_target="tpu_custom_call" | custom-call | flops 1509949440 | bytes 13574144 | tf_op jit(solution)/shard_map/pallas_call | solution.py:346
  168.7 14.8 %collective-permute-done.41.refs_10_ = bf16[1280,768]{1,0:T(8,128)(2,1)S(1)} collective-permute-done((bf16[1280,768]{1,0:T(8,128)(2,1)}, bf16[1280,768]{1,0:T(8,128)(2,1)S(1)}, u32[]{:S(2)}, u32[]{:S(2)}) %collective-permute-start.41) | collective-permute-done | bytes 1966112 | tf_op jit(solution)/shard_map/ppermute | solution.py:179
  183.5 1.8 convolution_convert_fusion
  186.2 10.9 %collective-permute-done.37 = bf16[1280,256]{1,0:T(8,128)(2,1)S(1)} collective-permute-done((bf16[1280,256]{1,0:T(8,128)(2,1)S(1)}, bf16[1280,256]{1,0:T(8,128)(2,1)S(1)}, u32[]{:S(2)}, u32[]{:S(2)}) %collective-permute-start.37) | collective-permute-done | bytes 655392 | tf_op jit(solution)/shard_map/ppermute | solution.py:179
  197.9 1.3 collective-permute-start.43
  200.0 1.3 collective-permute-start.62
  201.4 5.7 %collective-permute-done.43.refs_9_ = bf16[128,768]{1,0:T(8,128)(2,1)S(1)} collective-permute-done((bf16[128,768]{1,0:T(8,128)(2,1)S(1)}, bf16[128,768]{1,0:T(8,128)(2,1)S(1)}, u32[]{:S(2)}, u32[]{:S(2)}) %collective-permute-start.43) | collective-permute-done | bytes 196640 | tf_op jit(solution)/shard_map/ppermute | solution.py:179
  207.2 1.3 collective-permute-start.39
  208.5 1.6 collective-permute-start.40
  210.4 7.5 %collective-permute-done.40.refs_7_.refs_11_ = bf16[128,768]{1,0:T(8,128)(2,1)S(1)} collective-permute-done((bf16[128,768]{1,0:T(8,128)(2,1)S(1)}, bf16[128,768]{1,0:T(8,128)(2,1)S(1)}, u32[]{:S(2)}, u32[]{:S(2)}) %collective-permute-start.40) | collective-permute-done | bytes 196640 | tf_op jit(solution)/shard_map/ppermute | solution.py:179
  217.9 1.7 collective-permute-start.20
  219.7 4.4 %shard_map.90 = (f32[128,768]{1,0:T(8,128)}, bf16[128,768]{1,0:T(8,128)(2,1)S(1)}, bf16[128,768]{1,0:T(8,128)(2,1)S(1)}, bf16[128,768]{1,0:T(8,128)(2,1)}) custom-call(f32[128,16]{1,0:T(8,128)S(1)} %convert_select_fusion.marks_ref.refs_0_, bf16[128,768]{1,0:T(8,128)(2,1)S(1)} %get-tuple-element.82.refs_1_.refs_2_.refs_9_, ...), custom_call_target="tpu_custom_call" | custom-call | flops 1660944384 | bytes 14950400 | tf_op jit(solution)/shard_map/pallas_call | solution.py:346
  225.1 1.7 collective-permute-start.21
  226.8 2.5 collective-permute-start.22
  230.7 1.3 collective-permute-start.46
  232.1 3.0 %collective-permute-start.44 = (bf16[128,768]{1,0:T(8,128)(2,1)S(1)}, bf16[128,768]{1,0:T(8,128)(2,1)S(1)}, u32[]{:S(2)}, u32[]{:S(2)}) collective-permute-start(bf16[128,768]{1,0:T(8,128)(2,1)S(1)} %get-tuple-element.70.refs_4_), channel_id=1, source_target_pairs={{0,2},{1,3},{2,0},{3,1},{4,6},{5,7},{6,4},{7,5},{8,10},{9,11},{10,... | collective-permute-start | bytes 589832 | tf_op jit(solution)/shard_map/ppermute | solution.py:170
  235.1 5.1 %spread.1 = (bf16[512,256]{1,0:T(8,128)(2,1)S(1)}, bf16[512,256]{1,0:T(8,128)(2,1)S(1)}, bf16[512,256]{1,0:T(8,128)(2,1)S(1)}, bf16[512,256]{1,0:T(8,128)(2,1)S(1)}) custom-call(bf16[1280,256]{1,0:T(8,128)(2,1)S(1)} %add_convert_fusion.5.refs_0_, bf16[1280,768]{1,0:T(8,128)(2,1)S(1)} %pad_maximum_fusion.refs_1_, ...), custom_call_target="tpu_custom_call" | custom-call | flops 2516582400 | bytes 12845056 | tf_op jit(solution)/shard_map/spread/pallas_call | solution.py:417
  240.2 14.7 %collective-permute-done.21.refs_2_ = bf16[512,256]{1,0:T(8,128)(2,1)S(1)} collective-permute-done((bf16[512,256]{1,0:T(8,128)(2,1)S(1)}, bf16[512,256]{1,0:T(8,128)(2,1)S(1)}, u32[]{:S(2)}, u32[]{:S(2)}) %collective-permute-start.21) | collective-permute-done | bytes 262176 | tf_op jit(solution)/shard_map/ppermute | solution.py:170
  255.5 12.9 %collective-permute-done.45.refs_6_ = bf16[128,768]{1,0:T(8,128)(2,1)S(1)} collective-permute-done((bf16[128,768]{1,0:T(8,128)(2,1)S(1)}, bf16[128,768]{1,0:T(8,128)(2,1)S(1)}, u32[]{:S(2)}, u32[]{:S(2)}) %collective-permute-start.45) | collective-permute-done | bytes 196640 | tf_op jit(solution)/shard_map/ppermute | solution.py:170
  269.0 2.0 collective-permute-start.58
  271.0 2.4 collective-permute-start.59
  275.1 6.6 %collective-permute-done.57.refs_6_ = bf16[512,256]{1,0:T(8,128)(2,1)S(1)} collective-permute-done((bf16[512,256]{1,0:T(8,128)(2,1)S(1)}, bf16[512,256]{1,0:T(8,128)(2,1)S(1)}, u32[]{:S(2)}, u32[]{:S(2)}) %collective-permute-start.57) | collective-permute-done | bytes 262176 | tf_op jit(solution)/shard_map/ppermute | solution.py:170
  281.7 8.7 %collective-permute-done.58.refs_7_ = bf16[512,256]{1,0:T(8,128)(2,1)S(1)} collective-permute-done((bf16[512,256]{1,0:T(8,128)(2,1)S(1)}, bf16[512,256]{1,0:T(8,128)(2,1)S(1)}, u32[]{:S(2)}, u32[]{:S(2)}) %collective-permute-start.58) | collective-permute-done | bytes 262176 | tf_op jit(solution)/shard_map/ppermute | solution.py:170
  290.4 2.2 shard_map.92
  (187 shorter events, 23.7 us)
Async XLA Ops:
  5.5 9.4 %collective-permute-start.1 = (bf16[128,768]{1,0:T(8,128)(2,1)S(1)}, bf16[128,768]{1,0:T(8,128)(2,1)}, u32[]{:S(2)}, u32[]{:S(2)}) collective-permute-start(bf16[128,768]{1,0:T(8,128)(2,1)S(1)} %slice.179), channel_id=1, source_target_pairs={{0,1},{1,0},{2,3},{3,2},{4,5},{5,4},{6,7},{7,6},{8,9},{9,8},{10,11... | collective-permute-start | bytes 589832 | tf_op jit(solution)/shard_map/ppermute | solution.py:175
  7.4 8.8 %collective-permute-start = (bf16[1280,128]{1,0:T(8,128)(2,1)S(1)}, bf16[1280,128]{1,0:T(8,128)(2,1)}, u32[]{:S(2)}, u32[]{:S(2)}) collective-permute-start(bf16[1280,128]{1,0:T(8,128)(2,1)S(1)} %pad_maximum_fusion.3), channel_id=1, source_target_pairs={{0,1},{1,0},{2,3},{3,2},{4,5},{5,4},{6,7},{7,6},{8,9},{9,8},{10,11... | collective-permute-start | bytes 983048 | tf_op jit(solution)/shard_map/ppermute | solution.py:175
  8.7 3.7 %collective-permute-start.17 = (bf16[1280,128]{1,0:T(8,128)(2,1)S(1)}, bf16[1280,128]{1,0:T(8,128)(2,1)S(1)}, u32[]{:S(2)}, u32[]{:S(2)}) collective-permute-start(bf16[1280,128]{1,0:T(8,128)(2,1)S(1)} %pad_maximum_fusion.4), channel_id=1, source_target_pairs={{0,1},{1,0},{2,3},{3,2},{4,5},{5,4},{6,7},{7,6},{8,9},{9,8},{10,11... | collective-permute-start | bytes 983048 | tf_op jit(solution)/shard_map/ppermute | solution.py:175
  9.9 25.5 %collective-permute-start.5 = (bf16[768,768]{1,0:T(8,128)(2,1)S(1)}, bf16[768,768]{1,0:T(8,128)(2,1)S(1)}, u32[]{:S(2)}, u32[]{:S(2)}) collective-permute-start(bf16[768,768]{1,0:T(8,128)(2,1)S(1)} %bitcast.41), channel_id=1, source_target_pairs={{2,4},{3,5},{4,2},{5,3},{10,12},{11,13},{12,10},{13,11},{18,20},{1... | collective-permute-start | bytes 3538952 | tf_op jit(solution)/shard_map/ppermute | solution.py:170
  13.1 8.5 %collective-permute-start.18 = (f32[128,768]{1,0:T(8,128)S(1)}, f32[128,768]{1,0:T(8,128)}, u32[]{:S(2)}, u32[]{:S(2)}) collective-permute-start(f32[128,768]{1,0:T(8,128)S(1)} %slice.195), channel_id=1, source_target_pairs={{0,1},{1,0},{2,3},{3,2},{4,5},{5,4},{6,7},{7,6},{8,9},{9,8},{10,11... | collective-permute-start | bytes 1179656 | tf_op jit(solution)/shard_map/ppermute | solution.py:175
  13.6 19.2 %collective-permute-start.23 = (bf16[1280,256]{1,0:T(8,128)(2,1)S(1)}, bf16[1280,256]{1,0:T(8,128)(2,1)S(1)}, u32[]{:S(2)}, u32[]{:S(2)}) collective-permute-start(bf16[1280,256]{1,0:T(8,128)(2,1)S(1)} %pad_maximum_fusion.2), channel_id=1, source_target_pairs={{24,16},{8,0},{25,17},{9,1},{26,18},{10,2},{27,19},{11,3},{28,20},... | collective-permute-start | bytes 1966088 | tf_op jit(solution)/shard_map/ppermute | solution.py:179
  14.9 19.2 %collective-permute-start.28 = (bf16[1280,256]{1,0:T(8,128)(2,1)S(1)}, bf16[1280,256]{1,0:T(8,128)(2,1)S(1)}, u32[]{:S(2)}, u32[]{:S(2)}) collective-permute-start(bf16[1280,256]{1,0:T(8,128)(2,1)S(1)} %pad_maximum_fusion.2), channel_id=1, source_target_pairs={{24,8},{16,0},{25,9},{17,1},{26,10},{18,2},{27,11},{19,3},{28,12},... | collective-permute-start | bytes 1966088 | tf_op jit(solution)/shard_map/ppermute | solution.py:179
  16.2 32.0 %collective-permute-start.3 = (bf16[768,768]{1,0:T(8,128)(2,1)S(1)}, bf16[768,768]{1,0:T(8,128)(2,1)S(1)}, u32[]{:S(2)}, u32[]{:S(2)}) collective-permute-start(bf16[768,768]{1,0:T(8,128)(2,1)S(1)} %bitcast.42), channel_id=1, source_target_pairs={{0,2},{1,3},{2,0},{3,1},{4,6},{5,7},{6,4},{7,5},{8,10},{9,11},{10,... | collective-permute-start | bytes 3538952 | tf_op jit(solution)/shard_map/ppermute | solution.py:170
  21.6 27.7 %collective-permute-start.2 = (bf16[768,768]{1,0:T(8,128)(2,1)S(1)}, bf16[768,768]{1,0:T(8,128)(2,1)S(1)}, u32[]{:S(2)}, u32[]{:S(2)}) collective-permute-start(bf16[768,768]{1,0:T(8,128)(2,1)S(1)} %bitcast.43), channel_id=1, source_target_pairs={{0,1},{1,0},{2,3},{3,2},{4,5},{5,4},{6,7},{7,6},{8,9},{9,8},{10,11... | collective-permute-start | bytes 3538952 | tf_op jit(solution)/shard_map/ppermute | solution.py:175
  32.8 19.1 %collective-permute-start.19 = (bf16[768,768]{1,0:T(8,128)(2,1)}, bf16[768,768]{1,0:T(8,128)(2,1)}, u32[]{:S(2)}, u32[]{:S(2)}) collective-permute-start(bf16[768,768]{1,0:T(8,128)(2,1)} %convolution_convert_fusion.4), channel_id=1, source_target_pairs={{0,1},{1,0},{2,3},{3,2},{4,5},{5,4},{6,7},{7,6},{8,9},{9,8},{10,11... | collective-permute-start | bytes 3538952 | tf_op jit(solution)/shard_map/ppermute | solution.py:175
  34.1 46.4 %collective-permute-start.32 = (bf16[1280,768]{1,0:T(8,128)(2,1)S(1)}, bf16[1280,768]{1,0:T(8,128)(2,1)}, u32[]{:S(2)}, u32[]{:S(2)}) collective-permute-start(bf16[1280,768]{1,0:T(8,128)(2,1)S(1)} %pad_maximum_fusion.refs_1_), channel_id=1, source_target_pairs={{24,8},{16,0},{25,9},{17,1},{26,10},{18,2},{27,11},{19,3},{28,12},... | collective-permute-start | bytes 5898248 | tf_op jit(solution)/shard_map/ppermute | solution.py:179
  35.4 46.4 %collective-permute-start.26 = (bf16[1280,768]{1,0:T(8,128)(2,1)S(1)}, bf16[1280,768]{1,0:T(8,128)(2,1)}, u32[]{:S(2)}, u32[]{:S(2)}) collective-permute-start(bf16[1280,768]{1,0:T(8,128)(2,1)S(1)} %pad_maximum_fusion.refs_1_), channel_id=1, source_target_pairs={{24,16},{8,0},{25,17},{9,1},{26,18},{10,2},{27,19},{11,3},{28,20},... | collective-permute-start | bytes 5898248 | tf_op jit(solution)/shard_map/ppermute | solution.py:179
  48.2 4.2 %collective-permute-start.24 = (f32[128,768]{1,0:T(8,128)}, f32[128,768]{1,0:T(8,128)}, u32[]{:S(2)}, u32[]{:S(2)}) collective-permute-start(f32[128,768]{1,0:T(8,128)} %slice.211), channel_id=1, source_target_pairs={{0,1},{1,0},{2,3},{3,2},{4,5},{5,4},{6,7},{7,6},{8,9},{9,8},{10,11... | collective-permute-start | bytes 1179656 | tf_op jit(solution)/shard_map/ppermute | solution.py:175
  50.3 3.7 %collective-permute-start.11 = (bf16[384,768]{1,0:T(8,128)(2,1)}, bf16[384,768]{1,0:T(8,128)(2,1)}, u32[]{:S(2)}, u32[]{:S(2)}) collective-permute-start(bf16[384,768]{1,0:T(8,128)(2,1)} %get-tuple-element.92), channel_id=1, source_target_pairs={{2,4},{3,5},{4,2},{5,3},{10,12},{11,13},{12,10},{13,11},{18,20},{1... | collective-permute-start | bytes 1769480 | tf_op jit(solution)/shard_map/ppermute | solution.py:170
  51.9 30.9 %collective-permute-start.7 = (bf16[768,768]{1,0:T(8,128)(2,1)}, bf16[768,768]{1,0:T(8,128)(2,1)}, u32[]{:S(2)}, u32[]{:S(2)}) collective-permute-start(bf16[768,768]{1,0:T(8,128)(2,1)} %copy-done.2), channel_id=1, source_target_pairs={{0,1},{1,0},{2,3},{3,2},{4,5},{5,4},{6,7},{7,6},{8,9},{9,8},{10,11... | collective-permute-start | bytes 3538952 | tf_op jit(solution)/shard_map/ppermute | solution.py:175
  52.5 4.3 %collective-permute-start.9 = (bf16[384,768]{1,0:T(8,128)(2,1)}, bf16[384,768]{1,0:T(8,128)(2,1)}, u32[]{:S(2)}, u32[]{:S(2)}) collective-permute-start(bf16[384,768]{1,0:T(8,128)(2,1)} %get-tuple-element.93), channel_id=1, source_target_pairs={{2,4},{3,5},{4,2},{5,3},{10,12},{11,13},{12,10},{13,11},{18,20},{1... | collective-permute-start | bytes 1769480 | tf_op jit(solution)/shard_map/ppermute | solution.py:170
  54.1 44.7 %collective-permute-start.6 = (bf16[768,768]{1,0:T(8,128)(2,1)}, bf16[768,768]{1,0:T(8,128)(2,1)S(1)}, u32[]{:S(2)}, u32[]{:S(2)}) collective-permute-start(bf16[768,768]{1,0:T(8,128)(2,1)} %copy-done.2), channel_id=1, source_target_pairs={{2,0},{3,1},{4,6},{5,7},{10,8},{11,9},{12,14},{13,15},{18,16},{19,... | collective-permute-start | bytes 3538952 | tf_op jit(solution)/shard_map/ppermute | solution.py:170
  56.8 43.3 %collective-permute-start.15 = (bf16[384,768]{1,0:T(8,128)(2,1)}, bf16[384,768]{1,0:T(8,128)(2,1)S(1)}, u32[]{:S(2)}, u32[]{:S(2)}) collective-permute-start(bf16[384,768]{1,0:T(8,128)(2,1)} %collective-permute-done.11.refs_8_), channel_id=1, source_target_pairs={{0,1},{1,0},{2,3},{3,2},{4,5},{5,4},{6,7},{7,6},{8,9},{9,8},{10,11... | collective-permute-start | bytes 1769480 | tf_op jit(solution)/shard_map/ppermute | solution.py:175
  80.5 30.9 %collective-permute-start.12 = (bf16[384,768]{1,0:T(8,128)(2,1)}, bf16[384,768]{1,0:T(8,128)(2,1)S(1)}, u32[]{:S(2)}, u32[]{:S(2)}) collective-permute-start(bf16[384,768]{1,0:T(8,128)(2,1)} %collective-permute-done.11.refs_8_), channel_id=1, source_target_pairs={{2,0},{3,1},{4,6},{5,7},{10,8},{11,9},{12,14},{13,15},{18,16},{19,... | collective-permute-start | bytes 1769480 | tf_op jit(solution)/shard_map/ppermute | solution.py:170
  81.8 40.7 %collective-permute-start.4 = (bf16[768,768]{1,0:T(8,128)(2,1)S(1)}, bf16[768,768]{1,0:T(8,128)(2,1)S(1)}, u32[]{:S(2)}, u32[]{:S(2)}) collective-permute-start(bf16[768,768]{1,0:T(8,128)(2,1)S(1)} %collective-permute-done.3.refs_2_), channel_id=1, source_target_pairs={{0,1},{1,0},{2,3},{3,2},{4,5},{5,4},{6,7},{7,6},{8,9},{9,8},{10,11... | collective-permute-start | bytes 3538952 | tf_op jit(solution)/shard_map/ppermute | solution.py:175
  82.7 32.0 %collective-permute-start.13 = (bf16[384,768]{1,0:T(8,128)(2,1)}, bf16[384,768]{1,0:T(8,128)(2,1)S(1)}, u32[]{:S(2)}, u32[]{:S(2)}) collective-permute-start(bf16[384,768]{1,0:T(8,128)(2,1)} %collective-permute-done.9.refs_6_), channel_id=1, source_target_pairs={{0,1},{1,0},{2,3},{3,2},{4,5},{5,4},{6,7},{7,6},{8,9},{9,8},{10,11... | collective-permute-start | bytes 1769480 | tf_op jit(solution)/shard_map/ppermute | solution.py:175
  98.8 23.8 %collective-permute-start.10 = (bf16[384,768]{1,0:T(8,128)(2,1)}, bf16[384,768]{1,0:T(8,128)(2,1)S(1)}, u32[]{:S(2)}, u32[]{:S(2)}) collective-permute-start(bf16[384,768]{1,0:T(8,128)(2,1)} %collective-permute-done.9.refs_6_), channel_id=1, source_target_pairs={{2,0},{3,1},{4,6},{5,7},{10,8},{11,9},{12,14},{13,15},{18,16},{19,... | collective-permute-start | bytes 1769480 | tf_op jit(solution)/shard_map/ppermute | solution.py:170
  100.1 57.9 %collective-permute-start.35 = (bf16[1280,768]{1,0:T(8,128)(2,1)}, bf16[1280,768]{1,0:T(8,128)(2,1)S(1)}, u32[]{:S(2)}, u32[]{:S(2)}) collective-permute-start(bf16[1280,768]{1,0:T(8,128)(2,1)} %collective-permute-done.32.refs_4_), channel_id=1, source_target_pairs={{0,8},{1,9},{2,10},{3,11},{4,12},{5,13},{6,14},{7,15}} | collective-permute-start | bytes 5898248 | tf_op jit(solution)/shard_map/ppermute | solution.py:179
  111.4 16.2 %collective-permute-start.8 = (bf16[768,768]{1,0:T(8,128)(2,1)S(1)}, bf16[768,768]{1,0:T(8,128)(2,1)S(1)}, u32[]{:S(2)}, u32[]{:S(2)}) collective-permute-start(bf16[768,768]{1,0:T(8,128)(2,1)S(1)} %collective-permute-done.6.refs_5_), channel_id=1, source_target_pairs={{0,1},{1,0},{2,3},{3,2},{4,5},{5,4},{6,7},{7,6},{8,9},{9,8},{10,11... | collective-permute-start | bytes 3538952 | tf_op jit(solution)/shard_map/ppermute | solution.py:175
  114.7 27.2 %collective-permute-start.27 = (bf16[768,768]{1,0:T(8,128)(2,1)S(1)}, bf16[768,768]{1,0:T(8,128)(2,1)S(1)}, u32[]{:S(2)}, u32[]{:S(2)}) collective-permute-start(bf16[768,768]{1,0:T(8,128)(2,1)S(1)} %convolution_convert_fusion.3), channel_id=1, source_target_pairs={{0,1},{1,0},{2,3},{3,2},{4,5},{5,4},{6,7},{7,6},{8,9},{9,8},{10,11... | collective-permute-start | bytes 3538952 | tf_op jit(solution)/shard_map/ppermute | solution.py:175
  122.6 13.1 %collective-permute-start.16 = (bf16[384,768]{1,0:T(8,128)(2,1)S(1)}, bf16[384,768]{1,0:T(8,128)(2,1)S(1)}, u32[]{:S(2)}, u32[]{:S(2)}) collective-permute-start(bf16[384,768]{1,0:T(8,128)(2,1)S(1)} %collective-permute-done.12.refs_9_), channel_id=1, source_target_pairs={{0,1},{1,0},{2,3},{3,2},{4,5},{5,4},{6,7},{7,6},{8,9},{9,8},{10,11... | collective-permute-start | bytes 1769480 | tf_op jit(solution)/shard_map/ppermute | solution.py:175
  122.6 13.2 %collective-permute-start.14 = (bf16[384,768]{1,0:T(8,128)(2,1)S(1)}, bf16[384,768]{1,0:T(8,128)(2,1)S(1)}, u32[]{:S(2)}, u32[]{:S(2)}) collective-permute-start(bf16[384,768]{1,0:T(8,128)(2,1)S(1)} %collective-permute-done.10.refs_7_), channel_id=1, source_target_pairs={{0,1},{1,0},{2,3},{3,2},{4,5},{5,4},{6,7},{7,6},{8,9},{9,8},{10,11... | collective-permute-start | bytes 1769480 | tf_op jit(solution)/shard_map/ppermute | solution.py:175
  127.6 30.3 %collective-permute-start.29 = (bf16[1280,256]{1,0:T(8,128)(2,1)S(1)}, bf16[1280,256]{1,0:T(8,128)(2,1)S(1)}, u32[]{:S(2)}, u32[]{:S(2)}) collective-permute-start(bf16[1280,256]{1,0:T(8,128)(2,1)S(1)} %copy-done.25), channel_id=1, source_target_pairs={{0,8},{1,9},{2,10},{3,11},{4,12},{5,13},{6,14},{7,15}} | collective-permute-start | bytes 1966088 | tf_op jit(solution)/shard_map/ppermute | solution.py:179
  135.6 27.0 %collective-permute-start.33 = (bf16[768,768]{1,0:T(8,128)(2,1)S(1)}, bf16[768,768]{1,0:T(8,128)(2,1)S(1)}, u32[]{:S(2)}, u32[]{:S(2)}) collective-permute-start(bf16[768,768]{1,0:T(8,128)(2,1)S(1)} %convolution_convert_fusion.2), channel_id=1, source_target_pairs={{0,1},{1,0},{2,3},{3,2},{4,5},{5,4},{6,7},{7,6},{8,9},{9,8},{10,11... | collective-permute-start | bytes 3538952 | tf_op jit(solution)/shard_map/ppermute | solution.py:175
  135.7 47.8 %collective-permute-start.41 = (bf16[1280,768]{1,0:T(8,128)(2,1)}, bf16[1280,768]{1,0:T(8,128)(2,1)S(1)}, u32[]{:S(2)}, u32[]{:S(2)}) collective-permute-start(bf16[1280,768]{1,0:T(8,128)(2,1)} %collective-permute-done.26.refs_13_), channel_id=1, source_target_pairs={{16,0},{17,1},{18,2},{19,3},{20,4},{21,5},{22,6},{23,7}} | collective-permute-start | bytes 5898248 | tf_op jit(solution)/shard_map/ppermute | solution.py:179
  159.8 4.6 %collective-permute-start.36 = (bf16[768,768]{1,0:T(8,128)(2,1)S(1)}, bf16[768,768]{1,0:T(8,128)(2,1)S(1)}, u32[]{:S(2)}, u32[]{:S(2)}) collective-permute-start(bf16[768,768]{1,0:T(8,128)(2,1)S(1)} %convolution_convert_fusion.1), channel_id=1, source_target_pairs={{0,1},{1,0},{2,3},{3,2},{4,5},{5,4},{6,7},{7,6},{8,9},{9,8},{10,11... | collective-permute-start | bytes 3538952 | tf_op jit(solution)/shard_map/ppermute | solution.py:175
  160.8 2.9 collective-permute-start.30
  161.3 35.8 %collective-permute-start.37 = (bf16[1280,256]{1,0:T(8,128)(2,1)S(1)}, bf16[1280,256]{1,0:T(8,128)(2,1)S(1)}, u32[]{:S(2)}, u32[]{:S(2)}) collective-permute-start(bf16[1280,256]{1,0:T(8,128)(2,1)S(1)} %copy-done.10), channel_id=1, source_target_pairs={{16,0},{17,1},{18,2},{19,3},{20,4},{21,5},{22,6},{23,7}} | collective-permute-start | bytes 1966088 | tf_op jit(solution)/shard_map/ppermute | solution.py:179
  162.9 1.7 collective-permute-start.31
  185.3 23.2 %collective-permute-start.42 = (bf16[768,768]{1,0:T(8,128)(2,1)S(1)}, bf16[768,768]{1,0:T(8,128)(2,1)S(1)}, u32[]{:S(2)}, u32[]{:S(2)}) collective-permute-start(bf16[768,768]{1,0:T(8,128)(2,1)S(1)} %convolution_convert_fusion), channel_id=1, source_target_pairs={{0,1},{1,0},{2,3},{3,2},{4,5},{5,4},{6,7},{7,6},{8,9},{9,8},{10,11... | collective-permute-start | bytes 3538952 | tf_op jit(solution)/shard_map/ppermute | solution.py:175
  197.8 9.3 %collective-permute-start.38 = (f32[128,768]{1,0:T(8,128)S(1)}, f32[128,768]{1,0:T(8,128)S(1)}, u32[]{:S(2)}, u32[]{:S(2)}) collective-permute-start(f32[128,768]{1,0:T(8,128)S(1)} %slice.215), channel_id=1, source_target_pairs={{0,1},{1,0},{2,3},{3,2},{4,5},{5,4},{6,7},{7,6},{8,9},{9,8},{10,11... | collective-permute-start | bytes 1179656 | tf_op jit(solution)/shard_map/ppermute | solution.py:175
  197.9 9.2 %collective-permute-start.43 = (bf16[128,768]{1,0:T(8,128)(2,1)S(1)}, bf16[128,768]{1,0:T(8,128)(2,1)S(1)}, u32[]{:S(2)}, u32[]{:S(2)}) collective-permute-start(bf16[128,768]{1,0:T(8,128)(2,1)S(1)} %get-tuple-element.66), channel_id=1, source_target_pairs={{8,0},{9,1},{10,2},{11,3},{12,4},{13,5},{14,6},{15,7}} | collective-permute-start | bytes 589832 | tf_op jit(solution)/shard_map/ppermute | solution.py:179
  200.0 24.4 %collective-permute-start.62 = (bf16[128,768]{1,0:T(8,128)(2,1)S(1)}, bf16[128,768]{1,0:T(8,128)(2,1)S(1)}, u32[]{:S(2)}, u32[]{:S(2)}) collective-permute-start(bf16[128,768]{1,0:T(8,128)(2,1)S(1)} %get-tuple-element.82.refs_1_.refs_2_.refs_9_), channel_id=1, source_target_pairs={{0,6},{1,7},{2,4},{3,5},{4,2},{5,3},{6,0},{7,1},{8,14},{9,15},{10,... | collective-permute-start | bytes 589832 | tf_op jit(solution)/shard_map/ppermute | solution.py:170
  201.4 23.6 %collective-permute-start.61 = (bf16[128,768]{1,0:T(8,128)(2,1)S(1)}, bf16[128,768]{1,0:T(8,128)(2,1)S(1)}, u32[]{:S(2)}, u32[]{:S(2)}) collective-permute-start(bf16[128,768]{1,0:T(8,128)(2,1)S(1)} %get-tuple-element.82.refs_1_.refs_2_.refs_9_), channel_id=1, source_target_pairs={{0,4},{1,5},{2,6},{3,7},{4,0},{5,1},{6,2},{7,3},{8,12},{9,13},{10,... | collective-permute-start | bytes 589832 | tf_op jit(solution)/shard_map/ppermute | solution.py:170
  207.1 18.0 %collective-permute-start.60 = (bf16[128,768]{1,0:T(8,128)(2,1)S(1)}, bf16[128,768]{1,0:T(8,128)(2,1)S(1)}, u32[]{:S(2)}, u32[]{:S(2)}) collective-permute-start(bf16[128,768]{1,0:T(8,128)(2,1)S(1)} %get-tuple-element.82.refs_1_.refs_2_.refs_9_), channel_id=1, source_target_pairs={{0,2},{1,3},{2,0},{3,1},{4,6},{5,7},{6,4},{7,5},{8,10},{9,11},{10,... | collective-permute-start | bytes 589832 | tf_op jit(solution)/shard_map/ppermute | solution.py:170
  207.2 12.5 %collective-permute-start.39 = (bf16[128,768]{1,0:T(8,128)(2,1)S(1)}, bf16[128,768]{1,0:T(8,128)(2,1)S(1)}, u32[]{:S(2)}, u32[]{:S(2)}) collective-permute-start(bf16[128,768]{1,0:T(8,128)(2,1)S(1)} %get-tuple-element.62), channel_id=1, source_target_pairs={{16,0},{17,1},{18,2},{19,3},{20,4},{21,5},{22,6},{23,7}} | collective-permute-start | bytes 589832 | tf_op jit(solution)/shard_map/ppermute | solution.py:179
  208.5 9.3 %collective-permute-start.40 = (bf16[128,768]{1,0:T(8,128)(2,1)S(1)}, bf16[128,768]{1,0:T(8,128)(2,1)S(1)}, u32[]{:S(2)}, u32[]{:S(2)}) collective-permute-start(bf16[128,768]{1,0:T(8,128)(2,1)S(1)} %get-tuple-element.68), channel_id=1, source_target_pairs={{24,0},{25,1},{26,2},{27,3},{28,4},{29,5},{30,6},{31,7}} | collective-permute-start | bytes 589832 | tf_op jit(solution)/shard_map/ppermute | solution.py:179
  217.9 8.9 %collective-permute-start.20 = (bf16[512,256]{1,0:T(8,128)(2,1)S(1)}, bf16[512,256]{1,0:T(8,128)(2,1)S(1)}, u32[]{:S(2)}, u32[]{:S(2)}) collective-permute-start(bf16[512,256]{1,0:T(8,128)(2,1)S(1)} %get-tuple-element.53), channel_id=1, source_target_pairs={{0,2},{1,3},{2,0},{3,1},{4,6},{5,7},{6,4},{7,5},{8,10},{9,11},{10,... | collective-permute-start | bytes 786440 | tf_op jit(solution)/shard_map/ppermute | solution.py:170
  219.7 9.6 %collective-permute-start.55 = (bf16[128,768]{1,0:T(8,128)(2,1)S(1)}, bf16[128,768]{1,0:T(8,128)(2,1)S(1)}, u32[]{:S(2)}, u32[]{:S(2)}) collective-permute-start(bf16[128,768]{1,0:T(8,128)(2,1)S(1)} %add.239.refs_14_), channel_id=1, source_target_pairs={{0,1},{1,0},{2,3},{3,2},{4,5},{5,4},{6,7},{7,6},{8,9},{9,8},{10,11... | collective-permute-start | bytes 589832 | tf_op jit(solution)/shard_map/ppermute | solution.py:175
  224.4 4.9 %collective-permute-start.56 = (bf16[128,768]{1,0:T(8,128)(2,1)S(1)}, bf16[128,768]{1,0:T(8,128)(2,1)S(1)}, u32[]{:S(2)}, u32[]{:S(2)}) collective-permute-start(bf16[128,768]{1,0:T(8,128)(2,1)S(1)} %get-tuple-element.114), channel_id=1, source_target_pairs={{0,1},{1,0},{2,3},{3,2},{4,5},{5,4},{6,7},{7,6},{8,9},{9,8},{10,11... | collective-permute-start | bytes 589832 | tf_op jit(solution)/shard_map/ppermute | solution.py:175
  225.0 4.8 %collective-permute-start.51 = (bf16[128,768]{1,0:T(8,128)(2,1)S(1)}, bf16[128,768]{1,0:T(8,128)(2,1)S(1)}, u32[]{:S(2)}, u32[]{:S(2)}) collective-permute-start(bf16[128,768]{1,0:T(8,128)(2,1)S(1)} %get-tuple-element.82.refs_1_.refs_2_.refs_9_), channel_id=1, source_target_pairs={{0,1},{1,0},{2,3},{3,2},{4,5},{5,4},{6,7},{7,6},{8,9},{9,8},{10,11... | collective-permute-start | bytes 589832 | tf_op jit(solution)/shard_map/ppermute | solution.py:175
  225.1 29.9 %collective-permute-start.21 = (bf16[512,256]{1,0:T(8,128)(2,1)S(1)}, bf16[512,256]{1,0:T(8,128)(2,1)S(1)}, u32[]{:S(2)}, u32[]{:S(2)}) collective-permute-start(bf16[512,256]{1,0:T(8,128)(2,1)S(1)} %get-tuple-element.54), channel_id=1, source_target_pairs={{0,4},{1,5},{2,6},{3,7},{4,0},{5,1},{6,2},{7,3},{8,12},{9,13},{10,... | collective-permute-start | bytes 786440 | tf_op jit(solution)/shard_map/ppermute | solution.py:170
  226.8 28.2 %collective-permute-start.22 = (bf16[512,256]{1,0:T(8,128)(2,1)S(1)}, bf16[512,256]{1,0:T(8,128)(2,1)S(1)}, u32[]{:S(2)}, u32[]{:S(2)}) collective-permute-start(bf16[512,256]{1,0:T(8,128)(2,1)S(1)} %get-tuple-element.55), channel_id=1, source_target_pairs={{0,6},{1,7},{2,4},{3,5},{4,2},{5,3},{6,0},{7,1},{8,14},{9,15},{10,... | collective-permute-start | bytes 786440 | tf_op jit(solution)/shard_map/ppermute | solution.py:170
  229.3 1.4 collective-permute-start.52
  229.3 2.8 collective-permute-start.53
  229.8 2.3 collective-permute-start.54
  230.7 24.7 %collective-permute-start.46 = (bf16[128,768]{1,0:T(8,128)(2,1)S(1)}, bf16[128,768]{1,0:T(8,128)(2,1)S(1)}, u32[]{:S(2)}, u32[]{:S(2)}) collective-permute-start(bf16[128,768]{1,0:T(8,128)(2,1)S(1)} %get-tuple-element.70.refs_4_), channel_id=1, source_target_pairs={{0,6},{1,7},{2,4},{3,5},{4,2},{5,3},{6,0},{7,1},{8,14},{9,15},{10,... | collective-permute-start | bytes 589832 | tf_op jit(solution)/shard_map/ppermute | solution.py:170
  232.1 36.4 %collective-permute-start.45 = (bf16[128,768]{1,0:T(8,128)(2,1)S(1)}, bf16[128,768]{1,0:T(8,128)(2,1)S(1)}, u32[]{:S(2)}, u32[]{:S(2)}) collective-permute-start(bf16[128,768]{1,0:T(8,128)(2,1)S(1)} %get-tuple-element.70.refs_4_), channel_id=1, source_target_pairs={{0,4},{1,5},{2,6},{3,7},{4,0},{5,1},{6,2},{7,3},{8,12},{9,13},{10,... | collective-permute-start | bytes 589832 | tf_op jit(solution)/shard_map/ppermute | solution.py:170
  232.1 36.4 %collective-permute-start.44 = (bf16[128,768]{1,0:T(8,128)(2,1)S(1)}, bf16[128,768]{1,0:T(8,128)(2,1)S(1)}, u32[]{:S(2)}, u32[]{:S(2)}) collective-permute-start(bf16[128,768]{1,0:T(8,128)(2,1)S(1)} %get-tuple-element.70.refs_4_), channel_id=1, source_target_pairs={{0,2},{1,3},{2,0},{3,1},{4,6},{5,7},{6,4},{7,5},{8,10},{9,11},{10,... | collective-permute-start | bytes 589832 | tf_op jit(solution)/shard_map/ppermute | solution.py:170
  255.0 14.0 %collective-permute-start.47 = (bf16[128,768]{1,0:T(8,128)(2,1)S(1)}, bf16[128,768]{1,0:T(8,128)(2,1)S(1)}, u32[]{:S(2)}, u32[]{:S(2)}) collective-permute-start(bf16[128,768]{1,0:T(8,128)(2,1)S(1)} %get-tuple-element.70.refs_4_), channel_id=1, source_target_pairs={{0,1},{1,0},{2,3},{3,2},{4,5},{5,4},{6,7},{7,6},{8,9},{9,8},{10,11... | collective-permute-start | bytes 589832 | tf_op jit(solution)/shard_map/ppermute | solution.py:175
  255.0 14.0 %collective-permute-start.63 = (bf16[128,768]{1,0:T(8,128)(2,1)S(1)}, bf16[128,768]{1,0:T(8,128)(2,1)S(1)}, u32[]{:S(2)}, u32[]{:S(2)}) collective-permute-start(bf16[128,768]{1,0:T(8,128)(2,1)S(1)} %collective-permute-done.60.refs_10_), channel_id=1, source_target_pairs={{0,1},{1,0},{2,3},{3,2},{4,5},{5,4},{6,7},{7,6},{8,9},{9,8},{10,11... | collective-permute-start | bytes 589832 | tf_op jit(solution)/shard_map/ppermute | solution.py:175
  255.5 15.5 %collective-permute-start.50 = (bf16[128,768]{1,0:T(8,128)(2,1)S(1)}, bf16[128,768]{1,0:T(8,128)(2,1)S(1)}, u32[]{:S(2)}, u32[]{:S(2)}) collective-permute-start(bf16[128,768]{1,0:T(8,128)(2,1)S(1)} %collective-permute-done.46.refs_7_), channel_id=1, source_target_pairs={{0,1},{1,0},{2,3},{3,2},{4,5},{5,4},{6,7},{7,6},{8,9},{9,8},{10,11... | collective-permute-start | bytes 589832 | tf_op jit(solution)/shard_map/ppermute | solution.py:175
  268.5 4.9 %collective-permute-start.49 = (bf16[128,768]{1,0:T(8,128)(2,1)S(1)}, bf16[128,768]{1,0:T(8,128)(2,1)S(1)}, u32[]{:S(2)}, u32[]{:S(2)}) collective-permute-start(bf16[128,768]{1,0:T(8,128)(2,1)S(1)} %collective-permute-done.45.refs_6_), channel_id=1, source_target_pairs={{0,1},{1,0},{2,3},{3,2},{4,5},{5,4},{6,7},{7,6},{8,9},{9,8},{10,11... | collective-permute-start | bytes 589832 | tf_op jit(solution)/shard_map/ppermute | solution.py:175
  268.5 4.9 %collective-permute-start.48 = (bf16[128,768]{1,0:T(8,128)(2,1)S(1)}, bf16[128,768]{1,0:T(8,128)(2,1)S(1)}, u32[]{:S(2)}, u32[]{:S(2)}) collective-permute-start(bf16[128,768]{1,0:T(8,128)(2,1)S(1)} %collective-permute-done.44.refs_5_), channel_id=1, source_target_pairs={{0,1},{1,0},{2,3},{3,2},{4,5},{5,4},{6,7},{7,6},{8,9},{9,8},{10,11... | collective-permute-start | bytes 589832 | tf_op jit(solution)/shard_map/ppermute | solution.py:175
  269.0 12.7 %collective-permute-start.57 = (bf16[512,256]{1,0:T(8,128)(2,1)S(1)}, bf16[512,256]{1,0:T(8,128)(2,1)S(1)}, u32[]{:S(2)}, u32[]{:S(2)}) collective-permute-start(bf16[512,256]{1,0:T(8,128)(2,1)S(1)} %get-tuple-element.78), channel_id=1, source_target_pairs={{0,2},{1,3},{2,0},{3,1},{4,6},{5,7},{6,4},{7,5},{8,10},{9,11},{10,... | collective-permute-start | bytes 786440 | tf_op jit(solution)/shard_map/ppermute | solution.py:170
  269.0 21.4 %collective-permute-start.58 = (bf16[512,256]{1,0:T(8,128)(2,1)S(1)}, bf16[512,256]{1,0:T(8,128)(2,1)S(1)}, u32[]{:S(2)}, u32[]{:S(2)}) collective-permute-start(bf16[512,256]{1,0:T(8,128)(2,1)S(1)} %get-tuple-element.79), channel_id=1, source_target_pairs={{0,4},{1,5},{2,6},{3,7},{4,0},{5,1},{6,2},{7,3},{8,12},{9,13},{10,... | collective-permute-start | bytes 786440 | tf_op jit(solution)/shard_map/ppermute | solution.py:170
  271.0 19.4 %collective-permute-start.59 = (bf16[512,256]{1,0:T(8,128)(2,1)S(1)}, bf16[512,256]{1,0:T(8,128)(2,1)S(1)}, u32[]{:S(2)}, u32[]{:S(2)}) collective-permute-start(bf16[512,256]{1,0:T(8,128)(2,1)S(1)} %get-tuple-element.80), channel_id=1, source_target_pairs={{0,6},{1,7},{2,4},{3,5},{4,2},{5,3},{6,0},{7,1},{8,14},{9,15},{10,... | collective-permute-start | bytes 786440 | tf_op jit(solution)/shard_map/ppermute | solution.py:170
  273.4 1.4 collective-permute-start.64
  273.4 1.7 collective-permute-start.65
  (29 other events, 185.6 us)

commit v7 on v5

--- a/solution.py
+++ b/solution.py
@@ -286,8 +286,17 @@
     early = CHIPS * CORES - 2
     held, refs = refs[:early], refs[early:]
     sources = [(refs[0], refs[1]), (refs[2], refs[3]), refs[4], refs[5]]
-    scaled_ref, slope_ref, score_ref, chain_ref, near_ref, far_ref = refs[6:12]
-    own_ref, gram_ref, arrived = refs[12:]
+    token_refs, refs = refs[6 : 5 + CHIPS], refs[5 + CHIPS :]
+    scaled_ref, slope_ref, score_ref, chain_ref = refs[:4]
+    sent_refs, (near_ref, far_ref) = refs[4 : 3 + CHIPS], refs[3 + CHIPS : 5 + CHIPS]
+    own_ref, gram_ref, arrived, moved = refs[5 + CHIPS :]
+    tall, width = token_refs[0].shape
+    moves = [
+        pltpu.make_async_copy(token_ref, sent_ref.at[pl.ds(0, tall), :], moved.at[place])
+        for place, (token_ref, sent_ref) in enumerate(zip(token_refs, sent_refs))
+    ]
+    for move in moves:
+        move.start()
     last = [near_ref, far_ref]
     copies = fetch(middle_ref[0] > 0, sources, [*last, own_ref, gram_ref], arrived)
     core_refs, count = [*held, *last], early + 2
@@ -302,12 +311,20 @@
     copies[3].wait()
     score = own_ref[...] + dot(scaled, gram_ref[...])
     scaled_ref[...] = scaled
+    rows = scaled.shape[0]
+    for sent_ref in sent_refs:
+        for group in range(scaled.shape[1] // width):
+            sent_ref[pl.ds(tall + group * rows, rows), :] = scaled[
+                :, group * width : (group + 1) * width
+            ]
     slope_ref[...] = slope
     score_ref[...] = score
     _, grad_proj = backward_rows(score, slope, marks, core_refs)
     chain_ref[...] = (scaled.astype(jnp.float32) + grad_proj.astype(jnp.float32)).astype(
         jnp.bfloat16
     )
+    for move in moves:
+        move.wait()
 
 
 def turn_kernel(terms, late, marks_ref, scaled_ref, slope_ref, score_ref, *refs):
@@ -432,12 +449,29 @@
     refs[-1][...] = block_products(refs[-1].shape[0], refs[:-1])
 
 
+def grouped_rows(ref, start, rows):
+    groups = (ref.shape[0] - start) // rows
+    return jnp.concatenate(
+        [ref[start + group * rows : start + (group + 1) * rows, :] for group in range(groups)],
+        axis=1,
+    )
+
+
 def last_kernel(*refs):
     token_refs, refs = refs[:CHIPS], refs[CHIPS:]
-    total_ref, product_refs = refs[0], refs[1:-2]
+    total_ref, product_refs, scaled_refs = refs[0], refs[1 : 1 + CHIPS], refs[1 + CHIPS : -2]
     share_ref, core_ref = refs[-2:]
     count = share_ref.shape[0]
-    share_ref[...] = total_ref[...] + block_products(count, product_refs)
+    rows, tall = scaled_refs[0].shape[0], token_refs[0].shape[0]
+    total = total_ref[...]
+    for step in range(CHIPS):
+        if step == 0:
+            near, far = scaled_refs[0][...], scaled_refs[1][...]
+        else:
+            near = grouped_rows(token_refs[step], tall, rows)
+            far = grouped_rows(scaled_refs[1 + step], 0, rows)
+        total = total + dot(product_refs[step][:count, :], jnp.concatenate([near, far], axis=0))
+    share_ref[...] = total
     width = token_refs[0].shape[1]
     slots = (token_refs[0].shape[0] - count) * width // core_ref.shape[0]
 
@@ -543,23 +577,24 @@
     flag = middle.astype(jnp.int32).reshape(1)
     block = pltpu.VMEM((ranks, ranks), bf16)
 
-    def core_call(body, sources, outs, arrays, scratch, products):
+    def core_call(body, sources, outs, arrays, scratch, products, extra=()):
         flat = [ref for source in sources for ref in (source if type(source) is tuple else [source])]
+        moved = [pltpu.SemaphoreType.DMA((len(extra),))] if extra else []
         return pl.pallas_call(
             body,
             out_shape=outs,
             in_specs=[pl.BlockSpec(memory_space=pltpu.SMEM)]
             + [pl.BlockSpec(memory_space=pltpu.VMEM)] * len(arrays)
-            + [pl.BlockSpec(memory_space=pl.ANY)] * len(flat),
+            + [pl.BlockSpec(memory_space=pl.ANY)] * (len(flat) + len(extra)),
             out_specs=[pl.BlockSpec(memory_space=pltpu.VMEM)] * len(outs),
-            scratch_shapes=scratch + [pltpu.SemaphoreType.DMA((len(sources),))],
+            scratch_shapes=scratch + [pltpu.SemaphoreType.DMA((len(sources),))] + moved,
             compiler_params=pltpu.CompilerParams(vmem_limit_bytes=ROOM),
             cost_estimate=pl.CostEstimate(
                 flops=product_flops * products,
                 bytes_accessed=2 * len(sources) * ranks * ranks,
                 transcendentals=0,
             ),
-        )(flag, *arrays, *flat)
+        )(flag, *arrays, *flat, *extra)
 
     part, *held = core_call(
         early_kernel,
@@ -569,14 +604,19 @@
         [],
         devices - 2,
     )
+    sent = pltpu.VMEM((token_blocks[0].shape[0] + ranks // CORES, CORES * rows), bf16)
     scaled, slope, score, chain, *last = core_call(
         first_kernel,
         [*travelled[-2:], own_score, gram],
-        [jax.ShapeDtypeStruct(wide, kind) for kind in (bf16, f32, f32, bf16)] + [block] * 2,
+        [jax.ShapeDtypeStruct(wide, kind) for kind in (bf16, f32, f32, bf16)]
+        + [sent] * (CHIPS - 1)
+        + [block] * 2,
         [projected, marks, part, *held],
         [pltpu.VMEM(wide, f32), pltpu.VMEM((ranks, ranks), bf16)],
         devices + 3,
-    )
+        token_blocks[1:],
+    )
+    sent, last = last[: CHIPS - 1], last[CHIPS - 1 :]
     pieces = [*held, *last]
 
     def turn(score, late, terms):
@@ -595,9 +635,8 @@
     chain_first = chain
     first_down = between_layers(chain, [(3, 2)])
     first_two = between_layers(chain, [(3, 1)])
-    scaled_rows = [scaled] + [across_chips(after(scaled, chain), step) for step in range(1, CHIPS)]
     token_blocks = token_blocks[:1] + [
-        across_chips(after(token_blocks[step], chain), step) for step in range(1, CHIPS)
+        across_chips(sent[step - 1], step) for step in range(1, CHIPS)
     ]
     score, _, _, chain = turn(score, [down_score], [(first_down, down_gram)])
 
@@ -650,11 +689,12 @@
         *grad_slots,
     )
     mixed_first = mixed_blocks[0]
-    scaled_rows = [after(rows, mixed_first) for rows in scaled_rows]
+    tall = token_blocks[0].shape[0]
+    scaled_parts = [after(part, mixed_first)[tall:] for part in token_blocks[1:]]
     mixed_blocks = list(mixed_blocks[:1]) + [
         across_chips(mixed_blocks[step], step) for step in range(1, CHIPS)
     ]
-    scaled_rows = scaled_rows + [scaled_pair[1]] + [swap_cores(rows) for rows in scaled_rows[1:]]
+    scaled_rows = [*scaled_pair, *(swap_cores(part) for part in scaled_parts)]
     share = jax.ShapeDtypeStruct((channels // devices, ranks), f32)
     share_flops = 2 * channels * rows * ranks
     token_share = block_call(token_kernel, [share], token_blocks + proj_rows, share_flops)

time: 291 us -> 318 us (1.093)
  waiting for transfers between devices: 163 us -> 198 us
    ppermute x14, waiting for transfers between devices: 98.1 us -> 143 us  [between_layers(): return lax.ppermute(value, 'section', pairs)]
    ppermute x17 -> x14, waiting for transfers between devices: 63.5 us -> 53.2 us  [on_chips(): return lax.ppermute(value, 'expert', perm)]
    ppermute x17 -> x14, starting transfers between devices: 25.8 us -> 22.8 us  [on_chips(): return lax.ppermute(value, 'expert', perm)]
  transfers between devices with their start and end apart: 62 -> 59, of which waited for: 19 -> 19; matrix products, arithmetic and copies ran while one was open for 11% -> 9% of each run, Pallas kernels for 9% -> 8%
where the time goes in v7:
time: 318 us; the launch traced here: 315 us
  waiting for transfers between devices  198 us (62%)
  starting transfers between devices  51.7 us (16%)
  Pallas kernels  28.4 us (9%)
  matrix products  17.4 us (5%)
  other arithmetic  9.73 us (3%)
  local copies, waits for them, and re-layouts  7.98 us (3%)
    ppermute x14, waiting for transfers between devices, between_layers(): return lax.ppermute(value, 'section', pairs)  143 us
    ppermute x14, waiting for transfers between devices, on_chips(): return lax.ppermute(value, 'expert', perm)  53.2 us
    ppermute x14, starting transfers between devices, on_chips(): return lax.ppermute(value, 'expert', perm)  22.8 us
    ppermute x14, starting transfers between devices, between_layers(): return lax.ppermute(value, 'section', pairs)  21.1 us
    dot_general x9, matrix products, dot_first(): lax.dot_general(left, right, (((0,), (0,)), ((), ())), preferred_element_...  16.2 us
    pallas_call x3, Pallas kernels, call_rows(): pl.pallas_call(body, out_shape=[jax.ShapeDtypeStruct(shape, kind) for sha...  12.2 us
    pallas_call x2, Pallas kernels, core_call(): pl.pallas_call(body, out_shape=outs, in_specs=[pl.BlockSpec(memory_space=...  8.54 us
    ppermute x31, starting transfers between devices, swap_cores(): lax.ppermute(value, 'expert', [(index, index ^ 1) for index in range(coun...  7.76 us
  transfers between devices with their start and end apart: 59, of which 19 were waited for; matrix products, arithmetic and copies ran while one was open for 9% of the time, Pallas kernels for 8%

profile of v7, /device:TPU:0, one launch (start us, length us, event | category | flops | bytes accessed | tf_op | source)
XLA Modules:
  0.0 315.0 jit_solution(4875072332227689453)
XLA Ops:
  0.7 1.4 copy.11
  2.2 0.8 constant_dynamic-slice_fusion.15
  2.9 0.7 pad_maximum_fusion.3
  4.7 0.7 constant_dynamic-slice_fusion.7
  5.5 0.7 pad_maximum_fusion.4
  6.2 3.1 collective-permute-start.3
  9.4 1.7 dynamic-slice_bitcast_fusion.3
  11.3 2.0 copy-done.1
  14.2 1.9 pad_maximum_fusion.2
  16.1 1.3 collective-permute-start.19
  17.4 1.7 fusion.15
  20.1 1.1 collective-permute-done.1
  21.2 1.7 collective-permute-start.5
  23.2 1.3 collective-permute-start.28
  24.5 10.1 %collective-permute-done.19 = bf16[1280,256]{1,0:T(8,128)(2,1)} collective-permute-done((bf16[1280,256]{1,0:T(8,128)(2,1)}, bf16[1280,256]{1,0:T(8,128)(2,1)}, u32[]{:S(2)}, u32[]{:S(2)}) %collective-permute-start.19) | collective-permute-done | bytes 655392 | tf_op jit(solution)/shard_map/ppermute | solution.py:179
  34.7 1.3 collective-permute-start.24
  36.0 2.8 convolution_convert_fusion.4
  38.9 45.4 %collective-permute-done.24 = bf16[1280,256]{1,0:T(8,128)(2,1)} collective-permute-done((bf16[1280,256]{1,0:T(8,128)(2,1)}, bf16[1280,256]{1,0:T(8,128)(2,1)}, u32[]{:S(2)}, u32[]{:S(2)}) %collective-permute-start.24) | collective-permute-done | bytes 655392 | tf_op jit(solution)/shard_map/ppermute | solution.py:179
  84.2 0.7 collective-permute-start.9
  85.0 1.2 pad_maximum_fusion.1
  86.2 1.3 collective-permute-start.22
  87.5 1.8 fusion.17
  91.3 1.3 collective-permute-start.6
  92.6 1.3 collective-permute-start.10
  94.6 39.9 %collective-permute-done.22.refs_13_ = bf16[1280,768]{1,0:T(8,128)(2,1)S(1)} collective-permute-done((bf16[1280,768]{1,0:T(8,128)(2,1)S(1)}, bf16[1280,768]{1,0:T(8,128)(2,1)S(1)}, u32[]{:S(2)}, u32[]{:S(2)}) %collective-permute-start.22) | collective-permute-done | bytes 1966112 | tf_op jit(solution)/shard_map/ppermute | solution.py:179
  134.5 1.6 collective-permute-start.31
  136.6 12.6 %collective-permute-done.10.refs_7_ = bf16[768,768]{1,0:T(8,128)(2,1)S(1)} collective-permute-done((bf16[768,768]{1,0:T(8,128)(2,1)S(1)}, bf16[768,768]{1,0:T(8,128)(2,1)S(1)}, u32[]{:S(2)}, u32[]{:S(2)}) %collective-permute-start.10) | collective-permute-done | bytes 1179680 | tf_op jit(solution)/shard_map/ppermute | solution.py:170
  149.2 1.8 convolution_convert_fusion.3
  152.0 3.3 %convolution_convert_fusion.2 = bf16[768,768]{1,0:T(8,128)(2,1)S(1)} fusion(bf16[1280,768]{1,0:T(8,128)(2,1)} %collective-permute-done.28.refs_4_, bf16[1280,768]{1,0:T(8,128)(2,1)S(1)} %pad_maximum_fusion.refs_1_), kind=kOutput, calls=%fused_computation.10 | convolution fusion | flops 1510539264 | bytes 5111808 | tf_op jit(solution)/shard_map/dot_general | solution.py:159
  155.3 5.7 %collective-permute-start.25 = (bf16[1280,256]{1,0:T(8,128)(2,1)}, bf16[1280,256]{1,0:T(8,128)(2,1)S(1)}, u32[]{:S(2)}, u32[]{:S(2)}) collective-permute-start(bf16[1280,256]{1,0:T(8,128)(2,1)} %collective-permute-done.24), channel_id=1, source_target_pairs={{0,8},{1,9},{2,10},{3,11},{4,12},{5,13},{6,14},{7,15}} | collective-permute-start | bytes 1966088 | tf_op jit(solution)/shard_map/ppermute | solution.py:179
  161.0 3.5 %shard_map.86 = (f32[128,768]{1,0:T(8,128)S(1)}, bf16[768,768]{1,0:T(8,128)(2,1)S(1)}, bf16[768,768]{1,0:T(8,128)(2,1)S(1)}, bf16[768,768]{1,0:T(8,128)(2,1)S(1)...) custom-call(s32[1]{0:T(128)} %bitcast.3.middle_ref, ...), custom_call_target="tpu_custom_call" | custom-call | flops 905969664 | bytes 7077888 | tf_op jit(solution)/shard_map/pallas_call | solution.py:583
  164.7 1.3 collective-permute-start.37
  166.0 5.0 %shard_map.87 = (bf16[128,768]{1,0:T(8,128)(2,1)S(1)}, f32[128,768]{1,0:T(8,128)S(1)}, f32[128,768]{1,0:T(8,128)S(1)}, bf16[128,768]{1,0:T(8,128)(2,1)S(1)}, bf1...) custom-call(s32[1]{0:T(128)} %bitcast.3.middle_ref, ...), custom_call_target="tpu_custom_call" | custom-call | flops 1660944384 | bytes 4718592 | tf_op jit(solution)/shard_map/pallas_call | solution.py:583
  172.0 3.8 %shard_map.88 = (f32[128,768]{1,0:T(8,128)S(1)}, bf16[128,768]{1,0:T(8,128)(2,1)}, bf16[128,768]{1,0:T(8,128)(2,1)}, bf16[128,768]{1,0:T(8,128)(2,1)S(1)}) custom-call(f32[128,16]{1,0:T(8,128)S(1)} %convert_select_fusion.marks_ref.refs_0_, bf16[128,768]{1,0:T(8,128)(2,1)S(1)} %get-tuple-element.70.refs_1_.refs_2_.refs_9_, ...), custom_call_target="tpu_custom_call" | custom-call | flops 1358954496 | bytes 12197888 | tf_op jit(solution)/shard_map/pallas_call | solution.py:349
  175.8 3.7 %collective-permute-done.31.refs_7_ = bf16[1280,768]{1,0:T(8,128)(2,1)S(1)} collective-permute-done((bf16[1280,768]{1,0:T(8,128)(2,1)}, bf16[1280,768]{1,0:T(8,128)(2,1)S(1)}, u32[]{:S(2)}, u32[]{:S(2)}) %collective-permute-start.31) | collective-permute-done | bytes 1966112 | tf_op jit(solution)/shard_map/ppermute | solution.py:179
  179.4 1.8 convolution_convert_fusion.1
  181.2 11.4 %collective-permute-done.25 = bf16[1280,256]{1,0:T(8,128)(2,1)S(1)} collective-permute-done((bf16[1280,256]{1,0:T(8,128)(2,1)}, bf16[1280,256]{1,0:T(8,128)(2,1)S(1)}, u32[]{:S(2)}, u32[]{:S(2)}) %collective-permute-start.25) | collective-permute-done | bytes 655392 | tf_op jit(solution)/shard_map/ppermute | solution.py:179
  192.6 1.3 add_convert_fusion.6
  195.2 1.3 collective-permute-start.33
  197.5 0.9 collective-permute-start.30
  198.8 4.0 %shard_map.89 = (f32[128,768]{1,0:T(8,128)S(1)}, bf16[128,768]{1,0:T(8,128)(2,1)}, bf16[128,768]{1,0:T(8,128)(2,1)}, bf16[128,768]{1,0:T(8,128)(2,1)S(1)}) custom-call(f32[128,16]{1,0:T(8,128)S(1)} %convert_select_fusion.marks_ref.refs_0_, bf16[128,768]{1,0:T(8,128)(2,1)S(1)} %get-tuple-element.70.refs_1_.refs_2_.refs_9_, ...), custom_call_target="tpu_custom_call" | custom-call | flops 1509949440 | bytes 13574144 | tf_op jit(solution)/shard_map/pallas_call | solution.py:349
  202.8 9.4 %collective-permute-done.37.refs_10_ = bf16[1280,768]{1,0:T(8,128)(2,1)S(1)} collective-permute-done((bf16[1280,768]{1,0:T(8,128)(2,1)S(1)}, bf16[1280,768]{1,0:T(8,128)(2,1)S(1)}, u32[]{:S(2)}, u32[]{:S(2)}) %collective-permute-start.37) | collective-permute-done | bytes 1966112 | tf_op jit(solution)/shard_map/ppermute | solution.py:179
  212.2 1.7 convolution_convert_fusion
  214.1 11.7 %collective-permute-done.33 = bf16[1280,256]{1,0:T(8,128)(2,1)S(1)} collective-permute-done((bf16[1280,256]{1,0:T(8,128)(2,1)}, bf16[1280,256]{1,0:T(8,128)(2,1)S(1)}, u32[]{:S(2)}, u32[]{:S(2)}) %collective-permute-start.33) | collective-permute-done | bytes 655392 | tf_op jit(solution)/shard_map/ppermute | solution.py:179
  226.6 1.3 collective-permute-start.39
  227.9 2.7 collective-permute-start.18
  230.6 1.3 collective-permute-start.35
  231.9 3.9 %collective-permute-done.39.refs_9_ = bf16[128,768]{1,0:T(8,128)(2,1)S(1)} collective-permute-done((bf16[128,768]{1,0:T(8,128)(2,1)S(1)}, bf16[128,768]{1,0:T(8,128)(2,1)S(1)}, u32[]{:S(2)}, u32[]{:S(2)}) %collective-permute-start.39) | collective-permute-done | bytes 196640 | tf_op jit(solution)/shard_map/ppermute | solution.py:179
  235.8 1.3 collective-permute-start.36
  237.6 7.4 %collective-permute-done.36.refs_7_.refs_11_ = bf16[128,768]{1,0:T(8,128)(2,1)S(1)} collective-permute-done((bf16[128,768]{1,0:T(8,128)(2,1)S(1)}, bf16[128,768]{1,0:T(8,128)(2,1)S(1)}, u32[]{:S(2)}, u32[]{:S(2)}) %collective-permute-start.36) | collective-permute-done | bytes 196640 | tf_op jit(solution)/shard_map/ppermute | solution.py:179
  245.0 4.4 %shard_map.90 = (f32[128,768]{1,0:T(8,128)}, bf16[128,768]{1,0:T(8,128)(2,1)S(1)}, bf16[128,768]{1,0:T(8,128)(2,1)S(1)}, bf16[128,768]{1,0:T(8,128)(2,1)}) custom-call(f32[128,16]{1,0:T(8,128)S(1)} %convert_select_fusion.marks_ref.refs_0_, bf16[128,768]{1,0:T(8,128)(2,1)S(1)} %get-tuple-element.70.refs_1_.refs_2_.refs_9_, ...), custom_call_target="tpu_custom_call" | custom-call | flops 1660944384 | bytes 14950400 | tf_op jit(solution)/shard_map/pallas_call | solution.py:349
  250.4 3.3 %collective-permute-start.17 = (bf16[896,256]{1,0:T(8,128)(2,1)S(1)}, bf16[896,256]{1,0:T(8,128)(2,1)S(1)}, u32[]{:S(2)}, u32[]{:S(2)}) collective-permute-start(bf16[896,256]{1,0:T(8,128)(2,1)S(1)} %get-tuple-element.51), channel_id=1, source_target_pairs={{0,4},{1,5},{2,6},{3,7},{4,0},{5,1},{6,2},{7,3},{8,12},{9,13},{10,... | collective-permute-start | bytes 1376264 | tf_op jit(solution)/shard_map/ppermute | solution.py:170
  254.2 1.5 add_convert_fusion.5.refs_0_
  255.8 1.3 collective-permute-start.42
  257.3 2.9 collective-permute-start.40
  260.2 4.7 %spread.1 = (bf16[512,256]{1,0:T(8,128)(2,1)S(1)}, bf16[512,256]{1,0:T(8,128)(2,1)S(1)}, bf16[512,256]{1,0:T(8,128)(2,1)S(1)}, bf16[512,256]{1,0:T(8,128)(2,1)S(1)}) custom-call(bf16[1280,256]{1,0:T(8,128)(2,1)S(1)} %add_convert_fusion.5.refs_0_, bf16[1280,768]{1,0:T(8,128)(2,1)S(1)} %pad_maximum_fusion.refs_1_, ...), custom_call_target="tpu_custom_call" | custom-call | flops 2516582400 | bytes 12845056 | tf_op jit(solution)/shard_map/spread/pallas_call | solution.py:420
  265.0 7.9 %collective-permute-done.16.refs_1_ = bf16[896,256]{1,0:T(8,128)(2,1)S(1)} collective-permute-done((bf16[896,256]{1,0:T(8,128)(2,1)S(1)}, bf16[896,256]{1,0:T(8,128)(2,1)S(1)}, u32[]{:S(2)}, u32[]{:S(2)}) %collective-permute-start.16) | collective-permute-done | bytes 458784 | tf_op jit(solution)/shard_map/ppermute | solution.py:170
  272.9 10.4 %collective-permute-done.17.refs_2_ = bf16[896,256]{1,0:T(8,128)(2,1)S(1)} collective-permute-done((bf16[896,256]{1,0:T(8,128)(2,1)S(1)}, bf16[896,256]{1,0:T(8,128)(2,1)S(1)}, u32[]{:S(2)}, u32[]{:S(2)}) %collective-permute-start.17) | collective-permute-done | bytes 458784 | tf_op jit(solution)/shard_map/ppermute | solution.py:170
  283.8 7.0 %collective-permute-done.41.refs_6_ = bf16[128,768]{1,0:T(8,128)(2,1)S(1)} collective-permute-done((bf16[128,768]{1,0:T(8,128)(2,1)S(1)}, bf16[128,768]{1,0:T(8,128)(2,1)S(1)}, u32[]{:S(2)}, u32[]{:S(2)}) %collective-permute-start.41) | collective-permute-done | bytes 196640 | tf_op jit(solution)/shard_map/ppermute | solution.py:170
  291.4 2.9 collective-permute-start.54
  294.3 1.5 collective-permute-start.55
  297.6 7.1 %collective-permute-done.53.refs_6_ = bf16[512,256]{1,0:T(8,128)(2,1)S(1)} collective-permute-done((bf16[512,256]{1,0:T(8,128)(2,1)S(1)}, bf16[512,256]{1,0:T(8,128)(2,1)S(1)}, u32[]{:S(2)}, u32[]{:S(2)}) %collective-permute-start.53) | collective-permute-done | bytes 262176 | tf_op jit(solution)/shard_map/ppermute | solution.py:170
  304.7 8.1 %collective-permute-done.54.refs_7_ = bf16[512,256]{1,0:T(8,128)(2,1)S(1)} collective-permute-done((bf16[512,256]{1,0:T(8,128)(2,1)S(1)}, bf16[512,256]{1,0:T(8,128)(2,1)S(1)}, u32[]{:S(2)}, u32[]{:S(2)}) %collective-permute-start.54) | collective-permute-done | bytes 262176 | tf_op jit(solution)/shard_map/ppermute | solution.py:170
  312.8 2.2 shard_map.92
  (161 shorter events, 17.5 us)
Async XLA Ops:
  3.7 19.2 %collective-permute-start = (bf16[1280,128]{1,0:T(8,128)(2,1)}, bf16[1280,128]{1,0:T(8,128)(2,1)}, u32[]{:S(2)}, u32[]{:S(2)}) collective-permute-start(bf16[1280,128]{1,0:T(8,128)(2,1)} %pad_maximum_fusion.3), channel_id=1, source_target_pairs={{0,1},{1,0},{2,3},{3,2},{4,5},{5,4},{6,7},{7,6},{8,9},{9,8},{10,11... | collective-permute-start | bytes 983048 | tf_op jit(solution)/shard_map/ppermute | solution.py:175
  6.2 7.7 %collective-permute-start.13 = (bf16[1280,128]{1,0:T(8,128)(2,1)}, bf16[1280,128]{1,0:T(8,128)(2,1)}, u32[]{:S(2)}, u32[]{:S(2)}) collective-permute-start(bf16[1280,128]{1,0:T(8,128)(2,1)} %pad_maximum_fusion.4), channel_id=1, source_target_pairs={{0,1},{1,0},{2,3},{3,2},{4,5},{5,4},{6,7},{7,6},{8,9},{9,8},{10,11... | collective-permute-start | bytes 983048 | tf_op jit(solution)/shard_map/ppermute | solution.py:175
  6.2 78.0 %collective-permute-start.3 = (bf16[768,768]{1,0:T(8,128)(2,1)S(1)}, bf16[768,768]{1,0:T(8,128)(2,1)}, u32[]{:S(2)}, u32[]{:S(2)}) collective-permute-start(bf16[768,768]{1,0:T(8,128)(2,1)S(1)} %bitcast.41), channel_id=1, source_target_pairs={{0,2},{1,3},{2,0},{3,1},{4,6},{5,7},{6,4},{7,5},{8,10},{9,11},{10,... | collective-permute-start | bytes 3538952 | tf_op jit(solution)/shard_map/ppermute | solution.py:170
  16.1 18.6 %collective-permute-start.19 = (bf16[1280,256]{1,0:T(8,128)(2,1)}, bf16[1280,256]{1,0:T(8,128)(2,1)}, u32[]{:S(2)}, u32[]{:S(2)}) collective-permute-start(bf16[1280,256]{1,0:T(8,128)(2,1)} %pad_maximum_fusion.2), channel_id=1, source_target_pairs={{24,16},{8,0},{25,17},{9,1},{26,18},{10,2},{27,19},{11,3},{28,20},... | collective-permute-start | bytes 1966088 | tf_op jit(solution)/shard_map/ppermute | solution.py:179
  19.1 4.1 %collective-permute-start.14 = (f32[128,768]{1,0:T(8,128)S(1)}, f32[128,768]{1,0:T(8,128)S(1)}, u32[]{:S(2)}, u32[]{:S(2)}) collective-permute-start(f32[128,768]{1,0:T(8,128)S(1)} %slice.190), channel_id=1, source_target_pairs={{0,1},{1,0},{2,3},{3,2},{4,5},{5,4},{6,7},{7,6},{8,9},{9,8},{10,11... | collective-permute-start | bytes 1179656 | tf_op jit(solution)/shard_map/ppermute | solution.py:175
  19.5 19.2 %copy-start.19 = (f32[1,2,64]{2,1,0:T(2,128)S(1)}, f32[1,2,64]{2,1,0:T(2,128)}, u32[]{:S(2)}) copy-start(f32[1,2,64]{2,1,0:T(2,128)} %param.9) | copy-start | bytes 1540
  19.5 1.7 collective-permute-start.1
  21.2 13.5 %copy-start.15 = (bf16[128,768]{1,0:T(8,128)(2,1)}, bf16[128,768]{1,0:T(8,128)(2,1)S(1)}, u32[]{:S(2)}) copy-start(bf16[128,768]{1,0:T(8,128)(2,1)S(1)} %collective-permute-done.1) | copy-start | bytes 589828
  21.2 65.0 %collective-permute-start.5 = (bf16[768,768]{1,0:T(8,128)(2,1)S(1)}, bf16[768,768]{1,0:T(8,128)(2,1)}, u32[]{:S(2)}, u32[]{:S(2)}) collective-permute-start(bf16[768,768]{1,0:T(8,128)(2,1)S(1)} %bitcast.42), channel_id=1, source_target_pairs={{2,4},{3,5},{4,2},{5,3},{10,12},{11,13},{12,10},{13,11},{18,20},{1... | collective-permute-start | bytes 3538952 | tf_op jit(solution)/shard_map/ppermute | solution.py:170
  22.9 66.5 %collective-permute-start.2 = (bf16[768,768]{1,0:T(8,128)(2,1)S(1)}, bf16[768,768]{1,0:T(8,128)(2,1)}, u32[]{:S(2)}, u32[]{:S(2)}) collective-permute-start(bf16[768,768]{1,0:T(8,128)(2,1)S(1)} %bitcast.43), channel_id=1, source_target_pairs={{0,1},{1,0},{2,3},{3,2},{4,5},{5,4},{6,7},{7,6},{8,9},{9,8},{10,11... | collective-permute-start | bytes 3538952 | tf_op jit(solution)/shard_map/ppermute | solution.py:175
  23.2 70.8 %collective-permute-start.28 = (bf16[1280,768]{1,0:T(8,128)(2,1)S(1)}, bf16[1280,768]{1,0:T(8,128)(2,1)}, u32[]{:S(2)}, u32[]{:S(2)}) collective-permute-start(bf16[1280,768]{1,0:T(8,128)(2,1)S(1)} %pad_maximum_fusion.refs_1_), channel_id=1, source_target_pairs={{24,8},{16,0},{25,9},{17,1},{26,10},{18,2},{27,11},{19,3},{28,12},... | collective-permute-start | bytes 5898248 | tf_op jit(solution)/shard_map/ppermute | solution.py:179
  34.7 49.5 %collective-permute-start.24 = (bf16[1280,256]{1,0:T(8,128)(2,1)}, bf16[1280,256]{1,0:T(8,128)(2,1)}, u32[]{:S(2)}, u32[]{:S(2)}) collective-permute-start(bf16[1280,256]{1,0:T(8,128)(2,1)} %pad_maximum_fusion.2), channel_id=1, source_target_pairs={{24,8},{16,0},{25,9},{17,1},{26,10},{18,2},{27,11},{19,3},{28,12},... | collective-permute-start | bytes 1966088 | tf_op jit(solution)/shard_map/ppermute | solution.py:179
  84.2 6.1 %collective-permute-start.15 = (bf16[768,768]{1,0:T(8,128)(2,1)}, bf16[768,768]{1,0:T(8,128)(2,1)S(1)}, u32[]{:S(2)}, u32[]{:S(2)}) collective-permute-start(bf16[768,768]{1,0:T(8,128)(2,1)} %convolution_convert_fusion.4), channel_id=1, source_target_pairs={{0,1},{1,0},{2,3},{3,2},{4,5},{5,4},{6,7},{7,6},{8,9},{9,8},{10,11... | collective-permute-start | bytes 3538952 | tf_op jit(solution)/shard_map/ppermute | solution.py:175
  84.2 8.4 %collective-permute-start.9 = (bf16[768,768]{1,0:T(8,128)(2,1)}, bf16[768,768]{1,0:T(8,128)(2,1)S(1)}, u32[]{:S(2)}, u32[]{:S(2)}) collective-permute-start(bf16[768,768]{1,0:T(8,128)(2,1)} %collective-permute-done.3.refs_2_), channel_id=1, source_target_pairs={{2,4},{3,5},{4,2},{5,3},{10,12},{11,13},{12,10},{13,11},{18,20},{1... | collective-permute-start | bytes 3538952 | tf_op jit(solution)/shard_map/ppermute | solution.py:170
  86.2 48.2 %collective-permute-start.22 = (bf16[1280,768]{1,0:T(8,128)(2,1)S(1)}, bf16[1280,768]{1,0:T(8,128)(2,1)S(1)}, u32[]{:S(2)}, u32[]{:S(2)}) collective-permute-start(bf16[1280,768]{1,0:T(8,128)(2,1)S(1)} %pad_maximum_fusion.refs_1_), channel_id=1, source_target_pairs={{24,16},{8,0},{25,17},{9,1},{26,18},{10,2},{27,19},{11,3},{28,20},... | collective-permute-start | bytes 5898248 | tf_op jit(solution)/shard_map/ppermute | solution.py:179
  89.4 5.1 %copy-start.7 = (f32[256,768]{1,0:T(8,128)S(1)}, f32[256,768]{1,0:T(8,128)}, u32[]{:S(2)}) copy-start(f32[256,768]{1,0:T(8,128)} %copy-done.6) | copy-start | bytes 2359300
  89.4 5.1 %copy-start.14 = (f32[128,768]{1,0:T(8,128)S(1)}, f32[128,768]{1,0:T(8,128)}, u32[]{:S(2)}) copy-start(f32[128,768]{1,0:T(8,128)} %copy-done.13) | copy-start | bytes 1179652
  89.4 1.9 collective-permute-start.20
  90.3 45.7 %collective-permute-start.7 = (bf16[768,768]{1,0:T(8,128)(2,1)}, bf16[768,768]{1,0:T(8,128)(2,1)S(1)}, u32[]{:S(2)}, u32[]{:S(2)}) collective-permute-start(bf16[768,768]{1,0:T(8,128)(2,1)} %collective-permute-done.5.refs_4_), channel_id=1, source_target_pairs={{0,1},{1,0},{2,3},{3,2},{4,5},{5,4},{6,7},{7,6},{8,9},{9,8},{10,11... | collective-permute-start | bytes 3538952 | tf_op jit(solution)/shard_map/ppermute | solution.py:175
  91.3 44.8 %collective-permute-start.6 = (bf16[768,768]{1,0:T(8,128)(2,1)}, bf16[768,768]{1,0:T(8,128)(2,1)S(1)}, u32[]{:S(2)}, u32[]{:S(2)}) collective-permute-start(bf16[768,768]{1,0:T(8,128)(2,1)} %collective-permute-done.5.refs_4_), channel_id=1, source_target_pairs={{2,0},{3,1},{4,6},{5,7},{10,8},{11,9},{12,14},{13,15},{18,16},{19,... | collective-permute-start | bytes 3538952 | tf_op jit(solution)/shard_map/ppermute | solution.py:170
  92.6 56.6 %collective-permute-start.10 = (bf16[768,768]{1,0:T(8,128)(2,1)S(1)}, bf16[768,768]{1,0:T(8,128)(2,1)S(1)}, u32[]{:S(2)}, u32[]{:S(2)}) collective-permute-start(bf16[768,768]{1,0:T(8,128)(2,1)S(1)} %collective-permute-done.9.refs_6_), channel_id=1, source_target_pairs={{2,0},{3,1},{4,6},{5,7},{10,8},{11,9},{12,14},{13,15},{18,16},{19,... | collective-permute-start | bytes 3538952 | tf_op jit(solution)/shard_map/ppermute | solution.py:170
  94.0 57.0 %collective-permute-start.4 = (bf16[768,768]{1,0:T(8,128)(2,1)}, bf16[768,768]{1,0:T(8,128)(2,1)S(1)}, u32[]{:S(2)}, u32[]{:S(2)}) collective-permute-start(bf16[768,768]{1,0:T(8,128)(2,1)} %collective-permute-done.3.refs_2_), channel_id=1, source_target_pairs={{0,1},{1,0},{2,3},{3,2},{4,5},{5,4},{6,7},{7,6},{8,9},{9,8},{10,11... | collective-permute-start | bytes 3538952 | tf_op jit(solution)/shard_map/ppermute | solution.py:175
  94.5 57.1 %copy-start.5 = (bf16[768,768]{1,0:T(8,128)(2,1)S(1)}, bf16[768,768]{1,0:T(8,128)(2,1)}, u32[]{:S(2)}) copy-start(bf16[768,768]{1,0:T(8,128)(2,1)} %convolution_convert_fusion.4) | copy-start | bytes 3538948
  134.5 45.0 %collective-permute-start.31 = (bf16[1280,768]{1,0:T(8,128)(2,1)}, bf16[1280,768]{1,0:T(8,128)(2,1)S(1)}, u32[]{:S(2)}, u32[]{:S(2)}) collective-permute-start(bf16[1280,768]{1,0:T(8,128)(2,1)} %collective-permute-done.28.refs_4_), channel_id=1, source_target_pairs={{0,8},{1,9},{2,10},{3,11},{4,12},{5,13},{6,14},{7,15}} | collective-permute-start | bytes 5898248 | tf_op jit(solution)/shard_map/ppermute | solution.py:179
  136.1 28.5 %collective-permute-start.11 = (bf16[768,768]{1,0:T(8,128)(2,1)S(1)}, bf16[768,768]{1,0:T(8,128)(2,1)S(1)}, u32[]{:S(2)}, u32[]{:S(2)}) collective-permute-start(bf16[768,768]{1,0:T(8,128)(2,1)S(1)} %collective-permute-done.9.refs_6_), channel_id=1, source_target_pairs={{0,1},{1,0},{2,3},{3,2},{4,5},{5,4},{6,7},{7,6},{8,9},{9,8},{10,11... | collective-permute-start | bytes 3538952 | tf_op jit(solution)/shard_map/ppermute | solution.py:175
  136.2 19.1 %collective-permute-start.8 = (bf16[768,768]{1,0:T(8,128)(2,1)S(1)}, bf16[768,768]{1,0:T(8,128)(2,1)S(1)}, u32[]{:S(2)}, u32[]{:S(2)}) collective-permute-start(bf16[768,768]{1,0:T(8,128)(2,1)S(1)} %collective-permute-done.6.refs_5_), channel_id=1, source_target_pairs={{0,1},{1,0},{2,3},{3,2},{4,5},{5,4},{6,7},{7,6},{8,9},{9,8},{10,11... | collective-permute-start | bytes 3538952 | tf_op jit(solution)/shard_map/ppermute | solution.py:175
  149.2 15.4 %collective-permute-start.12 = (bf16[768,768]{1,0:T(8,128)(2,1)S(1)}, bf16[768,768]{1,0:T(8,128)(2,1)S(1)}, u32[]{:S(2)}, u32[]{:S(2)}) collective-permute-start(bf16[768,768]{1,0:T(8,128)(2,1)S(1)} %collective-permute-done.10.refs_7_), channel_id=1, source_target_pairs={{0,1},{1,0},{2,3},{3,2},{4,5},{5,4},{6,7},{7,6},{8,9},{9,8},{10,11... | collective-permute-start | bytes 3538952 | tf_op jit(solution)/shard_map/ppermute | solution.py:175
  151.0 20.0 %collective-permute-start.23 = (bf16[768,768]{1,0:T(8,128)(2,1)S(1)}, bf16[768,768]{1,0:T(8,128)(2,1)S(1)}, u32[]{:S(2)}, u32[]{:S(2)}) collective-permute-start(bf16[768,768]{1,0:T(8,128)(2,1)S(1)} %convolution_convert_fusion.3), channel_id=1, source_target_pairs={{0,1},{1,0},{2,3},{3,2},{4,5},{5,4},{6,7},{7,6},{8,9},{9,8},{10,11... | collective-permute-start | bytes 3538952 | tf_op jit(solution)/shard_map/ppermute | solution.py:175
  155.3 37.3 %collective-permute-start.25 = (bf16[1280,256]{1,0:T(8,128)(2,1)}, bf16[1280,256]{1,0:T(8,128)(2,1)S(1)}, u32[]{:S(2)}, u32[]{:S(2)}) collective-permute-start(bf16[1280,256]{1,0:T(8,128)(2,1)} %collective-permute-done.24), channel_id=1, source_target_pairs={{0,8},{1,9},{2,10},{3,11},{4,12},{5,13},{6,14},{7,15}} | collective-permute-start | bytes 1966088 | tf_op jit(solution)/shard_map/ppermute | solution.py:179
  164.6 31.9 %collective-permute-start.29 = (bf16[768,768]{1,0:T(8,128)(2,1)S(1)}, bf16[768,768]{1,0:T(8,128)(2,1)S(1)}, u32[]{:S(2)}, u32[]{:S(2)}) collective-permute-start(bf16[768,768]{1,0:T(8,128)(2,1)S(1)} %convolution_convert_fusion.2), channel_id=1, source_target_pairs={{0,1},{1,0},{2,3},{3,2},{4,5},{5,4},{6,7},{7,6},{8,9},{9,8},{10,11... | collective-permute-start | bytes 3538952 | tf_op jit(solution)/shard_map/ppermute | solution.py:175
  164.7 47.6 %collective-permute-start.37 = (bf16[1280,768]{1,0:T(8,128)(2,1)S(1)}, bf16[1280,768]{1,0:T(8,128)(2,1)S(1)}, u32[]{:S(2)}, u32[]{:S(2)}) collective-permute-start(bf16[1280,768]{1,0:T(8,128)(2,1)S(1)} %collective-permute-done.22.refs_13_), channel_id=1, source_target_pairs={{16,0},{17,1},{18,2},{19,3},{20,4},{21,5},{22,6},{23,7}} | collective-permute-start | bytes 5898248 | tf_op jit(solution)/shard_map/ppermute | solution.py:179
  171.0 1.0 collective-permute-start.21
  192.6 5.9 %collective-permute-start.32 = (bf16[768,768]{1,0:T(8,128)(2,1)S(1)}, bf16[768,768]{1,0:T(8,128)(2,1)S(1)}, u32[]{:S(2)}, u32[]{:S(2)}) collective-permute-start(bf16[768,768]{1,0:T(8,128)(2,1)S(1)} %convolution_convert_fusion.1), channel_id=1, source_target_pairs={{0,1},{1,0},{2,3},{3,2},{4,5},{5,4},{6,7},{7,6},{8,9},{9,8},{10,11... | collective-permute-start | bytes 3538952 | tf_op jit(solution)/shard_map/ppermute | solution.py:175
  194.6 2.9 collective-permute-start.26
  195.2 30.6 %collective-permute-start.33 = (bf16[1280,256]{1,0:T(8,128)(2,1)}, bf16[1280,256]{1,0:T(8,128)(2,1)S(1)}, u32[]{:S(2)}, u32[]{:S(2)}) collective-permute-start(bf16[1280,256]{1,0:T(8,128)(2,1)} %collective-permute-done.19), channel_id=1, source_target_pairs={{16,0},{17,1},{18,2},{19,3},{20,4},{21,5},{22,6},{23,7}} | collective-permute-start | bytes 1966088 | tf_op jit(solution)/shard_map/ppermute | solution.py:179
  196.8 2.0 collective-permute-start.27
  197.5 1.3 collective-permute-start.30
  214.0 23.3 %collective-permute-start.38 = (bf16[768,768]{1,0:T(8,128)(2,1)S(1)}, bf16[768,768]{1,0:T(8,128)(2,1)S(1)}, u32[]{:S(2)}, u32[]{:S(2)}) collective-permute-start(bf16[768,768]{1,0:T(8,128)(2,1)S(1)} %convolution_convert_fusion), channel_id=1, source_target_pairs={{0,1},{1,0},{2,3},{3,2},{4,5},{5,4},{6,7},{7,6},{8,9},{9,8},{10,11... | collective-permute-start | bytes 3538952 | tf_op jit(solution)/shard_map/ppermute | solution.py:175
  226.5 10.6 %collective-permute-start.34 = (f32[128,768]{1,0:T(8,128)S(1)}, f32[128,768]{1,0:T(8,128)S(1)}, u32[]{:S(2)}, u32[]{:S(2)}) collective-permute-start(f32[128,768]{1,0:T(8,128)S(1)} %slice.217), channel_id=1, source_target_pairs={{0,1},{1,0},{2,3},{3,2},{4,5},{5,4},{6,7},{7,6},{8,9},{9,8},{10,11... | collective-permute-start | bytes 1179656 | tf_op jit(solution)/shard_map/ppermute | solution.py:175
  226.6 9.2 %collective-permute-start.39 = (bf16[128,768]{1,0:T(8,128)(2,1)S(1)}, bf16[128,768]{1,0:T(8,128)(2,1)S(1)}, u32[]{:S(2)}, u32[]{:S(2)}) collective-permute-start(bf16[128,768]{1,0:T(8,128)(2,1)S(1)} %get-tuple-element.64), channel_id=1, source_target_pairs={{8,0},{9,1},{10,2},{11,3},{12,4},{13,5},{14,6},{15,7}} | collective-permute-start | bytes 589832 | tf_op jit(solution)/shard_map/ppermute | solution.py:179
  227.9 22.4 %collective-permute-start.18 = (bf16[896,256]{1,0:T(8,128)(2,1)S(1)}, bf16[896,256]{1,0:T(8,128)(2,1)S(1)}, u32[]{:S(2)}, u32[]{:S(2)}) collective-permute-start(bf16[896,256]{1,0:T(8,128)(2,1)S(1)} %get-tuple-element.52), channel_id=1, source_target_pairs={{0,6},{1,7},{2,4},{3,5},{4,2},{5,3},{6,0},{7,1},{8,14},{9,15},{10,... | collective-permute-start | bytes 1376264 | tf_op jit(solution)/shard_map/ppermute | solution.py:170
  230.6 14.4 %collective-permute-start.35 = (bf16[128,768]{1,0:T(8,128)(2,1)S(1)}, bf16[128,768]{1,0:T(8,128)(2,1)S(1)}, u32[]{:S(2)}, u32[]{:S(2)}) collective-permute-start(bf16[128,768]{1,0:T(8,128)(2,1)S(1)} %get-tuple-element.60), channel_id=1, source_target_pairs={{16,0},{17,1},{18,2},{19,3},{20,4},{21,5},{22,6},{23,7}} | collective-permute-start | bytes 589832 | tf_op jit(solution)/shard_map/ppermute | solution.py:179
  235.8 9.2 %collective-permute-start.36 = (bf16[128,768]{1,0:T(8,128)(2,1)S(1)}, bf16[128,768]{1,0:T(8,128)(2,1)S(1)}, u32[]{:S(2)}, u32[]{:S(2)}) collective-permute-start(bf16[128,768]{1,0:T(8,128)(2,1)S(1)} %get-tuple-element.66), channel_id=1, source_target_pairs={{24,0},{25,1},{26,2},{27,3},{28,4},{29,5},{30,6},{31,7}} | collective-permute-start | bytes 589832 | tf_op jit(solution)/shard_map/ppermute | solution.py:179
  237.2 16.4 %collective-permute-start.51 = (bf16[128,768]{1,0:T(8,128)(2,1)S(1)}, bf16[128,768]{1,0:T(8,128)(2,1)S(1)}, u32[]{:S(2)}, u32[]{:S(2)}) collective-permute-start(bf16[128,768]{1,0:T(8,128)(2,1)S(1)} %add.239.refs_14_), channel_id=1, source_target_pairs={{0,1},{1,0},{2,3},{3,2},{4,5},{5,4},{6,7},{7,6},{8,9},{9,8},{10,11... | collective-permute-start | bytes 589832 | tf_op jit(solution)/shard_map/ppermute | solution.py:175
  249.7 3.9 %collective-permute-start.52 = (bf16[128,768]{1,0:T(8,128)(2,1)S(1)}, bf16[128,768]{1,0:T(8,128)(2,1)S(1)}, u32[]{:S(2)}, u32[]{:S(2)}) collective-permute-start(bf16[128,768]{1,0:T(8,128)(2,1)S(1)} %get-tuple-element.108), channel_id=1, source_target_pairs={{0,1},{1,0},{2,3},{3,2},{4,5},{5,4},{6,7},{7,6},{8,9},{9,8},{10,11... | collective-permute-start | bytes 589832 | tf_op jit(solution)/shard_map/ppermute | solution.py:175
  249.8 4.3 %collective-permute-start.47 = (bf16[128,768]{1,0:T(8,128)(2,1)S(1)}, bf16[128,768]{1,0:T(8,128)(2,1)S(1)}, u32[]{:S(2)}, u32[]{:S(2)}) collective-permute-start(bf16[128,768]{1,0:T(8,128)(2,1)S(1)} %get-tuple-element.70.refs_1_.refs_2_.refs_9_), channel_id=1, source_target_pairs={{0,1},{1,0},{2,3},{3,2},{4,5},{5,4},{6,7},{7,6},{8,9},{9,8},{10,11... | collective-permute-start | bytes 589832 | tf_op jit(solution)/shard_map/ppermute | solution.py:175
  250.3 22.6 %collective-permute-start.16 = (bf16[896,256]{1,0:T(8,128)(2,1)S(1)}, bf16[896,256]{1,0:T(8,128)(2,1)S(1)}, u32[]{:S(2)}, u32[]{:S(2)}) collective-permute-start(bf16[896,256]{1,0:T(8,128)(2,1)S(1)} %get-tuple-element.50), channel_id=1, source_target_pairs={{0,2},{1,3},{2,0},{3,1},{4,6},{5,7},{6,4},{7,5},{8,10},{9,11},{10,... | collective-permute-start | bytes 1376264 | tf_op jit(solution)/shard_map/ppermute | solution.py:170
  250.4 33.0 %collective-permute-start.17 = (bf16[896,256]{1,0:T(8,128)(2,1)S(1)}, bf16[896,256]{1,0:T(8,128)(2,1)S(1)}, u32[]{:S(2)}, u32[]{:S(2)}) collective-permute-start(bf16[896,256]{1,0:T(8,128)(2,1)S(1)} %get-tuple-element.51), channel_id=1, source_target_pairs={{0,4},{1,5},{2,6},{3,7},{4,0},{5,1},{6,2},{7,3},{8,12},{9,13},{10,... | collective-permute-start | bytes 1376264 | tf_op jit(solution)/shard_map/ppermute | solution.py:170
  253.6 2.1 collective-permute-start.48
  253.6 3.4 %collective-permute-start.49 = (bf16[128,768]{1,0:T(8,128)(2,1)S(1)}, bf16[128,768]{1,0:T(8,128)(2,1)S(1)}, u32[]{:S(2)}, u32[]{:S(2)}) collective-permute-start(bf16[128,768]{1,0:T(8,128)(2,1)S(1)} %collective-permute-done.30.refs_7_.refs_8_), channel_id=1, source_target_pairs={{0,1},{1,0},{2,3},{3,2},{4,5},{5,4},{6,7},{7,6},{8,9},{9,8},{10,11... | collective-permute-start | bytes 589832 | tf_op jit(solution)/shard_map/ppermute | solution.py:175
  254.1 3.2 %collective-permute-start.50 = (bf16[128,768]{1,0:T(8,128)(2,1)S(1)}, bf16[128,768]{1,0:T(8,128)(2,1)S(1)}, u32[]{:S(2)}, u32[]{:S(2)}) collective-permute-start(bf16[128,768]{1,0:T(8,128)(2,1)S(1)} %collective-permute-done.36.refs_7_.refs_11_), channel_id=1, source_target_pairs={{0,1},{1,0},{2,3},{3,2},{4,5},{5,4},{6,7},{7,6},{8,9},{9,8},{10,11... | collective-permute-start | bytes 589832 | tf_op jit(solution)/shard_map/ppermute | solution.py:175
  255.8 27.6 %collective-permute-start.42 = (bf16[128,768]{1,0:T(8,128)(2,1)S(1)}, bf16[128,768]{1,0:T(8,128)(2,1)S(1)}, u32[]{:S(2)}, u32[]{:S(2)}) collective-permute-start(bf16[128,768]{1,0:T(8,128)(2,1)S(1)} %get-tuple-element.68.refs_4_), channel_id=1, source_target_pairs={{0,6},{1,7},{2,4},{3,5},{4,2},{5,3},{6,0},{7,1},{8,14},{9,15},{10,... | collective-permute-start | bytes 589832 | tf_op jit(solution)/shard_map/ppermute | solution.py:170
  257.0 33.8 %collective-permute-start.41 = (bf16[128,768]{1,0:T(8,128)(2,1)S(1)}, bf16[128,768]{1,0:T(8,128)(2,1)S(1)}, u32[]{:S(2)}, u32[]{:S(2)}) collective-permute-start(bf16[128,768]{1,0:T(8,128)(2,1)S(1)} %get-tuple-element.68.refs_4_), channel_id=1, source_target_pairs={{0,4},{1,5},{2,6},{3,7},{4,0},{5,1},{6,2},{7,3},{8,12},{9,13},{10,... | collective-permute-start | bytes 589832 | tf_op jit(solution)/shard_map/ppermute | solution.py:170
  257.3 33.6 %collective-permute-start.40 = (bf16[128,768]{1,0:T(8,128)(2,1)S(1)}, bf16[128,768]{1,0:T(8,128)(2,1)S(1)}, u32[]{:S(2)}, u32[]{:S(2)}) collective-permute-start(bf16[128,768]{1,0:T(8,128)(2,1)S(1)} %get-tuple-element.68.refs_4_), channel_id=1, source_target_pairs={{0,2},{1,3},{2,0},{3,1},{4,6},{5,7},{6,4},{7,5},{8,10},{9,11},{10,... | collective-permute-start | bytes 589832 | tf_op jit(solution)/shard_map/ppermute | solution.py:170
  272.9 18.5 %collective-permute-start.43 = (bf16[128,768]{1,0:T(8,128)(2,1)S(1)}, bf16[128,768]{1,0:T(8,128)(2,1)S(1)}, u32[]{:S(2)}, u32[]{:S(2)}) collective-permute-start(bf16[128,768]{1,0:T(8,128)(2,1)S(1)} %get-tuple-element.68.refs_4_), channel_id=1, source_target_pairs={{0,1},{1,0},{2,3},{3,2},{4,5},{5,4},{6,7},{7,6},{8,9},{9,8},{10,11... | collective-permute-start | bytes 589832 | tf_op jit(solution)/shard_map/ppermute | solution.py:175
  283.3 8.1 %collective-permute-start.58 = (bf16[384,256]{1,0:T(8,128)(2,1)S(1)}, bf16[384,256]{1,0:T(8,128)(2,1)S(1)}, u32[]{:S(2)}, u32[]{:S(2)}) collective-permute-start(bf16[384,256]{1,0:T(8,128)(2,1)S(1)} %slice.180), channel_id=1, source_target_pairs={{0,1},{1,0},{2,3},{3,2},{4,5},{5,4},{6,7},{7,6},{8,9},{9,8},{10,11... | collective-permute-start | bytes 589832 | tf_op jit(solution)/shard_map/ppermute | solution.py:175
  283.3 11.0 %collective-permute-start.46 = (bf16[128,768]{1,0:T(8,128)(2,1)S(1)}, bf16[128,768]{1,0:T(8,128)(2,1)S(1)}, u32[]{:S(2)}, u32[]{:S(2)}) collective-permute-start(bf16[128,768]{1,0:T(8,128)(2,1)S(1)} %collective-permute-done.42.refs_7_), channel_id=1, source_target_pairs={{0,1},{1,0},{2,3},{3,2},{4,5},{5,4},{6,7},{7,6},{8,9},{9,8},{10,11... | collective-permute-start | bytes 589832 | tf_op jit(solution)/shard_map/ppermute | solution.py:175
  290.9 5.0 %collective-permute-start.45 = (bf16[128,768]{1,0:T(8,128)(2,1)S(1)}, bf16[128,768]{1,0:T(8,128)(2,1)S(1)}, u32[]{:S(2)}, u32[]{:S(2)}) collective-permute-start(bf16[128,768]{1,0:T(8,128)(2,1)S(1)} %collective-permute-done.41.refs_6_), channel_id=1, source_target_pairs={{0,1},{1,0},{2,3},{3,2},{4,5},{5,4},{6,7},{7,6},{8,9},{9,8},{10,11... | collective-permute-start | bytes 589832 | tf_op jit(solution)/shard_map/ppermute | solution.py:175
  290.9 5.0 %collective-permute-start.44 = (bf16[128,768]{1,0:T(8,128)(2,1)S(1)}, bf16[128,768]{1,0:T(8,128)(2,1)S(1)}, u32[]{:S(2)}, u32[]{:S(2)}) collective-permute-start(bf16[128,768]{1,0:T(8,128)(2,1)S(1)} %collective-permute-done.40.refs_5_), channel_id=1, source_target_pairs={{0,1},{1,0},{2,3},{3,2},{4,5},{5,4},{6,7},{7,6},{8,9},{9,8},{10,11... | collective-permute-start | bytes 589832 | tf_op jit(solution)/shard_map/ppermute | solution.py:175
  291.4 13.3 %collective-permute-start.53 = (bf16[512,256]{1,0:T(8,128)(2,1)S(1)}, bf16[512,256]{1,0:T(8,128)(2,1)S(1)}, u32[]{:S(2)}, u32[]{:S(2)}) collective-permute-start(bf16[512,256]{1,0:T(8,128)(2,1)S(1)} %get-tuple-element.76), channel_id=1, source_target_pairs={{0,2},{1,3},{2,0},{3,1},{4,6},{5,7},{6,4},{7,5},{8,10},{9,11},{10,... | collective-permute-start | bytes 786440 | tf_op jit(solution)/shard_map/ppermute | solution.py:170
  291.4 21.4 %collective-permute-start.54 = (bf16[512,256]{1,0:T(8,128)(2,1)S(1)}, bf16[512,256]{1,0:T(8,128)(2,1)S(1)}, u32[]{:S(2)}, u32[]{:S(2)}) collective-permute-start(bf16[512,256]{1,0:T(8,128)(2,1)S(1)} %get-tuple-element.77), channel_id=1, source_target_pairs={{0,4},{1,5},{2,6},{3,7},{4,0},{5,1},{6,2},{7,3},{8,12},{9,13},{10,... | collective-permute-start | bytes 786440 | tf_op jit(solution)/shard_map/ppermute | solution.py:170
  294.3 18.5 %collective-permute-start.55 = (bf16[512,256]{1,0:T(8,128)(2,1)S(1)}, bf16[512,256]{1,0:T(8,128)(2,1)S(1)}, u32[]{:S(2)}, u32[]{:S(2)}) collective-permute-start(bf16[512,256]{1,0:T(8,128)(2,1)S(1)} %get-tuple-element.78), channel_id=1, source_target_pairs={{0,6},{1,7},{2,4},{3,5},{4,2},{5,3},{6,0},{7,1},{8,14},{9,15},{10,... | collective-permute-start | bytes 786440 | tf_op jit(solution)/shard_map/ppermute | solution.py:170
  295.8 1.5 collective-permute-start.57
  295.9 1.7 collective-permute-start.56
  (15 other events, 43.0 us)

commit v8 on v7

--- a/solution.py
+++ b/solution.py
@@ -203,11 +203,6 @@
 
 def across_chips(value, step):
     return on_chips(value, [(chip, chip ^ step) for chip in range(CHIPS)])
-
-
-def gather_rows(rows):
-    held = [rows] + [across_chips(rows, step) for step in range(1, CHIPS)]
-    return held + [swap_cores(piece) for piece in held]
 
 
 def chip_blocks(wide, chip, core):
@@ -433,20 +428,20 @@
     )(*arrays)
 
 
-def pair_products(block_ref, count, near_ref, far_ref):
-    return dot(block_ref[:count, :], jnp.concatenate([near_ref[...], far_ref[...]], axis=0))
-
-
-def block_products(count, refs):
+def token_kernel(flag_ref, *refs):
+    blocks, pieces, out_ref = refs[:CHIPS], refs[CHIPS:-1], refs[-1]
+    count, rows = out_ref.shape[0], pieces[0].shape[0]
+    middle = flag_ref[0] > 0
+    third, fourth = blocks[2][:count, :], blocks[3][:count, :]
+    lefts = [blocks[0][:count, :], blocks[1][:count, :]]
+    lefts += [jnp.where(middle, fourth, third), jnp.where(middle, third, fourth)]
+    rights = [[ref[...] for ref in pieces[:2]], [ref[...] for ref in pieces[2:4]]]
+    rights += [[ref[start : start + rows, :] for ref in pieces[4:]] for start in (0, rows)]
     total = None
-    for step in range(CHIPS):
-        term = pair_products(refs[step], count, refs[CHIPS + step], refs[2 * CHIPS + step])
+    for left, right in zip(lefts, rights):
+        term = dot(left, jnp.concatenate(right, axis=0))
         total = term if total is None else total + term
-    return total
-
-
-def token_kernel(*refs):
-    refs[-1][...] = block_products(refs[-1].shape[0], refs[:-1])
+    out_ref[...] = total
 
 
 def grouped_rows(ref, start, rows):
@@ -488,11 +483,12 @@
             ] = product.astype(jnp.bfloat16)
 
 
-def block_call(body, outs, arrays, flops):
+def block_call(body, outs, arrays, flops, scalars=()):
     return pl.pallas_call(
         body,
         out_shape=outs,
-        in_specs=[pl.BlockSpec(memory_space=pltpu.VMEM)] * len(arrays),
+        in_specs=[pl.BlockSpec(memory_space=pltpu.SMEM)] * len(scalars)
+        + [pl.BlockSpec(memory_space=pltpu.VMEM)] * len(arrays),
         out_specs=[pl.BlockSpec(memory_space=pltpu.VMEM)] * len(outs),
         compiler_params=pltpu.CompilerParams(vmem_limit_bytes=ROOM),
         cost_estimate=pl.CostEstimate(
@@ -500,7 +496,7 @@
             bytes_accessed=sum(array.size * array.dtype.itemsize for array in arrays),
             transcendentals=0,
         ),
-    )(*arrays)
+    )(*scalars, *arrays)
 
 
 def after(value, earlier):
@@ -670,7 +666,7 @@
     def with_swap(values):
         return values, swap_cores(values)
 
-    proj_rows = gather_rows(grad_proj)
+    near_rows = on_chips(grad_proj, [(0, 1), (1, 0), (2, 3), (3, 2)])
     grad_slots = to_slots(grad_pre)
     scaled_pair = with_swap(after(scaled, grad_proj))
     two_pair = with_swap(first_two + after(second_two, grad_proj))
@@ -689,15 +685,22 @@
         *grad_slots,
     )
     mixed_first = mixed_blocks[0]
+    both_rows = jnp.concatenate([grad_proj, near_rows], axis=0)
+    mid_rows = on_chips(both_rows, [(1, 2), (2, 1)])
     tall = token_blocks[0].shape[0]
-    scaled_parts = [after(part, mixed_first)[tall:] for part in token_blocks[1:]]
+    scaled_parts = [after(part, mid_rows)[tall:] for part in token_blocks[1:]]
+    end_rows = on_chips(mid_rows, [(1, 0), (2, 3)])
+    far_rows = jnp.where(middle, mid_rows, end_rows)
+    proj_rows = [grad_proj, swap_cores(after(grad_proj, mixed_first))]
+    proj_rows += [near_rows, swap_cores(after(near_rows, mixed_first))]
+    proj_rows += [far_rows, swap_cores(far_rows)]
     mixed_blocks = list(mixed_blocks[:1]) + [
         across_chips(mixed_blocks[step], step) for step in range(1, CHIPS)
     ]
     scaled_rows = [*scaled_pair, *(swap_cores(part) for part in scaled_parts)]
     share = jax.ShapeDtypeStruct((channels // devices, ranks), f32)
     share_flops = 2 * channels * rows * ranks
-    token_share = block_call(token_kernel, [share], token_blocks + proj_rows, share_flops)
+    token_share = block_call(token_kernel, [share], token_blocks + proj_rows, share_flops, [flag])
     factor_share, core_total = block_call(
         last_kernel,
         [share, jax.ShapeDtypeStruct((ranks, ranks), bf16)],

time: 318 us -> 331 us (1.041)
  waiting for transfers between devices: 198 us -> 206 us
  starting transfers between devices: 51.7 us -> 58 us
    ppermute x14, waiting for transfers between devices: 53.2 us -> 62.6 us  [on_chips(): return lax.ppermute(value, 'expert', perm)]
    ppermute x14, starting transfers between devices: 22.8 us -> 29.8 us  [on_chips(): return lax.ppermute(value, 'expert', perm)]
    ppermute x31 -> x30, starting transfers between devices: 7.76 us -> 7.11 us  [swap_cores(): lax.ppermute(value, 'expert', [(index, index ^ 1) for index in range(coun...]
  transfers between devices with their start and end apart: 59 -> 58, of which waited for: 19 -> 18; matrix products, arithmetic and copies ran while one was open for 9% -> 9% of each run, Pallas kernels for 8% -> 7%
where the time goes in v8:
time: 331 us; the launch traced here: 329 us
  waiting for transfers between devices  206 us (62%)
  starting transfers between devices  58 us (18%)
  Pallas kernels  28.3 us (9%)
  matrix products  17.4 us (5%)
  other arithmetic  9.82 us (3%)
  local copies, waits for them, and re-layouts  7.98 us (2%)
    ppermute x14, waiting for transfers between devices, between_layers(): return lax.ppermute(value, 'section', pairs)  141 us
    ppermute x14, waiting for transfers between devices, on_chips(): return lax.ppermute(value, 'expert', perm)  62.6 us
    ppermute x14, starting transfers between devices, on_chips(): return lax.ppermute(value, 'expert', perm)  29.8 us
    ppermute x14, starting transfers between devices, between_layers(): return lax.ppermute(value, 'section', pairs)  21.1 us
    dot_general x9, matrix products, dot_first(): lax.dot_general(left, right, (((0,), (0,)), ((), ())), preferred_element_...  16.2 us
    pallas_call x3, Pallas kernels, call_rows(): pl.pallas_call(body, out_shape=[jax.ShapeDtypeStruct(shape, kind) for sha...  12.2 us
    pallas_call x2, Pallas kernels, core_call(): pl.pallas_call(body, out_shape=outs, in_specs=[pl.BlockSpec(memory_space=...  8.54 us
    ppermute x30, starting transfers between devices, swap_cores(): lax.ppermute(value, 'expert', [(index, index ^ 1) for index in range(coun...  7.11 us
  transfers between devices with their start and end apart: 58, of which 18 were waited for; matrix products, arithmetic and copies ran while one was open for 9% of the time, Pallas kernels for 7%

profile of v8, /device:TPU:0, one launch (start us, length us, event | category | flops | bytes accessed | tf_op | source)
XLA Modules:
  0.0 328.9 jit_solution(7000338312745729779)
XLA Ops:
  0.7 1.4 copy.11
  2.2 0.8 constant_dynamic-slice_fusion.15
  2.9 0.7 pad_maximum_fusion.4
  4.7 0.7 constant_dynamic-slice_fusion.7
  5.5 0.7 pad_maximum_fusion.5
  6.2 3.1 collective-permute-start.3
  9.4 1.7 dynamic-slice_bitcast_fusion.3
  11.3 2.0 copy-done.1
  14.2 1.9 pad_maximum_fusion.2
  16.1 1.3 collective-permute-start.19
  17.4 1.7 fusion.15
  20.1 1.1 collective-permute-done.1
  21.2 1.7 collective-permute-start.5
  23.2 1.3 collective-permute-start.28
  24.5 10.1 %collective-permute-done.19 = bf16[1280,256]{1,0:T(8,128)(2,1)} collective-permute-done((bf16[1280,256]{1,0:T(8,128)(2,1)}, bf16[1280,256]{1,0:T(8,128)(2,1)}, u32[]{:S(2)}, u32[]{:S(2)}) %collective-permute-start.19) | collective-permute-done | bytes 655392 | tf_op jit(solution)/shard_map/ppermute | solution.py:179
  34.7 1.3 collective-permute-start.24
  36.0 2.8 convolution_convert_fusion.4
  38.9 45.4 %collective-permute-done.24 = bf16[1280,256]{1,0:T(8,128)(2,1)} collective-permute-done((bf16[1280,256]{1,0:T(8,128)(2,1)}, bf16[1280,256]{1,0:T(8,128)(2,1)}, u32[]{:S(2)}, u32[]{:S(2)}) %collective-permute-start.24) | collective-permute-done | bytes 655392 | tf_op jit(solution)/shard_map/ppermute | solution.py:179
  85.1 1.2 pad_maximum_fusion.1
  86.2 1.3 collective-permute-start.22
  87.5 1.8 fusion.17
  91.3 1.3 collective-permute-start.6
  92.6 1.3 collective-permute-start.10
  94.6 39.9 %collective-permute-done.22.refs_13_ = bf16[1280,768]{1,0:T(8,128)(2,1)S(1)} collective-permute-done((bf16[1280,768]{1,0:T(8,128)(2,1)S(1)}, bf16[1280,768]{1,0:T(8,128)(2,1)S(1)}, u32[]{:S(2)}, u32[]{:S(2)}) %collective-permute-start.22) | collective-permute-done | bytes 1966112 | tf_op jit(solution)/shard_map/ppermute | solution.py:179
  134.5 1.6 collective-permute-start.31
  136.6 12.6 %collective-permute-done.10.refs_7_ = bf16[768,768]{1,0:T(8,128)(2,1)S(1)} collective-permute-done((bf16[768,768]{1,0:T(8,128)(2,1)S(1)}, bf16[768,768]{1,0:T(8,128)(2,1)S(1)}, u32[]{:S(2)}, u32[]{:S(2)}) %collective-permute-start.10) | collective-permute-done | bytes 1179680 | tf_op jit(solution)/shard_map/ppermute | solution.py:170
  149.2 1.8 convolution_convert_fusion.3
  152.0 3.3 %convolution_convert_fusion.2 = bf16[768,768]{1,0:T(8,128)(2,1)S(1)} fusion(bf16[1280,768]{1,0:T(8,128)(2,1)} %collective-permute-done.28.refs_4_, bf16[1280,768]{1,0:T(8,128)(2,1)S(1)} %pad_maximum_fusion.refs_1_), kind=kOutput, calls=%fused_computation.10 | convolution fusion | flops 1510539264 | bytes 5111808 | tf_op jit(solution)/shard_map/dot_general | solution.py:159
  155.3 5.7 %collective-permute-start.25 = (bf16[1280,256]{1,0:T(8,128)(2,1)}, bf16[1280,256]{1,0:T(8,128)(2,1)S(1)}, u32[]{:S(2)}, u32[]{:S(2)}) collective-permute-start(bf16[1280,256]{1,0:T(8,128)(2,1)} %collective-permute-done.24), channel_id=1, source_target_pairs={{0,8},{1,9},{2,10},{3,11},{4,12},{5,13},{6,14},{7,15}} | collective-permute-start | bytes 1966088 | tf_op jit(solution)/shard_map/ppermute | solution.py:179
  161.0 3.5 %shard_map.86 = (f32[128,768]{1,0:T(8,128)S(1)}, bf16[768,768]{1,0:T(8,128)(2,1)S(1)}, bf16[768,768]{1,0:T(8,128)(2,1)S(1)}, bf16[768,768]{1,0:T(8,128)(2,1)S(1)...) custom-call(s32[1]{0:T(128)} %bitcast.3.middle_ref.flag_ref, ...), custom_call_target="tpu_custom_call" | custom-call | flops 905969664 | bytes 7077888 | tf_op jit(solution)/shard_map/pallas_call | solution.py:579
  164.6 1.3 collective-permute-start.37
  165.9 5.0 %shard_map.87 = (bf16[128,768]{1,0:T(8,128)(2,1)S(1)}, f32[128,768]{1,0:T(8,128)S(1)}, f32[128,768]{1,0:T(8,128)S(1)}, bf16[128,768]{1,0:T(8,128)(2,1)S(1)}, bf1...) custom-call(s32[1]{0:T(128)} %bitcast.3.middle_ref.flag_ref, ...), custom_call_target="tpu_custom_call" | custom-call | flops 1660944384 | bytes 4718592 | tf_op jit(solution)/shard_map/pallas_call | solution.py:579
  172.0 3.8 %shard_map.88 = (f32[128,768]{1,0:T(8,128)S(1)}, bf16[128,768]{1,0:T(8,128)(2,1)}, bf16[128,768]{1,0:T(8,128)(2,1)}, bf16[128,768]{1,0:T(8,128)(2,1)S(1)}) custom-call(f32[128,16]{1,0:T(8,128)S(1)} %convert_select_fusion.marks_ref.refs_0_, bf16[128,768]{1,0:T(8,128)(2,1)S(1)} %get-tuple-element.72.refs_1_.refs_2_.refs_9_, ...), custom_call_target="tpu_custom_call" | custom-call | flops 1358954496 | bytes 12197888 | tf_op jit(solution)/shard_map/pallas_call | solution.py:344
  175.8 3.7 %collective-permute-done.31.refs_7_ = bf16[1280,768]{1,0:T(8,128)(2,1)S(1)} collective-permute-done((bf16[1280,768]{1,0:T(8,128)(2,1)}, bf16[1280,768]{1,0:T(8,128)(2,1)S(1)}, u32[]{:S(2)}, u32[]{:S(2)}) %collective-permute-start.31) | collective-permute-done | bytes 1966112 | tf_op jit(solution)/shard_map/ppermute | solution.py:179
  179.4 1.8 convolution_convert_fusion.1
  181.2 11.4 %collective-permute-done.25 = bf16[1280,256]{1,0:T(8,128)(2,1)S(1)} collective-permute-done((bf16[1280,256]{1,0:T(8,128)(2,1)}, bf16[1280,256]{1,0:T(8,128)(2,1)S(1)}, u32[]{:S(2)}, u32[]{:S(2)}) %collective-permute-start.25) | collective-permute-done | bytes 655392 | tf_op jit(solution)/shard_map/ppermute | solution.py:179
  192.6 1.3 add_convert_fusion.6
  195.2 1.3 collective-permute-start.33
  197.5 0.9 collective-permute-start.30
  198.8 4.0 %shard_map.89 = (f32[128,768]{1,0:T(8,128)S(1)}, bf16[128,768]{1,0:T(8,128)(2,1)}, bf16[128,768]{1,0:T(8,128)(2,1)}, bf16[128,768]{1,0:T(8,128)(2,1)S(1)}) custom-call(f32[128,16]{1,0:T(8,128)S(1)} %convert_select_fusion.marks_ref.refs_0_, bf16[128,768]{1,0:T(8,128)(2,1)S(1)} %get-tuple-element.72.refs_1_.refs_2_.refs_9_, ...), custom_call_target="tpu_custom_call" | custom-call | flops 1509949440 | bytes 13574144 | tf_op jit(solution)/shard_map/pallas_call | solution.py:344
  202.8 9.4 %collective-permute-done.37.refs_10_ = bf16[1280,768]{1,0:T(8,128)(2,1)S(1)} collective-permute-done((bf16[1280,768]{1,0:T(8,128)(2,1)S(1)}, bf16[1280,768]{1,0:T(8,128)(2,1)S(1)}, u32[]{:S(2)}, u32[]{:S(2)}) %collective-permute-start.37) | collective-permute-done | bytes 1966112 | tf_op jit(solution)/shard_map/ppermute | solution.py:179
  212.2 1.7 convolution_convert_fusion
  214.1 11.7 %collective-permute-done.33 = bf16[1280,256]{1,0:T(8,128)(2,1)S(1)} collective-permute-done((bf16[1280,256]{1,0:T(8,128)(2,1)}, bf16[1280,256]{1,0:T(8,128)(2,1)S(1)}, u32[]{:S(2)}, u32[]{:S(2)}) %collective-permute-start.33) | collective-permute-done | bytes 655392 | tf_op jit(solution)/shard_map/ppermute | solution.py:179
  226.6 1.3 collective-permute-start.35
  227.9 1.3 collective-permute-start.36
  229.2 1.3 collective-permute-start.39
  230.9 7.2 %collective-permute-done.36.refs_7_.refs_11_ = bf16[128,768]{1,0:T(8,128)(2,1)S(1)} collective-permute-done((bf16[128,768]{1,0:T(8,128)(2,1)S(1)}, bf16[128,768]{1,0:T(8,128)(2,1)S(1)}, u32[]{:S(2)}, u32[]{:S(2)}) %collective-permute-start.36) | collective-permute-done | bytes 196640 | tf_op jit(solution)/shard_map/ppermute | solution.py:179
  238.1 1.9 collective-permute-done.35.refs_5_
  240.0 4.4 %shard_map.90 = (f32[128,768]{1,0:T(8,128)}, bf16[128,768]{1,0:T(8,128)(2,1)S(1)}, bf16[128,768]{1,0:T(8,128)(2,1)S(1)}, bf16[128,768]{1,0:T(8,128)(2,1)}) custom-call(f32[128,16]{1,0:T(8,128)S(1)} %convert_select_fusion.marks_ref.refs_0_, bf16[128,768]{1,0:T(8,128)(2,1)S(1)} %get-tuple-element.72.refs_1_.refs_2_.refs_9_, ...), custom_call_target="tpu_custom_call" | custom-call | flops 1660944384 | bytes 14950400 | tf_op jit(solution)/shard_map/pallas_call | solution.py:344
  244.6 6.3 %collective-permute-done.47.refs_6_ = bf16[128,768]{1,0:T(8,128)(2,1)S(1)} collective-permute-done((bf16[128,768]{1,0:T(8,128)(2,1)S(1)}, bf16[128,768]{1,0:T(8,128)(2,1)S(1)}, u32[]{:S(2)}, u32[]{:S(2)}) %collective-permute-start.47) | collective-permute-done | bytes 196640 | tf_op jit(solution)/shard_map/ppermute | solution.py:170
  252.6 1.5 collective-permute-start.50
  254.2 1.5 add_convert_fusion.5.refs_0_
  255.8 10.6 %collective-permute-start.16 = (bf16[896,256]{1,0:T(8,128)(2,1)S(1)}, bf16[896,256]{1,0:T(8,128)(2,1)S(1)}, u32[]{:S(2)}, u32[]{:S(2)}) collective-permute-start(bf16[896,256]{1,0:T(8,128)(2,1)S(1)} %get-tuple-element.52), channel_id=1, source_target_pairs={{0,2},{1,3},{2,0},{3,1},{4,6},{5,7},{6,4},{7,5},{8,10},{9,11},{10,... | collective-permute-start | bytes 1376264 | tf_op jit(solution)/shard_map/ppermute | solution.py:170
  266.3 1.2 collective-permute-start.17
  267.6 1.4 collective-permute-start.18
  269.0 13.7 %collective-permute-done.50 = bf16[256,768]{1,0:T(8,128)(2,1)S(1)} collective-permute-done((bf16[256,768]{1,0:T(8,128)(2,1)S(1)}, bf16[256,768]{1,0:T(8,128)(2,1)S(1)}, u32[]{:S(2)}, u32[]{:S(2)}) %collective-permute-start.50) | collective-permute-done | bytes 393248 | tf_op jit(solution)/shard_map/ppermute | solution.py:170
  283.4 0.8 collective-permute-done.43.refs_12_
  284.1 4.7 %spread.1 = (bf16[512,256]{1,0:T(8,128)(2,1)S(1)}, bf16[512,256]{1,0:T(8,128)(2,1)S(1)}, bf16[512,256]{1,0:T(8,128)(2,1)S(1)}, bf16[512,256]{1,0:T(8,128)(2,1)S(1)}) custom-call(bf16[1280,256]{1,0:T(8,128)(2,1)S(1)} %add_convert_fusion.5.refs_0_, bf16[1280,768]{1,0:T(8,128)(2,1)S(1)} %pad_maximum_fusion.refs_1_, ...), custom_call_target="tpu_custom_call" | custom-call | flops 2516582400 | bytes 12845056 | tf_op jit(solution)/shard_map/spread/pallas_call | solution.py:415
  289.1 14.7 %collective-permute-done.16.refs_1_ = bf16[896,256]{1,0:T(8,128)(2,1)S(1)} collective-permute-done((bf16[896,256]{1,0:T(8,128)(2,1)S(1)}, bf16[896,256]{1,0:T(8,128)(2,1)S(1)}, u32[]{:S(2)}, u32[]{:S(2)}) %collective-permute-start.16) | collective-permute-done | bytes 458784 | tf_op jit(solution)/shard_map/ppermute | solution.py:170
  303.9 5.0 %collective-permute-start.53 = (bf16[512,256]{1,0:T(8,128)(2,1)S(1)}, bf16[512,256]{1,0:T(8,128)(2,1)S(1)}, u32[]{:S(2)}, u32[]{:S(2)}) collective-permute-start(bf16[512,256]{1,0:T(8,128)(2,1)S(1)} %get-tuple-element.81), channel_id=1, source_target_pairs={{0,4},{1,5},{2,6},{3,7},{4,0},{5,1},{6,2},{7,3},{8,12},{9,13},{10,... | collective-permute-start | bytes 786440 | tf_op jit(solution)/shard_map/ppermute | solution.py:170
  308.9 1.2 collective-permute-start.54
  310.3 2.3 collective-permute-done.52.refs_6_
  313.7 13.0 %collective-permute-done.53.refs_7_ = bf16[512,256]{1,0:T(8,128)(2,1)S(1)} collective-permute-done((bf16[512,256]{1,0:T(8,128)(2,1)S(1)}, bf16[512,256]{1,0:T(8,128)(2,1)S(1)}, u32[]{:S(2)}, u32[]{:S(2)}) %collective-permute-start.53) | collective-permute-done | bytes 262176 | tf_op jit(solution)/shard_map/ppermute | solution.py:170
  326.7 2.2 shard_map.92
  (161 shorter events, 17.5 us)
Async XLA Ops:
  3.7 19.2 %collective-permute-start = (bf16[1280,128]{1,0:T(8,128)(2,1)}, bf16[1280,128]{1,0:T(8,128)(2,1)}, u32[]{:S(2)}, u32[]{:S(2)}) collective-permute-start(bf16[1280,128]{1,0:T(8,128)(2,1)} %pad_maximum_fusion.4), channel_id=1, source_target_pairs={{0,1},{1,0},{2,3},{3,2},{4,5},{5,4},{6,7},{7,6},{8,9},{9,8},{10,11... | collective-permute-start | bytes 983048 | tf_op jit(solution)/shard_map/ppermute | solution.py:175
  6.2 7.7 %collective-permute-start.13 = (bf16[1280,128]{1,0:T(8,128)(2,1)}, bf16[1280,128]{1,0:T(8,128)(2,1)}, u32[]{:S(2)}, u32[]{:S(2)}) collective-permute-start(bf16[1280,128]{1,0:T(8,128)(2,1)} %pad_maximum_fusion.5), channel_id=1, source_target_pairs={{0,1},{1,0},{2,3},{3,2},{4,5},{5,4},{6,7},{7,6},{8,9},{9,8},{10,11... | collective-permute-start | bytes 983048 | tf_op jit(solution)/shard_map/ppermute | solution.py:175
  6.2 78.0 %collective-permute-start.3 = (bf16[768,768]{1,0:T(8,128)(2,1)S(1)}, bf16[768,768]{1,0:T(8,128)(2,1)}, u32[]{:S(2)}, u32[]{:S(2)}) collective-permute-start(bf16[768,768]{1,0:T(8,128)(2,1)S(1)} %bitcast.41), channel_id=1, source_target_pairs={{0,2},{1,3},{2,0},{3,1},{4,6},{5,7},{6,4},{7,5},{8,10},{9,11},{10,... | collective-permute-start | bytes 3538952 | tf_op jit(solution)/shard_map/ppermute | solution.py:170
  16.1 18.6 %collective-permute-start.19 = (bf16[1280,256]{1,0:T(8,128)(2,1)}, bf16[1280,256]{1,0:T(8,128)(2,1)}, u32[]{:S(2)}, u32[]{:S(2)}) collective-permute-start(bf16[1280,256]{1,0:T(8,128)(2,1)} %pad_maximum_fusion.2), channel_id=1, source_target_pairs={{24,16},{8,0},{25,17},{9,1},{26,18},{10,2},{27,19},{11,3},{28,20},... | collective-permute-start | bytes 1966088 | tf_op jit(solution)/shard_map/ppermute | solution.py:179
  19.1 4.1 %collective-permute-start.14 = (f32[128,768]{1,0:T(8,128)S(1)}, f32[128,768]{1,0:T(8,128)S(1)}, u32[]{:S(2)}, u32[]{:S(2)}) collective-permute-start(f32[128,768]{1,0:T(8,128)S(1)} %slice.190), channel_id=1, source_target_pairs={{0,1},{1,0},{2,3},{3,2},{4,5},{5,4},{6,7},{7,6},{8,9},{9,8},{10,11... | collective-permute-start | bytes 1179656 | tf_op jit(solution)/shard_map/ppermute | solution.py:175
  19.5 19.2 %copy-start.19 = (f32[1,2,64]{2,1,0:T(2,128)S(1)}, f32[1,2,64]{2,1,0:T(2,128)}, u32[]{:S(2)}) copy-start(f32[1,2,64]{2,1,0:T(2,128)} %param.9) | copy-start | bytes 1540
  19.5 1.7 collective-permute-start.1
  21.2 13.5 %copy-start.15 = (bf16[128,768]{1,0:T(8,128)(2,1)}, bf16[128,768]{1,0:T(8,128)(2,1)S(1)}, u32[]{:S(2)}) copy-start(bf16[128,768]{1,0:T(8,128)(2,1)S(1)} %collective-permute-done.1) | copy-start | bytes 589828
  21.2 65.0 %collective-permute-start.5 = (bf16[768,768]{1,0:T(8,128)(2,1)S(1)}, bf16[768,768]{1,0:T(8,128)(2,1)}, u32[]{:S(2)}, u32[]{:S(2)}) collective-permute-start(bf16[768,768]{1,0:T(8,128)(2,1)S(1)} %bitcast.42), channel_id=1, source_target_pairs={{2,4},{3,5},{4,2},{5,3},{10,12},{11,13},{12,10},{13,11},{18,20},{1... | collective-permute-start | bytes 3538952 | tf_op jit(solution)/shard_map/ppermute | solution.py:170
  22.9 66.5 %collective-permute-start.2 = (bf16[768,768]{1,0:T(8,128)(2,1)S(1)}, bf16[768,768]{1,0:T(8,128)(2,1)}, u32[]{:S(2)}, u32[]{:S(2)}) collective-permute-start(bf16[768,768]{1,0:T(8,128)(2,1)S(1)} %bitcast.43), channel_id=1, source_target_pairs={{0,1},{1,0},{2,3},{3,2},{4,5},{5,4},{6,7},{7,6},{8,9},{9,8},{10,11... | collective-permute-start | bytes 3538952 | tf_op jit(solution)/shard_map/ppermute | solution.py:175
  23.2 70.8 %collective-permute-start.28 = (bf16[1280,768]{1,0:T(8,128)(2,1)S(1)}, bf16[1280,768]{1,0:T(8,128)(2,1)}, u32[]{:S(2)}, u32[]{:S(2)}) collective-permute-start(bf16[1280,768]{1,0:T(8,128)(2,1)S(1)} %pad_maximum_fusion.refs_1_), channel_id=1, source_target_pairs={{24,8},{16,0},{25,9},{17,1},{26,10},{18,2},{27,11},{19,3},{28,12},... | collective-permute-start | bytes 5898248 | tf_op jit(solution)/shard_map/ppermute | solution.py:179
  34.7 49.5 %collective-permute-start.24 = (bf16[1280,256]{1,0:T(8,128)(2,1)}, bf16[1280,256]{1,0:T(8,128)(2,1)}, u32[]{:S(2)}, u32[]{:S(2)}) collective-permute-start(bf16[1280,256]{1,0:T(8,128)(2,1)} %pad_maximum_fusion.2), channel_id=1, source_target_pairs={{24,8},{16,0},{25,9},{17,1},{26,10},{18,2},{27,11},{19,3},{28,12},... | collective-permute-start | bytes 1966088 | tf_op jit(solution)/shard_map/ppermute | solution.py:179
  84.2 6.1 %collective-permute-start.15 = (bf16[768,768]{1,0:T(8,128)(2,1)}, bf16[768,768]{1,0:T(8,128)(2,1)S(1)}, u32[]{:S(2)}, u32[]{:S(2)}) collective-permute-start(bf16[768,768]{1,0:T(8,128)(2,1)} %convolution_convert_fusion.4), channel_id=1, source_target_pairs={{0,1},{1,0},{2,3},{3,2},{4,5},{5,4},{6,7},{7,6},{8,9},{9,8},{10,11... | collective-permute-start | bytes 3538952 | tf_op jit(solution)/shard_map/ppermute | solution.py:175
  84.2 8.4 %collective-permute-start.9 = (bf16[768,768]{1,0:T(8,128)(2,1)}, bf16[768,768]{1,0:T(8,128)(2,1)S(1)}, u32[]{:S(2)}, u32[]{:S(2)}) collective-permute-start(bf16[768,768]{1,0:T(8,128)(2,1)} %collective-permute-done.3.refs_2_), channel_id=1, source_target_pairs={{2,4},{3,5},{4,2},{5,3},{10,12},{11,13},{12,10},{13,11},{18,20},{1... | collective-permute-start | bytes 3538952 | tf_op jit(solution)/shard_map/ppermute | solution.py:170
  86.2 48.2 %collective-permute-start.22 = (bf16[1280,768]{1,0:T(8,128)(2,1)S(1)}, bf16[1280,768]{1,0:T(8,128)(2,1)S(1)}, u32[]{:S(2)}, u32[]{:S(2)}) collective-permute-start(bf16[1280,768]{1,0:T(8,128)(2,1)S(1)} %pad_maximum_fusion.refs_1_), channel_id=1, source_target_pairs={{24,16},{8,0},{25,17},{9,1},{26,18},{10,2},{27,19},{11,3},{28,20},... | collective-permute-start | bytes 5898248 | tf_op jit(solution)/shard_map/ppermute | solution.py:179
  89.4 5.1 %copy-start.7 = (f32[256,768]{1,0:T(8,128)S(1)}, f32[256,768]{1,0:T(8,128)}, u32[]{:S(2)}) copy-start(f32[256,768]{1,0:T(8,128)} %copy-done.6) | copy-start | bytes 2359300
  89.4 1.9 collective-permute-start.20
  90.4 45.7 %collective-permute-start.7 = (bf16[768,768]{1,0:T(8,128)(2,1)}, bf16[768,768]{1,0:T(8,128)(2,1)S(1)}, u32[]{:S(2)}, u32[]{:S(2)}) collective-permute-start(bf16[768,768]{1,0:T(8,128)(2,1)} %collective-permute-done.5.refs_4_), channel_id=1, source_target_pairs={{0,1},{1,0},{2,3},{3,2},{4,5},{5,4},{6,7},{7,6},{8,9},{9,8},{10,11... | collective-permute-start | bytes 3538952 | tf_op jit(solution)/shard_map/ppermute | solution.py:175
  91.3 44.8 %collective-permute-start.6 = (bf16[768,768]{1,0:T(8,128)(2,1)}, bf16[768,768]{1,0:T(8,128)(2,1)S(1)}, u32[]{:S(2)}, u32[]{:S(2)}) collective-permute-start(bf16[768,768]{1,0:T(8,128)(2,1)} %collective-permute-done.5.refs_4_), channel_id=1, source_target_pairs={{2,0},{3,1},{4,6},{5,7},{10,8},{11,9},{12,14},{13,15},{18,16},{19,... | collective-permute-start | bytes 3538952 | tf_op jit(solution)/shard_map/ppermute | solution.py:170
  92.6 56.6 %collective-permute-start.10 = (bf16[768,768]{1,0:T(8,128)(2,1)S(1)}, bf16[768,768]{1,0:T(8,128)(2,1)S(1)}, u32[]{:S(2)}, u32[]{:S(2)}) collective-permute-start(bf16[768,768]{1,0:T(8,128)(2,1)S(1)} %collective-permute-done.9.refs_6_), channel_id=1, source_target_pairs={{2,0},{3,1},{4,6},{5,7},{10,8},{11,9},{12,14},{13,15},{18,16},{19,... | collective-permute-start | bytes 3538952 | tf_op jit(solution)/shard_map/ppermute | solution.py:170
  94.0 57.0 %collective-permute-start.4 = (bf16[768,768]{1,0:T(8,128)(2,1)}, bf16[768,768]{1,0:T(8,128)(2,1)S(1)}, u32[]{:S(2)}, u32[]{:S(2)}) collective-permute-start(bf16[768,768]{1,0:T(8,128)(2,1)} %collective-permute-done.3.refs_2_), channel_id=1, source_target_pairs={{0,1},{1,0},{2,3},{3,2},{4,5},{5,4},{6,7},{7,6},{8,9},{9,8},{10,11... | collective-permute-start | bytes 3538952 | tf_op jit(solution)/shard_map/ppermute | solution.py:175
  94.5 57.0 %copy-start.5 = (bf16[768,768]{1,0:T(8,128)(2,1)S(1)}, bf16[768,768]{1,0:T(8,128)(2,1)}, u32[]{:S(2)}) copy-start(bf16[768,768]{1,0:T(8,128)(2,1)} %convolution_convert_fusion.4) | copy-start | bytes 3538948
  134.5 45.0 %collective-permute-start.31 = (bf16[1280,768]{1,0:T(8,128)(2,1)}, bf16[1280,768]{1,0:T(8,128)(2,1)S(1)}, u32[]{:S(2)}, u32[]{:S(2)}) collective-permute-start(bf16[1280,768]{1,0:T(8,128)(2,1)} %collective-permute-done.28.refs_4_), channel_id=1, source_target_pairs={{0,8},{1,9},{2,10},{3,11},{4,12},{5,13},{6,14},{7,15}} | collective-permute-start | bytes 5898248 | tf_op jit(solution)/shard_map/ppermute | solution.py:179
  136.1 28.5 %collective-permute-start.11 = (bf16[768,768]{1,0:T(8,128)(2,1)S(1)}, bf16[768,768]{1,0:T(8,128)(2,1)S(1)}, u32[]{:S(2)}, u32[]{:S(2)}) collective-permute-start(bf16[768,768]{1,0:T(8,128)(2,1)S(1)} %collective-permute-done.9.refs_6_), channel_id=1, source_target_pairs={{0,1},{1,0},{2,3},{3,2},{4,5},{5,4},{6,7},{7,6},{8,9},{9,8},{10,11... | collective-permute-start | bytes 3538952 | tf_op jit(solution)/shard_map/ppermute | solution.py:175
  136.1 19.1 %collective-permute-start.8 = (bf16[768,768]{1,0:T(8,128)(2,1)S(1)}, bf16[768,768]{1,0:T(8,128)(2,1)S(1)}, u32[]{:S(2)}, u32[]{:S(2)}) collective-permute-start(bf16[768,768]{1,0:T(8,128)(2,1)S(1)} %collective-permute-done.6.refs_5_), channel_id=1, source_target_pairs={{0,1},{1,0},{2,3},{3,2},{4,5},{5,4},{6,7},{7,6},{8,9},{9,8},{10,11... | collective-permute-start | bytes 3538952 | tf_op jit(solution)/shard_map/ppermute | solution.py:175
  149.2 15.4 %collective-permute-start.12 = (bf16[768,768]{1,0:T(8,128)(2,1)S(1)}, bf16[768,768]{1,0:T(8,128)(2,1)S(1)}, u32[]{:S(2)}, u32[]{:S(2)}) collective-permute-start(bf16[768,768]{1,0:T(8,128)(2,1)S(1)} %collective-permute-done.10.refs_7_), channel_id=1, source_target_pairs={{0,1},{1,0},{2,3},{3,2},{4,5},{5,4},{6,7},{7,6},{8,9},{9,8},{10,11... | collective-permute-start | bytes 3538952 | tf_op jit(solution)/shard_map/ppermute | solution.py:175
  151.0 20.0 %collective-permute-start.23 = (bf16[768,768]{1,0:T(8,128)(2,1)S(1)}, bf16[768,768]{1,0:T(8,128)(2,1)S(1)}, u32[]{:S(2)}, u32[]{:S(2)}) collective-permute-start(bf16[768,768]{1,0:T(8,128)(2,1)S(1)} %convolution_convert_fusion.3), channel_id=1, source_target_pairs={{0,1},{1,0},{2,3},{3,2},{4,5},{5,4},{6,7},{7,6},{8,9},{9,8},{10,11... | collective-permute-start | bytes 3538952 | tf_op jit(solution)/shard_map/ppermute | solution.py:175
  155.3 37.3 %collective-permute-start.25 = (bf16[1280,256]{1,0:T(8,128)(2,1)}, bf16[1280,256]{1,0:T(8,128)(2,1)S(1)}, u32[]{:S(2)}, u32[]{:S(2)}) collective-permute-start(bf16[1280,256]{1,0:T(8,128)(2,1)} %collective-permute-done.24), channel_id=1, source_target_pairs={{0,8},{1,9},{2,10},{3,11},{4,12},{5,13},{6,14},{7,15}} | collective-permute-start | bytes 1966088 | tf_op jit(solution)/shard_map/ppermute | solution.py:179
  164.6 31.9 %collective-permute-start.29 = (bf16[768,768]{1,0:T(8,128)(2,1)S(1)}, bf16[768,768]{1,0:T(8,128)(2,1)S(1)}, u32[]{:S(2)}, u32[]{:S(2)}) collective-permute-start(bf16[768,768]{1,0:T(8,128)(2,1)S(1)} %convolution_convert_fusion.2), channel_id=1, source_target_pairs={{0,1},{1,0},{2,3},{3,2},{4,5},{5,4},{6,7},{7,6},{8,9},{9,8},{10,11... | collective-permute-start | bytes 3538952 | tf_op jit(solution)/shard_map/ppermute | solution.py:175
  164.6 47.6 %collective-permute-start.37 = (bf16[1280,768]{1,0:T(8,128)(2,1)S(1)}, bf16[1280,768]{1,0:T(8,128)(2,1)S(1)}, u32[]{:S(2)}, u32[]{:S(2)}) collective-permute-start(bf16[1280,768]{1,0:T(8,128)(2,1)S(1)} %collective-permute-done.22.refs_13_), channel_id=1, source_target_pairs={{16,0},{17,1},{18,2},{19,3},{20,4},{21,5},{22,6},{23,7}} | collective-permute-start | bytes 5898248 | tf_op jit(solution)/shard_map/ppermute | solution.py:179
  171.0 1.0 collective-permute-start.21
  192.6 5.9 %collective-permute-start.32 = (bf16[768,768]{1,0:T(8,128)(2,1)S(1)}, bf16[768,768]{1,0:T(8,128)(2,1)S(1)}, u32[]{:S(2)}, u32[]{:S(2)}) collective-permute-start(bf16[768,768]{1,0:T(8,128)(2,1)S(1)} %convolution_convert_fusion.1), channel_id=1, source_target_pairs={{0,1},{1,0},{2,3},{3,2},{4,5},{5,4},{6,7},{7,6},{8,9},{9,8},{10,11... | collective-permute-start | bytes 3538952 | tf_op jit(solution)/shard_map/ppermute | solution.py:175
  194.6 2.9 collective-permute-start.26
  195.2 30.6 %collective-permute-start.33 = (bf16[1280,256]{1,0:T(8,128)(2,1)}, bf16[1280,256]{1,0:T(8,128)(2,1)S(1)}, u32[]{:S(2)}, u32[]{:S(2)}) collective-permute-start(bf16[1280,256]{1,0:T(8,128)(2,1)} %collective-permute-done.19), channel_id=1, source_target_pairs={{16,0},{17,1},{18,2},{19,3},{20,4},{21,5},{22,6},{23,7}} | collective-permute-start | bytes 1966088 | tf_op jit(solution)/shard_map/ppermute | solution.py:179
  196.8 2.0 collective-permute-start.27
  197.5 1.3 collective-permute-start.30
  214.0 16.6 %collective-permute-start.38 = (bf16[768,768]{1,0:T(8,128)(2,1)S(1)}, bf16[768,768]{1,0:T(8,128)(2,1)S(1)}, u32[]{:S(2)}, u32[]{:S(2)}) collective-permute-start(bf16[768,768]{1,0:T(8,128)(2,1)S(1)} %convolution_convert_fusion), channel_id=1, source_target_pairs={{0,1},{1,0},{2,3},{3,2},{4,5},{5,4},{6,7},{7,6},{8,9},{9,8},{10,11... | collective-permute-start | bytes 3538952 | tf_op jit(solution)/shard_map/ppermute | solution.py:175
  226.5 4.0 %collective-permute-start.34 = (f32[128,768]{1,0:T(8,128)S(1)}, f32[128,768]{1,0:T(8,128)S(1)}, u32[]{:S(2)}, u32[]{:S(2)}) collective-permute-start(f32[128,768]{1,0:T(8,128)S(1)} %slice.217), channel_id=1, source_target_pairs={{0,1},{1,0},{2,3},{3,2},{4,5},{5,4},{6,7},{7,6},{8,9},{9,8},{10,11... | collective-permute-start | bytes 1179656 | tf_op jit(solution)/shard_map/ppermute | solution.py:175
  226.6 13.4 %collective-permute-start.35 = (bf16[128,768]{1,0:T(8,128)(2,1)S(1)}, bf16[128,768]{1,0:T(8,128)(2,1)S(1)}, u32[]{:S(2)}, u32[]{:S(2)}) collective-permute-start(bf16[128,768]{1,0:T(8,128)(2,1)S(1)} %get-tuple-element.62), channel_id=1, source_target_pairs={{16,0},{17,1},{18,2},{19,3},{20,4},{21,5},{22,6},{23,7}} | collective-permute-start | bytes 589832 | tf_op jit(solution)/shard_map/ppermute | solution.py:179
  227.9 10.2 %collective-permute-start.36 = (bf16[128,768]{1,0:T(8,128)(2,1)S(1)}, bf16[128,768]{1,0:T(8,128)(2,1)S(1)}, u32[]{:S(2)}, u32[]{:S(2)}) collective-permute-start(bf16[128,768]{1,0:T(8,128)(2,1)S(1)} %get-tuple-element.68), channel_id=1, source_target_pairs={{24,0},{25,1},{26,2},{27,3},{28,4},{29,5},{30,6},{31,7}} | collective-permute-start | bytes 589832 | tf_op jit(solution)/shard_map/ppermute | solution.py:179
  229.2 10.8 %collective-permute-start.39 = (bf16[128,768]{1,0:T(8,128)(2,1)S(1)}, bf16[128,768]{1,0:T(8,128)(2,1)S(1)}, u32[]{:S(2)}, u32[]{:S(2)}) collective-permute-start(bf16[128,768]{1,0:T(8,128)(2,1)S(1)} %get-tuple-element.66), channel_id=1, source_target_pairs={{8,0},{9,1},{10,2},{11,3},{12,4},{13,5},{14,6},{15,7}} | collective-permute-start | bytes 589832 | tf_op jit(solution)/shard_map/ppermute | solution.py:179
  244.4 6.4 %collective-permute-start.47 = (bf16[128,768]{1,0:T(8,128)(2,1)S(1)}, bf16[128,768]{1,0:T(8,128)(2,1)S(1)}, u32[]{:S(2)}, u32[]{:S(2)}) collective-permute-start(bf16[128,768]{1,0:T(8,128)(2,1)S(1)} %get-tuple-element.78.refs_4_), channel_id=1, source_target_pairs={{0,2},{1,3},{2,0},{3,1},{4,6},{5,7},{6,4},{7,5},{8,10},{9,11},{10,... | collective-permute-start | bytes 589832 | tf_op jit(solution)/shard_map/ppermute | solution.py:170
  244.5 9.7 %copy-start.9 = (bf16[320,128]{1,0:T(8,128)(2,1)S(1)}, bf16[320,128]{1,0:T(8,128)(2,1)}, u32[]{:S(2)}) copy-start(bf16[320,128]{1,0:T(8,128)(2,1)} %get-tuple-element.102) | copy-start | bytes 245764
  244.5 9.7 %copy-start.11 = (bf16[320,128]{1,0:T(8,128)(2,1)S(1)}, bf16[320,128]{1,0:T(8,128)(2,1)}, u32[]{:S(2)}) copy-start(bf16[320,128]{1,0:T(8,128)(2,1)} %get-tuple-element.103) | copy-start | bytes 245764
  244.5 11.3 %collective-permute-start.44 = (bf16[128,768]{1,0:T(8,128)(2,1)S(1)}, bf16[128,768]{1,0:T(8,128)(2,1)S(1)}, u32[]{:S(2)}, u32[]{:S(2)}) collective-permute-start(bf16[128,768]{1,0:T(8,128)(2,1)S(1)} %add.239.refs_14_), channel_id=1, source_target_pairs={{0,1},{1,0},{2,3},{3,2},{4,5},{5,4},{6,7},{7,6},{8,9},{9,8},{10,11... | collective-permute-start | bytes 589832 | tf_op jit(solution)/shard_map/ppermute | solution.py:175
  250.9 1.8 collective-permute-start.49
  251.9 14.5 %collective-permute-start.45 = (bf16[128,768]{1,0:T(8,128)(2,1)S(1)}, bf16[128,768]{1,0:T(8,128)(2,1)S(1)}, u32[]{:S(2)}, u32[]{:S(2)}) collective-permute-start(bf16[128,768]{1,0:T(8,128)(2,1)S(1)} %get-tuple-element.112), channel_id=1, source_target_pairs={{0,1},{1,0},{2,3},{3,2},{4,5},{5,4},{6,7},{7,6},{8,9},{9,8},{10,11... | collective-permute-start | bytes 589832 | tf_op jit(solution)/shard_map/ppermute | solution.py:175
  251.9 15.6 %collective-permute-start.40 = (bf16[128,768]{1,0:T(8,128)(2,1)S(1)}, bf16[128,768]{1,0:T(8,128)(2,1)S(1)}, u32[]{:S(2)}, u32[]{:S(2)}) collective-permute-start(bf16[128,768]{1,0:T(8,128)(2,1)S(1)} %get-tuple-element.72.refs_1_.refs_2_.refs_9_), channel_id=1, source_target_pairs={{0,1},{1,0},{2,3},{3,2},{4,5},{5,4},{6,7},{7,6},{8,9},{9,8},{10,11... | collective-permute-start | bytes 589832 | tf_op jit(solution)/shard_map/ppermute | solution.py:175
  252.5 16.5 %collective-permute-start.41 = (bf16[128,768]{1,0:T(8,128)(2,1)S(1)}, bf16[128,768]{1,0:T(8,128)(2,1)S(1)}, u32[]{:S(2)}, u32[]{:S(2)}) collective-permute-start(bf16[128,768]{1,0:T(8,128)(2,1)S(1)} %add.238.refs_5_), channel_id=1, source_target_pairs={{0,1},{1,0},{2,3},{3,2},{4,5},{5,4},{6,7},{7,6},{8,9},{9,8},{10,11... | collective-permute-start | bytes 589832 | tf_op jit(solution)/shard_map/ppermute | solution.py:175
  252.6 30.1 %collective-permute-start.50 = (bf16[256,768]{1,0:T(8,128)(2,1)S(1)}, bf16[256,768]{1,0:T(8,128)(2,1)S(1)}, u32[]{:S(2)}, u32[]{:S(2)}) collective-permute-start(bf16[256,768]{1,0:T(8,128)(2,1)S(1)} %collective-permute-done.49), channel_id=1, source_target_pairs={{2,0},{3,1},{4,6},{5,7},{10,8},{11,9},{12,14},{13,15},{18,16},{19,... | collective-permute-start | bytes 1179656 | tf_op jit(solution)/shard_map/ppermute | solution.py:170
  255.8 48.1 %collective-permute-start.16 = (bf16[896,256]{1,0:T(8,128)(2,1)S(1)}, bf16[896,256]{1,0:T(8,128)(2,1)S(1)}, u32[]{:S(2)}, u32[]{:S(2)}) collective-permute-start(bf16[896,256]{1,0:T(8,128)(2,1)S(1)} %get-tuple-element.52), channel_id=1, source_target_pairs={{0,2},{1,3},{2,0},{3,1},{4,6},{5,7},{6,4},{7,5},{8,10},{9,11},{10,... | collective-permute-start | bytes 1376264 | tf_op jit(solution)/shard_map/ppermute | solution.py:170
  266.3 37.5 %collective-permute-start.17 = (bf16[896,256]{1,0:T(8,128)(2,1)S(1)}, bf16[896,256]{1,0:T(8,128)(2,1)S(1)}, u32[]{:S(2)}, u32[]{:S(2)}) collective-permute-start(bf16[896,256]{1,0:T(8,128)(2,1)S(1)} %get-tuple-element.53), channel_id=1, source_target_pairs={{0,4},{1,5},{2,6},{3,7},{4,0},{5,1},{6,2},{7,3},{8,12},{9,13},{10,... | collective-permute-start | bytes 1376264 | tf_op jit(solution)/shard_map/ppermute | solution.py:170
  267.6 36.3 %collective-permute-start.18 = (bf16[896,256]{1,0:T(8,128)(2,1)S(1)}, bf16[896,256]{1,0:T(8,128)(2,1)S(1)}, u32[]{:S(2)}, u32[]{:S(2)}) collective-permute-start(bf16[896,256]{1,0:T(8,128)(2,1)S(1)} %get-tuple-element.54), channel_id=1, source_target_pairs={{0,6},{1,7},{2,4},{3,5},{4,2},{5,3},{6,0},{7,1},{8,14},{9,15},{10,... | collective-permute-start | bytes 1376264 | tf_op jit(solution)/shard_map/ppermute | solution.py:170
  269.0 13.7 %collective-permute-start.42 = (bf16[128,768]{1,0:T(8,128)(2,1)S(1)}, bf16[128,768]{1,0:T(8,128)(2,1)S(1)}, u32[]{:S(2)}, u32[]{:S(2)}) collective-permute-start(bf16[128,768]{1,0:T(8,128)(2,1)S(1)} %collective-permute-done.30.refs_7_.refs_8_), channel_id=1, source_target_pairs={{0,1},{1,0},{2,3},{3,2},{4,5},{5,4},{6,7},{7,6},{8,9},{9,8},{10,11... | collective-permute-start | bytes 589832 | tf_op jit(solution)/shard_map/ppermute | solution.py:175
  282.7 1.4 collective-permute-start.43
  282.8 29.8 %collective-permute-start.51 = (bf16[256,768]{1,0:T(8,128)(2,1)S(1)}, bf16[256,768]{1,0:T(8,128)(2,1)S(1)}, u32[]{:S(2)}, u32[]{:S(2)}) collective-permute-start(bf16[256,768]{1,0:T(8,128)(2,1)S(1)} %broadcast_select_fusion.refs_8_), channel_id=1, source_target_pairs={{0,1},{1,0},{2,3},{3,2},{4,5},{5,4},{6,7},{7,6},{8,9},{9,8},{10,11... | collective-permute-start | bytes 1179656 | tf_op jit(solution)/shard_map/ppermute | solution.py:175
  288.9 20.0 %collective-permute-start.46 = (bf16[128,768]{1,0:T(8,128)(2,1)S(1)}, bf16[128,768]{1,0:T(8,128)(2,1)S(1)}, u32[]{:S(2)}, u32[]{:S(2)}) collective-permute-start(bf16[128,768]{1,0:T(8,128)(2,1)S(1)} %get-tuple-element.78.refs_4_), channel_id=1, source_target_pairs={{0,1},{1,0},{2,3},{3,2},{4,5},{5,4},{6,7},{7,6},{8,9},{9,8},{10,11... | collective-permute-start | bytes 589832 | tf_op jit(solution)/shard_map/ppermute | solution.py:175
  303.8 8.7 %collective-permute-start.52 = (bf16[512,256]{1,0:T(8,128)(2,1)S(1)}, bf16[512,256]{1,0:T(8,128)(2,1)S(1)}, u32[]{:S(2)}, u32[]{:S(2)}) collective-permute-start(bf16[512,256]{1,0:T(8,128)(2,1)S(1)} %get-tuple-element.80), channel_id=1, source_target_pairs={{0,2},{1,3},{2,0},{3,1},{4,6},{5,7},{6,4},{7,5},{8,10},{9,11},{10,... | collective-permute-start | bytes 786440 | tf_op jit(solution)/shard_map/ppermute | solution.py:170
  303.8 6.3 %collective-permute-start.48 = (bf16[128,768]{1,0:T(8,128)(2,1)S(1)}, bf16[128,768]{1,0:T(8,128)(2,1)S(1)}, u32[]{:S(2)}, u32[]{:S(2)}) collective-permute-start(bf16[128,768]{1,0:T(8,128)(2,1)S(1)} %collective-permute-done.47.refs_6_), channel_id=1, source_target_pairs={{0,1},{1,0},{2,3},{3,2},{4,5},{5,4},{6,7},{7,6},{8,9},{9,8},{10,11... | collective-permute-start | bytes 589832 | tf_op jit(solution)/shard_map/ppermute | solution.py:175
  303.9 22.9 %collective-permute-start.53 = (bf16[512,256]{1,0:T(8,128)(2,1)S(1)}, bf16[512,256]{1,0:T(8,128)(2,1)S(1)}, u32[]{:S(2)}, u32[]{:S(2)}) collective-permute-start(bf16[512,256]{1,0:T(8,128)(2,1)S(1)} %get-tuple-element.81), channel_id=1, source_target_pairs={{0,4},{1,5},{2,6},{3,7},{4,0},{5,1},{6,2},{7,3},{8,12},{9,13},{10,... | collective-permute-start | bytes 786440 | tf_op jit(solution)/shard_map/ppermute | solution.py:170
  308.9 17.8 %collective-permute-start.54 = (bf16[512,256]{1,0:T(8,128)(2,1)S(1)}, bf16[512,256]{1,0:T(8,128)(2,1)S(1)}, u32[]{:S(2)}, u32[]{:S(2)}) collective-permute-start(bf16[512,256]{1,0:T(8,128)(2,1)S(1)} %get-tuple-element.82), channel_id=1, source_target_pairs={{0,6},{1,7},{2,4},{3,5},{4,2},{5,3},{6,0},{7,1},{8,14},{9,15},{10,... | collective-permute-start | bytes 786440 | tf_op jit(solution)/shard_map/ppermute | solution.py:170
  310.2 16.6 %collective-permute-start.57 = (bf16[384,256]{1,0:T(8,128)(2,1)S(1)}, bf16[384,256]{1,0:T(8,128)(2,1)S(1)}, u32[]{:S(2)}, u32[]{:S(2)}) collective-permute-start(bf16[384,256]{1,0:T(8,128)(2,1)S(1)} %slice.180), channel_id=1, source_target_pairs={{0,1},{1,0},{2,3},{3,2},{4,5},{5,4},{6,7},{7,6},{8,9},{9,8},{10,11... | collective-permute-start | bytes 589832 | tf_op jit(solution)/shard_map/ppermute | solution.py:175
  312.5 14.2 %collective-permute-start.56 = (bf16[384,256]{1,0:T(8,128)(2,1)S(1)}, bf16[384,256]{1,0:T(8,128)(2,1)S(1)}, u32[]{:S(2)}, u32[]{:S(2)}) collective-permute-start(bf16[384,256]{1,0:T(8,128)(2,1)S(1)} %slice.179), channel_id=1, source_target_pairs={{0,1},{1,0},{2,3},{3,2},{4,5},{5,4},{6,7},{7,6},{8,9},{9,8},{10,11... | collective-permute-start | bytes 589832 | tf_op jit(solution)/shard_map/ppermute | solution.py:175
  312.5 14.2 %collective-permute-start.55 = (bf16[384,256]{1,0:T(8,128)(2,1)S(1)}, bf16[384,256]{1,0:T(8,128)(2,1)S(1)}, u32[]{:S(2)}, u32[]{:S(2)}) collective-permute-start(bf16[384,256]{1,0:T(8,128)(2,1)S(1)} %slice.178), channel_id=1, source_target_pairs={{0,1},{1,0},{2,3},{3,2},{4,5},{5,4},{6,7},{7,6},{8,9},{9,8},{10,11... | collective-permute-start | bytes 589832 | tf_op jit(solution)/shard_map/ppermute | solution.py:175
  (14 other events, 38.5 us)
